TPU v7x, 256 devices: a whole 4x4x8 slice. The times are simulated.
256 devices in a mesh: gx: 16 (over z, x_lo), gy: 16 (over x_hi, y, core).
Axes of the slice: x: 4 (x_hi: 2, x_lo: 2; x = x_hi * 2 + x_lo), y: 4, z: 8, core: 2. Of those that a mesh axis runs over, the one named last changes fastest.
Arguments:
- object_field: float32 [2, 4096, 4096], P(None, 'gx', 'gy'), may hold values from -4.5 to 4.5
- probe_field: float32 [2, 2, 256, 256], replicated, may hold values from -4.2 to 4.2
- amplitude: float32 [64, 16, 256, 256], P('gx', 'gy'), may hold values from 0.2 to 3
- offsets: int32 [64, 16, 2], P('gx', 'gy'), may hold values from -128 to 128
Outputs:
- updated_object: float32 [2, 4096, 4096], P(None, 'gx', 'gy')
- updated_probe: float32 [2, 2, 256, 256], replicated
All inputs are finite; a program needn't handle non-finite values.
Results may differ from a plain program's by a relative error of at most 0.0006.
The roundings to bfloat16 on the way count: a program that leaves them out, or rounds other values in their place, can miss the bound.
Values sent between devices are 32-bit elements; how exact they have to be, the bound alone decides.
No kernel may reach another device: no remote copies, remote signals or barrier semaphores. Data moves between devices by JAX's collectives and lax.ppermute only.
A program may use at most 64 MiB of HBM per device.

v0:
```python
import math

import jax
import jax.numpy as jnp
from jax import lax
from jax.sharding import PartitionSpec as P


def extended_2(array, sides, width):
    for axis, dim in sides:
        size, length = (lax.axis_size(axis), array.shape[dim])
        up = [(i, (i + 1) % size) for i in range(size)]
        down = [(j, i) for i, j in up]
        last = lax.slice_in_dim(array, length - width, length, axis=dim)
        leading = lax.slice_in_dim(array, 0, width, axis=dim)
        before = lax.ppermute(last, axis, up)
        after = lax.ppermute(leading, axis, down)
        array = jnp.concatenate([before, array, after], axis=dim)
    return array


def dft_tables(extent):
    indices = jnp.arange(extent, dtype=jnp.int32)
    phases = indices[:, None] * indices[None, :] % extent
    angles = phases.astype(jnp.float32) * (2.0 * math.pi / extent)
    norm_factor = 1.0 / math.sqrt(extent)
    return (
        (jnp.cos(angles) * norm_factor).astype(jnp.bfloat16),
        (jnp.sin(angles) * norm_factor).astype(jnp.bfloat16),
    )


def row_pass(cosine, sine, real_part, imag_part, orient):
    amount = real_part.shape[0]
    stacked = jnp.concatenate([real_part, imag_part], 0)
    with_cos = jnp.einsum("jk,bkl->bjl", cosine, stacked, preferred_element_type=jnp.float32)
    with_sin = jnp.einsum("jk,bkl->bjl", sine, stacked, preferred_element_type=jnp.float32)
    return (
        with_cos[:amount] + orient * with_sin[amount:],
        with_cos[amount:] - orient * with_sin[:amount],
    )


def col_pass(cosine, sine, real_part, imag_part, orient):
    amount = real_part.shape[0]
    stacked = jnp.concatenate([real_part, imag_part], 0)
    with_cos = jnp.einsum("bjk,kl->bjl", stacked, cosine, preferred_element_type=jnp.float32)
    with_sin = jnp.einsum("bjk,kl->bjl", stacked, sine, preferred_element_type=jnp.float32)
    return (
        with_cos[:amount] + orient * with_sin[amount:],
        with_cos[amount:] - orient * with_sin[:amount],
    )


def corrections(windows, probe_field, amplitude, cosine, sine):
    extent = probe_field.shape[-1]
    obj_real = windows[:, None, 0]
    obj_imag = windows[:, None, 1]
    probe_real = probe_field[None, :, 0]
    probe_imag = probe_field[None, :, 1]
    psi_real = probe_real * obj_real - probe_imag * obj_imag
    psi_imag = probe_real * obj_imag + probe_imag * obj_real
    amount = psi_real.shape[0]
    mode_count = psi_real.shape[1]
    shape_flat = (amount * mode_count, extent, extent)
    shape_full = (amount, mode_count, extent, extent)
    half_type = jnp.bfloat16
    rows_real, rows_imag = row_pass(
        cosine,
        sine,
        psi_real.reshape(shape_flat).astype(half_type),
        psi_imag.reshape(shape_flat).astype(half_type),
        1.0,
    )
    far_real, far_imag = col_pass(
        cosine, sine, rows_real.astype(half_type), rows_imag.astype(half_type), 1.0
    )
    far_real = far_real.reshape(shape_full)
    far_imag = far_imag.reshape(shape_full)
    intensity = jnp.sum(far_real * far_real + far_imag * far_imag, axis=1)
    factor = (amplitude / jnp.maximum(jnp.sqrt(intensity), 0.25))[:, None]
    proj_real = (far_real * factor).reshape(shape_flat).astype(half_type)
    proj_imag = (far_imag * factor).reshape(shape_flat).astype(half_type)
    back_rows_real, back_rows_imag = row_pass(cosine, sine, proj_real, proj_imag, -1.0)
    back_real, back_imag = col_pass(
        cosine, sine, back_rows_real.astype(half_type), back_rows_imag.astype(half_type), -1.0
    )
    diff_real = back_real.reshape(shape_full) - psi_real
    diff_imag = back_imag.reshape(shape_full) - psi_imag
    object_real = jnp.sum(probe_real * diff_real + probe_imag * diff_imag, axis=1)
    object_imag = jnp.sum(probe_real * diff_imag - probe_imag * diff_real, axis=1)
    grad_real = jnp.sum(obj_real * diff_real + obj_imag * diff_imag, axis=0)
    grad_imag = jnp.sum(obj_real * diff_imag - obj_imag * diff_real, axis=0)
    weight = jnp.sum(windows[:, 0] * windows[:, 0] + windows[:, 1] * windows[:, 1], axis=0)
    return (jnp.stack([object_real, object_imag], 1), grad_real, grad_imag, weight)


def body(object_field, probe_field, amplitude, offsets):
    extent = probe_field.shape[-1]
    margin = extent // 2
    tile_size = object_field.shape[1]
    extended = extended_2(object_field, (("gx", 1), ("gy", 2)), margin)
    starts = offsets[:, 0, :] + margin

    def take_window(row_start, col_start):
        return lax.dynamic_slice(extended, (0, row_start, col_start), (2, extent, extent))

    windows = jax.vmap(take_window)(starts[:, 0], starts[:, 1])
    cosine, sine = dft_tables(extent)
    object_terms, grad_real, grad_imag, weight = corrections(
        windows, probe_field, amplitude[:, 0], cosine, sine
    )

    def add_window(position, accum):
        where = (0, starts[position, 0], starts[position, 1])
        current = lax.dynamic_slice(accum, where, (2, extent, extent))
        return lax.dynamic_update_slice(accum, current + object_terms[position], where)

    accum = lax.fori_loop(0, starts.shape[0], add_window, jnp.zeros_like(extended))
    rows_total = accum.shape[1]
    gap_cols = jnp.zeros((2, rows_total, tile_size - 2 * margin), jnp.float32)
    outgoing = jnp.concatenate(
        [accum[:, :, :margin], gap_cols, accum[:, :, tile_size + margin :]], 2
    )
    incoming = extended_2(outgoing, (("gy", 2),), margin)
    folded = accum[:, :, margin : tile_size + margin] + jnp.concatenate(
        [incoming[:, :, :margin], gap_cols, incoming[:, :, tile_size + margin :]], 2
    )
    gap_rows = jnp.zeros((2, tile_size - 2 * margin, tile_size), jnp.float32)
    outgoing_rows = jnp.concatenate(
        [folded[:, :margin], gap_rows, folded[:, tile_size + margin :]], 1
    )
    incoming_rows = extended_2(outgoing_rows, (("gx", 1),), margin)
    object_step = folded[:, margin : tile_size + margin] + jnp.concatenate(
        [incoming_rows[:, :margin], gap_rows, incoming_rows[:, tile_size + margin :]], 1
    )
    power = jnp.sum(probe_field * probe_field, axis=(0, 1))
    scale_max = jnp.max(power) + 1e-06
    updated_object = object_field + object_step / scale_max
    total_real, total_imag, total_weight = lax.psum((grad_real, grad_imag, weight), ("gx", "gy"))
    updated_probe = probe_field + jnp.stack([total_real, total_imag], 1) / (total_weight + 1e-05)
    return (updated_object, updated_probe)


def solution(mesh):
    in_specs = (P(None, "gx", "gy"), P(), P("gx", "gy", None, None), P("gx", "gy", None))
    out_specs = (P(None, "gx", "gy"), P())
    return jax.shard_map(body, mesh=mesh, in_specs=in_specs, out_specs=out_specs, check_vma=False)
```

profile of v0, /device:TPU:1, one launch (start us, length us, event | category | flops | bytes accessed | tf_op | source)
XLA Modules:
  0.0 422.2 jit_solution(3478085513682789013)
XLA Ops:
  7.2 1.1 fusion.90
  8.3 2.1 collective-permute-start
  10.4 5.4 %collective-permute-start.1 = (f32[2,128,256]{2,1,0:T(8,128)S(1)}, f32[2,128,256]{2,1,0:T(8,128)S(1)}, u32[]{:S(2)}, u32[]{:S(2)}) collective-permute-start(f32[2,128,256]{2,1,0:T(8,128)S(1)} %get-tuple-element.171), channel_id=1, source_target_pairs={{16,0},{32,16},{48,32},{64,48},{80,64},{96,80},{112,96},{128,112},... | collective-permute-start | bytes 786440 | tf_op jit(solution)/shard_map/ppermute | solution.py:17
  16.5 5.3 %collective-permute-done = f32[2,128,256]{2,1,0:T(8,128)S(1)} collective-permute-done((f32[2,128,256]{2,1,0:T(8,128)S(1)}, f32[2,128,256]{2,1,0:T(8,128)S(1)}, u32[]{:S(2)}, u32[]{:S(2)}) %collective-permute-start) | collective-permute-done | bytes 262176 | tf_op jit(solution)/shard_map/ppermute | solution.py:16
  21.8 1.1 constant_dynamic-update-slice_fusion.1
  22.9 1.0 fusion.89
  23.9 3.2 collective-permute-start.2
  28.4 1.0 copy.64
  29.4 4.2 collective-permute-done.2
  33.6 2.8 collective-permute-done.3
  36.3 1.4 pad_maximum_fusion
  37.8 11.6 %while.15 = (s32[]{:T(128)}, f32[2,512,512]{2,1,0:T(8,128)S(1)}, s32[4,3]{1,0:T(4,128)S(1)}, f32[4,2,256,256]{3,2,1,0:T(8,128)}, s32[]{:T(128)}) while((s32[]{:T(128)}, f32[2,512,512]{2,1,0:T(8,128)S(1)}, s32[4,3]{1,0:T(4,128)S(1)}, f32[4,2,256,256]{3,2,1,0:T(8,128)}, s32[]{:T(128)}) %tuple.74), condition=%wide.while_cond, body=%wide.while_body.sunk | while | flops 2 | bytes 1050217 | solution.py:106
  38.4 2.3 bitcast_dynamic-update-slice_fusion.2
  41.3 2.3 bitcast_dynamic-update-slice_fusion.2
  44.1 2.3 bitcast_dynamic-update-slice_fusion.2
  47.1 2.3 bitcast_dynamic-update-slice_fusion.2
  49.4 1.4 slice_bitcast_fusion.1
  51.3 1.0 slice_bitcast_fusion
  52.6 1.6 copy.66
  54.8 1.7 convolution_bitcast_fusion.3
  56.5 1.7 convolution_bitcast_fusion.2
  59.1 1.7 fusion.17
  60.8 1.7 fusion.16
  64.1 1.0 fusion
  65.1 1.9 convolution_bitcast_fusion.1
  67.0 1.7 convolution_bitcast_fusion
  69.7 1.8 fusion.15
  71.4 1.8 fusion.14
  73.8 3.3 add_reduce_fusion
  77.1 1.5 pad_maximum_fusion.5
  78.8 60.7 %while.14 = (s32[]{:T(128)}, f32[2,512,512]{2,1,0:T(8,128)S(1)}, s32[4,2]{0,1:T(2,128)S(1)}, f32[4,2,256,256]{2,3,0,1:T(8,128)}, s32[]{:T(128)}, /*index=5*/s32[]{:T(128)}, s32[]{:T(128)}) while((s32[]{:T(128)}, f32[2,512,512]{2,1,0:T(8,128)S(1)}, s32[4,2]{0,1:T(2,128)S(1)}, f32[4,2,256,256]{2,3,0,1:T(8,128)}, s32[]{:T(128)}, ...), condition=%wide.region_4.5_spmd, body=%wide.region_3.4_spmd.sunk | while | flops 131080 | bytes 4718773 | solution.py:119
  83.4 1.1 constant_dynamic-slice_fusion.7
  84.9 7.9 %dynamic_update_slice.8 = f32[2,512,512]{2,1,0:T(8,128)S(1)} dynamic-update-slice(f32[2,512,512]{2,1,0:T(8,128)S(1)} %get-tuple-element.256, f32[2,256,256]{2,1,0:T(8,128)S(1)} %bitcast_add_fusion.2, s32[]{:T(128)} %constant.54.clone.1..sunk, s32[]{:T(128)S(6)} %select_n.76, s32[]{:T(128)S(6)} %select_n.77) | dynamic-update-slice | bytes 1048580 | tf_op jit(solution)/shard_map/while/body/eval_jaxpr/dynamic_update_slice | solution.py:117
  97.5 1.1 constant_dynamic-slice_fusion.7
  99.0 10.8 %dynamic_update_slice.8 = f32[2,512,512]{2,1,0:T(8,128)S(1)} dynamic-update-slice(f32[2,512,512]{2,1,0:T(8,128)S(1)} %get-tuple-element.256, f32[2,256,256]{2,1,0:T(8,128)S(1)} %bitcast_add_fusion.2, s32[]{:T(128)} %constant.54.clone.1..sunk, s32[]{:T(128)S(6)} %select_n.76, s32[]{:T(128)S(6)} %select_n.77) | dynamic-update-slice | bytes 1048580 | tf_op jit(solution)/shard_map/while/body/eval_jaxpr/dynamic_update_slice | solution.py:117
  114.4 1.1 constant_dynamic-slice_fusion.7
  116.0 8.9 %dynamic_update_slice.8 = f32[2,512,512]{2,1,0:T(8,128)S(1)} dynamic-update-slice(f32[2,512,512]{2,1,0:T(8,128)S(1)} %get-tuple-element.256, f32[2,256,256]{2,1,0:T(8,128)S(1)} %bitcast_add_fusion.2, s32[]{:T(128)} %constant.54.clone.1..sunk, s32[]{:T(128)S(6)} %select_n.76, s32[]{:T(128)S(6)} %select_n.77) | dynamic-update-slice | bytes 1048580 | tf_op jit(solution)/shard_map/while/body/eval_jaxpr/dynamic_update_slice | solution.py:117
  129.5 1.1 constant_dynamic-slice_fusion.7
  131.0 8.5 %dynamic_update_slice.8 = f32[2,512,512]{2,1,0:T(8,128)S(1)} dynamic-update-slice(f32[2,512,512]{2,1,0:T(8,128)S(1)} %get-tuple-element.256, f32[2,256,256]{2,1,0:T(8,128)S(1)} %bitcast_add_fusion.2, s32[]{:T(128)} %constant.54.clone.1..sunk, s32[]{:T(128)S(6)} %select_n.76, s32[]{:T(128)S(6)} %select_n.77) | dynamic-update-slice | bytes 1048580 | tf_op jit(solution)/shard_map/while/body/eval_jaxpr/dynamic_update_slice | solution.py:117
  139.5 1.0 fusion.87
  141.1 1.3 copy.79
  142.4 2.4 add_reduce_fusion.2
  147.0 2.8 collective-permute-done.5
  149.8 1.4 maximum_add_fusion
  152.2 6.9 %collective-permute-start.7 = (f32[2,128,256]{2,1,0:T(8,128)}, f32[2,128,256]{2,1,0:T(8,128)S(1)}, u32[]{:S(2)}, u32[]{:S(2)}) collective-permute-start(f32[2,128,256]{2,1,0:T(8,128)} %get-tuple-element.166), channel_id=1, source_target_pairs={{16,0},{32,16},{48,32},{64,48},{80,64},{96,80},{112,96},{128,112},... | collective-permute-start | bytes 786440 | tf_op jit(solution)/shard_map/ppermute | solution.py:17
  159.1 251.2 %all-reduce.3.cloned.1.call-done = (f32[2,1,256,256]{2,3,0,1:T(8,128)}, f32[2,1,256,256]{2,3,0,1:T(8,128)}, f32[256,256]{1,0:T(8,128)}) async-done(((f32[2,1,256,256]{2,3,0,1:T(8,128)}, f32[2,1,256,256]{2,3,0,1:T(8,128)}, f32[256,256]{1,0:T(8,128)}), (f32[2,1,256,256]{2,3,0,1:T(8,128)}, f32[2,1,256,256]{2,3,0,1:T(8,128)}, f32[256,256]{1,0:T(8,128)})) %all-reduce.3.cloned.1.call-update) | async-done | bytes 1310736 | tf_op jit(solution)/shard_map/psum | solution.py:140
  411.4 1.7 fusion.18
  413.1 1.3 copy.80
  (68 shorter events, 19.4 us)
Async XLA Ops:
  7.2 403.1 %all-reduce.3.cloned.1.call-start = ((), (), s32[]{:S(2)}) async-start(), calls=%async_computation | async-start | bytes 2621440 | tf_op jit(solution)/shard_map/psum | solution.py:140
  8.3 13.5 %collective-permute-start = (f32[2,128,256]{2,1,0:T(8,128)S(1)}, f32[2,128,256]{2,1,0:T(8,128)S(1)}, u32[]{:S(2)}, u32[]{:S(2)}) collective-permute-start(f32[2,128,256]{2,1,0:T(8,128)S(1)} %get-tuple-element.172), channel_id=1, source_target_pairs={{0,16},{16,32},{32,48},{48,64},{64,80},{80,96},{96,112},{112,128},... | collective-permute-start | bytes 786440 | tf_op jit(solution)/shard_map/ppermute | solution.py:16
  10.4 12.5 %collective-permute-start.1 = (f32[2,128,256]{2,1,0:T(8,128)S(1)}, f32[2,128,256]{2,1,0:T(8,128)S(1)}, u32[]{:S(2)}, u32[]{:S(2)}) collective-permute-start(f32[2,128,256]{2,1,0:T(8,128)S(1)} %get-tuple-element.171), channel_id=1, source_target_pairs={{16,0},{32,16},{48,32},{64,48},{80,64},{96,80},{112,96},{128,112},... | collective-permute-start | bytes 786440 | tf_op jit(solution)/shard_map/ppermute | solution.py:17
  16.5 10.8 %copy-start = (f32[2,2,256,256]{3,2,1,0:T(8,128)S(1)}, f32[2,2,256,256]{3,2,1,0:T(8,128)}, u32[]{:S(2)}) copy-start(f32[2,2,256,256]{3,2,1,0:T(8,128)} %param.7) | copy-start | bytes 3145732
  23.9 9.6 %collective-permute-start.2 = (f32[2,512,128]{2,1,0:T(8,128)}, f32[2,512,128]{2,1,0:T(8,128)}, u32[]{:S(2)}, u32[]{:S(2)}) collective-permute-start(f32[2,512,128]{2,1,0:T(8,128)} %get-tuple-element.169), channel_id=1, source_target_pairs={{0,1},{1,2},{2,3},{3,4},{4,5},{5,6},{6,7},{7,8},{8,9},{9,10},{10,1... | collective-permute-start | bytes 1572872 | tf_op jit(solution)/shard_map/ppermute | solution.py:16
  27.1 9.2 %collective-permute-start.3 = (f32[2,512,128]{2,1,0:T(8,128)}, f32[2,512,128]{2,1,0:T(8,128)}, u32[]{:S(2)}, u32[]{:S(2)}) collective-permute-start(f32[2,512,128]{2,1,0:T(8,128)} %get-tuple-element.170), channel_id=1, source_target_pairs={{1,0},{2,1},{3,2},{4,3},{5,4},{6,5},{7,6},{8,7},{9,8},{10,9},{11,1... | collective-permute-start | bytes 1572872 | tf_op jit(solution)/shard_map/ppermute | solution.py:17
  49.4 1.9 copy-start.2
  52.3 1.9 copy-start.3
  52.3 1.9 copy-start.4
  62.5 1.2 copy-start.6
  139.5 1.6 copy-start.1
  140.6 6.4 %collective-permute-start.4 = (f32[2,512,128]{2,1,0:T(8,128)}, f32[2,512,128]{2,1,0:T(8,128)}, u32[]{:S(2)}, u32[]{:S(2)}) collective-permute-start(f32[2,512,128]{2,1,0:T(8,128)} %get-tuple-element.163), channel_id=1, source_target_pairs={{0,1},{1,2},{2,3},{3,4},{4,5},{5,6},{6,7},{7,8},{8,9},{9,10},{10,1... | collective-permute-start | bytes 1572872 | tf_op jit(solution)/shard_map/ppermute | solution.py:16
  140.6 9.2 %collective-permute-start.5 = (f32[2,512,128]{2,1,0:T(8,128)}, f32[2,512,128]{2,1,0:T(8,128)}, u32[]{:S(2)}, u32[]{:S(2)}) collective-permute-start(f32[2,512,128]{2,1,0:T(8,128)} %get-tuple-element.164), channel_id=1, source_target_pairs={{1,0},{2,1},{3,2},{4,3},{5,4},{6,5},{7,6},{8,7},{9,8},{10,9},{11,1... | collective-permute-start | bytes 1572872 | tf_op jit(solution)/shard_map/ppermute | solution.py:17
  152.0 262.4 %collective-permute-start.6 = (f32[2,128,256]{2,1,0:T(8,128)}, f32[2,128,256]{2,1,0:T(8,128)S(1)}, u32[]{:S(2)}, u32[]{:S(2)}) collective-permute-start(f32[2,128,256]{2,1,0:T(8,128)} %get-tuple-element.165), channel_id=1, source_target_pairs={{0,16},{16,32},{32,48},{48,64},{64,80},{80,96},{96,112},{112,128},... | collective-permute-start | bytes 786440 | tf_op jit(solution)/shard_map/ppermute | solution.py:16
  152.2 262.3 %collective-permute-start.7 = (f32[2,128,256]{2,1,0:T(8,128)}, f32[2,128,256]{2,1,0:T(8,128)S(1)}, u32[]{:S(2)}, u32[]{:S(2)}) collective-permute-start(f32[2,128,256]{2,1,0:T(8,128)} %get-tuple-element.166), channel_id=1, source_target_pairs={{16,0},{32,16},{48,32},{64,48},{80,64},{96,80},{112,96},{128,112},... | collective-permute-start | bytes 786440 | tf_op jit(solution)/shard_map/ppermute | solution.py:17
  411.4 3.1 copy-start.5
Sparse Core Ops, SparseCore 0:
  145.0 265.2 all-reduce.2
where the time goes:
time: 424 us; the launch traced here: 422 us
  waiting for transfers between devices  267 us (63%)
  local copies, waits for them, and re-layouts  71.1 us (17%)
  other arithmetic  21 us (5%)
  starting transfers between devices  18.3 us (4%)
  loops' own time  16 us (4%)
  between operations  14.9 us (4%)
  matrix products  13.9 us (3%)
    psum x1, waiting for transfers between devices, body(): lax.psum((grad_real, grad_imag, weight), ('gx', 'gy'))  251 us
    dynamic_update_slice x4, local copies, waits for them, and re-layouts, add_window(): lax.dynamic_update_slice(accum, current + object_terms[position], where)  36.1 us
    another operation x1, loops' own time, body(): lax.fori_loop(0, starts.shape[0], add_window, jnp.zeros_like(extended))  16 us
    ppermute x4, starting transfers between devices, extended_2(): after = lax.ppermute(leading, axis, down)  12.8 us
    gather x12, local copies, waits for them, and re-layouts  11.6 us
    ppermute x4, waiting for transfers between devices, extended_2(): before = lax.ppermute(last, axis, up)  10.3 us
  transfers between devices with their start and end apart: 9, of which 6 were waited for; matrix products, arithmetic and copies ran while one was open for 4% of the time, Pallas kernels for 0%

commit v1 on v0

v1 whole, which is shorter than its diff:
```python
import functools
import math

import jax
import jax.numpy as jnp
import ml_dtypes
import numpy as np
from jax import lax
from jax.experimental import pallas as pl
from jax.experimental.pallas import tpu as pltpu
from jax.sharding import Mesh
from jax.sharding import PartitionSpec as P

W = 256
HALF = 128
POS = 4
MODES = 2
CH = 32
BF = jnp.bfloat16
F32 = jnp.float32


def dft_matrices():
    k = np.arange(W)
    phase = (k[:, None] * k[None, :]) % W
    angle = phase.astype(np.float32) * np.float32(2.0 * math.pi / W)
    norm = np.float32(1.0 / math.sqrt(W))
    c = (np.cos(angle) * norm).astype(ml_dtypes.bfloat16)
    s = (np.sin(angle) * norm).astype(ml_dtypes.bfloat16)
    fwd = np.block([[c, s], [-s, c]])
    bwd = np.block([[c, -s], [s, c]])
    return fwd, bwd


def kernel(
    offs, half, tile, top, bot, left, right, probe, amp, fwd, bwd,
    mine, other, acc,
    ext, win, stack, side, far, weight, grads,
):
    lanes = lax.broadcasted_iota(jnp.int32, (CH, HALF), 1)
    for q in range(2):
        cols = pl.ds(q * HALF, HALF)
        ext[:, q + 1, 0:HALF, :] = top[:, :, cols]
        ext[:, q + 1, HALF : HALF + W, :] = tile[:, :, cols]
        ext[:, q + 1, HALF + W :, :] = bot[:, :, cols]
    ext[:, 0] = left[...]
    ext[:, 3] = right[...]
    acc[...] = jnp.zeros_like(acc)
    weight[...] = jnp.zeros_like(weight)
    grads[...] = jnp.zeros_like(grads)

    def position(p, carry):
        r = offs[p, 0, 0] + HALF
        c = offs[p, 0, 1] + HALF
        q = c // HALF
        s = c - q * HALF
        back_shift = lax.rem(HALF - s, HALF)
        keep = lanes < HALF - s
        q2 = jnp.minimum(q + 2, 3)

        def cut(i, carry):
            rows = pl.ds(pl.multiple_of(i * CH, CH), CH)
            w = []
            for d in range(2):
                src = pl.ds(r + i * CH, CH)
                a = pltpu.roll(ext[d, q, src, :], back_shift, 1)
                b = pltpu.roll(ext[d, q + 1, src, :], back_shift, 1)
                e = pltpu.roll(ext[d, q2, src, :], back_shift, 1)
                w.append(jnp.concatenate([jnp.where(keep, a, b), jnp.where(keep, b, e)], 1))
                win[d, rows, :] = w[d]
            weight[rows, :] += w[0] * w[0] + w[1] * w[1]
            for k in range(MODES):
                pr = probe[k, 0, rows, :]
                pi = probe[k, 1, rows, :]
                stack[k, rows, :] = (pr * w[0] - pi * w[1]).astype(BF)
                stack[k, pl.ds(pl.multiple_of(W + i * CH, CH), CH), :] = (pr * w[1] + pi * w[0]).astype(BF)
            return carry

        lax.fori_loop(0, W // CH, cut, 0)
        for k in range(MODES):
            rows_f = jnp.dot(fwd[...], stack[k], preferred_element_type=F32)
            side[k, :, 0:W] = rows_f[0:W].astype(BF)
            side[k, :, W:] = rows_f[W:].astype(BF)
        for k in range(MODES):
            far[k] = jnp.dot(side[k], bwd[...], preferred_element_type=F32)

        def project(i, carry):
            rows = pl.ds(pl.multiple_of(i * CH, CH), CH)
            rows_im = pl.ds(pl.multiple_of(W + i * CH, CH), CH)
            f = [far[k, rows, :] for k in range(MODES)]
            total = f[0] * f[0] + f[1] * f[1]
            intensity = total[:, 0:W] + total[:, W:]
            factor = amp[p, 0, rows, :] * lax.rsqrt(jnp.maximum(intensity, 0.0625))
            for k in range(MODES):
                stack[k, rows, :] = (f[k][:, 0:W] * factor).astype(BF)
                stack[k, rows_im, :] = (f[k][:, W:] * factor).astype(BF)
            return carry

        lax.fori_loop(0, W // CH, project, 0)
        for k in range(MODES):
            rows_b = jnp.dot(bwd[...], stack[k], preferred_element_type=F32)
            side[k, :, 0:W] = rows_b[0:W].astype(BF)
            side[k, :, W:] = rows_b[W:].astype(BF)
        for k in range(MODES):
            far[k] = jnp.dot(side[k], fwd[...], preferred_element_type=F32)

        def spread(i, carry):
            rows = pl.ds(pl.multiple_of(i * CH, CH), CH)
            wr = win[0, rows, :]
            wi = win[1, rows, :]
            power = jnp.zeros((CH, W), F32)
            tr = jnp.zeros((CH, W), F32)
            ti = jnp.zeros((CH, W), F32)
            for k in range(MODES):
                pr = probe[k, 0, rows, :]
                pi = probe[k, 1, rows, :]
                br = far[k, rows, 0:W]
                bi = far[k, rows, W:]
                power += pr * pr + pi * pi
                tr += pr * br + pi * bi
                ti += pr * bi - pi * br
                grads[2 * k, rows, :] += wr * br + wi * bi
                grads[2 * k + 1, rows, :] += wr * bi - wi * br
            dst = pl.ds(r + i * CH, CH)
            for d, t in ((0, tr - power * wr), (1, ti - power * wi)):
                a = pltpu.roll(t[:, 0:HALF], s, 1)
                b = pltpu.roll(t[:, HALF:], s, 1)
                low = lanes < s
                acc[d, q, dst, :] += jnp.where(low, 0.0, a)
                acc[d, q + 1, dst, :] += jnp.where(low, a, b)
                acc[d, q2, dst, :] += jnp.where(low, b, 0.0)
            return carry

        lax.fori_loop(0, W // CH, spread, 0)
        return carry

    lax.fori_loop(0, POS, position, 0)
    h = half[0]
    for out, side_of in ((mine, h), (other, 1 - h)):

        def flush(i, carry):
            rows = pl.ds(pl.multiple_of(side_of * HALF + i * 8, 8), 8)
            for n in range(2 * MODES):
                out[i, n] = grads[n, rows, :]
            out[i, 2 * MODES] = weight[rows, :]
            return carry

        lax.fori_loop(0, 16, flush, 0)


def correct(offsets, half, tile, top, bot, left, right, probe, amplitude):
    fwd, bwd = dft_matrices()
    vmem = pl.BlockSpec(memory_space=pltpu.VMEM)
    smem = pl.BlockSpec(memory_space=pltpu.SMEM)
    part = jax.ShapeDtypeStruct((16, 2 * MODES + 1, 8, W), F32)
    return pl.pallas_call(
        kernel,
        out_shape=(part, part, jax.ShapeDtypeStruct((2, 4, 2 * W, HALF), F32)),
        in_specs=[smem, smem] + [vmem] * 9,
        out_specs=(vmem, vmem, vmem),
        scratch_shapes=[
            pltpu.VMEM((2, 4, 2 * W, HALF), F32),
            pltpu.VMEM((2, W, W), F32),
            pltpu.VMEM((MODES, 2 * W, W), BF),
            pltpu.VMEM((MODES, W, 2 * W), BF),
            pltpu.VMEM((MODES, W, 2 * W), F32),
            pltpu.VMEM((W, W), F32),
            pltpu.VMEM((2 * MODES, W, W), F32),
        ],
        compiler_params=pltpu.CompilerParams(vmem_limit_bytes=48 << 20),
    )(offsets, half, tile, top, bot, left, right, probe, amplitude, jnp.asarray(fwd), jnp.asarray(bwd))


GX = ("z", "xl")
GY = ("xh", "y", "co")
UP = [(i, (i + 1) % 16) for i in range(16)]
DOWN = [(j, i) for i, j in UP]
SWAP = [(0, 1), (1, 0)]


def body(object_field, probe_field, amplitude, offsets):
    top = lax.ppermute(object_field[:, HALF:], GX, UP)
    bot = lax.ppermute(object_field[:, :HALF], GX, DOWN)
    cols = lambda sl: jnp.concatenate([top[:, :, sl], object_field[:, :, sl], bot[:, :, sl]], 1)
    left = lax.ppermute(cols(slice(HALF, W)), GY, UP)
    right = lax.ppermute(cols(slice(0, HALF)), GY, DOWN)
    co = lax.axis_index("co")
    mine, other, acc = correct(
        offsets, co.reshape(1), object_field, top, bot, left, right, probe_field, amplitude
    )
    group = ("xh", "xl", "y")
    part = mine + lax.ppermute(other, "co", SWAP)
    from_right = lax.ppermute(acc[:, 0], GY, DOWN)
    from_left = lax.ppermute(acc[:, 3], GY, UP)
    part = jnp.sum(lax.all_to_all(part, group, 0, 0, tiled=True), 0)
    for step in (1, 2, 4):
        part = part + lax.ppermute(part, "z", [(i, i ^ step) for i in range(8)])
    block = co * 16 + lax.axis_index(group)
    planes = probe_field.reshape(2 * MODES, W, W)
    local = lax.dynamic_slice_in_dim(planes, block * 8, 8, 1)
    weight = part[2 * MODES]
    local = local + (part[: 2 * MODES] - local * weight) / (weight + 1e-05)
    gathered = lax.all_to_all(jnp.broadcast_to(local[None], (16,) + local.shape), group, 0, 0, tiled=True)
    opposite = lax.ppermute(gathered, "co", SWAP)
    halves = jnp.where(co == 0, jnp.stack([gathered, opposite]), jnp.stack([opposite, gathered]))
    updated_probe = halves.transpose(2, 0, 1, 3, 4).reshape(MODES, 2, W, W)

    folded = jnp.concatenate([acc[:, 1] + from_left, acc[:, 2] + from_right], 2)
    from_below = lax.ppermute(folded[:, :HALF], GX, DOWN)
    from_above = lax.ppermute(folded[:, HALF + W :], GX, UP)
    object_step = folded[:, HALF : HALF + W] + jnp.concatenate([from_above, from_below], 1)
    scale_max = jnp.max(jnp.sum(probe_field * probe_field, axis=(0, 1))) + 1e-06
    return (object_field + object_step / scale_max, updated_probe)


def solution(mesh):
    fine = Mesh(mesh.devices.reshape(8, 2, 2, 4, 2), ("z", "xl", "xh", "y", "co"))
    in_specs = (P(None, GX, GY), P(), P(GX, GY, None, None), P(GX, GY, None))
    out_specs = (P(None, GX, GY), P())
    return jax.shard_map(body, mesh=fine, in_specs=in_specs, out_specs=out_specs, check_vma=False)
```

time: 424 us -> 132 us (0.31)
  waiting for transfers between devices: 267 us -> 33.9 us
  local copies, waits for them, and re-layouts: 71.1 us -> 6.36 us
  starting transfers between devices: 18.3 us -> 48.2 us
  Pallas kernels: 0 us -> 17.5 us
  loops' own time: 16 us -> 0 us
  blocking collectives: 0 us -> 14.9 us
  matrix products: 13.9 us -> 0 us
  between operations: 14.9 us -> 1.38 us
  other arithmetic: 21 us -> 9.07 us
    psum x1 -> x0, waiting for transfers between devices: 251 us -> none  [body(): lax.psum((grad_real, grad_imag, weight), ('gx', 'gy'))]
    dynamic_update_slice x4 -> x0, local copies, waits for them, and re-layouts: 36.1 us -> none  [add_window(): lax.dynamic_update_slice(accum, current + object_terms[position], where)]
    ppermute x8 -> x13, starting transfers between devices: 18.3 us -> 42 us  [the longest x3 10.6 us: body(): part = part + lax.ppermute(part, 'z', [(i, i ^ step) for i in range(8)])]
    pallas_call x0 -> x1, Pallas kernels: none -> 17.5 us  [correct(): pl.pallas_call(kernel, out_shape=(part, part, jax.ShapeDtypeStruct((2, 4,...]
    another operation x2 -> x0, loops' own time: 16 us -> none  [the longest x1 16 us: body(): lax.fori_loop(0, starts.shape[0], add_window, jnp.zeros_like(extended))]
    all_to_all x0 -> x1, blocking collectives: none -> 14.9 us  [body(): part = jnp.sum(lax.all_to_all(part, group, 0, 0, tiled=True), 0)]
    dot_general x8 -> x0, matrix products: 13.9 us -> none  [the longest x2 3.59 us: row_pass(): jnp.einsum('jk,bkl->bjl', cosine, stacked, preferred_element_type=jnp.flo...]
    ppermute x8 -> x13, waiting for transfers between devices: 15.8 us -> 27.9 us  [the longest x1 6.88 us: body(): from_above = lax.ppermute(folded[:, HALF + W:], GX, UP)]
  transfers between devices with their start and end apart: 9 -> 14, of which waited for: 6 -> 11; matrix products, arithmetic and copies ran while one was open for 4% -> 8% of each run, Pallas kernels for 0% -> 0%
where the time goes in v1:
time: 132 us; the launch traced here: 131 us
  starting transfers between devices  48.2 us (37%)
  waiting for transfers between devices  33.9 us (26%)
  Pallas kernels  17.5 us (13%)
  blocking collectives  14.9 us (11%)
  other arithmetic  9.07 us (7%)
  local copies, waits for them, and re-layouts  6.36 us (5%)
  between operations  1.38 us (1%)
    pallas_call x1, Pallas kernels, correct(): pl.pallas_call(kernel, out_shape=(part, part, jax.ShapeDtypeStruct((2, 4,...  17.5 us
    all_to_all x1, blocking collectives, body(): part = jnp.sum(lax.all_to_all(part, group, 0, 0, tiled=True), 0)  14.9 us
    ppermute x3, starting transfers between devices, body(): part = part + lax.ppermute(part, 'z', [(i, i ^ step) for i in range(8)])  10.6 us
    ppermute x1, starting transfers between devices, body(): part = mine + lax.ppermute(other, 'co', SWAP)  8.93 us
    ppermute x1, waiting for transfers between devices, body(): from_above = lax.ppermute(folded[:, HALF + W:], GX, UP)  6.88 us
    ppermute x1, waiting for transfers between devices, body(): right = lax.ppermute(cols(slice(0, HALF)), GY, DOWN)  6.25 us
    all_to_all x1, starting transfers between devices, body(): lax.all_to_all(jnp.broadcast_to(local[None], (16,) + local.shape), group,...  6.24 us
    all_to_all x1, waiting for transfers between devices, body(): lax.all_to_all(jnp.broadcast_to(local[None], (16,) + local.shape), group,...  6.03 us
  transfers between devices with their start and end apart: 14, of which 11 were waited for; matrix products, arithmetic and copies ran while one was open for 8% of the time, Pallas kernels for 0%

profile of v1, /device:TPU:1, one launch (start us, length us, event | category | flops | bytes accessed | tf_op | source)
XLA Modules:
  0.0 131.3 jit_solution(18252155360056103682)
XLA Ops:
  0.6 1.1 fusion.10
  1.7 2.1 %collective-permute-start = (f32[2,128,256]{2,1,0:T(8,128)S(1)}, f32[2,128,256]{2,1,0:T(8,128)S(1)}, u32[]{:S(2)}, u32[]{:S(2)}) collective-permute-start(f32[2,128,256]{2,1,0:T(8,128)S(1)} %get-tuple-element.17), channel_id=1, source_target_pairs={{0,16},{16,32},{32,48},{48,64},{64,80},{80,96},{96,112},{112,128},... | collective-permute-start | bytes 786440 | tf_op jit(solution)/shard_map/ppermute | solution.py:182
  3.8 0.0 copy-start.3
  3.8 5.4 %collective-permute-start.1 = (f32[2,128,256]{2,1,0:T(8,128)S(1)}, f32[2,128,256]{2,1,0:T(8,128)S(1)}, u32[]{:S(2)}, u32[]{:S(2)}) collective-permute-start(f32[2,128,256]{2,1,0:T(8,128)S(1)} %get-tuple-element.16), channel_id=1, source_target_pairs={{16,0},{32,16},{48,32},{64,48},{80,64},{96,80},{112,96},{128,112},... | collective-permute-start | bytes 786440 | tf_op jit(solution)/shard_map/ppermute | solution.py:183
  9.3 1.1 fusion.9
  10.3 4.9 %collective-permute-done.top = f32[2,128,256]{2,1,0:T(8,128)S(1)} collective-permute-done((f32[2,128,256]{2,1,0:T(8,128)S(1)}, f32[2,128,256]{2,1,0:T(8,128)S(1)}, u32[]{:S(2)}, u32[]{:S(2)}) %collective-permute-start) | collective-permute-done | bytes 262176 | tf_op jit(solution)/shard_map/ppermute | solution.py:182
  15.2 1.2 collective-permute-done.1.bot
  16.4 0.8 pad_maximum_fusion.1
  17.2 2.0 %collective-permute-start.3 = (f32[2,512,128]{2,1,0:T(8,128)}, f32[2,512,128]{2,1,0:T(8,128)}, u32[]{:S(2)}, u32[]{:S(2)}) collective-permute-start(f32[2,512,128]{2,1,0:T(8,128)} %pad_maximum_fusion.1), channel_id=1, source_target_pairs={{1,0},{2,1},{3,2},{4,3},{5,4},{6,5},{7,6},{8,7},{9,8},{10,9},{11,1... | collective-permute-start | bytes 1572872 | tf_op jit(solution)/shard_map/ppermute | solution.py:186
  19.3 0.8 pad_maximum_fusion
  20.1 1.2 collective-permute-start.2
  21.3 0.1 copy.22.offs
  21.4 6.3 %collective-permute-done.3.right = f32[2,512,128]{2,1,0:T(8,128)} collective-permute-done((f32[2,512,128]{2,1,0:T(8,128)}, f32[2,512,128]{2,1,0:T(8,128)}, u32[]{:S(2)}, u32[]{:S(2)}) %collective-permute-start.3) | collective-permute-done | bytes 524320 | tf_op jit(solution)/shard_map/ppermute | solution.py:186
  27.6 0.1 collective-permute-done.2.left
  27.7 0.0 copy-done.1
  27.7 17.5 %shard_map.77 = (f32[16,5,8,256]{3,2,1,0:T(8,128)S(1)}, f32[16,5,8,256]{3,2,1,0:T(8,128)S(1)}, f32[2,4,512,128]{3,2,1,0:T(8,128)}) custom-call(s32[4,1,2]{2,1,0:T(1,128)S(1)} %copy.22.offs, s32[1]{0:T(128)} %bitcast.half, f32[2,256,256]{2,1,0:T(8,128)S(1)} %copy-done, f32[2,128,256]{2,1,0:T(8,128)S(1)} %collective-permute-done.top, ...), custom_call_target="tpu_custom_call" | custom-call | tf_op jit(solution)/shard_map/pallas_call | solution.py:156
  45.2 8.9 %collective-permute-start.8 = (f32[16,5,8,256]{3,2,1,0:T(8,128)S(1)}, f32[16,5,8,256]{3,2,1,0:T(8,128)S(1)}, u32[]{:S(2)}, u32[]{:S(2)}) collective-permute-start(f32[16,5,8,256]{3,2,1,0:T(8,128)S(1)} %get-tuple-element.7), channel_id=1, source_target_pairs={{0,1},{1,0},{2,3},{3,2},{4,5},{5,4},{6,7},{7,6},{8,9},{9,8},{10,11... | collective-permute-start | bytes 1966088 | tf_op jit(solution)/shard_map/ppermute | solution.py:192
  54.2 1.7 %collective-permute-done.8 = f32[16,5,8,256]{3,2,1,0:T(8,128)S(1)} collective-permute-done((f32[16,5,8,256]{3,2,1,0:T(8,128)S(1)}, f32[16,5,8,256]{3,2,1,0:T(8,128)S(1)}, u32[]{:S(2)}, u32[]{:S(2)}) %collective-permute-start.8) | collective-permute-done | bytes 655392 | tf_op jit(solution)/shard_map/ppermute | solution.py:192
  55.9 0.1 add.58
  56.0 14.9 %all_to_all.10 = f32[16,5,8,256]{3,2,1,0:T(8,128)S(1)} all-to-all(f32[16,5,8,256]{3,2,1,0:T(8,128)S(1)} %add.58), channel_id=1, replica_groups=mesh['z'=8,'xl'=2,'xh'=2,'y'=4,'co'=2] {'xh','xl','y'}, dimensions={0} | all-to-all | bytes 1310720 | tf_op jit(solution)/shard_map/all_to_all | solution.py:195
  70.9 2.2 %collective-permute-start.9 = (f32[5,8,256]{2,1,0:T(8,128)S(1)}, f32[5,8,256]{2,1,0:T(8,128)S(1)}, u32[]{:S(2)}, u32[]{:S(2)}) collective-permute-start(f32[5,8,256]{2,1,0:T(8,128)S(1)} %reduce_sum.19), channel_id=1, source_target_pairs={{0,32},{32,0},{64,96},{96,64},{128,160},{160,128},{192,224},{224,1... | collective-permute-start | bytes 122888 | tf_op jit(solution)/shard_map/ppermute | solution.py:197
  73.1 1.4 %collective-permute-done.9 = f32[5,8,256]{2,1,0:T(8,128)S(1)} collective-permute-done((f32[5,8,256]{2,1,0:T(8,128)S(1)}, f32[5,8,256]{2,1,0:T(8,128)S(1)}, u32[]{:S(2)}, u32[]{:S(2)}) %collective-permute-start.9) | collective-permute-done | bytes 40992 | tf_op jit(solution)/shard_map/ppermute | solution.py:197
  74.5 3.0 %collective-permute-start.10 = (f32[5,8,256]{2,1,0:T(8,128)S(1)}, f32[5,8,256]{2,1,0:T(8,128)S(1)}, u32[]{:S(2)}, u32[]{:S(2)}) collective-permute-start(f32[5,8,256]{2,1,0:T(8,128)S(1)} %add.59), channel_id=1, source_target_pairs={{0,64},{32,96},{64,0},{96,32},{128,192},{160,224},{192,128},{224,1... | collective-permute-start | bytes 122888 | tf_op jit(solution)/shard_map/ppermute | solution.py:197
  77.5 1.1 slice_bitcast_fusion.1
  78.6 0.3 collective-permute-done.10
  78.9 5.4 %collective-permute-start.11 = (f32[5,8,256]{2,1,0:T(8,128)S(1)}, f32[5,8,256]{2,1,0:T(8,128)S(1)}, u32[]{:S(2)}, u32[]{:S(2)}) collective-permute-start(f32[5,8,256]{2,1,0:T(8,128)S(1)} %add.60), channel_id=1, source_target_pairs={{0,128},{32,160},{64,192},{96,224},{128,0},{160,32},{192,64},{224,... | collective-permute-start | bytes 122888 | tf_op jit(solution)/shard_map/ppermute | solution.py:197
  84.3 1.1 slice_bitcast_fusion.3
  85.4 4.0 %collective-permute-start.4 = (f32[2,512,128]{2,1,0:T(8,128)S(1)}, f32[2,512,128]{2,1,0:T(8,128)S(1)}, u32[]{:S(2)}, u32[]{:S(2)}) collective-permute-start(f32[2,512,128]{2,1,0:T(8,128)S(1)} %slice_bitcast_fusion.1), channel_id=1, source_target_pairs={{0,1},{1,2},{2,3},{3,4},{4,5},{5,6},{6,7},{7,8},{8,9},{9,10},{10,1... | collective-permute-start | bytes 1572872 | tf_op jit(solution)/shard_map/ppermute | solution.py:194
  89.3 0.0 collective-permute-start.5
  89.3 0.0 collective-permute-done.11
  89.4 0.8 broadcast_in_dim.2
  90.2 6.2 %all-to-all-start.1 = ((f32[16,4,8,256]{3,2,1,0:T(8,128)}), f32[16,4,8,256]{3,2,1,0:T(8,128)}, u32[]{:S(2)}, u32[]{:S(2)}) async-start(f32[16,4,8,256]{3,2,1,0:T(8,128)} %broadcast_in_dim.2), calls=%async_computation.1 | async-start | bytes 1048576 | tf_op jit(solution)/shard_map/all_to_all | solution.py:203
  96.5 0.0 collective-permute-done.4
  96.5 1.7 %collective-permute-done.5 = f32[2,512,128]{2,1,0:T(8,128)} collective-permute-done((f32[2,512,128]{2,1,0:T(8,128)S(1)}, f32[2,512,128]{2,1,0:T(8,128)}, u32[]{:S(2)}, u32[]{:S(2)}) %collective-permute-start.5) | collective-permute-done | bytes 524320 | tf_op jit(solution)/shard_map/ppermute | solution.py:193
  98.2 1.5 %fusion.4 = (f32[2,512,128]{2,1,0:T(8,128)S(1)}, f32[2,512,128]{2,1,0:T(8,128)S(1)}) fusion(f32[2,512,128]{2,1,0:T(8,128)} %collective-permute-done.5, f32[2,512,128]{2,1,0:T(8,128)S(1)} %collective-permute-done.4, f32[2,4,512,128]{3,2,1,0:T(8,128)} %get-tuple-element.5), kind=kLoop, calls=%fused_computation.11 | loop fusion | flops 262144 | bytes 3145728 | tf_op jit(solution)/shard_map/add | solution.py:208
  99.7 6.0 %all-to-all-done.1 = f32[16,4,8,256]{3,2,1,0:T(8,128)} async-done(((f32[16,4,8,256]{3,2,1,0:T(8,128)}), f32[16,4,8,256]{3,2,1,0:T(8,128)}, u32[]{:S(2)}, u32[]{:S(2)}) %all-to-all-start.1) | async-done | bytes 524320 | tf_op jit(solution)/shard_map/all_to_all | solution.py:203
  105.7 1.1 copy.34
  106.8 4.1 %collective-permute-start.12 = (f32[16,4,8,256]{3,2,0,1:T(8,128)S(1)}, f32[16,4,8,256]{3,2,0,1:T(8,128)}, u32[]{:S(2)}, u32[]{:S(2)}) collective-permute-start(f32[16,4,8,256]{3,2,0,1:T(8,128)S(1)} %copy.34), channel_id=1, source_target_pairs={{0,1},{1,0},{2,3},{3,2},{4,5},{5,4},{6,7},{7,6},{8,9},{9,8},{10,11... | collective-permute-start | bytes 1572872 | tf_op jit(solution)/shard_map/ppermute | solution.py:204
  111.0 0.8 fusion.6
  111.8 0.0 collective-permute-start.6
  111.8 3.6 %collective-permute-start.7 = (f32[2,128,256]{2,1,0:T(8,128)}, f32[2,128,256]{2,1,0:T(8,128)}, u32[]{:S(2)}, u32[]{:S(2)}) collective-permute-start(f32[2,128,256]{2,1,0:T(8,128)} %get-tuple-element.11), channel_id=1, source_target_pairs={{16,0},{32,16},{48,32},{64,48},{80,64},{96,80},{112,96},{128,112},... | collective-permute-start | bytes 786440 | tf_op jit(solution)/shard_map/ppermute | solution.py:209
  115.4 0.1 multiply_reduce_fusion
  115.4 0.7 reduce_max.9
  116.8 6.9 %collective-permute-done.6 = f32[2,128,256]{2,1,0:T(8,128)} collective-permute-done((f32[2,128,256]{2,1,0:T(8,128)}, f32[2,128,256]{2,1,0:T(8,128)}, u32[]{:S(2)}, u32[]{:S(2)}) %collective-permute-start.6) | collective-permute-done | bytes 262176 | tf_op jit(solution)/shard_map/ppermute | solution.py:210
  123.6 3.4 %collective-permute-done.7 = f32[2,128,256]{2,1,0:T(8,128)} collective-permute-done((f32[2,128,256]{2,1,0:T(8,128)}, f32[2,128,256]{2,1,0:T(8,128)}, u32[]{:S(2)}, u32[]{:S(2)}) %collective-permute-start.7) | collective-permute-done | bytes 262176 | tf_op jit(solution)/shard_map/ppermute | solution.py:209
  127.1 1.9 %fusion.3 = f32[2,256,256]{2,1,0:T(8,128)} fusion(f32[2,256,256]{2,1,0:T(8,128)S(1)} %copy-done, f32[2,512,128]{2,1,0:T(8,128)S(1)} %get-tuple-element.9, f32[2,512,128]{2,1,0:T(8,128)S(1)} %get-tuple-element.8, f32[2,128,256]{2,1,0:T(8,128)} %collective-permute-done.7, f32[2,128,256]{2,1,0:T(8,128)} %collective-permute-done.6, f32[]{:T(128)S(6)} %add.52), kind=kLoop, calls=%fused_computation.9 | loop fusion | flops 655360 | bytes 2621444 | tf_op jit(solution)/shard_map/add | solution.py:213
  129.0 0.0 collective-permute-done.12
  129.0 2.3 %maximum_select_fusion = f32[2,16,4,8,256]{4,3,1,0,2:T(8,128)} fusion(f32[1,16,4,8,256]{4,3,1,0,2:T(8,128)} %bitcast.9, f32[1,16,4,8,256]{4,3,1,0,2:T(8,128)S(1)} %bitcast.26, pred[]{:T(512)S(6)} %eq.3), kind=kLoop, calls=%fused_computation.4 | loop fusion | flops 786432 | bytes 2097153 | tf_op jit(solution)/shard_map/jit(_where)/select_n | solution.py:205
  (16 shorter events, 0.1 us)
Async XLA Ops:
  1.7 13.5 %collective-permute-start = (f32[2,128,256]{2,1,0:T(8,128)S(1)}, f32[2,128,256]{2,1,0:T(8,128)S(1)}, u32[]{:S(2)}, u32[]{:S(2)}) collective-permute-start(f32[2,128,256]{2,1,0:T(8,128)S(1)} %get-tuple-element.17), channel_id=1, source_target_pairs={{0,16},{16,32},{32,48},{48,64},{64,80},{80,96},{96,112},{112,128},... | collective-permute-start | bytes 786440 | tf_op jit(solution)/shard_map/ppermute | solution.py:182
  3.8 17.5 %copy-start.4 = (s32[4,1,2]{0,2,1:T(2,128)S(1)}, s32[4,1,2]{0,2,1:T(2,128)}, u32[]{:S(2)}) copy-start(s32[4,1,2]{0,2,1:T(2,128)} %param.9) | copy-start | bytes 100
  3.8 23.9 %copy-start = (f32[2,256,256]{2,1,0:T(8,128)S(1)}, f32[2,256,256]{2,1,0:T(8,128)}, u32[]{:S(2)}) copy-start(f32[2,256,256]{2,1,0:T(8,128)} %tile.1) | copy-start | bytes 1572868
  3.8 23.9 %copy-start.1 = (f32[2,2,256,256]{3,2,1,0:T(8,128)S(1)}, f32[2,2,256,256]{3,2,1,0:T(8,128)}, u32[]{:S(2)}) copy-start(f32[2,2,256,256]{3,2,1,0:T(8,128)} %probe.1) | copy-start | bytes 3145732
  3.8 23.9 %copy-start.2 = (bf16[512,512]{1,0:T(8,128)(2,1)S(1)}, bf16[512,512]{1,0:T(8,128)(2,1)}, u32[]{:S(2)}) copy-start(bf16[512,512]{1,0:T(8,128)(2,1)} %constant.37.clone.fwd) | copy-start | bytes 1572868
  3.8 23.9 %copy-start.3 = (bf16[512,512]{1,0:T(8,128)(2,1)S(1)}, bf16[512,512]{1,0:T(8,128)(2,1)}, u32[]{:S(2)}) copy-start(bf16[512,512]{1,0:T(8,128)(2,1)} %constant.38.clone.bwd) | copy-start | bytes 1572868
  3.8 12.5 %collective-permute-start.1 = (f32[2,128,256]{2,1,0:T(8,128)S(1)}, f32[2,128,256]{2,1,0:T(8,128)S(1)}, u32[]{:S(2)}, u32[]{:S(2)}) collective-permute-start(f32[2,128,256]{2,1,0:T(8,128)S(1)} %get-tuple-element.16), channel_id=1, source_target_pairs={{16,0},{32,16},{48,32},{64,48},{80,64},{96,80},{112,96},{128,112},... | collective-permute-start | bytes 786440 | tf_op jit(solution)/shard_map/ppermute | solution.py:183
  17.2 10.4 %collective-permute-start.3 = (f32[2,512,128]{2,1,0:T(8,128)}, f32[2,512,128]{2,1,0:T(8,128)}, u32[]{:S(2)}, u32[]{:S(2)}) collective-permute-start(f32[2,512,128]{2,1,0:T(8,128)} %pad_maximum_fusion.1), channel_id=1, source_target_pairs={{1,0},{2,1},{3,2},{4,3},{5,4},{6,5},{7,6},{8,7},{9,8},{10,9},{11,1... | collective-permute-start | bytes 1572872 | tf_op jit(solution)/shard_map/ppermute | solution.py:186
  20.1 7.6 %collective-permute-start.2 = (f32[2,512,128]{2,1,0:T(8,128)}, f32[2,512,128]{2,1,0:T(8,128)}, u32[]{:S(2)}, u32[]{:S(2)}) collective-permute-start(f32[2,512,128]{2,1,0:T(8,128)} %pad_maximum_fusion), channel_id=1, source_target_pairs={{0,1},{1,2},{2,3},{3,4},{4,5},{5,6},{6,7},{7,8},{8,9},{9,10},{10,1... | collective-permute-start | bytes 1572872 | tf_op jit(solution)/shard_map/ppermute | solution.py:185
  45.2 10.7 %collective-permute-start.8 = (f32[16,5,8,256]{3,2,1,0:T(8,128)S(1)}, f32[16,5,8,256]{3,2,1,0:T(8,128)S(1)}, u32[]{:S(2)}, u32[]{:S(2)}) collective-permute-start(f32[16,5,8,256]{3,2,1,0:T(8,128)S(1)} %get-tuple-element.7), channel_id=1, source_target_pairs={{0,1},{1,0},{2,3},{3,2},{4,5},{5,4},{6,7},{7,6},{8,9},{9,8},{10,11... | collective-permute-start | bytes 1966088 | tf_op jit(solution)/shard_map/ppermute | solution.py:192
  70.9 3.6 %collective-permute-start.9 = (f32[5,8,256]{2,1,0:T(8,128)S(1)}, f32[5,8,256]{2,1,0:T(8,128)S(1)}, u32[]{:S(2)}, u32[]{:S(2)}) collective-permute-start(f32[5,8,256]{2,1,0:T(8,128)S(1)} %reduce_sum.19), channel_id=1, source_target_pairs={{0,32},{32,0},{64,96},{96,64},{128,160},{160,128},{192,224},{224,1... | collective-permute-start | bytes 122888 | tf_op jit(solution)/shard_map/ppermute | solution.py:197
  74.5 4.4 %collective-permute-start.10 = (f32[5,8,256]{2,1,0:T(8,128)S(1)}, f32[5,8,256]{2,1,0:T(8,128)S(1)}, u32[]{:S(2)}, u32[]{:S(2)}) collective-permute-start(f32[5,8,256]{2,1,0:T(8,128)S(1)} %add.59), channel_id=1, source_target_pairs={{0,64},{32,96},{64,0},{96,32},{128,192},{160,224},{192,128},{224,1... | collective-permute-start | bytes 122888 | tf_op jit(solution)/shard_map/ppermute | solution.py:197
  78.9 10.4 %collective-permute-start.11 = (f32[5,8,256]{2,1,0:T(8,128)S(1)}, f32[5,8,256]{2,1,0:T(8,128)S(1)}, u32[]{:S(2)}, u32[]{:S(2)}) collective-permute-start(f32[5,8,256]{2,1,0:T(8,128)S(1)} %add.60), channel_id=1, source_target_pairs={{0,128},{32,160},{64,192},{96,224},{128,0},{160,32},{192,64},{224,... | collective-permute-start | bytes 122888 | tf_op jit(solution)/shard_map/ppermute | solution.py:197
  85.4 11.1 %collective-permute-start.4 = (f32[2,512,128]{2,1,0:T(8,128)S(1)}, f32[2,512,128]{2,1,0:T(8,128)S(1)}, u32[]{:S(2)}, u32[]{:S(2)}) collective-permute-start(f32[2,512,128]{2,1,0:T(8,128)S(1)} %slice_bitcast_fusion.1), channel_id=1, source_target_pairs={{0,1},{1,2},{2,3},{3,4},{4,5},{5,6},{6,7},{7,8},{8,9},{9,10},{10,1... | collective-permute-start | bytes 1572872 | tf_op jit(solution)/shard_map/ppermute | solution.py:194
  89.3 8.9 %collective-permute-start.5 = (f32[2,512,128]{2,1,0:T(8,128)S(1)}, f32[2,512,128]{2,1,0:T(8,128)}, u32[]{:S(2)}, u32[]{:S(2)}) collective-permute-start(f32[2,512,128]{2,1,0:T(8,128)S(1)} %slice_bitcast_fusion.3), channel_id=1, source_target_pairs={{1,0},{2,1},{3,2},{4,3},{5,4},{6,5},{7,6},{8,7},{9,8},{10,9},{11,1... | collective-permute-start | bytes 1572872 | tf_op jit(solution)/shard_map/ppermute | solution.py:193
  90.2 15.5 %all-to-all-start.1 = ((f32[16,4,8,256]{3,2,1,0:T(8,128)}), f32[16,4,8,256]{3,2,1,0:T(8,128)}, u32[]{:S(2)}, u32[]{:S(2)}) async-start(f32[16,4,8,256]{3,2,1,0:T(8,128)} %broadcast_in_dim.2), calls=%async_computation.1 | async-start | bytes 1048576 | tf_op jit(solution)/shard_map/all_to_all | solution.py:203
  106.8 22.2 %collective-permute-start.12 = (f32[16,4,8,256]{3,2,0,1:T(8,128)S(1)}, f32[16,4,8,256]{3,2,0,1:T(8,128)}, u32[]{:S(2)}, u32[]{:S(2)}) collective-permute-start(f32[16,4,8,256]{3,2,0,1:T(8,128)S(1)} %copy.34), channel_id=1, source_target_pairs={{0,1},{1,0},{2,3},{3,2},{4,5},{5,4},{6,7},{7,6},{8,9},{9,8},{10,11... | collective-permute-start | bytes 1572872 | tf_op jit(solution)/shard_map/ppermute | solution.py:204
  111.8 11.9 %collective-permute-start.6 = (f32[2,128,256]{2,1,0:T(8,128)}, f32[2,128,256]{2,1,0:T(8,128)}, u32[]{:S(2)}, u32[]{:S(2)}) collective-permute-start(f32[2,128,256]{2,1,0:T(8,128)} %get-tuple-element.10), channel_id=1, source_target_pairs={{0,16},{16,32},{32,48},{48,64},{64,80},{80,96},{96,112},{112,128},... | collective-permute-start | bytes 786440 | tf_op jit(solution)/shard_map/ppermute | solution.py:210
  111.8 15.3 %collective-permute-start.7 = (f32[2,128,256]{2,1,0:T(8,128)}, f32[2,128,256]{2,1,0:T(8,128)}, u32[]{:S(2)}, u32[]{:S(2)}) collective-permute-start(f32[2,128,256]{2,1,0:T(8,128)} %get-tuple-element.11), channel_id=1, source_target_pairs={{16,0},{32,16},{48,32},{64,48},{80,64},{96,80},{112,96},{128,112},... | collective-permute-start | bytes 786440 | tf_op jit(solution)/shard_map/ppermute | solution.py:209

commit v2 on v1

--- a/solution.py
+++ b/solution.py
@@ -33,7 +33,7 @@
 
 
 def kernel(
-    offs, half, tile, top, bot, left, right, probe, amp, fwd, bwd,
+    offs, half, tile, top, bot, left, right, left_ends, right_ends, probe, amp, fwd, bwd,
     mine, other, acc,
     ext, win, stack, side, far, weight, grads,
 ):
@@ -43,8 +43,10 @@
         ext[:, q + 1, 0:HALF, :] = top[:, :, cols]
         ext[:, q + 1, HALF : HALF + W, :] = tile[:, :, cols]
         ext[:, q + 1, HALF + W :, :] = bot[:, :, cols]
-    ext[:, 0] = left[...]
-    ext[:, 3] = right[...]
+    for q, middle, ends in ((0, left, left_ends), (3, right, right_ends)):
+        ext[:, q, 0:HALF, :] = ends[0]
+        ext[:, q, HALF : HALF + W, :] = middle[...]
+        ext[:, q, HALF + W :, :] = ends[1]
     acc[...] = jnp.zeros_like(acc)
     weight[...] = jnp.zeros_like(weight)
     grads[...] = jnp.zeros_like(grads)
@@ -76,7 +78,7 @@
                 stack[k, pl.ds(pl.multiple_of(W + i * CH, CH), CH), :] = (pr * w[1] + pi * w[0]).astype(BF)
             return carry
 
-        lax.fori_loop(0, W // CH, cut, 0)
+        lax.fori_loop(0, W // CH, cut, 0, unroll=True)
         for k in range(MODES):
             rows_f = jnp.dot(fwd[...], stack[k], preferred_element_type=F32)
             side[k, :, 0:W] = rows_f[0:W].astype(BF)
@@ -96,7 +98,7 @@
                 stack[k, rows_im, :] = (f[k][:, W:] * factor).astype(BF)
             return carry
 
-        lax.fori_loop(0, W // CH, project, 0)
+        lax.fori_loop(0, W // CH, project, 0, unroll=True)
         for k in range(MODES):
             rows_b = jnp.dot(bwd[...], stack[k], preferred_element_type=F32)
             side[k, :, 0:W] = rows_b[0:W].astype(BF)
@@ -131,7 +133,7 @@
                 acc[d, q2, dst, :] += jnp.where(low, b, 0.0)
             return carry
 
-        lax.fori_loop(0, W // CH, spread, 0)
+        lax.fori_loop(0, W // CH, spread, 0, unroll=True)
         return carry
 
     lax.fori_loop(0, POS, position, 0)
@@ -148,7 +150,7 @@
         lax.fori_loop(0, 16, flush, 0)
 
 
-def correct(offsets, half, tile, top, bot, left, right, probe, amplitude):
+def correct(offsets, half, border, probe, amplitude):
     fwd, bwd = dft_matrices()
     vmem = pl.BlockSpec(memory_space=pltpu.VMEM)
     smem = pl.BlockSpec(memory_space=pltpu.SMEM)
@@ -156,7 +158,7 @@
     return pl.pallas_call(
         kernel,
         out_shape=(part, part, jax.ShapeDtypeStruct((2, 4, 2 * W, HALF), F32)),
-        in_specs=[smem, smem] + [vmem] * 9,
+        in_specs=[smem, smem] + [vmem] * 11,
         out_specs=(vmem, vmem, vmem),
         scratch_shapes=[
             pltpu.VMEM((2, 4, 2 * W, HALF), F32),
@@ -168,7 +170,7 @@
             pltpu.VMEM((2 * MODES, W, W), F32),
         ],
         compiler_params=pltpu.CompilerParams(vmem_limit_bytes=48 << 20),
-    )(offsets, half, tile, top, bot, left, right, probe, amplitude, jnp.asarray(fwd), jnp.asarray(bwd))
+    )(offsets, half, *border, probe, amplitude, jnp.asarray(fwd), jnp.asarray(bwd))
 
 
 GX = ("z", "xl")
@@ -178,21 +180,46 @@
 SWAP = [(0, 1), (1, 0)]
 
 
+def arrange_kernel(half, own, swapped, out):
+    h = half[0]
+    for source, side_of in ((own, h), (swapped, 1 - h)):
+        for i in range(16):
+            rows = pl.ds(pl.multiple_of(side_of * HALF + i * 8, 8), 8)
+            for n in range(2 * MODES):
+                out[n // 2, n % 2, rows, :] = source[i, n]
+
+
+def arrange(half, own, swapped):
+    vmem = pl.BlockSpec(memory_space=pltpu.VMEM)
+    return pl.pallas_call(
+        arrange_kernel,
+        out_shape=jax.ShapeDtypeStruct((MODES, 2, W, W), F32),
+        in_specs=[pl.BlockSpec(memory_space=pltpu.SMEM), vmem, vmem],
+        out_specs=vmem,
+    )(half, own, swapped)
+
+
 def body(object_field, probe_field, amplitude, offsets):
-    top = lax.ppermute(object_field[:, HALF:], GX, UP)
-    bot = lax.ppermute(object_field[:, :HALF], GX, DOWN)
-    cols = lambda sl: jnp.concatenate([top[:, :, sl], object_field[:, :, sl], bot[:, :, sl]], 1)
-    left = lax.ppermute(cols(slice(HALF, W)), GY, UP)
-    right = lax.ppermute(cols(slice(0, HALF)), GY, DOWN)
+    first, last = slice(0, HALF), slice(HALF, W)
+    top = lax.ppermute(object_field[:, last], GX, UP)
+    bot = lax.ppermute(object_field[:, first], GX, DOWN)
+    left = lax.ppermute(object_field[:, :, last], GY, UP)
+    right = lax.ppermute(object_field[:, :, first], GY, DOWN)
+    left_ends = lax.ppermute(jnp.stack([top[:, :, last], bot[:, :, last]]), GY, UP)
+    right_ends = lax.ppermute(jnp.stack([top[:, :, first], bot[:, :, first]]), GY, DOWN)
     co = lax.axis_index("co")
-    mine, other, acc = correct(
-        offsets, co.reshape(1), object_field, top, bot, left, right, probe_field, amplitude
-    )
+    half = co.reshape(1)
+    border = (object_field, top, bot, left, right, left_ends, right_ends)
+    mine, other, acc = correct(offsets, half, border, probe_field, amplitude)
+    from_right = lax.ppermute(acc[:, 0], GY, DOWN)
+    from_left = lax.ppermute(acc[:, 3], GY, UP)
     group = ("xh", "xl", "y")
     part = mine + lax.ppermute(other, "co", SWAP)
-    from_right = lax.ppermute(acc[:, 0], GY, DOWN)
-    from_left = lax.ppermute(acc[:, 3], GY, UP)
     part = jnp.sum(lax.all_to_all(part, group, 0, 0, tiled=True), 0)
+    folded = jnp.concatenate([acc[:, 1] + from_left, acc[:, 2] + from_right], 2)
+    part, folded = lax.optimization_barrier((part, folded))
+    from_below = lax.ppermute(folded[:, :HALF], GX, DOWN)
+    from_above = lax.ppermute(folded[:, HALF + W :], GX, UP)
     for step in (1, 2, 4):
         part = part + lax.ppermute(part, "z", [(i, i ^ step) for i in range(8)])
     block = co * 16 + lax.axis_index(group)
@@ -200,14 +227,10 @@
     local = lax.dynamic_slice_in_dim(planes, block * 8, 8, 1)
     weight = part[2 * MODES]
     local = local + (part[: 2 * MODES] - local * weight) / (weight + 1e-05)
+    local, from_below, from_above = lax.optimization_barrier((local, from_below, from_above))
     gathered = lax.all_to_all(jnp.broadcast_to(local[None], (16,) + local.shape), group, 0, 0, tiled=True)
-    opposite = lax.ppermute(gathered, "co", SWAP)
-    halves = jnp.where(co == 0, jnp.stack([gathered, opposite]), jnp.stack([opposite, gathered]))
-    updated_probe = halves.transpose(2, 0, 1, 3, 4).reshape(MODES, 2, W, W)
-
-    folded = jnp.concatenate([acc[:, 1] + from_left, acc[:, 2] + from_right], 2)
-    from_below = lax.ppermute(folded[:, :HALF], GX, DOWN)
-    from_above = lax.ppermute(folded[:, HALF + W :], GX, UP)
+    updated_probe = arrange(half, gathered, lax.ppermute(gathered, "co", SWAP))
+
     object_step = folded[:, HALF : HALF + W] + jnp.concatenate([from_above, from_below], 1)
     scale_max = jnp.max(jnp.sum(probe_field * probe_field, axis=(0, 1))) + 1e-06
     return (object_field + object_step / scale_max, updated_probe)

time: 132 us -> 115 us (0.87)
  starting transfers between devices: 48.2 us -> 35.3 us
  Pallas kernels: 17.5 us -> 13.8 us
  blocking collectives: 14.9 us -> 18.2 us
  other arithmetic: 9.07 us -> 6.8 us
  waiting for transfers between devices: 33.9 us -> 32.4 us
    ppermute x1, starting transfers between devices: 8.93 us -> 2.06 us  [body(): part = mine + lax.ppermute(other, 'co', SWAP)]
    pallas_call x1, Pallas kernels: 17.5 us -> 11.5 us  [correct(): pl.pallas_call(kernel, out_shape=(part, part, jax.ShapeDtypeStruct((2, 4,...]
    ppermute x1, waiting for transfers between devices: 6.88 us -> 1.3 us  [body(): from_above = lax.ppermute(folded[:, HALF + W:], GX, UP)]
    ppermute x3, waiting for transfers between devices: 1.7 us -> 5.93 us  [body(): part = part + lax.ppermute(part, 'z', [(i, i ^ step) for i in range(8)])]
    ppermute x3, starting transfers between devices: 10.6 us -> 6.4 us  [body(): part = part + lax.ppermute(part, 'z', [(i, i ^ step) for i in range(8)])]
    ppermute x1, starting transfers between devices: 3.96 us -> 0.08 us  [body(): from_left = lax.ppermute(acc[:, 3], GY, UP)]
    ppermute x1, starting transfers between devices: 3.57 us -> 0.08 us  [body(): from_below = lax.ppermute(folded[:, :HALF], GX, DOWN)]
    all_to_all x1, blocking collectives: 14.9 us -> 18.2 us  [body(): lax.all_to_all(jnp.broadcast_to(local[None], (16,) + local.shape), group,...]
  transfers between devices with their start and end apart: 14 -> 16, of which waited for: 11 -> 11; matrix products, arithmetic and copies ran while one was open for 8% -> 10% of each run, Pallas kernels for 0% -> 0%
where the time goes in v2:
time: 115 us; the launch traced here: 114 us
  starting transfers between devices  35.3 us (31%)
  waiting for transfers between devices  32.4 us (28%)
  blocking collectives  18.2 us (16%)
  Pallas kernels  13.8 us (12%)
  other arithmetic  6.8 us (6%)
  local copies, waits for them, and re-layouts  6.17 us (5%)
  between operations  1.45 us (1%)
    all_to_all x1, blocking collectives, body(): lax.all_to_all(jnp.broadcast_to(local[None], (16,) + local.shape), group,...  18.2 us
    pallas_call x1, Pallas kernels, correct(): pl.pallas_call(kernel, out_shape=(part, part, jax.ShapeDtypeStruct((2, 4,...  11.5 us
    all_to_all x1, waiting for transfers between devices, body(): part = jnp.sum(lax.all_to_all(part, group, 0, 0, tiled=True), 0)  9.33 us
    all_to_all x1, starting transfers between devices, body(): part = jnp.sum(lax.all_to_all(part, group, 0, 0, tiled=True), 0)  7.57 us
    ppermute x1, starting transfers between devices, body(): bot = lax.ppermute(object_field[:, first], GX, DOWN)  7.41 us
    ppermute x3, starting transfers between devices, body(): part = part + lax.ppermute(part, 'z', [(i, i ^ step) for i in range(8)])  6.4 us
    ppermute x3, waiting for transfers between devices, body(): part = part + lax.ppermute(part, 'z', [(i, i ^ step) for i in range(8)])  5.93 us
    ppermute x1, starting transfers between devices, body(): updated_probe = arrange(half, gathered, lax.ppermute(gathered, 'co', SWAP))  4.52 us
  transfers between devices with their start and end apart: 16, of which 11 were waited for; matrix products, arithmetic and copies ran while one was open for 10% of the time, Pallas kernels for 0%

profile of v2, /device:TPU:1, one launch (start us, length us, event | category | flops | bytes accessed | tf_op | source)
XLA Modules:
  0.0 114.1 jit_solution(6788878889599661940)
XLA Ops:
  0.6 0.0 copy-start.2
  0.6 0.0 copy-start.3
  0.7 0.0 copy-start
  0.7 1.2 %fusion.8 = (f32[2,128,256]{2,1,0:T(8,128)S(1)}, f32[2,128,256]{2,1,0:T(8,128)S(1)}) fusion(f32[2,256,256]{2,1,0:T(8,128)} %tile.1), kind=kLoop, calls=%fused_computation.24 | loop fusion | bytes 1048576 | tf_op jit(solution)/shard_map/slice | solution.py:205
  1.9 7.4 %collective-permute-start.1 = (f32[2,128,256]{2,1,0:T(8,128)S(1)}, f32[2,128,256]{2,1,0:T(8,128)S(1)}, u32[]{:S(2)}, u32[]{:S(2)}) collective-permute-start(f32[2,128,256]{2,1,0:T(8,128)S(1)} %get-tuple-element.24), channel_id=1, source_target_pairs={{16,0},{32,16},{48,32},{64,48},{80,64},{96,80},{112,96},{128,112},... | collective-permute-start | bytes 786440 | tf_op jit(solution)/shard_map/ppermute | solution.py:205
  9.3 1.9 %fusion.7 = (f32[2,256,128]{2,1,0:T(8,128)}, f32[2,256,128]{2,1,0:T(8,128)}) fusion(f32[2,256,256]{2,1,0:T(8,128)} %tile.1), kind=kLoop, calls=%fused_computation.23 | loop fusion | bytes 1048576 | tf_op jit(solution)/shard_map/slice | solution.py:207
  11.2 2.1 %collective-permute-start.2 = (f32[2,256,128]{2,1,0:T(8,128)}, f32[2,256,128]{2,1,0:T(8,128)S(1)}, u32[]{:S(2)}, u32[]{:S(2)}) collective-permute-start(f32[2,256,128]{2,1,0:T(8,128)} %get-tuple-element.23), channel_id=1, source_target_pairs={{0,1},{1,2},{2,3},{3,4},{4,5},{5,6},{6,7},{7,8},{8,9},{9,10},{10,1... | collective-permute-start | bytes 786440 | tf_op jit(solution)/shard_map/ppermute | solution.py:206
  13.3 1.0 collective-permute-done.1.bot
  14.4 3.9 %collective-permute-done.top = f32[2,128,256]{2,1,0:T(8,128)S(1)} collective-permute-done((f32[2,128,256]{2,1,0:T(8,128)S(1)}, f32[2,128,256]{2,1,0:T(8,128)S(1)}, u32[]{:S(2)}, u32[]{:S(2)}) %collective-permute-start) | collective-permute-done | bytes 262176 | tf_op jit(solution)/shard_map/ppermute | solution.py:204
  18.3 0.7 pad_maximum_fusion.1
  19.0 3.0 %collective-permute-start.4 = (f32[2,2,128,128]{3,2,1,0:T(8,128)}, f32[2,2,128,128]{3,2,1,0:T(8,128)}, u32[]{:S(2)}, u32[]{:S(2)}) collective-permute-start(f32[2,2,128,128]{3,2,1,0:T(8,128)} %pad_maximum_fusion.1), channel_id=1, source_target_pairs={{0,1},{1,2},{2,3},{3,4},{4,5},{5,6},{6,7},{7,8},{8,9},{9,10},{10,1... | collective-permute-start | bytes 786440 | tf_op jit(solution)/shard_map/ppermute | solution.py:208
  22.1 0.7 pad_maximum_fusion.2
  22.8 0.0 collective-permute-start.5
  22.8 0.1 copy.12.offs
  22.9 0.0 collective-permute-done.2.left
  22.9 0.0 collective-permute-done.3.right
  22.9 2.8 %collective-permute-done.4.left_ends = f32[2,2,128,128]{3,2,1,0:T(8,128)} collective-permute-done((f32[2,2,128,128]{3,2,1,0:T(8,128)}, f32[2,2,128,128]{3,2,1,0:T(8,128)}, u32[]{:S(2)}, u32[]{:S(2)}) %collective-permute-start.4) | collective-permute-done | bytes 262176 | tf_op jit(solution)/shard_map/ppermute | solution.py:208
  25.7 3.5 %collective-permute-done.5.right_ends = f32[2,2,128,128]{3,2,1,0:T(8,128)} collective-permute-done((f32[2,2,128,128]{3,2,1,0:T(8,128)}, f32[2,2,128,128]{3,2,1,0:T(8,128)}, u32[]{:S(2)}, u32[]{:S(2)}) %collective-permute-start.5) | collective-permute-done | bytes 262176 | tf_op jit(solution)/shard_map/ppermute | solution.py:209
  29.2 11.5 %shard_map.77 = (f32[16,5,8,256]{3,2,1,0:T(8,128)S(1)}, f32[16,5,8,256]{3,2,1,0:T(8,128)S(1)}, f32[2,4,512,128]{3,2,1,0:T(8,128)}) custom-call(s32[4,1,2]{2,1,0:T(1,128)S(1)} %copy.12.offs, s32[1]{0:T(128)} %bitcast.half, f32[2,256,256]{2,1,0:T(8,128)S(1)} %copy-done, f32[2,128,256]{2,1,0:T(8,128)S(1)} %collective-permute-done.top, ...), custom_call_target="tpu_custom_call" | custom-call | tf_op jit(solution)/shard_map/pallas_call | solution.py:158
  40.7 2.1 %collective-permute-start.6 = (f32[16,5,8,256]{3,2,1,0:T(8,128)S(1)}, f32[16,5,8,256]{3,2,1,0:T(8,128)S(1)}, u32[]{:S(2)}, u32[]{:S(2)}) collective-permute-start(f32[16,5,8,256]{3,2,1,0:T(8,128)S(1)} %get-tuple-element.11), channel_id=1, source_target_pairs={{0,1},{1,0},{2,3},{3,2},{4,5},{5,4},{6,7},{7,6},{8,9},{9,8},{10,11... | collective-permute-start | bytes 1966088 | tf_op jit(solution)/shard_map/ppermute | solution.py:217
  42.8 1.1 slice_bitcast_fusion.1
  43.9 1.1 slice_bitcast_fusion.3
  45.0 0.1 collective-permute-start.7
  45.1 0.5 collective-permute-start.8
  45.6 0.9 add.49
  46.5 7.6 %all-to-all-start = ((f32[16,5,8,256]{3,2,1,0:T(8,128)}), f32[16,5,8,256]{3,2,1,0:T(8,128)S(1)}, u32[]{:S(2)}, u32[]{:S(2)}) async-start(f32[16,5,8,256]{3,2,1,0:T(8,128)} %add.49), calls=%async_computation | async-start | bytes 1310720 | tf_op jit(solution)/shard_map/all_to_all | solution.py:218
  54.1 0.1 collective-permute-done.8
  54.1 1.6 %fusion.1 = (f32[2,512,128]{2,1,0:T(8,128)S(1)}, f32[2,512,128]{2,1,0:T(8,128)S(1)}) fusion(f32[2,512,128]{2,1,0:T(8,128)} %collective-permute-done.7, f32[2,512,128]{2,1,0:T(8,128)} %collective-permute-done.8, f32[2,4,512,128]{3,2,1,0:T(8,128)} %get-tuple-element.12), kind=kLoop, calls=%fused_computation.6 | loop fusion | flops 262144 | bytes 3145728 | tf_op jit(solution)/shard_map/add | solution.py:219
  55.8 0.1 pad_maximum_fusion
  55.8 9.3 %all-to-all-done = f32[16,5,8,256]{3,2,1,0:T(8,128)S(1)} async-done(((f32[16,5,8,256]{3,2,1,0:T(8,128)}), f32[16,5,8,256]{3,2,1,0:T(8,128)S(1)}, u32[]{:S(2)}, u32[]{:S(2)}) %all-to-all-start) | async-done | bytes 655392 | tf_op jit(solution)/shard_map/all_to_all | solution.py:218
  65.2 0.1 collective-permute-start.9
  65.3 2.8 %collective-permute-done.9 = f32[5,8,256]{2,1,0:T(8,128)S(1)} collective-permute-done((f32[5,8,256]{2,1,0:T(8,128)S(1)}, f32[5,8,256]{2,1,0:T(8,128)S(1)}, u32[]{:S(2)}, u32[]{:S(2)}) %collective-permute-start.9) | collective-permute-done | bytes 40992 | tf_op jit(solution)/shard_map/ppermute | solution.py:224
  68.2 1.5 %collective-permute-start.10 = (f32[5,8,256]{2,1,0:T(8,128)S(1)}, f32[5,8,256]{2,1,0:T(8,128)S(1)}, u32[]{:S(2)}, u32[]{:S(2)}) collective-permute-start(f32[5,8,256]{2,1,0:T(8,128)S(1)} %add.56), channel_id=1, source_target_pairs={{0,64},{32,96},{64,0},{96,32},{128,192},{160,224},{192,128},{224,1... | collective-permute-start | bytes 122888 | tf_op jit(solution)/shard_map/ppermute | solution.py:224
  69.7 2.7 %collective-permute-done.10 = f32[5,8,256]{2,1,0:T(8,128)S(1)} collective-permute-done((f32[5,8,256]{2,1,0:T(8,128)S(1)}, f32[5,8,256]{2,1,0:T(8,128)S(1)}, u32[]{:S(2)}, u32[]{:S(2)}) %collective-permute-start.10) | collective-permute-done | bytes 40992 | tf_op jit(solution)/shard_map/ppermute | solution.py:224
  72.4 4.8 %collective-permute-start.11 = (f32[5,8,256]{2,1,0:T(8,128)S(1)}, f32[5,8,256]{2,1,0:T(8,128)S(1)}, u32[]{:S(2)}, u32[]{:S(2)}) collective-permute-start(f32[5,8,256]{2,1,0:T(8,128)S(1)} %add.57), channel_id=1, source_target_pairs={{0,128},{32,160},{64,192},{96,224},{128,0},{160,32},{192,64},{224,... | collective-permute-start | bytes 122888 | tf_op jit(solution)/shard_map/ppermute | solution.py:224
  77.2 0.1 collective-permute-start.12
  77.3 1.5 %collective-permute-start.13 = (f32[2,128,256]{2,1,0:T(8,128)S(1)}, f32[2,128,256]{2,1,0:T(8,128)}, u32[]{:S(2)}, u32[]{:S(2)}) collective-permute-start(f32[2,128,256]{2,1,0:T(8,128)S(1)} %get-tuple-element.20), channel_id=1, source_target_pairs={{0,16},{16,32},{32,48},{48,64},{64,80},{80,96},{96,112},{112,128},... | collective-permute-start | bytes 786440 | tf_op jit(solution)/shard_map/ppermute | solution.py:222
  78.7 0.4 collective-permute-done.11
  79.2 4.5 %collective-permute-done.12 = f32[2,128,256]{2,1,0:T(8,128)S(1)} collective-permute-done((f32[2,128,256]{2,1,0:T(8,128)S(1)}, f32[2,128,256]{2,1,0:T(8,128)S(1)}, u32[]{:S(2)}, u32[]{:S(2)}) %collective-permute-start.12) | collective-permute-done | bytes 262176 | tf_op jit(solution)/shard_map/ppermute | solution.py:221
  83.7 0.7 copy-done.5
  84.4 1.3 %collective-permute-done.13 = f32[2,128,256]{2,1,0:T(8,128)} collective-permute-done((f32[2,128,256]{2,1,0:T(8,128)S(1)}, f32[2,128,256]{2,1,0:T(8,128)}, u32[]{:S(2)}, u32[]{:S(2)}) %collective-permute-start.13) | collective-permute-done | bytes 262176 | tf_op jit(solution)/shard_map/ppermute | solution.py:222
  85.7 18.2 %all_to_all.10.own = f32[16,4,8,256]{3,2,1,0:T(8,128)S(1)} all-to-all(f32[16,4,8,256]{3,2,1,0:T(8,128)S(1)} %broadcast_in_dim.2), channel_id=1, replica_groups=mesh['z'=8,'xl'=2,'xh'=2,'y'=4,'co'=2] {'xh','xl','y'}, dimensions={0} | all-to-all | bytes 1048576 | tf_op jit(solution)/shard_map/all_to_all | solution.py:231
  104.0 4.5 %collective-permute-start.14 = (f32[16,4,8,256]{3,2,1,0:T(8,128)S(1)}, f32[16,4,8,256]{3,2,1,0:T(8,128)}, u32[]{:S(2)}, u32[]{:S(2)}) collective-permute-start(f32[16,4,8,256]{3,2,1,0:T(8,128)S(1)} %all_to_all.10.own), channel_id=1, source_target_pairs={{0,1},{1,0},{2,3},{3,2},{4,5},{5,4},{6,7},{7,6},{8,9},{9,8},{10,11... | collective-permute-start | bytes 1572872 | tf_op jit(solution)/shard_map/ppermute | solution.py:232
  108.5 0.1 multiply_reduce_fusion
  108.6 0.7 reduce_max.9
  109.9 1.9 %fusion.3 = f32[2,256,256]{2,1,0:T(8,128)} fusion(f32[2,256,256]{2,1,0:T(8,128)S(1)} %copy-done, f32[2,128,256]{2,1,0:T(8,128)} %copy-done.5, f32[2,128,256]{2,1,0:T(8,128)} %collective-permute-done.13, f32[2,512,256]{2,1,0:T(8,128)S(1)} %pad_maximum_fusion, f32[]{:T(128)S(6)} %add.63), kind=kLoop, calls=%fused_computation.9 | loop fusion | flops 524288 | bytes 2097156 | tf_op jit(solution)/shard_map/add | solution.py:236
  111.8 0.0 collective-permute-done.14.swapped
  111.8 2.2 %shard_map.78 = f32[2,2,256,256]{3,2,1,0:T(8,128)} custom-call(s32[1]{0:T(128)} %bitcast.half, f32[16,4,8,256]{3,2,1,0:T(8,128)} %copy-done.4, f32[16,4,8,256]{3,2,1,0:T(8,128)} %collective-permute-done.14.swapped), custom_call_target="tpu_custom_call" | custom-call | tf_op jit(solution)/shard_map/pallas_call | solution.py:194
  (24 shorter events, 0.2 us)
Async XLA Ops:
  0.6 28.6 %copy-start.2 = (bf16[512,512]{1,0:T(8,128)(2,1)S(1)}, bf16[512,512]{1,0:T(8,128)(2,1)}, u32[]{:S(2)}) copy-start(bf16[512,512]{1,0:T(8,128)(2,1)} %constant.37.clone.fwd) | copy-start | bytes 1572868
  0.6 28.6 %copy-start.3 = (bf16[512,512]{1,0:T(8,128)(2,1)S(1)}, bf16[512,512]{1,0:T(8,128)(2,1)}, u32[]{:S(2)}) copy-start(bf16[512,512]{1,0:T(8,128)(2,1)} %constant.38.clone.bwd) | copy-start | bytes 1572868
  0.7 28.5 %copy-start = (f32[2,256,256]{2,1,0:T(8,128)S(1)}, f32[2,256,256]{2,1,0:T(8,128)}, u32[]{:S(2)}) copy-start(f32[2,256,256]{2,1,0:T(8,128)} %tile.1) | copy-start | bytes 1572868
  0.7 22.1 %copy-start.6 = (s32[4,1,2]{0,2,1:T(2,128)S(1)}, s32[4,1,2]{0,2,1:T(2,128)}, u32[]{:S(2)}) copy-start(s32[4,1,2]{0,2,1:T(2,128)} %param.9) | copy-start | bytes 100
  0.7 28.5 %copy-start.1 = (f32[2,2,256,256]{3,2,1,0:T(8,128)S(1)}, f32[2,2,256,256]{3,2,1,0:T(8,128)}, u32[]{:S(2)}) copy-start(f32[2,2,256,256]{3,2,1,0:T(8,128)} %probe.1) | copy-start | bytes 3145732
  1.9 12.4 %collective-permute-start.1 = (f32[2,128,256]{2,1,0:T(8,128)S(1)}, f32[2,128,256]{2,1,0:T(8,128)S(1)}, u32[]{:S(2)}, u32[]{:S(2)}) collective-permute-start(f32[2,128,256]{2,1,0:T(8,128)S(1)} %get-tuple-element.24), channel_id=1, source_target_pairs={{16,0},{32,16},{48,32},{64,48},{80,64},{96,80},{112,96},{128,112},... | collective-permute-start | bytes 786440 | tf_op jit(solution)/shard_map/ppermute | solution.py:205
  9.3 9.0 %collective-permute-start = (f32[2,128,256]{2,1,0:T(8,128)S(1)}, f32[2,128,256]{2,1,0:T(8,128)S(1)}, u32[]{:S(2)}, u32[]{:S(2)}) collective-permute-start(f32[2,128,256]{2,1,0:T(8,128)S(1)} %get-tuple-element.25), channel_id=1, source_target_pairs={{0,16},{16,32},{32,48},{48,64},{64,80},{80,96},{96,112},{112,128},... | collective-permute-start | bytes 786440 | tf_op jit(solution)/shard_map/ppermute | solution.py:204
  11.2 11.7 %collective-permute-start.2 = (f32[2,256,128]{2,1,0:T(8,128)}, f32[2,256,128]{2,1,0:T(8,128)S(1)}, u32[]{:S(2)}, u32[]{:S(2)}) collective-permute-start(f32[2,256,128]{2,1,0:T(8,128)} %get-tuple-element.23), channel_id=1, source_target_pairs={{0,1},{1,2},{2,3},{3,4},{4,5},{5,6},{6,7},{7,8},{8,9},{9,10},{10,1... | collective-permute-start | bytes 786440 | tf_op jit(solution)/shard_map/ppermute | solution.py:206
  13.3 9.6 %collective-permute-start.3 = (f32[2,256,128]{2,1,0:T(8,128)}, f32[2,256,128]{2,1,0:T(8,128)}, u32[]{:S(2)}, u32[]{:S(2)}) collective-permute-start(f32[2,256,128]{2,1,0:T(8,128)} %get-tuple-element.22), channel_id=1, source_target_pairs={{1,0},{2,1},{3,2},{4,3},{5,4},{6,5},{7,6},{8,7},{9,8},{10,9},{11,1... | collective-permute-start | bytes 786440 | tf_op jit(solution)/shard_map/ppermute | solution.py:207
  19.0 6.7 %collective-permute-start.4 = (f32[2,2,128,128]{3,2,1,0:T(8,128)}, f32[2,2,128,128]{3,2,1,0:T(8,128)}, u32[]{:S(2)}, u32[]{:S(2)}) collective-permute-start(f32[2,2,128,128]{3,2,1,0:T(8,128)} %pad_maximum_fusion.1), channel_id=1, source_target_pairs={{0,1},{1,2},{2,3},{3,4},{4,5},{5,6},{6,7},{7,8},{8,9},{9,10},{10,1... | collective-permute-start | bytes 786440 | tf_op jit(solution)/shard_map/ppermute | solution.py:208
  22.8 6.4 %collective-permute-start.5 = (f32[2,2,128,128]{3,2,1,0:T(8,128)}, f32[2,2,128,128]{3,2,1,0:T(8,128)}, u32[]{:S(2)}, u32[]{:S(2)}) collective-permute-start(f32[2,2,128,128]{3,2,1,0:T(8,128)} %pad_maximum_fusion.2), channel_id=1, source_target_pairs={{1,0},{2,1},{3,2},{4,3},{5,4},{6,5},{7,6},{8,7},{9,8},{10,9},{11,1... | collective-permute-start | bytes 786440 | tf_op jit(solution)/shard_map/ppermute | solution.py:209
  40.7 4.8 %collective-permute-start.6 = (f32[16,5,8,256]{3,2,1,0:T(8,128)S(1)}, f32[16,5,8,256]{3,2,1,0:T(8,128)S(1)}, u32[]{:S(2)}, u32[]{:S(2)}) collective-permute-start(f32[16,5,8,256]{3,2,1,0:T(8,128)S(1)} %get-tuple-element.11), channel_id=1, source_target_pairs={{0,1},{1,0},{2,3},{3,2},{4,5},{5,4},{6,7},{7,6},{8,9},{9,8},{10,11... | collective-permute-start | bytes 1966088 | tf_op jit(solution)/shard_map/ppermute | solution.py:217
  45.0 9.1 %collective-permute-start.7 = (f32[2,512,128]{2,1,0:T(8,128)S(1)}, f32[2,512,128]{2,1,0:T(8,128)}, u32[]{:S(2)}, u32[]{:S(2)}) collective-permute-start(f32[2,512,128]{2,1,0:T(8,128)S(1)} %slice_bitcast_fusion.1), channel_id=1, source_target_pairs={{0,1},{1,2},{2,3},{3,4},{4,5},{5,6},{6,7},{7,8},{8,9},{9,10},{10,1... | collective-permute-start | bytes 1572872 | tf_op jit(solution)/shard_map/ppermute | solution.py:215
  45.1 9.1 %collective-permute-start.8 = (f32[2,512,128]{2,1,0:T(8,128)S(1)}, f32[2,512,128]{2,1,0:T(8,128)}, u32[]{:S(2)}, u32[]{:S(2)}) collective-permute-start(f32[2,512,128]{2,1,0:T(8,128)S(1)} %slice_bitcast_fusion.3), channel_id=1, source_target_pairs={{1,0},{2,1},{3,2},{4,3},{5,4},{6,5},{7,6},{8,7},{9,8},{10,9},{11,1... | collective-permute-start | bytes 1572872 | tf_op jit(solution)/shard_map/ppermute | solution.py:214
  46.5 18.7 %all-to-all-start = ((f32[16,5,8,256]{3,2,1,0:T(8,128)}), f32[16,5,8,256]{3,2,1,0:T(8,128)S(1)}, u32[]{:S(2)}, u32[]{:S(2)}) async-start(f32[16,5,8,256]{3,2,1,0:T(8,128)} %add.49), calls=%async_computation | async-start | bytes 1310720 | tf_op jit(solution)/shard_map/all_to_all | solution.py:218
  65.2 2.9 %collective-permute-start.9 = (f32[5,8,256]{2,1,0:T(8,128)S(1)}, f32[5,8,256]{2,1,0:T(8,128)S(1)}, u32[]{:S(2)}, u32[]{:S(2)}) collective-permute-start(f32[5,8,256]{2,1,0:T(8,128)S(1)} %reduce_sum.18), channel_id=1, source_target_pairs={{0,32},{32,0},{64,96},{96,64},{128,160},{160,128},{192,224},{224,1... | collective-permute-start | bytes 122888 | tf_op jit(solution)/shard_map/ppermute | solution.py:224
  68.2 4.2 %collective-permute-start.10 = (f32[5,8,256]{2,1,0:T(8,128)S(1)}, f32[5,8,256]{2,1,0:T(8,128)S(1)}, u32[]{:S(2)}, u32[]{:S(2)}) collective-permute-start(f32[5,8,256]{2,1,0:T(8,128)S(1)} %add.56), channel_id=1, source_target_pairs={{0,64},{32,96},{64,0},{96,32},{128,192},{160,224},{192,128},{224,1... | collective-permute-start | bytes 122888 | tf_op jit(solution)/shard_map/ppermute | solution.py:224
  72.4 6.8 %collective-permute-start.11 = (f32[5,8,256]{2,1,0:T(8,128)S(1)}, f32[5,8,256]{2,1,0:T(8,128)S(1)}, u32[]{:S(2)}, u32[]{:S(2)}) collective-permute-start(f32[5,8,256]{2,1,0:T(8,128)S(1)} %add.57), channel_id=1, source_target_pairs={{0,128},{32,160},{64,192},{96,224},{128,0},{160,32},{192,64},{224,... | collective-permute-start | bytes 122888 | tf_op jit(solution)/shard_map/ppermute | solution.py:224
  77.2 6.5 %collective-permute-start.12 = (f32[2,128,256]{2,1,0:T(8,128)S(1)}, f32[2,128,256]{2,1,0:T(8,128)S(1)}, u32[]{:S(2)}, u32[]{:S(2)}) collective-permute-start(f32[2,128,256]{2,1,0:T(8,128)S(1)} %get-tuple-element.21), channel_id=1, source_target_pairs={{16,0},{32,16},{48,32},{64,48},{80,64},{96,80},{112,96},{128,112},... | collective-permute-start | bytes 786440 | tf_op jit(solution)/shard_map/ppermute | solution.py:221
  77.3 8.4 %collective-permute-start.13 = (f32[2,128,256]{2,1,0:T(8,128)S(1)}, f32[2,128,256]{2,1,0:T(8,128)}, u32[]{:S(2)}, u32[]{:S(2)}) collective-permute-start(f32[2,128,256]{2,1,0:T(8,128)S(1)} %get-tuple-element.20), channel_id=1, source_target_pairs={{0,16},{16,32},{32,48},{48,64},{64,80},{80,96},{96,112},{112,128},... | collective-permute-start | bytes 786440 | tf_op jit(solution)/shard_map/ppermute | solution.py:222
  83.7 0.7 copy-start.5
  104.0 7.9 %copy-start.4 = (f32[16,4,8,256]{3,2,1,0:T(8,128)}, f32[16,4,8,256]{3,2,1,0:T(8,128)S(1)}, u32[]{:S(2)}) copy-start(f32[16,4,8,256]{3,2,1,0:T(8,128)S(1)} %all_to_all.10.own) | copy-start | bytes 1572868
  104.0 7.9 %collective-permute-start.14 = (f32[16,4,8,256]{3,2,1,0:T(8,128)S(1)}, f32[16,4,8,256]{3,2,1,0:T(8,128)}, u32[]{:S(2)}, u32[]{:S(2)}) collective-permute-start(f32[16,4,8,256]{3,2,1,0:T(8,128)S(1)} %all_to_all.10.own), channel_id=1, source_target_pairs={{0,1},{1,0},{2,3},{3,2},{4,5},{5,4},{6,7},{7,6},{8,9},{9,8},{10,11... | collective-permute-start | bytes 1572872 | tf_op jit(solution)/shard_map/ppermute | solution.py:232

commit v3 on v2

--- a/solution.py
+++ b/solution.py
@@ -34,8 +34,8 @@
 
 def kernel(
     offs, half, tile, top, bot, left, right, left_ends, right_ends, probe, amp, fwd, bwd,
-    mine, other, acc,
-    ext, win, stack, side, far, weight, grads,
+    mine, other, out_left, out_mid, out_right,
+    ext, acc, win, stack, side, far, weight, grads,
 ):
     lanes = lax.broadcasted_iota(jnp.int32, (CH, HALF), 1)
     for q in range(2):
@@ -137,6 +137,10 @@
         return carry
 
     lax.fori_loop(0, POS, position, 0)
+    out_left[...] = acc[:, 0]
+    out_mid[:, :, 0:HALF] = acc[:, 1]
+    out_mid[:, :, HALF:] = acc[:, 2]
+    out_right[...] = acc[:, 3]
     h = half[0]
     for out, side_of in ((mine, h), (other, 1 - h)):
 
@@ -155,12 +159,14 @@
     vmem = pl.BlockSpec(memory_space=pltpu.VMEM)
     smem = pl.BlockSpec(memory_space=pltpu.SMEM)
     part = jax.ShapeDtypeStruct((16, 2 * MODES + 1, 8, W), F32)
+    strip = jax.ShapeDtypeStruct((2, 2 * W, HALF), F32)
     return pl.pallas_call(
         kernel,
-        out_shape=(part, part, jax.ShapeDtypeStruct((2, 4, 2 * W, HALF), F32)),
+        out_shape=(part, part, strip, jax.ShapeDtypeStruct((2, 2 * W, W), F32), strip),
         in_specs=[smem, smem] + [vmem] * 11,
-        out_specs=(vmem, vmem, vmem),
+        out_specs=(vmem,) * 5,
         scratch_shapes=[
+            pltpu.VMEM((2, 4, 2 * W, HALF), F32),
             pltpu.VMEM((2, 4, 2 * W, HALF), F32),
             pltpu.VMEM((2, W, W), F32),
             pltpu.VMEM((MODES, 2 * W, W), BF),
@@ -169,7 +175,7 @@
             pltpu.VMEM((W, W), F32),
             pltpu.VMEM((2 * MODES, W, W), F32),
         ],
-        compiler_params=pltpu.CompilerParams(vmem_limit_bytes=48 << 20),
+        compiler_params=pltpu.CompilerParams(vmem_limit_bytes=20 << 20),
     )(offsets, half, *border, probe, amplitude, jnp.asarray(fwd), jnp.asarray(bwd))
 
 
@@ -196,6 +202,7 @@
         out_shape=jax.ShapeDtypeStruct((MODES, 2, W, W), F32),
         in_specs=[pl.BlockSpec(memory_space=pltpu.SMEM), vmem, vmem],
         out_specs=vmem,
+        compiler_params=pltpu.CompilerParams(vmem_limit_bytes=4 << 20),
     )(half, own, swapped)
 
 
@@ -209,30 +216,32 @@
     right_ends = lax.ppermute(jnp.stack([top[:, :, first], bot[:, :, first]]), GY, DOWN)
     co = lax.axis_index("co")
     half = co.reshape(1)
+    scale_max = jnp.max(jnp.sum(probe_field * probe_field, axis=(0, 1))) + 1e-06
+    half, scale_max = lax.optimization_barrier((half, scale_max))
     border = (object_field, top, bot, left, right, left_ends, right_ends)
-    mine, other, acc = correct(offsets, half, border, probe_field, amplitude)
-    from_right = lax.ppermute(acc[:, 0], GY, DOWN)
-    from_left = lax.ppermute(acc[:, 3], GY, UP)
+    mine, other, out_left, out_mid, out_right = correct(offsets, half, border, probe_field, amplitude)
     group = ("xh", "xl", "y")
     part = mine + lax.ppermute(other, "co", SWAP)
     part = jnp.sum(lax.all_to_all(part, group, 0, 0, tiled=True), 0)
-    folded = jnp.concatenate([acc[:, 1] + from_left, acc[:, 2] + from_right], 2)
-    part, folded = lax.optimization_barrier((part, folded))
-    from_below = lax.ppermute(folded[:, :HALF], GX, DOWN)
-    from_above = lax.ppermute(folded[:, HALF + W :], GX, UP)
-    for step in (1, 2, 4):
-        part = part + lax.ppermute(part, "z", [(i, i ^ step) for i in range(8)])
+    part, out_left, out_right = lax.optimization_barrier((part, out_left, out_right))
+    from_right = lax.ppermute(out_left, GY, DOWN)
+    from_left = lax.ppermute(out_right, GY, UP)
+    peers = [lax.ppermute(part, "z", [(i, i ^ step) for i in range(8)]) for step in (1, 2, 3)]
+    part = (part + peers[0]) + (peers[1] + peers[2])
+    part = part + lax.ppermute(part, "z", [(i, i ^ 4) for i in range(8)])
     block = co * 16 + lax.axis_index(group)
     planes = probe_field.reshape(2 * MODES, W, W)
     local = lax.dynamic_slice_in_dim(planes, block * 8, 8, 1)
     weight = part[2 * MODES]
     local = local + (part[: 2 * MODES] - local * weight) / (weight + 1e-05)
-    local, from_below, from_above = lax.optimization_barrier((local, from_below, from_above))
+    folded = out_mid + jnp.concatenate([from_left, from_right], 2)
+    local, folded = lax.optimization_barrier((local, folded))
+    from_below = lax.ppermute(folded[:, :HALF], GX, DOWN)
+    from_above = lax.ppermute(folded[:, HALF + W :], GX, UP)
     gathered = lax.all_to_all(jnp.broadcast_to(local[None], (16,) + local.shape), group, 0, 0, tiled=True)
+    gathered, from_below, from_above = lax.optimization_barrier((gathered, from_below, from_above))
     updated_probe = arrange(half, gathered, lax.ppermute(gathered, "co", SWAP))
-
     object_step = folded[:, HALF : HALF + W] + jnp.concatenate([from_above, from_below], 1)
-    scale_max = jnp.max(jnp.sum(probe_field * probe_field, axis=(0, 1))) + 1e-06
     return (object_field + object_step / scale_max, updated_probe)
 
 

time: 115 us -> 116 us (level)
  starting transfers between devices: 35.3 us -> 40 us
  waiting for transfers between devices: 32.4 us -> 29.2 us
  Pallas kernels: 13.8 us -> 11 us
  other arithmetic: 6.8 us -> 8.41 us
    ppermute x1, waiting for transfers between devices: 1.3 us -> 11.3 us  [body(): from_above = lax.ppermute(folded[:, HALF + W:], GX, UP)]
    all_to_all x1, waiting for transfers between devices: 9.33 us -> 0.01 us  [body(): lax.all_to_all(jnp.broadcast_to(local[None], (16,) + local.shape), group,...]
    ppermute x1, starting transfers between devices: 4.52 us -> 0.01 us  [body(): updated_probe = arrange(half, gathered, lax.ppermute(gathered, 'co', SWAP))]
    ppermute x5 -> x6, starting transfers between devices: 6.98 us -> 11 us  [the longest x1 5.01 us: body(): part = part + lax.ppermute(part, 'z', [(i, i ^ 4) for i in range(8)])]
    ppermute x1, starting transfers between devices: 0.08 us -> 3.33 us  [body(): from_below = lax.ppermute(folded[:, :HALF], GX, DOWN)]
    ppermute x1, waiting for transfers between devices: 2.81 us -> 0.01 us  [body(): lax.ppermute(jnp.stack([top[:, :, last], bot[:, :, last]]), GY, UP)]
    ppermute x1, waiting for transfers between devices: 4.49 us -> 2.1 us  [body(): from_below = lax.ppermute(folded[:, :HALF], GX, DOWN)]
    unnamed x15 -> x25, local copies, waits for them, and re-layouts: 0.83 us -> 3.18 us
  transfers between devices with their start and end apart: 16 -> 17, of which waited for: 11 -> 9; matrix products, arithmetic and copies ran while one was open for 10% -> 5% of each run, Pallas kernels for 0% -> 0%
where the time goes in v3:
time: 116 us; the launch traced here: 115 us
  starting transfers between devices  40 us (34%)
  waiting for transfers between devices  29.2 us (25%)
  blocking collectives  19.1 us (16%)
  Pallas kernels  11 us (9%)
  other arithmetic  8.41 us (7%)
  local copies, waits for them, and re-layouts  6.04 us (5%)
  between operations  1.51 us (1%)
    all_to_all x1, blocking collectives, body(): part = jnp.sum(lax.all_to_all(part, group, 0, 0, tiled=True), 0)  19.1 us
    ppermute x1, waiting for transfers between devices, body(): from_above = lax.ppermute(folded[:, HALF + W:], GX, UP)  11.3 us
    pallas_call x1, Pallas kernels, correct(): pl.pallas_call(kernel, out_shape=(part, part, strip, jax.ShapeDtypeStruct...  9.96 us
    all_to_all x1, starting transfers between devices, body(): lax.all_to_all(jnp.broadcast_to(local[None], (16,) + local.shape), group,...  9.58 us
    ppermute x1, starting transfers between devices, body(): bot = lax.ppermute(object_field[:, first], GX, DOWN)  7.41 us
    ppermute x1, starting transfers between devices, body(): part = part + lax.ppermute(part, 'z', [(i, i ^ 4) for i in range(8)])  5.01 us
    ppermute x1, waiting for transfers between devices, body(): top = lax.ppermute(object_field[:, last], GX, UP)  3.97 us
    ppermute x3, starting transfers between devices, body(): lax.ppermute(part, 'z', [(i, i ^ step) for i in range(8)])  3.63 us
  transfers between devices with their start and end apart: 17, of which 9 were waited for; matrix products, arithmetic and copies ran while one was open for 5% of the time, Pallas kernels for 0%

profile of v3, /device:TPU:1, one launch (start us, length us, event | category | flops | bytes accessed | tf_op | source)
XLA Modules:
  0.0 115.4 jit_solution(6112958231967434997)
XLA Ops:
  0.6 1.1 fusion.6
  1.8 7.4 %collective-permute-start.1 = (f32[2,128,256]{2,1,0:T(8,128)S(1)}, f32[2,128,256]{2,1,0:T(8,128)S(1)}, u32[]{:S(2)}, u32[]{:S(2)}) collective-permute-start(f32[2,128,256]{2,1,0:T(8,128)S(1)} %get-tuple-element.36), channel_id=1, source_target_pairs={{16,0},{32,16},{48,32},{64,48},{80,64},{96,80},{112,96},{128,112},... | collective-permute-start | bytes 786440 | tf_op jit(solution)/shard_map/ppermute | solution.py:212
  9.2 0.0 collective-permute-start
  9.2 0.8 fusion.5
  10.0 1.0 collective-permute-start.3
  11.0 1.2 %collective-permute-start.2 = (f32[2,256,128]{2,1,0:T(8,128)}, f32[2,256,128]{2,1,0:T(8,128)}, u32[]{:S(2)}, u32[]{:S(2)}) collective-permute-start(f32[2,256,128]{2,1,0:T(8,128)} %get-tuple-element.35), channel_id=1, source_target_pairs={{0,1},{1,2},{2,3},{3,4},{4,5},{5,6},{6,7},{7,8},{8,9},{9,10},{10,1... | collective-permute-start | bytes 786440 | tf_op jit(solution)/shard_map/ppermute | solution.py:213
  12.2 2.0 %collective-permute-done.1.bot = f32[2,128,256]{2,1,0:T(8,128)S(1)} collective-permute-done((f32[2,128,256]{2,1,0:T(8,128)S(1)}, f32[2,128,256]{2,1,0:T(8,128)S(1)}, u32[]{:S(2)}, u32[]{:S(2)}) %collective-permute-start.1) | collective-permute-done | bytes 262176 | tf_op jit(solution)/shard_map/ppermute | solution.py:212
  14.2 4.0 %collective-permute-done.top = f32[2,128,256]{2,1,0:T(8,128)S(1)} collective-permute-done((f32[2,128,256]{2,1,0:T(8,128)S(1)}, f32[2,128,256]{2,1,0:T(8,128)S(1)}, u32[]{:S(2)}, u32[]{:S(2)}) %collective-permute-start) | collective-permute-done | bytes 262176 | tf_op jit(solution)/shard_map/ppermute | solution.py:211
  18.2 0.0 copy-start.11
  18.2 0.7 pad_maximum_fusion
  19.0 3.0 %collective-permute-start.4 = (f32[2,2,128,128]{3,2,1,0:T(8,128)}, f32[2,2,128,128]{3,2,1,0:T(8,128)}, u32[]{:S(2)}, u32[]{:S(2)}) collective-permute-start(f32[2,2,128,128]{3,2,1,0:T(8,128)} %pad_maximum_fusion), channel_id=1, source_target_pairs={{0,1},{1,2},{2,3},{3,4},{4,5},{5,6},{6,7},{7,8},{8,9},{9,10},{10,1... | collective-permute-start | bytes 786440 | tf_op jit(solution)/shard_map/ppermute | solution.py:215
  22.0 0.7 pad_maximum_fusion.1
  22.7 0.0 collective-permute-start.5
  22.7 0.1 copy.9.offs
  22.8 0.8 multiply_reduce_fusion
  23.6 1.7 %reduce_max.9 = f32[]{:T(128)} reduce(f32[256,256]{1,0:T(8,128)} %multiply_reduce_fusion, f32[]{:T(128)} %constant.34.clone.1), dimensions={0,1}, to_apply=%region_1.0 | reduce | flops 65535 | bytes 262152 | tf_op jit(solution)/shard_map/reduce_max | solution.py:219
  25.9 0.0 collective-permute-done.3.right
  26.0 0.0 collective-permute-done.4.left_ends
  26.0 3.1 %collective-permute-done.5.right_ends = f32[2,2,128,128]{3,2,1,0:T(8,128)} collective-permute-done((f32[2,2,128,128]{3,2,1,0:T(8,128)}, f32[2,2,128,128]{3,2,1,0:T(8,128)}, u32[]{:S(2)}, u32[]{:S(2)}) %collective-permute-start.5) | collective-permute-done | bytes 262176 | tf_op jit(solution)/shard_map/ppermute | solution.py:216
  29.1 1.0 copy-done.5
  30.1 1.0 copy-done.6
  31.2 10.0 %shard_map.77 = (f32[16,5,8,256]{3,2,1,0:T(8,128)S(1)}, f32[16,5,8,256]{3,2,1,0:T(8,128)S(1)}, f32[2,512,128]{2,1,0:T(8,128)S(1)}, f32[2,512,256]{2,1,0:T(8,128)S(1)}, f32[2,512,128]{2,1,0:T(8,128)S(1)}) custom-call(s32[4,1,2]{2,1,0:T(1,128)S(1)} %copy.9.offs, s32[1]{0:T(128)} %bitcast.1.half, f32[2,256,256]{2,1,0:T(8,128)S(1)} %copy-done, ...), custom_call_target="tpu_custom_call" | custom-call | tf_op jit(solution)/shard_map/pallas_call | solution.py:163
  41.1 0.0 copy-start.3
  41.2 1.0 copy-done.3
  42.1 2.1 %collective-permute-start.6 = (f32[16,5,8,256]{3,2,1,0:T(8,128)S(1)}, f32[16,5,8,256]{3,2,1,0:T(8,128)S(1)}, u32[]{:S(2)}, u32[]{:S(2)}) collective-permute-start(f32[16,5,8,256]{3,2,1,0:T(8,128)S(1)} %get-tuple-element.19), channel_id=1, source_target_pairs={{0,1},{1,0},{2,3},{3,2},{4,5},{5,4},{6,7},{7,6},{8,9},{9,8},{10,11... | collective-permute-start | bytes 1966088 | tf_op jit(solution)/shard_map/ppermute | solution.py:224
  44.2 1.7 %collective-permute-done.6 = f32[16,5,8,256]{3,2,1,0:T(8,128)S(1)} collective-permute-done((f32[16,5,8,256]{3,2,1,0:T(8,128)S(1)}, f32[16,5,8,256]{3,2,1,0:T(8,128)S(1)}, u32[]{:S(2)}, u32[]{:S(2)}) %collective-permute-start.6) | collective-permute-done | bytes 655392 | tf_op jit(solution)/shard_map/ppermute | solution.py:224
  45.9 0.1 add.54
  46.0 0.0 copy-start.4
  46.1 19.1 %all_to_all.10 = f32[16,5,8,256]{3,2,1,0:T(8,128)} all-to-all(f32[16,5,8,256]{3,2,1,0:T(8,128)S(1)} %add.54), channel_id=1, replica_groups=mesh['z'=8,'xl'=2,'xh'=2,'y'=4,'co'=2] {'xh','xl','y'}, dimensions={0} | all-to-all | bytes 1310720 | tf_op jit(solution)/shard_map/all_to_all | solution.py:225
  65.2 1.2 %reduce_sum.19 = f32[5,8,256]{2,1,0:T(8,128)S(1)} reduce(f32[16,5,8,256]{3,2,1,0:T(8,128)} %all_to_all.10, f32[]{:T(128)} %constant.33.clone.1), dimensions={0}, to_apply=%region_2.0 | reduce | flops 153600 | bytes 696324 | tf_op jit(solution)/shard_map/reduce_sum | solution.py:225
  66.4 2.2 %collective-permute-start.9 = (f32[5,8,256]{2,1,0:T(8,128)S(1)}, f32[5,8,256]{2,1,0:T(8,128)S(1)}, u32[]{:S(2)}, u32[]{:S(2)}) collective-permute-start(f32[5,8,256]{2,1,0:T(8,128)S(1)} %reduce_sum.19), channel_id=1, source_target_pairs={{0,96},{32,64},{64,32},{96,0},{128,224},{160,192},{192,160},{224,1... | collective-permute-start | bytes 122888 | tf_op jit(solution)/shard_map/ppermute | solution.py:229
  68.5 0.0 collective-permute-start.8
  68.5 1.5 %collective-permute-start.7 = (f32[5,8,256]{2,1,0:T(8,128)S(1)}, f32[5,8,256]{2,1,0:T(8,128)S(1)}, u32[]{:S(2)}, u32[]{:S(2)}) collective-permute-start(f32[5,8,256]{2,1,0:T(8,128)S(1)} %reduce_sum.19), channel_id=1, source_target_pairs={{0,32},{32,0},{64,96},{96,64},{128,160},{160,128},{192,224},{224,1... | collective-permute-start | bytes 122888 | tf_op jit(solution)/shard_map/ppermute | solution.py:229
  70.0 2.4 %collective-permute-start.11 = (f32[2,512,128]{2,1,0:T(8,128)}, f32[2,512,128]{2,1,0:T(8,128)}, u32[]{:S(2)}, u32[]{:S(2)}) collective-permute-start(f32[2,512,128]{2,1,0:T(8,128)} %copy-done.9), channel_id=1, source_target_pairs={{0,1},{1,2},{2,3},{3,4},{4,5},{5,6},{6,7},{7,8},{8,9},{9,10},{10,1... | collective-permute-start | bytes 1572872 | tf_op jit(solution)/shard_map/ppermute | solution.py:228
  72.4 0.0 collective-permute-start.12
  72.5 5.0 %collective-permute-start.10 = (f32[5,8,256]{2,1,0:T(8,128)S(1)}, f32[5,8,256]{2,1,0:T(8,128)S(1)}, u32[]{:S(2)}, u32[]{:S(2)}) collective-permute-start(f32[5,8,256]{2,1,0:T(8,128)S(1)} %add_add_fusion), channel_id=1, source_target_pairs={{0,128},{32,160},{64,192},{96,224},{128,0},{160,32},{192,64},{224,... | collective-permute-start | bytes 122888 | tf_op jit(solution)/shard_map/ppermute | solution.py:231
  77.5 2.4 %collective-permute-done.10 = f32[5,8,256]{2,1,0:T(8,128)S(1)} collective-permute-done((f32[5,8,256]{2,1,0:T(8,128)S(1)}, f32[5,8,256]{2,1,0:T(8,128)S(1)}, u32[]{:S(2)}, u32[]{:S(2)}) %collective-permute-start.10) | collective-permute-done | bytes 40992 | tf_op jit(solution)/shard_map/ppermute | solution.py:231
  80.0 1.5 %collective-permute-done.12 = f32[2,512,128]{2,1,0:T(8,128)} collective-permute-done((f32[2,512,128]{2,1,0:T(8,128)S(1)}, f32[2,512,128]{2,1,0:T(8,128)}, u32[]{:S(2)}, u32[]{:S(2)}) %collective-permute-start.12) | collective-permute-done | bytes 524320 | tf_op jit(solution)/shard_map/ppermute | solution.py:227
  81.4 2.3 %maximum_add_fusion = f32[2,512,256]{2,1,0:T(8,128)} fusion(f32[2,512,256]{2,1,0:T(8,128)S(1)} %copy-done.4, f32[2,512,128]{2,1,0:T(8,128)} %collective-permute-done.12, f32[2,512,128]{2,1,0:T(8,128)} %collective-permute-done.11), kind=kLoop, calls=%fused_computation | loop fusion | flops 524288 | bytes 3145728 | tf_op jit(solution)/shard_map/add | solution.py:237
  83.7 0.8 broadcast_in_dim.2
  84.6 9.6 %all-to-all-start.1 = ((f32[16,4,8,256]{3,2,1,0:T(8,128)}), f32[16,4,8,256]{3,2,1,0:T(8,128)S(1)}, u32[]{:S(2)}, u32[]{:S(2)}) async-start(f32[16,4,8,256]{3,2,1,0:T(8,128)} %broadcast_in_dim.2), calls=%async_computation.1 | async-start | bytes 1048576 | tf_op jit(solution)/shard_map/all_to_all | solution.py:241
  94.2 1.4 %collective-permute-start.14 = (f32[2,128,256]{2,1,0:T(8,128)S(1)}, f32[2,128,256]{2,1,0:T(8,128)S(1)}, u32[]{:S(2)}, u32[]{:S(2)}) collective-permute-start(f32[2,128,256]{2,1,0:T(8,128)S(1)} %get-tuple-element.32), channel_id=1, source_target_pairs={{0,16},{16,32},{32,48},{48,64},{64,80},{80,96},{96,112},{112,128},... | collective-permute-start | bytes 786440 | tf_op jit(solution)/shard_map/ppermute | solution.py:240
  95.6 3.3 %collective-permute-start.13 = (f32[2,128,256]{2,1,0:T(8,128)S(1)}, f32[2,128,256]{2,1,0:T(8,128)S(1)}, u32[]{:S(2)}, u32[]{:S(2)}) collective-permute-start(f32[2,128,256]{2,1,0:T(8,128)S(1)} %get-tuple-element.33), channel_id=1, source_target_pairs={{16,0},{32,16},{48,32},{64,48},{80,64},{96,80},{112,96},{128,112},... | collective-permute-start | bytes 786440 | tf_op jit(solution)/shard_map/ppermute | solution.py:239
  99.0 11.3 %collective-permute-done.14 = f32[2,128,256]{2,1,0:T(8,128)S(1)} collective-permute-done((f32[2,128,256]{2,1,0:T(8,128)S(1)}, f32[2,128,256]{2,1,0:T(8,128)S(1)}, u32[]{:S(2)}, u32[]{:S(2)}) %collective-permute-start.14) | collective-permute-done | bytes 262176 | tf_op jit(solution)/shard_map/ppermute | solution.py:240
  110.3 2.1 %collective-permute-done.13 = f32[2,128,256]{2,1,0:T(8,128)S(1)} collective-permute-done((f32[2,128,256]{2,1,0:T(8,128)S(1)}, f32[2,128,256]{2,1,0:T(8,128)S(1)}, u32[]{:S(2)}, u32[]{:S(2)}) %collective-permute-start.13) | collective-permute-done | bytes 262176 | tf_op jit(solution)/shard_map/ppermute | solution.py:239
  112.4 0.9 fusion.1
  113.3 1.0 collective-permute-done.15.swapped
  114.3 1.0 shard_map.78
  (32 shorter events, 0.2 us)
Async XLA Ops:
  0.6 8.6 %copy-start = (f32[2,256,256]{2,1,0:T(8,128)S(1)}, f32[2,256,256]{2,1,0:T(8,128)}, u32[]{:S(2)}) copy-start(f32[2,256,256]{2,1,0:T(8,128)} %tile.1) | copy-start | bytes 1572868
  1.8 12.4 %collective-permute-start.1 = (f32[2,128,256]{2,1,0:T(8,128)S(1)}, f32[2,128,256]{2,1,0:T(8,128)S(1)}, u32[]{:S(2)}, u32[]{:S(2)}) collective-permute-start(f32[2,128,256]{2,1,0:T(8,128)S(1)} %get-tuple-element.36), channel_id=1, source_target_pairs={{16,0},{32,16},{48,32},{64,48},{80,64},{96,80},{112,96},{128,112},... | collective-permute-start | bytes 786440 | tf_op jit(solution)/shard_map/ppermute | solution.py:212
  9.2 9.0 %collective-permute-start = (f32[2,128,256]{2,1,0:T(8,128)S(1)}, f32[2,128,256]{2,1,0:T(8,128)S(1)}, u32[]{:S(2)}, u32[]{:S(2)}) collective-permute-start(f32[2,128,256]{2,1,0:T(8,128)S(1)} %get-tuple-element.37), channel_id=1, source_target_pairs={{0,16},{16,32},{32,48},{48,64},{64,80},{80,96},{96,112},{112,128},... | collective-permute-start | bytes 786440 | tf_op jit(solution)/shard_map/ppermute | solution.py:211
  10.0 15.9 %collective-permute-start.3 = (f32[2,256,128]{2,1,0:T(8,128)}, f32[2,256,128]{2,1,0:T(8,128)S(1)}, u32[]{:S(2)}, u32[]{:S(2)}) collective-permute-start(f32[2,256,128]{2,1,0:T(8,128)} %get-tuple-element.34), channel_id=1, source_target_pairs={{1,0},{2,1},{3,2},{4,3},{5,4},{6,5},{7,6},{8,7},{9,8},{10,9},{11,1... | collective-permute-start | bytes 786440 | tf_op jit(solution)/shard_map/ppermute | solution.py:214
  11.0 11.8 %copy-start.1 = (f32[2,2,256,256]{3,2,1,0:T(8,128)S(1)}, f32[2,2,256,256]{3,2,1,0:T(8,128)}, u32[]{:S(2)}) copy-start(f32[2,2,256,256]{3,2,1,0:T(8,128)} %probe.1) | copy-start | bytes 3145732
  11.0 15.0 %collective-permute-start.2 = (f32[2,256,128]{2,1,0:T(8,128)}, f32[2,256,128]{2,1,0:T(8,128)}, u32[]{:S(2)}, u32[]{:S(2)}) collective-permute-start(f32[2,256,128]{2,1,0:T(8,128)} %get-tuple-element.35), channel_id=1, source_target_pairs={{0,1},{1,2},{2,3},{3,4},{4,5},{5,6},{6,7},{7,8},{8,9},{9,10},{10,1... | collective-permute-start | bytes 786440 | tf_op jit(solution)/shard_map/ppermute | solution.py:213
  18.2 4.5 %copy-start.11 = (s32[4,1,2]{0,2,1:T(2,128)S(1)}, s32[4,1,2]{0,2,1:T(2,128)}, u32[]{:S(2)}) copy-start(s32[4,1,2]{0,2,1:T(2,128)} %param.9) | copy-start | bytes 100
  19.0 7.0 %collective-permute-start.4 = (f32[2,2,128,128]{3,2,1,0:T(8,128)}, f32[2,2,128,128]{3,2,1,0:T(8,128)}, u32[]{:S(2)}, u32[]{:S(2)}) collective-permute-start(f32[2,2,128,128]{3,2,1,0:T(8,128)} %pad_maximum_fusion), channel_id=1, source_target_pairs={{0,1},{1,2},{2,3},{3,4},{4,5},{5,6},{6,7},{7,8},{8,9},{9,10},{10,1... | collective-permute-start | bytes 786440 | tf_op jit(solution)/shard_map/ppermute | solution.py:215
  22.0 7.1 %copy-start.2 = (f32[4,1,256,256]{3,2,1,0:T(8,128)S(1)}, f32[4,1,256,256]{3,2,1,0:T(8,128)}, u32[]{:S(2)}) copy-start(f32[4,1,256,256]{3,2,1,0:T(8,128)} %amp.1) | copy-start | bytes 3145732
  22.7 6.4 %collective-permute-start.5 = (f32[2,2,128,128]{3,2,1,0:T(8,128)}, f32[2,2,128,128]{3,2,1,0:T(8,128)}, u32[]{:S(2)}, u32[]{:S(2)}) collective-permute-start(f32[2,2,128,128]{3,2,1,0:T(8,128)} %pad_maximum_fusion.1), channel_id=1, source_target_pairs={{1,0},{2,1},{3,2},{4,3},{5,4},{6,5},{7,6},{8,7},{9,8},{10,9},{11,1... | collective-permute-start | bytes 786440 | tf_op jit(solution)/shard_map/ppermute | solution.py:216
  29.1 1.0 copy-start.5
  30.1 1.0 copy-start.6
  41.1 1.0 copy-start.3
  42.1 3.9 %copy-start.7 = (f32[2,512,128]{2,1,0:T(8,128)}, f32[2,512,128]{2,1,0:T(8,128)S(1)}, u32[]{:S(2)}) copy-start(f32[2,512,128]{2,1,0:T(8,128)S(1)} %get-tuple-element.25) | copy-start | bytes 1572868
  42.1 3.9 %copy-start.9 = (f32[2,512,128]{2,1,0:T(8,128)}, f32[2,512,128]{2,1,0:T(8,128)S(1)}, u32[]{:S(2)}) copy-start(f32[2,512,128]{2,1,0:T(8,128)S(1)} %get-tuple-element.24) | copy-start | bytes 1572868
  42.1 3.8 %collective-permute-start.6 = (f32[16,5,8,256]{3,2,1,0:T(8,128)S(1)}, f32[16,5,8,256]{3,2,1,0:T(8,128)S(1)}, u32[]{:S(2)}, u32[]{:S(2)}) collective-permute-start(f32[16,5,8,256]{3,2,1,0:T(8,128)S(1)} %get-tuple-element.19), channel_id=1, source_target_pairs={{0,1},{1,0},{2,3},{3,2},{4,5},{5,4},{6,7},{7,6},{8,9},{9,8},{10,11... | collective-permute-start | bytes 1966088 | tf_op jit(solution)/shard_map/ppermute | solution.py:224
  46.0 35.4 %copy-start.4 = (f32[2,512,256]{2,1,0:T(8,128)S(1)}, f32[2,512,256]{2,1,0:T(8,128)}, u32[]{:S(2)}) copy-start(f32[2,512,256]{2,1,0:T(8,128)} %copy-done.3) | copy-start | bytes 3145732
  65.2 7.2 %copy-start.8 = (f32[2,512,128]{2,1,0:T(8,128)S(1)}, f32[2,512,128]{2,1,0:T(8,128)}, u32[]{:S(2)}) copy-start(f32[2,512,128]{2,1,0:T(8,128)} %copy-done.7) | copy-start | bytes 1572868
  66.4 6.0 %collective-permute-start.9 = (f32[5,8,256]{2,1,0:T(8,128)S(1)}, f32[5,8,256]{2,1,0:T(8,128)S(1)}, u32[]{:S(2)}, u32[]{:S(2)}) collective-permute-start(f32[5,8,256]{2,1,0:T(8,128)S(1)} %reduce_sum.19), channel_id=1, source_target_pairs={{0,96},{32,64},{64,32},{96,0},{128,224},{160,192},{192,160},{224,1... | collective-permute-start | bytes 122888 | tf_op jit(solution)/shard_map/ppermute | solution.py:229
  68.5 3.9 %collective-permute-start.8 = (f32[5,8,256]{2,1,0:T(8,128)S(1)}, f32[5,8,256]{2,1,0:T(8,128)S(1)}, u32[]{:S(2)}, u32[]{:S(2)}) collective-permute-start(f32[5,8,256]{2,1,0:T(8,128)S(1)} %reduce_sum.19), channel_id=1, source_target_pairs={{0,64},{32,96},{64,0},{96,32},{128,192},{160,224},{192,128},{224,1... | collective-permute-start | bytes 122888 | tf_op jit(solution)/shard_map/ppermute | solution.py:229
  68.5 3.9 %collective-permute-start.7 = (f32[5,8,256]{2,1,0:T(8,128)S(1)}, f32[5,8,256]{2,1,0:T(8,128)S(1)}, u32[]{:S(2)}, u32[]{:S(2)}) collective-permute-start(f32[5,8,256]{2,1,0:T(8,128)S(1)} %reduce_sum.19), channel_id=1, source_target_pairs={{0,32},{32,0},{64,96},{96,64},{128,160},{160,128},{192,224},{224,1... | collective-permute-start | bytes 122888 | tf_op jit(solution)/shard_map/ppermute | solution.py:229
  70.0 9.9 %collective-permute-start.11 = (f32[2,512,128]{2,1,0:T(8,128)}, f32[2,512,128]{2,1,0:T(8,128)}, u32[]{:S(2)}, u32[]{:S(2)}) collective-permute-start(f32[2,512,128]{2,1,0:T(8,128)} %copy-done.9), channel_id=1, source_target_pairs={{0,1},{1,2},{2,3},{3,4},{4,5},{5,6},{6,7},{7,8},{8,9},{9,10},{10,1... | collective-permute-start | bytes 1572872 | tf_op jit(solution)/shard_map/ppermute | solution.py:228
  72.4 9.0 %collective-permute-start.12 = (f32[2,512,128]{2,1,0:T(8,128)S(1)}, f32[2,512,128]{2,1,0:T(8,128)}, u32[]{:S(2)}, u32[]{:S(2)}) collective-permute-start(f32[2,512,128]{2,1,0:T(8,128)S(1)} %copy-done.8), channel_id=1, source_target_pairs={{1,0},{2,1},{3,2},{4,3},{5,4},{6,5},{7,6},{8,7},{9,8},{10,9},{11,1... | collective-permute-start | bytes 1572872 | tf_op jit(solution)/shard_map/ppermute | solution.py:227
  72.5 7.4 %collective-permute-start.10 = (f32[5,8,256]{2,1,0:T(8,128)S(1)}, f32[5,8,256]{2,1,0:T(8,128)S(1)}, u32[]{:S(2)}, u32[]{:S(2)}) collective-permute-start(f32[5,8,256]{2,1,0:T(8,128)S(1)} %add_add_fusion), channel_id=1, source_target_pairs={{0,128},{32,160},{64,192},{96,224},{128,0},{160,32},{192,64},{224,... | collective-permute-start | bytes 122888 | tf_op jit(solution)/shard_map/ppermute | solution.py:231
  83.7 10.4 %copy-start.10 = (f32[2,512,256]{2,1,0:T(8,128)S(1)}, f32[2,512,256]{2,1,0:T(8,128)}, u32[]{:S(2)}) copy-start(f32[2,512,256]{2,1,0:T(8,128)} %maximum_add_fusion) | copy-start | bytes 3145732
  84.6 27.9 %all-to-all-start.1 = ((f32[16,4,8,256]{3,2,1,0:T(8,128)}), f32[16,4,8,256]{3,2,1,0:T(8,128)S(1)}, u32[]{:S(2)}, u32[]{:S(2)}) async-start(f32[16,4,8,256]{3,2,1,0:T(8,128)} %broadcast_in_dim.2), calls=%async_computation.1 | async-start | bytes 1048576 | tf_op jit(solution)/shard_map/all_to_all | solution.py:241
  94.2 16.1 %collective-permute-start.14 = (f32[2,128,256]{2,1,0:T(8,128)S(1)}, f32[2,128,256]{2,1,0:T(8,128)S(1)}, u32[]{:S(2)}, u32[]{:S(2)}) collective-permute-start(f32[2,128,256]{2,1,0:T(8,128)S(1)} %get-tuple-element.32), channel_id=1, source_target_pairs={{0,16},{16,32},{32,48},{48,64},{64,80},{80,96},{96,112},{112,128},... | collective-permute-start | bytes 786440 | tf_op jit(solution)/shard_map/ppermute | solution.py:240
  95.6 16.8 %collective-permute-start.13 = (f32[2,128,256]{2,1,0:T(8,128)S(1)}, f32[2,128,256]{2,1,0:T(8,128)S(1)}, u32[]{:S(2)}, u32[]{:S(2)}) collective-permute-start(f32[2,128,256]{2,1,0:T(8,128)S(1)} %get-tuple-element.33), channel_id=1, source_target_pairs={{16,0},{32,16},{48,32},{64,48},{80,64},{96,80},{112,96},{128,112},... | collective-permute-start | bytes 786440 | tf_op jit(solution)/shard_map/ppermute | solution.py:239
  112.4 1.9 %collective-permute-start.15 = (f32[16,4,8,256]{3,2,1,0:T(8,128)S(1)}, f32[16,4,8,256]{3,2,1,0:T(8,128)S(1)}, u32[]{:S(2)}, u32[]{:S(2)}) collective-permute-start(f32[16,4,8,256]{3,2,1,0:T(8,128)S(1)} %all-to-all-done.1.own), channel_id=1, source_target_pairs={{0,1},{1,0},{2,3},{3,2},{4,5},{5,4},{6,7},{7,6},{8,9},{9,8},{10,11... | collective-permute-start | bytes 1572872 | tf_op jit(solution)/shard_map/ppermute | solution.py:243

commit v4 on v3

--- a/solution.py
+++ b/solution.py
@@ -33,10 +33,16 @@
 
 
 def kernel(
-    offs, half, tile, top, bot, left, right, left_ends, right_ends, probe, amp, fwd, bwd,
+    offs, half, tile, top, bot, left, right, left_ends, right_ends, probe, amp, fwd_hbm, bwd_hbm,
     mine, other, out_left, out_mid, out_right,
-    ext, acc, win, stack, side, far, weight, grads,
+    ext, acc, win, stack, side, far, weight, grads, power, fwd, bwd, sems,
 ):
+    copies = [
+        pltpu.make_async_copy(fwd_hbm, fwd, sems.at[0]),
+        pltpu.make_async_copy(bwd_hbm, bwd, sems.at[1]),
+    ]
+    for copy in copies:
+        copy.start()
     lanes = lax.broadcasted_iota(jnp.int32, (CH, HALF), 1)
     for q in range(2):
         cols = pl.ds(q * HALF, HALF)
@@ -50,10 +56,21 @@
     acc[...] = jnp.zeros_like(acc)
     weight[...] = jnp.zeros_like(weight)
     grads[...] = jnp.zeros_like(grads)
+    top_power = jnp.zeros((CH, W), F32)
+    for i in range(W // CH):
+        rows = pl.ds(i * CH, CH)
+        total = jnp.zeros((CH, W), F32)
+        for k in range(MODES):
+            total += probe[k, 0, rows, :] * probe[k, 0, rows, :] + probe[k, 1, rows, :] * probe[k, 1, rows, :]
+        power[rows, :] = total
+        top_power = jnp.maximum(top_power, total)
+    scale = 1.0 / (jnp.max(top_power, axis=(0, 1), keepdims=True) + 1e-06)
+    for copy in copies:
+        copy.wait()
 
     def position(p, carry):
-        r = offs[p, 0, 0] + HALF
-        c = offs[p, 0, 1] + HALF
+        r = offs[2 * p] + HALF
+        c = offs[2 * p + 1] + HALF
         q = c // HALF
         s = c - q * HALF
         back_shift = lax.rem(HALF - s, HALF)
@@ -110,7 +127,7 @@
             rows = pl.ds(pl.multiple_of(i * CH, CH), CH)
             wr = win[0, rows, :]
             wi = win[1, rows, :]
-            power = jnp.zeros((CH, W), F32)
+            both = power[rows, :]
             tr = jnp.zeros((CH, W), F32)
             ti = jnp.zeros((CH, W), F32)
             for k in range(MODES):
@@ -118,13 +135,12 @@
                 pi = probe[k, 1, rows, :]
                 br = far[k, rows, 0:W]
                 bi = far[k, rows, W:]
-                power += pr * pr + pi * pi
                 tr += pr * br + pi * bi
                 ti += pr * bi - pi * br
                 grads[2 * k, rows, :] += wr * br + wi * bi
                 grads[2 * k + 1, rows, :] += wr * bi - wi * br
             dst = pl.ds(r + i * CH, CH)
-            for d, t in ((0, tr - power * wr), (1, ti - power * wi)):
+            for d, t in ((0, tr - both * wr), (1, ti - both * wi)):
                 a = pltpu.roll(t[:, 0:HALF], s, 1)
                 b = pltpu.roll(t[:, HALF:], s, 1)
                 low = lanes < s
@@ -137,10 +153,17 @@
         return carry
 
     lax.fori_loop(0, POS, position, 0)
-    out_left[...] = acc[:, 0]
-    out_mid[:, :, 0:HALF] = acc[:, 1]
-    out_mid[:, :, HALF:] = acc[:, 2]
-    out_right[...] = acc[:, 3]
+    for d in range(2):
+        for i in range(2 * W // HALF):
+            rows = pl.ds(i * HALF, HALF)
+            out_left[d, rows, :] = acc[d, 0, rows, :] * scale
+            out_right[d, rows, :] = acc[d, 3, rows, :] * scale
+            for q in range(2):
+                cols = pl.ds(q * HALF, HALF)
+                step = acc[d, q + 1, rows, :] * scale
+                if 1 <= i <= 2:
+                    step += tile[d, pl.ds((i - 1) * HALF, HALF), cols]
+                out_mid[d, rows, cols] = step
     h = half[0]
     for out, side_of in ((mine, h), (other, 1 - h)):
 
@@ -163,7 +186,7 @@
     return pl.pallas_call(
         kernel,
         out_shape=(part, part, strip, jax.ShapeDtypeStruct((2, 2 * W, W), F32), strip),
-        in_specs=[smem, smem] + [vmem] * 11,
+        in_specs=[smem, smem] + [vmem] * 9 + [pl.BlockSpec(memory_space=pl.ANY)] * 2,
         out_specs=(vmem,) * 5,
         scratch_shapes=[
             pltpu.VMEM((2, 4, 2 * W, HALF), F32),
@@ -174,6 +197,10 @@
             pltpu.VMEM((MODES, W, 2 * W), F32),
             pltpu.VMEM((W, W), F32),
             pltpu.VMEM((2 * MODES, W, W), F32),
+            pltpu.VMEM((W, W), F32),
+            pltpu.VMEM((2 * W, 2 * W), BF),
+            pltpu.VMEM((2 * W, 2 * W), BF),
+            pltpu.SemaphoreType.DMA((2,)),
         ],
         compiler_params=pltpu.CompilerParams(vmem_limit_bytes=20 << 20),
     )(offsets, half, *border, probe, amplitude, jnp.asarray(fwd), jnp.asarray(bwd))
@@ -207,6 +234,12 @@
 
 
 def body(object_field, probe_field, amplitude, offsets):
+    group = ("xh", "xl", "y")
+    co = lax.axis_index("co")
+    half = co.reshape(1)
+    block = (co * 16 + lax.axis_index(group)) * 8
+    offs = offsets.reshape(2 * POS)
+    object_field, half, block, offs = lax.optimization_barrier((object_field, half, block, offs))
     first, last = slice(0, HALF), slice(HALF, W)
     top = lax.ppermute(object_field[:, last], GX, UP)
     bot = lax.ppermute(object_field[:, first], GX, DOWN)
@@ -214,35 +247,29 @@
     right = lax.ppermute(object_field[:, :, first], GY, DOWN)
     left_ends = lax.ppermute(jnp.stack([top[:, :, last], bot[:, :, last]]), GY, UP)
     right_ends = lax.ppermute(jnp.stack([top[:, :, first], bot[:, :, first]]), GY, DOWN)
-    co = lax.axis_index("co")
-    half = co.reshape(1)
-    scale_max = jnp.max(jnp.sum(probe_field * probe_field, axis=(0, 1))) + 1e-06
-    half, scale_max = lax.optimization_barrier((half, scale_max))
     border = (object_field, top, bot, left, right, left_ends, right_ends)
-    mine, other, out_left, out_mid, out_right = correct(offsets, half, border, probe_field, amplitude)
-    group = ("xh", "xl", "y")
-    part = mine + lax.ppermute(other, "co", SWAP)
-    part = jnp.sum(lax.all_to_all(part, group, 0, 0, tiled=True), 0)
-    part, out_left, out_right = lax.optimization_barrier((part, out_left, out_right))
+    mine, other, out_left, out_mid, out_right = correct(offs, half, border, probe_field, amplitude)
     from_right = lax.ppermute(out_left, GY, DOWN)
     from_left = lax.ppermute(out_right, GY, UP)
+    part = mine + lax.ppermute(other, "co", SWAP)
+    pieces = lax.all_to_all(part, group, 0, 0, tiled=True)
+    part = sum(pieces[i] for i in range(16))
+    part, from_left, from_right = lax.optimization_barrier((part, from_left, from_right))
+    folded = out_mid + jnp.concatenate([from_left, from_right], 2)
+    from_below = lax.ppermute(folded[:, :HALF], GX, DOWN)
+    from_above = lax.ppermute(folded[:, HALF + W :], GX, UP)
     peers = [lax.ppermute(part, "z", [(i, i ^ step) for i in range(8)]) for step in (1, 2, 3)]
     part = (part + peers[0]) + (peers[1] + peers[2])
+    part, from_below, from_above = lax.optimization_barrier((part, from_below, from_above))
     part = part + lax.ppermute(part, "z", [(i, i ^ 4) for i in range(8)])
-    block = co * 16 + lax.axis_index(group)
     planes = probe_field.reshape(2 * MODES, W, W)
-    local = lax.dynamic_slice_in_dim(planes, block * 8, 8, 1)
+    local = lax.dynamic_slice_in_dim(planes, block, 8, 1)
     weight = part[2 * MODES]
     local = local + (part[: 2 * MODES] - local * weight) / (weight + 1e-05)
-    folded = out_mid + jnp.concatenate([from_left, from_right], 2)
-    local, folded = lax.optimization_barrier((local, folded))
-    from_below = lax.ppermute(folded[:, :HALF], GX, DOWN)
-    from_above = lax.ppermute(folded[:, HALF + W :], GX, UP)
     gathered = lax.all_to_all(jnp.broadcast_to(local[None], (16,) + local.shape), group, 0, 0, tiled=True)
-    gathered, from_below, from_above = lax.optimization_barrier((gathered, from_below, from_above))
+    updated_object = folded[:, HALF : HALF + W] + jnp.concatenate([from_above, from_below], 1)
     updated_probe = arrange(half, gathered, lax.ppermute(gathered, "co", SWAP))
-    object_step = folded[:, HALF : HALF + W] + jnp.concatenate([from_above, from_below], 1)
-    return (object_field + object_step / scale_max, updated_probe)
+    return (updated_object, updated_probe)
 
 
 def solution(mesh):

time: 116 us -> 113 us (0.974)
  waiting for transfers between devices: 29.2 us -> 39 us
  blocking collectives: 19.1 us -> 14.5 us
  other arithmetic: 8.41 us -> 4.28 us
  local copies, waits for them, and re-layouts: 6.04 us -> 2.14 us
    all_to_all x1, waiting for transfers between devices: 0.01 us -> 9.46 us  [body(): pieces = lax.all_to_all(part, group, 0, 0, tiled=True)]
    ppermute x1, waiting for transfers between devices: 11.3 us -> 3.74 us  [body(): from_above = lax.ppermute(folded[:, HALF + W:], GX, UP)]
    ppermute x1, starting transfers between devices: 0.01 us -> 4.69 us  [body(): updated_probe = arrange(half, gathered, lax.ppermute(gathered, 'co', SWAP))]
    all_to_all x1, blocking collectives: 19.1 us -> 14.5 us  [body(): lax.all_to_all(jnp.broadcast_to(local[None], (16,) + local.shape), group,...]
    ppermute x1, waiting for transfers between devices: 0.01 us -> 3.18 us  [body(): lax.ppermute(jnp.stack([top[:, :, last], bot[:, :, last]]), GY, UP)]
    ppermute x1, waiting for transfers between devices: 2.1 us -> 4.84 us  [body(): from_below = lax.ppermute(folded[:, :HALF], GX, DOWN)]
    all_to_all x1, starting transfers between devices: 9.58 us -> 6.87 us  [body(): pieces = lax.all_to_all(part, group, 0, 0, tiled=True)]
    unnamed x25 -> x13, local copies, waits for them, and re-layouts: 3.18 us -> 0.78 us
  transfers between devices with their start and end apart: 17 -> 17, of which waited for: 9 -> 12; matrix products, arithmetic and copies ran while one was open for 5% -> 3% of each run, Pallas kernels for 0% -> 0%
where the time goes in v4:
time: 113 us; the launch traced here: 112 us
  starting transfers between devices  40.8 us (36%)
  waiting for transfers between devices  39 us (35%)
  blocking collectives  14.5 us (13%)
  Pallas kernels  10.8 us (10%)
  other arithmetic  4.28 us (4%)
  local copies, waits for them, and re-layouts  2.14 us (2%)
    all_to_all x1, blocking collectives, body(): lax.all_to_all(jnp.broadcast_to(local[None], (16,) + local.shape), group,...  14.5 us
    pallas_call x1, Pallas kernels, correct(): pl.pallas_call(kernel, out_shape=(part, part, strip, jax.ShapeDtypeStruct...  9.71 us
    all_to_all x1, waiting for transfers between devices, body(): pieces = lax.all_to_all(part, group, 0, 0, tiled=True)  9.46 us
    ppermute x1, starting transfers between devices, body(): bot = lax.ppermute(object_field[:, first], GX, DOWN)  7.41 us
    all_to_all x1, starting transfers between devices, body(): pieces = lax.all_to_all(part, group, 0, 0, tiled=True)  6.87 us
    ppermute x1, waiting for transfers between devices, body(): from_below = lax.ppermute(folded[:, :HALF], GX, DOWN)  4.84 us
    ppermute x1, starting transfers between devices, body(): part = part + lax.ppermute(part, 'z', [(i, i ^ 4) for i in range(8)])  4.72 us
    ppermute x1, starting transfers between devices, body(): updated_probe = arrange(half, gathered, lax.ppermute(gathered, 'co', SWAP))  4.69 us
  transfers between devices with their start and end apart: 17, of which 12 were waited for; matrix products, arithmetic and copies ran while one was open for 3% of the time, Pallas kernels for 0%

profile of v4, /device:TPU:1, one launch (start us, length us, event | category | flops | bytes accessed | tf_op | source)
XLA Modules:
  0.0 112.2 jit_solution(13308765630983226364)
XLA Ops:
  0.6 0.0 copy-start.5
  0.7 0.7 copy-done.5
  1.3 0.1 copy.9
  1.4 0.1 reshape.19.offs
  1.5 1.1 %fusion.5 = (f32[2,128,256]{2,1,0:T(8,128)S(1)}, f32[2,128,256]{2,1,0:T(8,128)S(1)}) fusion(f32[2,256,256]{2,1,0:T(8,128)} %tile), kind=kLoop, calls=%fused_computation.32 | loop fusion | bytes 1048576 | tf_op jit(solution)/shard_map/slice | solution.py:245
  2.6 7.4 %collective-permute-start.1 = (f32[2,128,256]{2,1,0:T(8,128)S(1)}, f32[2,128,256]{2,1,0:T(8,128)S(1)}, u32[]{:S(2)}, u32[]{:S(2)}) collective-permute-start(f32[2,128,256]{2,1,0:T(8,128)S(1)} %get-tuple-element.36), channel_id=1, source_target_pairs={{16,0},{32,16},{48,32},{64,48},{80,64},{96,80},{112,96},{128,112},... | collective-permute-start | bytes 786440 | tf_op jit(solution)/shard_map/ppermute | solution.py:245
  10.0 0.0 collective-permute-start
  10.0 0.0 copy-done
  10.1 1.0 collective-permute-start.3
  11.1 1.3 %collective-permute-start.2 = (f32[2,256,128]{2,1,0:T(8,128)S(1)}, f32[2,256,128]{2,1,0:T(8,128)S(1)}, u32[]{:S(2)}, u32[]{:S(2)}) collective-permute-start(f32[2,256,128]{2,1,0:T(8,128)S(1)} %get-tuple-element.35), channel_id=1, source_target_pairs={{0,1},{1,2},{2,3},{3,4},{4,5},{5,6},{6,7},{7,8},{8,9},{9,10},{10,1... | collective-permute-start | bytes 786440 | tf_op jit(solution)/shard_map/ppermute | solution.py:246
  12.4 2.6 %collective-permute-done.1.bot = f32[2,128,256]{2,1,0:T(8,128)S(1)} collective-permute-done((f32[2,128,256]{2,1,0:T(8,128)S(1)}, f32[2,128,256]{2,1,0:T(8,128)S(1)}, u32[]{:S(2)}, u32[]{:S(2)}) %collective-permute-start.1) | collective-permute-done | bytes 262176 | tf_op jit(solution)/shard_map/ppermute | solution.py:245
  15.1 4.0 %collective-permute-done.top = f32[2,128,256]{2,1,0:T(8,128)S(1)} collective-permute-done((f32[2,128,256]{2,1,0:T(8,128)S(1)}, f32[2,128,256]{2,1,0:T(8,128)S(1)}, u32[]{:S(2)}, u32[]{:S(2)}) %collective-permute-start) | collective-permute-done | bytes 262176 | tf_op jit(solution)/shard_map/ppermute | solution.py:244
  19.1 3.1 %collective-permute-start.4 = (f32[2,2,128,128]{3,2,1,0:T(8,128)S(1)}, f32[2,2,128,128]{3,2,1,0:T(8,128)S(1)}, u32[]{:S(2)}, u32[]{:S(2)}) collective-permute-start(f32[2,2,128,128]{3,2,1,0:T(8,128)S(1)} %pad_maximum_fusion), channel_id=1, source_target_pairs={{0,1},{1,2},{2,3},{3,4},{4,5},{5,6},{6,7},{7,8},{8,9},{9,10},{10,1... | collective-permute-start | bytes 786440 | tf_op jit(solution)/shard_map/ppermute | solution.py:248
  22.2 0.1 collective-permute-start.5
  22.3 0.0 collective-permute-done.3.right
  22.3 0.0 collective-permute-done.2.left
  22.3 3.2 %collective-permute-done.4.left_ends = f32[2,2,128,128]{3,2,1,0:T(8,128)S(1)} collective-permute-done((f32[2,2,128,128]{3,2,1,0:T(8,128)S(1)}, f32[2,2,128,128]{3,2,1,0:T(8,128)S(1)}, u32[]{:S(2)}, u32[]{:S(2)}) %collective-permute-start.4) | collective-permute-done | bytes 262176 | tf_op jit(solution)/shard_map/ppermute | solution.py:248
  25.5 2.9 %collective-permute-done.5.right_ends = f32[2,2,128,128]{3,2,1,0:T(8,128)S(1)} collective-permute-done((f32[2,2,128,128]{3,2,1,0:T(8,128)S(1)}, f32[2,2,128,128]{3,2,1,0:T(8,128)S(1)}, u32[]{:S(2)}, u32[]{:S(2)}) %collective-permute-start.5) | collective-permute-done | bytes 262176 | tf_op jit(solution)/shard_map/ppermute | solution.py:249
  28.4 0.0 copy-done.3
  28.4 9.7 %shard_map.77 = (f32[16,5,8,256]{3,2,1,0:T(8,128)S(1)}, f32[16,5,8,256]{3,2,1,0:T(8,128)S(1)}, f32[2,512,128]{2,1,0:T(8,128)S(1)}, f32[2,512,256]{2,1,0:T(8,128)S(1)}, f32[2,512,128]{2,1,0:T(8,128)S(1)}) custom-call(s32[8]{0:T(128)S(1)} %reshape.19.offs, s32[1]{0:T(128)} %bitcast.half, f32[2,256,256]{2,1,0:T(8,128)S(1)} %copy-done, ...), custom_call_target="tpu_custom_call" | custom-call | tf_op jit(solution)/shard_map/pallas_call | solution.py:186
  38.1 2.2 %collective-permute-start.6 = (f32[16,5,8,256]{3,2,1,0:T(8,128)S(1)}, f32[16,5,8,256]{3,2,1,0:T(8,128)S(1)}, u32[]{:S(2)}, u32[]{:S(2)}) collective-permute-start(f32[16,5,8,256]{3,2,1,0:T(8,128)S(1)} %get-tuple-element.22), channel_id=1, source_target_pairs={{0,1},{1,0},{2,3},{3,2},{4,5},{5,4},{6,7},{7,6},{8,9},{9,8},{10,11... | collective-permute-start | bytes 1966088 | tf_op jit(solution)/shard_map/ppermute | solution.py:254
  40.3 1.7 %collective-permute-done.6 = f32[16,5,8,256]{3,2,1,0:T(8,128)S(1)} collective-permute-done((f32[16,5,8,256]{3,2,1,0:T(8,128)S(1)}, f32[16,5,8,256]{3,2,1,0:T(8,128)S(1)}, u32[]{:S(2)}, u32[]{:S(2)}) %collective-permute-start.6) | collective-permute-done | bytes 655392 | tf_op jit(solution)/shard_map/ppermute | solution.py:254
  42.1 0.9 add.97
  43.0 6.9 %all-to-all-start = ((f32[16,5,8,256]{3,2,1,0:T(8,128)}), f32[16,5,8,256]{3,2,1,0:T(8,128)}, u32[]{:S(2)}, u32[]{:S(2)}) async-start(f32[16,5,8,256]{3,2,1,0:T(8,128)} %add.97), calls=%async_computation | async-start | bytes 1310720 | tf_op jit(solution)/shard_map/all_to_all | solution.py:255
  49.9 1.9 %collective-permute-start.7 = (f32[2,512,128]{2,1,0:T(8,128)S(1)}, f32[2,512,128]{2,1,0:T(8,128)}, u32[]{:S(2)}, u32[]{:S(2)}) collective-permute-start(f32[2,512,128]{2,1,0:T(8,128)S(1)} %get-tuple-element.23), channel_id=1, source_target_pairs={{0,1},{1,2},{2,3},{3,4},{4,5},{5,6},{6,7},{7,8},{8,9},{9,10},{10,1... | collective-permute-start | bytes 1572872 | tf_op jit(solution)/shard_map/ppermute | solution.py:253
  51.8 0.0 collective-permute-start.8
  51.8 9.5 %all-to-all-done = f32[16,5,8,256]{3,2,1,0:T(8,128)} async-done(((f32[16,5,8,256]{3,2,1,0:T(8,128)}), f32[16,5,8,256]{3,2,1,0:T(8,128)}, u32[]{:S(2)}, u32[]{:S(2)}) %all-to-all-start) | async-done | bytes 655392 | tf_op jit(solution)/shard_map/all_to_all | solution.py:255
  61.2 1.1 fusion
  62.4 0.8 collective-permute-done.7
  63.2 2.9 %collective-permute-done.8 = f32[2,512,128]{2,1,0:T(8,128)} collective-permute-done((f32[2,512,128]{2,1,0:T(8,128)S(1)}, f32[2,512,128]{2,1,0:T(8,128)}, u32[]{:S(2)}, u32[]{:S(2)}) %collective-permute-start.8) | collective-permute-done | bytes 524320 | tf_op jit(solution)/shard_map/ppermute | solution.py:252
  66.0 2.1 %collective-permute-start.11 = (f32[5,8,256]{2,1,0:T(8,128)S(1)}, f32[5,8,256]{2,1,0:T(8,128)S(1)}, u32[]{:S(2)}, u32[]{:S(2)}) collective-permute-start(f32[5,8,256]{2,1,0:T(8,128)S(1)} %fusion), channel_id=1, source_target_pairs={{0,96},{32,64},{64,32},{96,0},{128,224},{160,192},{192,160},{224,1... | collective-permute-start | bytes 122888 | tf_op jit(solution)/shard_map/ppermute | solution.py:261
  68.2 0.0 collective-permute-start.10
  68.2 1.4 %collective-permute-start.9 = (f32[5,8,256]{2,1,0:T(8,128)S(1)}, f32[5,8,256]{2,1,0:T(8,128)S(1)}, u32[]{:S(2)}, u32[]{:S(2)}) collective-permute-start(f32[5,8,256]{2,1,0:T(8,128)S(1)} %fusion), channel_id=1, source_target_pairs={{0,32},{32,0},{64,96},{96,64},{128,160},{160,128},{192,224},{224,1... | collective-permute-start | bytes 122888 | tf_op jit(solution)/shard_map/ppermute | solution.py:261
  69.6 1.3 %maximum_add_fusion = f32[2,512,256]{2,1,0:T(8,128)S(1)} fusion(f32[2,512,256]{2,1,0:T(8,128)S(1)} %get-tuple-element.20, f32[2,512,128]{2,1,0:T(8,128)} %collective-permute-done.8, f32[2,512,128]{2,1,0:T(8,128)} %collective-permute-done.7), kind=kLoop, calls=%fused_computation | loop fusion | flops 524288 | bytes 3145728 | tf_op jit(solution)/shard_map/add | solution.py:258
  70.9 0.6 collective-permute-start.13
  71.5 3.4 %collective-permute-start.12 = (f32[2,128,256]{2,1,0:T(8,128)S(1)}, f32[2,128,256]{2,1,0:T(8,128)S(1)}, u32[]{:S(2)}, u32[]{:S(2)}) collective-permute-start(f32[2,128,256]{2,1,0:T(8,128)S(1)} %get-tuple-element.33), channel_id=1, source_target_pairs={{16,0},{32,16},{48,32},{64,48},{80,64},{96,80},{112,96},{128,112},... | collective-permute-start | bytes 786440 | tf_op jit(solution)/shard_map/ppermute | solution.py:259
  74.9 0.0 collective-permute-done.11
  74.9 0.0 collective-permute-done.10
  74.9 0.0 collective-permute-done.9
  74.9 3.7 %collective-permute-done.13 = f32[2,128,256]{2,1,0:T(8,128)S(1)} collective-permute-done((f32[2,128,256]{2,1,0:T(8,128)S(1)}, f32[2,128,256]{2,1,0:T(8,128)S(1)}, u32[]{:S(2)}, u32[]{:S(2)}) %collective-permute-start.13) | collective-permute-done | bytes 262176 | tf_op jit(solution)/shard_map/ppermute | solution.py:260
  78.7 4.8 %collective-permute-done.12 = f32[2,128,256]{2,1,0:T(8,128)S(1)} collective-permute-done((f32[2,128,256]{2,1,0:T(8,128)S(1)}, f32[2,128,256]{2,1,0:T(8,128)S(1)}, u32[]{:S(2)}, u32[]{:S(2)}) %collective-permute-start.12) | collective-permute-done | bytes 262176 | tf_op jit(solution)/shard_map/ppermute | solution.py:259
  83.5 4.7 %collective-permute-start.14 = (f32[5,8,256]{2,1,0:T(8,128)S(1)}, f32[5,8,256]{2,1,0:T(8,128)S(1)}, u32[]{:S(2)}, u32[]{:S(2)}) collective-permute-start(f32[5,8,256]{2,1,0:T(8,128)S(1)} %add_add_fusion), channel_id=1, source_target_pairs={{0,128},{32,160},{64,192},{96,224},{128,0},{160,32},{192,64},{224,... | collective-permute-start | bytes 122888 | tf_op jit(solution)/shard_map/ppermute | solution.py:264
  88.2 2.1 %collective-permute-done.14 = f32[5,8,256]{2,1,0:T(8,128)S(1)} collective-permute-done((f32[5,8,256]{2,1,0:T(8,128)S(1)}, f32[5,8,256]{2,1,0:T(8,128)S(1)}, u32[]{:S(2)}, u32[]{:S(2)}) %collective-permute-start.14) | collective-permute-done | bytes 40992 | tf_op jit(solution)/shard_map/ppermute | solution.py:264
  90.5 14.5 %all_to_all.10.own = f32[16,4,8,256]{3,2,1,0:T(8,128)S(1)} all-to-all(f32[16,4,8,256]{3,2,1,0:T(8,128)S(1)} %broadcast_in_dim.2), channel_id=1, replica_groups=mesh['z'=8,'xl'=2,'xh'=2,'y'=4,'co'=2] {'xh','xl','y'}, dimensions={0} | all-to-all | bytes 1048576 | tf_op jit(solution)/shard_map/all_to_all | solution.py:269
  105.0 4.7 %collective-permute-start.15 = (f32[16,4,8,256]{3,2,1,0:T(8,128)S(1)}, f32[16,4,8,256]{3,2,1,0:T(8,128)S(1)}, u32[]{:S(2)}, u32[]{:S(2)}) collective-permute-start(f32[16,4,8,256]{3,2,1,0:T(8,128)S(1)} %all_to_all.10.own), channel_id=1, source_target_pairs={{0,1},{1,0},{2,3},{3,2},{4,5},{5,4},{6,7},{7,6},{8,9},{9,8},{10,11... | collective-permute-start | bytes 1572872 | tf_op jit(solution)/shard_map/ppermute | solution.py:271
  109.7 0.9 slice_add_fusion
  110.5 0.7 collective-permute-done.15.swapped
  111.2 1.0 shard_map.78
  (19 shorter events, 0.3 us)
Async XLA Ops:
  0.6 0.7 copy-start.5
  1.5 8.5 %copy-start = (f32[2,256,256]{2,1,0:T(8,128)S(1)}, f32[2,256,256]{2,1,0:T(8,128)}, u32[]{:S(2)}) copy-start(f32[2,256,256]{2,1,0:T(8,128)} %tile) | copy-start | bytes 1572868
  2.6 12.4 %collective-permute-start.1 = (f32[2,128,256]{2,1,0:T(8,128)S(1)}, f32[2,128,256]{2,1,0:T(8,128)S(1)}, u32[]{:S(2)}, u32[]{:S(2)}) collective-permute-start(f32[2,128,256]{2,1,0:T(8,128)S(1)} %get-tuple-element.36), channel_id=1, source_target_pairs={{16,0},{32,16},{48,32},{64,48},{80,64},{96,80},{112,96},{128,112},... | collective-permute-start | bytes 786440 | tf_op jit(solution)/shard_map/ppermute | solution.py:245
  10.0 9.0 %collective-permute-start = (f32[2,128,256]{2,1,0:T(8,128)S(1)}, f32[2,128,256]{2,1,0:T(8,128)S(1)}, u32[]{:S(2)}, u32[]{:S(2)}) collective-permute-start(f32[2,128,256]{2,1,0:T(8,128)S(1)} %get-tuple-element.37), channel_id=1, source_target_pairs={{0,16},{16,32},{32,48},{48,64},{64,80},{80,96},{96,112},{112,128},... | collective-permute-start | bytes 786440 | tf_op jit(solution)/shard_map/ppermute | solution.py:244
  10.0 18.3 %copy-start.3 = (bf16[512,512]{1,0:T(8,128)(2,1)S(1)}, bf16[512,512]{1,0:T(8,128)(2,1)}, u32[]{:S(2)}) copy-start(bf16[512,512]{1,0:T(8,128)(2,1)} %constant.32.clone.bwd_hbm) | copy-start | bytes 1572868
  10.0 18.3 %copy-start.4 = (bf16[512,512]{1,0:T(8,128)(2,1)S(1)}, bf16[512,512]{1,0:T(8,128)(2,1)}, u32[]{:S(2)}) copy-start(bf16[512,512]{1,0:T(8,128)(2,1)} %constant.31.clone.fwd_hbm) | copy-start | bytes 1572868
  10.1 12.2 %collective-permute-start.3 = (f32[2,256,128]{2,1,0:T(8,128)S(1)}, f32[2,256,128]{2,1,0:T(8,128)S(1)}, u32[]{:S(2)}, u32[]{:S(2)}) collective-permute-start(f32[2,256,128]{2,1,0:T(8,128)S(1)} %get-tuple-element.34), channel_id=1, source_target_pairs={{1,0},{2,1},{3,2},{4,3},{5,4},{6,5},{7,6},{8,7},{9,8},{10,9},{11,1... | collective-permute-start | bytes 786440 | tf_op jit(solution)/shard_map/ppermute | solution.py:247
  11.1 17.2 %copy-start.1 = (f32[2,2,256,256]{3,2,1,0:T(8,128)S(1)}, f32[2,2,256,256]{3,2,1,0:T(8,128)}, u32[]{:S(2)}) copy-start(f32[2,2,256,256]{3,2,1,0:T(8,128)} %probe.1) | copy-start | bytes 3145732
  11.1 17.2 %copy-start.2 = (f32[4,1,256,256]{3,2,1,0:T(8,128)S(1)}, f32[4,1,256,256]{3,2,1,0:T(8,128)}, u32[]{:S(2)}) copy-start(f32[4,1,256,256]{3,2,1,0:T(8,128)} %amp.1) | copy-start | bytes 3145732
  11.1 11.2 %collective-permute-start.2 = (f32[2,256,128]{2,1,0:T(8,128)S(1)}, f32[2,256,128]{2,1,0:T(8,128)S(1)}, u32[]{:S(2)}, u32[]{:S(2)}) collective-permute-start(f32[2,256,128]{2,1,0:T(8,128)S(1)} %get-tuple-element.35), channel_id=1, source_target_pairs={{0,1},{1,2},{2,3},{3,4},{4,5},{5,6},{6,7},{7,8},{8,9},{9,10},{10,1... | collective-permute-start | bytes 786440 | tf_op jit(solution)/shard_map/ppermute | solution.py:246
  19.1 6.4 %collective-permute-start.4 = (f32[2,2,128,128]{3,2,1,0:T(8,128)S(1)}, f32[2,2,128,128]{3,2,1,0:T(8,128)S(1)}, u32[]{:S(2)}, u32[]{:S(2)}) collective-permute-start(f32[2,2,128,128]{3,2,1,0:T(8,128)S(1)} %pad_maximum_fusion), channel_id=1, source_target_pairs={{0,1},{1,2},{2,3},{3,4},{4,5},{5,6},{6,7},{7,8},{8,9},{9,10},{10,1... | collective-permute-start | bytes 786440 | tf_op jit(solution)/shard_map/ppermute | solution.py:248
  22.2 6.2 %collective-permute-start.5 = (f32[2,2,128,128]{3,2,1,0:T(8,128)S(1)}, f32[2,2,128,128]{3,2,1,0:T(8,128)S(1)}, u32[]{:S(2)}, u32[]{:S(2)}) collective-permute-start(f32[2,2,128,128]{3,2,1,0:T(8,128)S(1)} %pad_maximum_fusion.1), channel_id=1, source_target_pairs={{1,0},{2,1},{3,2},{4,3},{5,4},{6,5},{7,6},{8,7},{9,8},{10,9},{11,1... | collective-permute-start | bytes 786440 | tf_op jit(solution)/shard_map/ppermute | solution.py:249
  38.1 4.0 %collective-permute-start.6 = (f32[16,5,8,256]{3,2,1,0:T(8,128)S(1)}, f32[16,5,8,256]{3,2,1,0:T(8,128)S(1)}, u32[]{:S(2)}, u32[]{:S(2)}) collective-permute-start(f32[16,5,8,256]{3,2,1,0:T(8,128)S(1)} %get-tuple-element.22), channel_id=1, source_target_pairs={{0,1},{1,0},{2,3},{3,2},{4,5},{5,4},{6,7},{7,6},{8,9},{9,8},{10,11... | collective-permute-start | bytes 1966088 | tf_op jit(solution)/shard_map/ppermute | solution.py:254
  43.0 18.3 %all-to-all-start = ((f32[16,5,8,256]{3,2,1,0:T(8,128)}), f32[16,5,8,256]{3,2,1,0:T(8,128)}, u32[]{:S(2)}, u32[]{:S(2)}) async-start(f32[16,5,8,256]{3,2,1,0:T(8,128)} %add.97), calls=%async_computation | async-start | bytes 1310720 | tf_op jit(solution)/shard_map/all_to_all | solution.py:255
  49.9 13.3 %collective-permute-start.7 = (f32[2,512,128]{2,1,0:T(8,128)S(1)}, f32[2,512,128]{2,1,0:T(8,128)}, u32[]{:S(2)}, u32[]{:S(2)}) collective-permute-start(f32[2,512,128]{2,1,0:T(8,128)S(1)} %get-tuple-element.23), channel_id=1, source_target_pairs={{0,1},{1,2},{2,3},{3,4},{4,5},{5,6},{6,7},{7,8},{8,9},{9,10},{10,1... | collective-permute-start | bytes 1572872 | tf_op jit(solution)/shard_map/ppermute | solution.py:253
  51.8 14.3 %collective-permute-start.8 = (f32[2,512,128]{2,1,0:T(8,128)S(1)}, f32[2,512,128]{2,1,0:T(8,128)}, u32[]{:S(2)}, u32[]{:S(2)}) collective-permute-start(f32[2,512,128]{2,1,0:T(8,128)S(1)} %get-tuple-element.24), channel_id=1, source_target_pairs={{1,0},{2,1},{3,2},{4,3},{5,4},{6,5},{7,6},{8,7},{9,8},{10,9},{11,1... | collective-permute-start | bytes 1572872 | tf_op jit(solution)/shard_map/ppermute | solution.py:252
  66.0 8.8 %collective-permute-start.11 = (f32[5,8,256]{2,1,0:T(8,128)S(1)}, f32[5,8,256]{2,1,0:T(8,128)S(1)}, u32[]{:S(2)}, u32[]{:S(2)}) collective-permute-start(f32[5,8,256]{2,1,0:T(8,128)S(1)} %fusion), channel_id=1, source_target_pairs={{0,96},{32,64},{64,32},{96,0},{128,224},{160,192},{192,160},{224,1... | collective-permute-start | bytes 122888 | tf_op jit(solution)/shard_map/ppermute | solution.py:261
  68.2 6.7 %collective-permute-start.10 = (f32[5,8,256]{2,1,0:T(8,128)S(1)}, f32[5,8,256]{2,1,0:T(8,128)S(1)}, u32[]{:S(2)}, u32[]{:S(2)}) collective-permute-start(f32[5,8,256]{2,1,0:T(8,128)S(1)} %fusion), channel_id=1, source_target_pairs={{0,64},{32,96},{64,0},{96,32},{128,192},{160,224},{192,128},{224,1... | collective-permute-start | bytes 122888 | tf_op jit(solution)/shard_map/ppermute | solution.py:261
  68.2 6.7 %collective-permute-start.9 = (f32[5,8,256]{2,1,0:T(8,128)S(1)}, f32[5,8,256]{2,1,0:T(8,128)S(1)}, u32[]{:S(2)}, u32[]{:S(2)}) collective-permute-start(f32[5,8,256]{2,1,0:T(8,128)S(1)} %fusion), channel_id=1, source_target_pairs={{0,32},{32,0},{64,96},{96,64},{128,160},{160,128},{192,224},{224,1... | collective-permute-start | bytes 122888 | tf_op jit(solution)/shard_map/ppermute | solution.py:261
  70.9 7.7 %collective-permute-start.13 = (f32[2,128,256]{2,1,0:T(8,128)S(1)}, f32[2,128,256]{2,1,0:T(8,128)S(1)}, u32[]{:S(2)}, u32[]{:S(2)}) collective-permute-start(f32[2,128,256]{2,1,0:T(8,128)S(1)} %get-tuple-element.32), channel_id=1, source_target_pairs={{0,16},{16,32},{32,48},{48,64},{64,80},{80,96},{96,112},{112,128},... | collective-permute-start | bytes 786440 | tf_op jit(solution)/shard_map/ppermute | solution.py:260
  71.5 12.0 %collective-permute-start.12 = (f32[2,128,256]{2,1,0:T(8,128)S(1)}, f32[2,128,256]{2,1,0:T(8,128)S(1)}, u32[]{:S(2)}, u32[]{:S(2)}) collective-permute-start(f32[2,128,256]{2,1,0:T(8,128)S(1)} %get-tuple-element.33), channel_id=1, source_target_pairs={{16,0},{32,16},{48,32},{64,48},{80,64},{96,80},{112,96},{128,112},... | collective-permute-start | bytes 786440 | tf_op jit(solution)/shard_map/ppermute | solution.py:259
  83.5 6.9 %collective-permute-start.14 = (f32[5,8,256]{2,1,0:T(8,128)S(1)}, f32[5,8,256]{2,1,0:T(8,128)S(1)}, u32[]{:S(2)}, u32[]{:S(2)}) collective-permute-start(f32[5,8,256]{2,1,0:T(8,128)S(1)} %add_add_fusion), channel_id=1, source_target_pairs={{0,128},{32,160},{64,192},{96,224},{128,0},{160,32},{192,64},{224,... | collective-permute-start | bytes 122888 | tf_op jit(solution)/shard_map/ppermute | solution.py:264
  105.0 6.2 %collective-permute-start.15 = (f32[16,4,8,256]{3,2,1,0:T(8,128)S(1)}, f32[16,4,8,256]{3,2,1,0:T(8,128)S(1)}, u32[]{:S(2)}, u32[]{:S(2)}) collective-permute-start(f32[16,4,8,256]{3,2,1,0:T(8,128)S(1)} %all_to_all.10.own), channel_id=1, source_target_pairs={{0,1},{1,0},{2,3},{3,2},{4,5},{5,4},{6,7},{7,6},{8,9},{9,8},{10,11... | collective-permute-start | bytes 1572872 | tf_op jit(solution)/shard_map/ppermute | solution.py:271

commit v5 on v4

--- a/solution.py
+++ b/solution.py
@@ -69,8 +69,8 @@
         copy.wait()
 
     def position(p, carry):
-        r = offs[2 * p] + HALF
-        c = offs[2 * p + 1] + HALF
+        r = offs[0, p] + HALF
+        c = offs[1, p] + HALF
         q = c // HALF
         s = c - q * HALF
         back_shift = lax.rem(HALF - s, HALF)
@@ -238,8 +238,8 @@
     co = lax.axis_index("co")
     half = co.reshape(1)
     block = (co * 16 + lax.axis_index(group)) * 8
-    offs = offsets.reshape(2 * POS)
-    object_field, half, block, offs = lax.optimization_barrier((object_field, half, block, offs))
+    offs = offsets.transpose(1, 2, 0).reshape(2, POS)
+    object_field, half, block = lax.optimization_barrier((object_field, half, block))
     first, last = slice(0, HALF), slice(HALF, W)
     top = lax.ppermute(object_field[:, last], GX, UP)
     bot = lax.ppermute(object_field[:, first], GX, DOWN)
@@ -249,19 +249,19 @@
     right_ends = lax.ppermute(jnp.stack([top[:, :, first], bot[:, :, first]]), GY, DOWN)
     border = (object_field, top, bot, left, right, left_ends, right_ends)
     mine, other, out_left, out_mid, out_right = correct(offs, half, border, probe_field, amplitude)
+    part = mine + lax.ppermute(other, "co", SWAP)
     from_right = lax.ppermute(out_left, GY, DOWN)
     from_left = lax.ppermute(out_right, GY, UP)
-    part = mine + lax.ppermute(other, "co", SWAP)
     pieces = lax.all_to_all(part, group, 0, 0, tiled=True)
     part = sum(pieces[i] for i in range(16))
-    part, from_left, from_right = lax.optimization_barrier((part, from_left, from_right))
     folded = out_mid + jnp.concatenate([from_left, from_right], 2)
+    part, folded = lax.optimization_barrier((part, folded))
     from_below = lax.ppermute(folded[:, :HALF], GX, DOWN)
     from_above = lax.ppermute(folded[:, HALF + W :], GX, UP)
-    peers = [lax.ppermute(part, "z", [(i, i ^ step) for i in range(8)]) for step in (1, 2, 3)]
+    peers = [lax.ppermute(part, "z", [(i, i ^ step) for i in range(8)]) for step in (2, 4, 6)]
     part = (part + peers[0]) + (peers[1] + peers[2])
+    part = part + lax.ppermute(part, "z", [(i, i ^ 1) for i in range(8)])
     part, from_below, from_above = lax.optimization_barrier((part, from_below, from_above))
-    part = part + lax.ppermute(part, "z", [(i, i ^ 4) for i in range(8)])
     planes = probe_field.reshape(2 * MODES, W, W)
     local = lax.dynamic_slice_in_dim(planes, block, 8, 1)
     weight = part[2 * MODES]

time: 113 us -> 102 us (0.903)
  waiting for transfers between devices: 39 us -> 32.9 us
  starting transfers between devices: 40.8 us -> 36.4 us
    ppermute x1, starting transfers between devices: 4.72 us -> 0.7 us  [body(): part = part + lax.ppermute(part, 'z', [(i, i ^ 1) for i in range(8)])]
    ppermute x1, waiting for transfers between devices: 3.74 us -> 0.58 us  [body(): from_above = lax.ppermute(folded[:, HALF + W:], GX, UP)]
    ppermute x1, waiting for transfers between devices: 2.88 us -> 0.01 us  [body(): from_right = lax.ppermute(out_left, GY, DOWN)]
    ppermute x3, starting transfers between devices: 3.55 us -> 6.26 us  [body(): lax.ppermute(part, 'z', [(i, i ^ step) for i in range(8)])]
    ppermute x1, starting transfers between devices: 1.92 us -> 0.01 us  [body(): from_left = lax.ppermute(out_right, GY, UP)]
    ppermute x1, waiting for transfers between devices: 4.84 us -> 3.11 us  [body(): from_below = lax.ppermute(folded[:, :HALF], GX, DOWN)]
    ppermute x1, starting transfers between devices: 4.69 us -> 3.25 us  [body(): updated_probe = arrange(half, gathered, lax.ppermute(gathered, 'co', SWAP))]
    ppermute x3, waiting for transfers between devices: 0.01 us -> 1.14 us  [body(): lax.ppermute(part, 'z', [(i, i ^ step) for i in range(8)])]
  transfers between devices with their start and end apart: 17 -> 17, of which waited for: 12 -> 11; matrix products, arithmetic and copies ran while one was open for 3% -> 3% of each run, Pallas kernels for 0% -> 0%
where the time goes in v5:
time: 102 us; the launch traced here: 101 us
  starting transfers between devices  36.4 us (36%)
  waiting for transfers between devices  32.9 us (32%)
  blocking collectives  15.1 us (15%)
  Pallas kernels  10.7 us (10%)
  other arithmetic  4.27 us (4%)
  local copies, waits for them, and re-layouts  1.3 us (1%)
    all_to_all x1, blocking collectives, body(): lax.all_to_all(jnp.broadcast_to(local[None], (16,) + local.shape), group,...  15.1 us
    all_to_all x1, waiting for transfers between devices, body(): pieces = lax.all_to_all(part, group, 0, 0, tiled=True)  10.4 us
    pallas_call x1, Pallas kernels, correct(): pl.pallas_call(kernel, out_shape=(part, part, strip, jax.ShapeDtypeStruct...  9.63 us
    ppermute x1, starting transfers between devices, body(): bot = lax.ppermute(object_field[:, first], GX, DOWN)  7.41 us
    all_to_all x1, starting transfers between devices, body(): pieces = lax.all_to_all(part, group, 0, 0, tiled=True)  6.91 us
    ppermute x3, starting transfers between devices, body(): lax.ppermute(part, 'z', [(i, i ^ step) for i in range(8)])  6.26 us
    ppermute x1, waiting for transfers between devices, body(): top = lax.ppermute(object_field[:, last], GX, UP)  3.97 us
    ppermute x1, starting transfers between devices, body(): from_below = lax.ppermute(folded[:, :HALF], GX, DOWN)  3.56 us
  transfers between devices with their start and end apart: 17, of which 11 were waited for; matrix products, arithmetic and copies ran while one was open for 3% of the time, Pallas kernels for 0%

profile of v5, /device:TPU:1, one launch (start us, length us, event | category | flops | bytes accessed | tf_op | source)
XLA Modules:
  0.0 101.5 jit_solution(8551746205653813519)
XLA Ops:
  0.6 0.0 copy-start
  0.7 1.1 %fusion.3 = (f32[2,128,256]{2,1,0:T(8,128)S(1)}, f32[2,128,256]{2,1,0:T(8,128)S(1)}) fusion(f32[2,256,256]{2,1,0:T(8,128)} %tile), kind=kLoop, calls=%fused_computation.30 | loop fusion | bytes 1048576 | tf_op jit(solution)/shard_map/slice | solution.py:245
  1.8 7.4 %collective-permute-start.1 = (f32[2,128,256]{2,1,0:T(8,128)S(1)}, f32[2,128,256]{2,1,0:T(8,128)S(1)}, u32[]{:S(2)}, u32[]{:S(2)}) collective-permute-start(f32[2,128,256]{2,1,0:T(8,128)S(1)} %get-tuple-element.32), channel_id=1, source_target_pairs={{16,0},{32,16},{48,32},{64,48},{80,64},{96,80},{112,96},{128,112},... | collective-permute-start | bytes 786440 | tf_op jit(solution)/shard_map/ppermute | solution.py:245
  9.2 0.0 collective-permute-start
  9.2 0.0 copy-done
  9.3 1.0 %collective-permute-start.3 = (f32[2,256,128]{2,1,0:T(8,128)S(1)}, f32[2,256,128]{2,1,0:T(8,128)S(1)}, u32[]{:S(2)}, u32[]{:S(2)}) collective-permute-start(f32[2,256,128]{2,1,0:T(8,128)S(1)} %get-tuple-element.30), channel_id=1, source_target_pairs={{1,0},{2,1},{3,2},{4,3},{5,4},{6,5},{7,6},{8,7},{9,8},{10,9},{11,1... | collective-permute-start | bytes 786440 | tf_op jit(solution)/shard_map/ppermute | solution.py:247
  10.3 1.3 %collective-permute-start.2 = (f32[2,256,128]{2,1,0:T(8,128)S(1)}, f32[2,256,128]{2,1,0:T(8,128)S(1)}, u32[]{:S(2)}, u32[]{:S(2)}) collective-permute-start(f32[2,256,128]{2,1,0:T(8,128)S(1)} %get-tuple-element.31), channel_id=1, source_target_pairs={{0,1},{1,2},{2,3},{3,4},{4,5},{5,6},{6,7},{7,8},{8,9},{9,10},{10,1... | collective-permute-start | bytes 786440 | tf_op jit(solution)/shard_map/ppermute | solution.py:246
  11.6 2.6 %collective-permute-done.1.bot = f32[2,128,256]{2,1,0:T(8,128)S(1)} collective-permute-done((f32[2,128,256]{2,1,0:T(8,128)S(1)}, f32[2,128,256]{2,1,0:T(8,128)S(1)}, u32[]{:S(2)}, u32[]{:S(2)}) %collective-permute-start.1) | collective-permute-done | bytes 262176 | tf_op jit(solution)/shard_map/ppermute | solution.py:245
  14.2 4.0 %collective-permute-done.top = f32[2,128,256]{2,1,0:T(8,128)S(1)} collective-permute-done((f32[2,128,256]{2,1,0:T(8,128)S(1)}, f32[2,128,256]{2,1,0:T(8,128)S(1)}, u32[]{:S(2)}, u32[]{:S(2)}) %collective-permute-start) | collective-permute-done | bytes 262176 | tf_op jit(solution)/shard_map/ppermute | solution.py:244
  18.3 3.1 %collective-permute-start.4 = (f32[2,2,128,128]{3,2,1,0:T(8,128)S(1)}, f32[2,2,128,128]{3,2,1,0:T(8,128)S(1)}, u32[]{:S(2)}, u32[]{:S(2)}) collective-permute-start(f32[2,2,128,128]{3,2,1,0:T(8,128)S(1)} %pad_maximum_fusion), channel_id=1, source_target_pairs={{0,1},{1,2},{2,3},{3,4},{4,5},{5,6},{6,7},{7,8},{8,9},{9,10},{10,1... | collective-permute-start | bytes 786440 | tf_op jit(solution)/shard_map/ppermute | solution.py:248
  21.4 0.0 copy-start.5
  21.4 0.1 collective-permute-start.5
  21.5 0.0 collective-permute-done.3.right
  21.5 0.0 collective-permute-done.2.left
  21.5 3.2 %collective-permute-done.4.left_ends = f32[2,2,128,128]{3,2,1,0:T(8,128)S(1)} collective-permute-done((f32[2,2,128,128]{3,2,1,0:T(8,128)S(1)}, f32[2,2,128,128]{3,2,1,0:T(8,128)S(1)}, u32[]{:S(2)}, u32[]{:S(2)}) %collective-permute-start.4) | collective-permute-done | bytes 262176 | tf_op jit(solution)/shard_map/ppermute | solution.py:248
  24.6 2.9 %collective-permute-done.5.right_ends = f32[2,2,128,128]{3,2,1,0:T(8,128)S(1)} collective-permute-done((f32[2,2,128,128]{3,2,1,0:T(8,128)S(1)}, f32[2,2,128,128]{3,2,1,0:T(8,128)S(1)}, u32[]{:S(2)}, u32[]{:S(2)}) %collective-permute-start.5) | collective-permute-done | bytes 262176 | tf_op jit(solution)/shard_map/ppermute | solution.py:249
  27.5 0.0 copy-done.3
  27.5 0.0 copy-done.4
  27.5 0.0 copy-done.1
  27.6 9.6 %shard_map.77 = (f32[16,5,8,256]{3,2,1,0:T(8,128)S(1)}, f32[16,5,8,256]{3,2,1,0:T(8,128)S(1)}, f32[2,512,128]{2,1,0:T(8,128)S(1)}, f32[2,512,256]{2,1,0:T(8,128)S(1)}, f32[2,512,128]{2,1,0:T(8,128)S(1)}) custom-call(s32[2,4]{1,0:T(2,128)S(1)} %bitcast.20, s32[1]{0:T(128)} %bitcast.2.half, f32[2,256,256]{2,1,0:T(8,128)S(1)} %copy-done, ...), custom_call_target="tpu_custom_call" | custom-call | tf_op jit(solution)/shard_map/pallas_call | solution.py:186
  37.2 2.2 %collective-permute-start.6 = (f32[16,5,8,256]{3,2,1,0:T(8,128)S(1)}, f32[16,5,8,256]{3,2,1,0:T(8,128)S(1)}, u32[]{:S(2)}, u32[]{:S(2)}) collective-permute-start(f32[16,5,8,256]{3,2,1,0:T(8,128)S(1)} %get-tuple-element.18), channel_id=1, source_target_pairs={{0,1},{1,0},{2,3},{3,2},{4,5},{5,4},{6,7},{7,6},{8,9},{9,8},{10,11... | collective-permute-start | bytes 1966088 | tf_op jit(solution)/shard_map/ppermute | solution.py:252
  39.4 0.0 collective-permute-start.7
  39.4 0.5 collective-permute-start.8
  39.9 1.2 %collective-permute-done.6 = f32[16,5,8,256]{3,2,1,0:T(8,128)S(1)} collective-permute-done((f32[16,5,8,256]{3,2,1,0:T(8,128)S(1)}, f32[16,5,8,256]{3,2,1,0:T(8,128)S(1)}, u32[]{:S(2)}, u32[]{:S(2)}) %collective-permute-start.6) | collective-permute-done | bytes 655392 | tf_op jit(solution)/shard_map/ppermute | solution.py:252
  41.1 0.9 add.97
  42.1 6.9 %all-to-all-start = ((f32[16,5,8,256]{3,2,1,0:T(8,128)}), f32[16,5,8,256]{3,2,1,0:T(8,128)}, u32[]{:S(2)}, u32[]{:S(2)}) async-start(f32[16,5,8,256]{3,2,1,0:T(8,128)} %add.97), calls=%async_computation | async-start | bytes 1310720 | tf_op jit(solution)/shard_map/all_to_all | solution.py:255
  49.0 0.0 collective-permute-done.7
  49.0 0.0 collective-permute-done.8
  49.0 1.3 %maximum_add_fusion = f32[2,512,256]{2,1,0:T(8,128)S(1)} fusion(f32[2,512,256]{2,1,0:T(8,128)S(1)} %get-tuple-element.19, f32[2,512,128]{2,1,0:T(8,128)} %collective-permute-done.8, f32[2,512,128]{2,1,0:T(8,128)} %collective-permute-done.7), kind=kLoop, calls=%fused_computation | loop fusion | flops 524288 | bytes 3145728 | tf_op jit(solution)/shard_map/add | solution.py:257
  50.3 10.4 %all-to-all-done = f32[16,5,8,256]{3,2,1,0:T(8,128)} async-done(((f32[16,5,8,256]{3,2,1,0:T(8,128)}), f32[16,5,8,256]{3,2,1,0:T(8,128)}, u32[]{:S(2)}, u32[]{:S(2)}) %all-to-all-start) | async-done | bytes 655392 | tf_op jit(solution)/shard_map/all_to_all | solution.py:255
  60.7 1.1 %fusion = f32[5,8,256]{2,1,0:T(8,128)S(1)} fusion(f32[16,5,8,256]{3,2,1,0:T(8,128)} %all-to-all-done), kind=kLoop, calls=%fused_computation.9 | loop fusion | flops 153600 | bytes 696320 | tf_op jit(solution)/shard_map/add | solution.py:256
  61.8 4.1 %collective-permute-start.11 = (f32[5,8,256]{2,1,0:T(8,128)S(1)}, f32[5,8,256]{2,1,0:T(8,128)S(1)}, u32[]{:S(2)}, u32[]{:S(2)}) collective-permute-start(f32[5,8,256]{2,1,0:T(8,128)S(1)} %fusion), channel_id=1, source_target_pairs={{0,192},{32,224},{64,128},{96,160},{128,64},{160,96},{192,0},{224,... | collective-permute-start | bytes 122888 | tf_op jit(solution)/shard_map/ppermute | solution.py:261
  65.9 0.8 collective-permute-start.10
  66.7 1.4 %collective-permute-start.9 = (f32[5,8,256]{2,1,0:T(8,128)S(1)}, f32[5,8,256]{2,1,0:T(8,128)S(1)}, u32[]{:S(2)}, u32[]{:S(2)}) collective-permute-start(f32[5,8,256]{2,1,0:T(8,128)S(1)} %fusion), channel_id=1, source_target_pairs={{0,64},{32,96},{64,0},{96,32},{128,192},{160,224},{192,128},{224,1... | collective-permute-start | bytes 122888 | tf_op jit(solution)/shard_map/ppermute | solution.py:261
  68.1 0.1 collective-permute-start.14
  68.2 3.6 %collective-permute-start.13 = (f32[2,128,256]{2,1,0:T(8,128)S(1)}, f32[2,128,256]{2,1,0:T(8,128)S(1)}, u32[]{:S(2)}, u32[]{:S(2)}) collective-permute-start(f32[2,128,256]{2,1,0:T(8,128)S(1)} %get-tuple-element.29), channel_id=1, source_target_pairs={{16,0},{32,16},{48,32},{64,48},{80,64},{96,80},{112,96},{128,112},... | collective-permute-start | bytes 786440 | tf_op jit(solution)/shard_map/ppermute | solution.py:259
  71.7 0.0 collective-permute-done.11
  71.7 1.1 %collective-permute-done.10 = f32[5,8,256]{2,1,0:T(8,128)S(1)} collective-permute-done((f32[5,8,256]{2,1,0:T(8,128)S(1)}, f32[5,8,256]{2,1,0:T(8,128)S(1)}, u32[]{:S(2)}, u32[]{:S(2)}) %collective-permute-start.10) | collective-permute-done | bytes 40992 | tf_op jit(solution)/shard_map/ppermute | solution.py:261
  72.9 0.0 collective-permute-done.9
  72.9 0.7 collective-permute-start.12
  73.6 3.1 %collective-permute-done.12 = f32[5,8,256]{2,1,0:T(8,128)S(1)} collective-permute-done((f32[5,8,256]{2,1,0:T(8,128)S(1)}, f32[5,8,256]{2,1,0:T(8,128)S(1)}, u32[]{:S(2)}, u32[]{:S(2)}) %collective-permute-start.12) | collective-permute-done | bytes 40992 | tf_op jit(solution)/shard_map/ppermute | solution.py:263
  76.7 0.6 collective-permute-done.14
  77.3 3.1 %collective-permute-done.13 = f32[2,128,256]{2,1,0:T(8,128)S(1)} collective-permute-done((f32[2,128,256]{2,1,0:T(8,128)S(1)}, f32[2,128,256]{2,1,0:T(8,128)S(1)}, u32[]{:S(2)}, u32[]{:S(2)}) %collective-permute-start.13) | collective-permute-done | bytes 262176 | tf_op jit(solution)/shard_map/ppermute | solution.py:259
  80.5 15.1 %all_to_all.10.own = f32[16,4,8,256]{3,2,1,0:T(8,128)S(1)} all-to-all(f32[16,4,8,256]{3,2,1,0:T(8,128)S(1)} %broadcast_in_dim.2), channel_id=1, replica_groups=mesh['z'=8,'xl'=2,'xh'=2,'y'=4,'co'=2] {'xh','xl','y'}, dimensions={0} | all-to-all | bytes 1048576 | tf_op jit(solution)/shard_map/all_to_all | solution.py:269
  95.6 3.2 %collective-permute-start.15 = (f32[16,4,8,256]{3,2,1,0:T(8,128)S(1)}, f32[16,4,8,256]{3,2,1,0:T(8,128)S(1)}, u32[]{:S(2)}, u32[]{:S(2)}) collective-permute-start(f32[16,4,8,256]{3,2,1,0:T(8,128)S(1)} %all_to_all.10.own), channel_id=1, source_target_pairs={{0,1},{1,0},{2,3},{3,2},{4,5},{5,4},{6,7},{7,6},{8,9},{9,8},{10,11... | collective-permute-start | bytes 1572872 | tf_op jit(solution)/shard_map/ppermute | solution.py:271
  98.9 0.9 maximum_add_fusion.1
  99.7 0.7 collective-permute-done.15.swapped
  100.4 1.0 %shard_map.78 = f32[2,2,256,256]{3,2,1,0:T(8,128)} custom-call(s32[1]{0:T(128)} %bitcast.2.half, f32[16,4,8,256]{3,2,1,0:T(8,128)S(1)} %all_to_all.10.own, f32[16,4,8,256]{3,2,1,0:T(8,128)S(1)} %collective-permute-done.15.swapped), custom_call_target="tpu_custom_call" | custom-call | tf_op jit(solution)/shard_map/pallas_call | solution.py:227
  (17 shorter events, 0.2 us)
Async XLA Ops:
  0.6 8.6 %copy-start = (f32[2,256,256]{2,1,0:T(8,128)S(1)}, f32[2,256,256]{2,1,0:T(8,128)}, u32[]{:S(2)}) copy-start(f32[2,256,256]{2,1,0:T(8,128)} %tile) | copy-start | bytes 1572868
  1.8 12.4 %collective-permute-start.1 = (f32[2,128,256]{2,1,0:T(8,128)S(1)}, f32[2,128,256]{2,1,0:T(8,128)S(1)}, u32[]{:S(2)}, u32[]{:S(2)}) collective-permute-start(f32[2,128,256]{2,1,0:T(8,128)S(1)} %get-tuple-element.32), channel_id=1, source_target_pairs={{16,0},{32,16},{48,32},{64,48},{80,64},{96,80},{112,96},{128,112},... | collective-permute-start | bytes 786440 | tf_op jit(solution)/shard_map/ppermute | solution.py:245
  9.2 9.0 %collective-permute-start = (f32[2,128,256]{2,1,0:T(8,128)S(1)}, f32[2,128,256]{2,1,0:T(8,128)S(1)}, u32[]{:S(2)}, u32[]{:S(2)}) collective-permute-start(f32[2,128,256]{2,1,0:T(8,128)S(1)} %get-tuple-element.33), channel_id=1, source_target_pairs={{0,16},{16,32},{32,48},{48,64},{64,80},{80,96},{96,112},{112,128},... | collective-permute-start | bytes 786440 | tf_op jit(solution)/shard_map/ppermute | solution.py:244
  9.2 18.3 %copy-start.3 = (bf16[512,512]{1,0:T(8,128)(2,1)S(1)}, bf16[512,512]{1,0:T(8,128)(2,1)}, u32[]{:S(2)}) copy-start(bf16[512,512]{1,0:T(8,128)(2,1)} %constant.32.clone.bwd_hbm) | copy-start | bytes 1572868
  9.2 18.3 %copy-start.4 = (bf16[512,512]{1,0:T(8,128)(2,1)S(1)}, bf16[512,512]{1,0:T(8,128)(2,1)}, u32[]{:S(2)}) copy-start(bf16[512,512]{1,0:T(8,128)(2,1)} %constant.31.clone.fwd_hbm) | copy-start | bytes 1572868
  9.3 12.2 %collective-permute-start.3 = (f32[2,256,128]{2,1,0:T(8,128)S(1)}, f32[2,256,128]{2,1,0:T(8,128)S(1)}, u32[]{:S(2)}, u32[]{:S(2)}) collective-permute-start(f32[2,256,128]{2,1,0:T(8,128)S(1)} %get-tuple-element.30), channel_id=1, source_target_pairs={{1,0},{2,1},{3,2},{4,3},{5,4},{6,5},{7,6},{8,7},{9,8},{10,9},{11,1... | collective-permute-start | bytes 786440 | tf_op jit(solution)/shard_map/ppermute | solution.py:247
  10.3 17.3 %copy-start.1 = (f32[2,2,256,256]{3,2,1,0:T(8,128)S(1)}, f32[2,2,256,256]{3,2,1,0:T(8,128)}, u32[]{:S(2)}) copy-start(f32[2,2,256,256]{3,2,1,0:T(8,128)} %probe.1) | copy-start | bytes 3145732
  10.3 17.3 %copy-start.2 = (f32[4,1,256,256]{3,2,1,0:T(8,128)S(1)}, f32[4,1,256,256]{3,2,1,0:T(8,128)}, u32[]{:S(2)}) copy-start(f32[4,1,256,256]{3,2,1,0:T(8,128)} %amp.1) | copy-start | bytes 3145732
  10.3 11.2 %collective-permute-start.2 = (f32[2,256,128]{2,1,0:T(8,128)S(1)}, f32[2,256,128]{2,1,0:T(8,128)S(1)}, u32[]{:S(2)}, u32[]{:S(2)}) collective-permute-start(f32[2,256,128]{2,1,0:T(8,128)S(1)} %get-tuple-element.31), channel_id=1, source_target_pairs={{0,1},{1,2},{2,3},{3,4},{4,5},{5,6},{6,7},{7,8},{8,9},{9,10},{10,1... | collective-permute-start | bytes 786440 | tf_op jit(solution)/shard_map/ppermute | solution.py:246
  18.3 6.4 %collective-permute-start.4 = (f32[2,2,128,128]{3,2,1,0:T(8,128)S(1)}, f32[2,2,128,128]{3,2,1,0:T(8,128)S(1)}, u32[]{:S(2)}, u32[]{:S(2)}) collective-permute-start(f32[2,2,128,128]{3,2,1,0:T(8,128)S(1)} %pad_maximum_fusion), channel_id=1, source_target_pairs={{0,1},{1,2},{2,3},{3,4},{4,5},{5,6},{6,7},{7,8},{8,9},{9,10},{10,1... | collective-permute-start | bytes 786440 | tf_op jit(solution)/shard_map/ppermute | solution.py:248
  21.4 6.2 %copy-start.5 = (s32[4,1,2]{0,2,1:T(2,128)S(1)}, s32[4,1,2]{0,2,1:T(2,128)}, u32[]{:S(2)}) copy-start(s32[4,1,2]{0,2,1:T(2,128)} %param.9) | copy-start | bytes 100
  21.4 6.2 %collective-permute-start.5 = (f32[2,2,128,128]{3,2,1,0:T(8,128)S(1)}, f32[2,2,128,128]{3,2,1,0:T(8,128)S(1)}, u32[]{:S(2)}, u32[]{:S(2)}) collective-permute-start(f32[2,2,128,128]{3,2,1,0:T(8,128)S(1)} %pad_maximum_fusion.1), channel_id=1, source_target_pairs={{1,0},{2,1},{3,2},{4,3},{5,4},{6,5},{7,6},{8,7},{9,8},{10,9},{11,1... | collective-permute-start | bytes 786440 | tf_op jit(solution)/shard_map/ppermute | solution.py:249
  37.2 3.9 %collective-permute-start.6 = (f32[16,5,8,256]{3,2,1,0:T(8,128)S(1)}, f32[16,5,8,256]{3,2,1,0:T(8,128)S(1)}, u32[]{:S(2)}, u32[]{:S(2)}) collective-permute-start(f32[16,5,8,256]{3,2,1,0:T(8,128)S(1)} %get-tuple-element.18), channel_id=1, source_target_pairs={{0,1},{1,0},{2,3},{3,2},{4,5},{5,4},{6,7},{7,6},{8,9},{9,8},{10,11... | collective-permute-start | bytes 1966088 | tf_op jit(solution)/shard_map/ppermute | solution.py:252
  39.4 9.6 %collective-permute-start.7 = (f32[2,512,128]{2,1,0:T(8,128)S(1)}, f32[2,512,128]{2,1,0:T(8,128)}, u32[]{:S(2)}, u32[]{:S(2)}) collective-permute-start(f32[2,512,128]{2,1,0:T(8,128)S(1)} %get-tuple-element.20), channel_id=1, source_target_pairs={{0,1},{1,2},{2,3},{3,4},{4,5},{5,6},{6,7},{7,8},{8,9},{9,10},{10,1... | collective-permute-start | bytes 1572872 | tf_op jit(solution)/shard_map/ppermute | solution.py:254
  39.4 9.6 %collective-permute-start.8 = (f32[2,512,128]{2,1,0:T(8,128)S(1)}, f32[2,512,128]{2,1,0:T(8,128)}, u32[]{:S(2)}, u32[]{:S(2)}) collective-permute-start(f32[2,512,128]{2,1,0:T(8,128)S(1)} %get-tuple-element.21), channel_id=1, source_target_pairs={{1,0},{2,1},{3,2},{4,3},{5,4},{6,5},{7,6},{8,7},{9,8},{10,9},{11,1... | collective-permute-start | bytes 1572872 | tf_op jit(solution)/shard_map/ppermute | solution.py:253
  42.1 18.6 %all-to-all-start = ((f32[16,5,8,256]{3,2,1,0:T(8,128)}), f32[16,5,8,256]{3,2,1,0:T(8,128)}, u32[]{:S(2)}, u32[]{:S(2)}) async-start(f32[16,5,8,256]{3,2,1,0:T(8,128)} %add.97), calls=%async_computation | async-start | bytes 1310720 | tf_op jit(solution)/shard_map/all_to_all | solution.py:255
  61.8 10.0 %collective-permute-start.11 = (f32[5,8,256]{2,1,0:T(8,128)S(1)}, f32[5,8,256]{2,1,0:T(8,128)S(1)}, u32[]{:S(2)}, u32[]{:S(2)}) collective-permute-start(f32[5,8,256]{2,1,0:T(8,128)S(1)} %fusion), channel_id=1, source_target_pairs={{0,192},{32,224},{64,128},{96,160},{128,64},{160,96},{192,0},{224,... | collective-permute-start | bytes 122888 | tf_op jit(solution)/shard_map/ppermute | solution.py:261
  65.9 7.0 %collective-permute-start.10 = (f32[5,8,256]{2,1,0:T(8,128)S(1)}, f32[5,8,256]{2,1,0:T(8,128)S(1)}, u32[]{:S(2)}, u32[]{:S(2)}) collective-permute-start(f32[5,8,256]{2,1,0:T(8,128)S(1)} %fusion), channel_id=1, source_target_pairs={{0,128},{32,160},{64,192},{96,224},{128,0},{160,32},{192,64},{224,... | collective-permute-start | bytes 122888 | tf_op jit(solution)/shard_map/ppermute | solution.py:261
  66.7 6.2 %collective-permute-start.9 = (f32[5,8,256]{2,1,0:T(8,128)S(1)}, f32[5,8,256]{2,1,0:T(8,128)S(1)}, u32[]{:S(2)}, u32[]{:S(2)}) collective-permute-start(f32[5,8,256]{2,1,0:T(8,128)S(1)} %fusion), channel_id=1, source_target_pairs={{0,64},{32,96},{64,0},{96,32},{128,192},{160,224},{192,128},{224,1... | collective-permute-start | bytes 122888 | tf_op jit(solution)/shard_map/ppermute | solution.py:261
  68.1 9.2 %collective-permute-start.14 = (f32[2,128,256]{2,1,0:T(8,128)S(1)}, f32[2,128,256]{2,1,0:T(8,128)S(1)}, u32[]{:S(2)}, u32[]{:S(2)}) collective-permute-start(f32[2,128,256]{2,1,0:T(8,128)S(1)} %get-tuple-element.28), channel_id=1, source_target_pairs={{0,16},{16,32},{32,48},{48,64},{64,80},{80,96},{96,112},{112,128},... | collective-permute-start | bytes 786440 | tf_op jit(solution)/shard_map/ppermute | solution.py:260
  68.2 12.3 %collective-permute-start.13 = (f32[2,128,256]{2,1,0:T(8,128)S(1)}, f32[2,128,256]{2,1,0:T(8,128)S(1)}, u32[]{:S(2)}, u32[]{:S(2)}) collective-permute-start(f32[2,128,256]{2,1,0:T(8,128)S(1)} %get-tuple-element.29), channel_id=1, source_target_pairs={{16,0},{32,16},{48,32},{64,48},{80,64},{96,80},{112,96},{128,112},... | collective-permute-start | bytes 786440 | tf_op jit(solution)/shard_map/ppermute | solution.py:259
  72.9 3.8 %collective-permute-start.12 = (f32[5,8,256]{2,1,0:T(8,128)S(1)}, f32[5,8,256]{2,1,0:T(8,128)S(1)}, u32[]{:S(2)}, u32[]{:S(2)}) collective-permute-start(f32[5,8,256]{2,1,0:T(8,128)S(1)} %add_add_fusion), channel_id=1, source_target_pairs={{0,32},{32,0},{64,96},{96,64},{128,160},{160,128},{192,224},{224,1... | collective-permute-start | bytes 122888 | tf_op jit(solution)/shard_map/ppermute | solution.py:263
  95.6 4.8 %collective-permute-start.15 = (f32[16,4,8,256]{3,2,1,0:T(8,128)S(1)}, f32[16,4,8,256]{3,2,1,0:T(8,128)S(1)}, u32[]{:S(2)}, u32[]{:S(2)}) collective-permute-start(f32[16,4,8,256]{3,2,1,0:T(8,128)S(1)} %all_to_all.10.own), channel_id=1, source_target_pairs={{0,1},{1,0},{2,3},{3,2},{4,5},{5,4},{6,7},{7,6},{8,9},{9,8},{10,11... | collective-permute-start | bytes 1572872 | tf_op jit(solution)/shard_map/ppermute | solution.py:271

commit v6 on v5

--- a/solution.py
+++ b/solution.py
@@ -255,13 +255,13 @@
     pieces = lax.all_to_all(part, group, 0, 0, tiled=True)
     part = sum(pieces[i] for i in range(16))
     folded = out_mid + jnp.concatenate([from_left, from_right], 2)
-    part, folded = lax.optimization_barrier((part, folded))
     from_below = lax.ppermute(folded[:, :HALF], GX, DOWN)
+    part, from_below = lax.optimization_barrier((part, from_below))
     from_above = lax.ppermute(folded[:, HALF + W :], GX, UP)
     peers = [lax.ppermute(part, "z", [(i, i ^ step) for i in range(8)]) for step in (2, 4, 6)]
     part = (part + peers[0]) + (peers[1] + peers[2])
     part = part + lax.ppermute(part, "z", [(i, i ^ 1) for i in range(8)])
-    part, from_below, from_above = lax.optimization_barrier((part, from_below, from_above))
+    part, from_above = lax.optimization_barrier((part, from_above))
     planes = probe_field.reshape(2 * MODES, W, W)
     local = lax.dynamic_slice_in_dim(planes, block, 8, 1)
     weight = part[2 * MODES]

time: 102 us -> 102 us (level)
  starting transfers between devices: 36.4 us -> 40.3 us
  waiting for transfers between devices: 32.9 us -> 30.3 us
    ppermute x1, waiting for transfers between devices: 3.11 us -> 0.01 us  [body(): from_below = lax.ppermute(folded[:, :HALF], GX, DOWN)]
    ppermute x3, waiting for transfers between devices: 1.14 us -> 3.59 us  [body(): lax.ppermute(part, 'z', [(i, i ^ step) for i in range(8)])]
    ppermute x1, starting transfers between devices: 3.25 us -> 5.37 us  [body(): updated_probe = arrange(half, gathered, lax.ppermute(gathered, 'co', SWAP))]
    ppermute x1, starting transfers between devices: 0.08 us -> 1.25 us  [body(): from_above = lax.ppermute(folded[:, HALF + W:], GX, UP)]
    ppermute x1, starting transfers between devices: 3.56 us -> 4.63 us  [body(): from_below = lax.ppermute(folded[:, :HALF], GX, DOWN)]
    all_to_all x1, waiting for transfers between devices: 10.4 us -> 9.29 us  [body(): pieces = lax.all_to_all(part, group, 0, 0, tiled=True)]
  transfers between devices with their start and end apart: 17 -> 17, of which waited for: 11 -> 10; matrix products, arithmetic and copies ran while one was open for 3% -> 4% of each run, Pallas kernels for 0% -> 0%
where the time goes in v6:
time: 102 us
  starting transfers between devices  40.3 us (40%)
  waiting for transfers between devices  30.3 us (30%)
  blocking collectives  14.5 us (14%)
  Pallas kernels  10.7 us (10%)
  other arithmetic  4.27 us (4%)
  local copies, waits for them, and re-layouts  1.3 us (1%)
    all_to_all x1, blocking collectives, body(): lax.all_to_all(jnp.broadcast_to(local[None], (16,) + local.shape), group,...  14.5 us
    pallas_call x1, Pallas kernels, correct(): pl.pallas_call(kernel, out_shape=(part, part, strip, jax.ShapeDtypeStruct...  9.63 us
    all_to_all x1, waiting for transfers between devices, body(): pieces = lax.all_to_all(part, group, 0, 0, tiled=True)  9.29 us
    ppermute x1, starting transfers between devices, body(): bot = lax.ppermute(object_field[:, first], GX, DOWN)  7.41 us
    all_to_all x1, starting transfers between devices, body(): pieces = lax.all_to_all(part, group, 0, 0, tiled=True)  6.91 us
    ppermute x3, starting transfers between devices, body(): lax.ppermute(part, 'z', [(i, i ^ step) for i in range(8)])  5.97 us
    ppermute x1, starting transfers between devices, body(): updated_probe = arrange(half, gathered, lax.ppermute(gathered, 'co', SWAP))  5.37 us
    ppermute x1, starting transfers between devices, body(): from_below = lax.ppermute(folded[:, :HALF], GX, DOWN)  4.63 us
  transfers between devices with their start and end apart: 17, of which 10 were waited for; matrix products, arithmetic and copies ran while one was open for 4% of the time, Pallas kernels for 0%

profile of v6, /device:TPU:1, one launch (start us, length us, event | category | flops | bytes accessed | tf_op | source)
XLA Modules:
  0.0 102.2 jit_solution(9906353994893987134)
XLA Ops:
  0.6 0.0 copy-start
  0.7 1.1 %fusion.3 = (f32[2,128,256]{2,1,0:T(8,128)S(1)}, f32[2,128,256]{2,1,0:T(8,128)S(1)}) fusion(f32[2,256,256]{2,1,0:T(8,128)} %tile), kind=kLoop, calls=%fused_computation.30 | loop fusion | bytes 1048576 | tf_op jit(solution)/shard_map/slice | solution.py:245
  1.8 7.4 %collective-permute-start.1 = (f32[2,128,256]{2,1,0:T(8,128)S(1)}, f32[2,128,256]{2,1,0:T(8,128)S(1)}, u32[]{:S(2)}, u32[]{:S(2)}) collective-permute-start(f32[2,128,256]{2,1,0:T(8,128)S(1)} %get-tuple-element.30), channel_id=1, source_target_pairs={{16,0},{32,16},{48,32},{64,48},{80,64},{96,80},{112,96},{128,112},... | collective-permute-start | bytes 786440 | tf_op jit(solution)/shard_map/ppermute | solution.py:245
  9.2 0.0 collective-permute-start
  9.2 0.0 copy-done
  9.3 1.0 %collective-permute-start.3 = (f32[2,256,128]{2,1,0:T(8,128)S(1)}, f32[2,256,128]{2,1,0:T(8,128)S(1)}, u32[]{:S(2)}, u32[]{:S(2)}) collective-permute-start(f32[2,256,128]{2,1,0:T(8,128)S(1)} %get-tuple-element.28), channel_id=1, source_target_pairs={{1,0},{2,1},{3,2},{4,3},{5,4},{6,5},{7,6},{8,7},{9,8},{10,9},{11,1... | collective-permute-start | bytes 786440 | tf_op jit(solution)/shard_map/ppermute | solution.py:247
  10.3 1.3 %collective-permute-start.2 = (f32[2,256,128]{2,1,0:T(8,128)S(1)}, f32[2,256,128]{2,1,0:T(8,128)S(1)}, u32[]{:S(2)}, u32[]{:S(2)}) collective-permute-start(f32[2,256,128]{2,1,0:T(8,128)S(1)} %get-tuple-element.29), channel_id=1, source_target_pairs={{0,1},{1,2},{2,3},{3,4},{4,5},{5,6},{6,7},{7,8},{8,9},{9,10},{10,1... | collective-permute-start | bytes 786440 | tf_op jit(solution)/shard_map/ppermute | solution.py:246
  11.6 2.6 %collective-permute-done.1.bot = f32[2,128,256]{2,1,0:T(8,128)S(1)} collective-permute-done((f32[2,128,256]{2,1,0:T(8,128)S(1)}, f32[2,128,256]{2,1,0:T(8,128)S(1)}, u32[]{:S(2)}, u32[]{:S(2)}) %collective-permute-start.1) | collective-permute-done | bytes 262176 | tf_op jit(solution)/shard_map/ppermute | solution.py:245
  14.2 4.0 %collective-permute-done.top = f32[2,128,256]{2,1,0:T(8,128)S(1)} collective-permute-done((f32[2,128,256]{2,1,0:T(8,128)S(1)}, f32[2,128,256]{2,1,0:T(8,128)S(1)}, u32[]{:S(2)}, u32[]{:S(2)}) %collective-permute-start) | collective-permute-done | bytes 262176 | tf_op jit(solution)/shard_map/ppermute | solution.py:244
  18.3 3.1 %collective-permute-start.4 = (f32[2,2,128,128]{3,2,1,0:T(8,128)S(1)}, f32[2,2,128,128]{3,2,1,0:T(8,128)S(1)}, u32[]{:S(2)}, u32[]{:S(2)}) collective-permute-start(f32[2,2,128,128]{3,2,1,0:T(8,128)S(1)} %pad_maximum_fusion), channel_id=1, source_target_pairs={{0,1},{1,2},{2,3},{3,4},{4,5},{5,6},{6,7},{7,8},{8,9},{9,10},{10,1... | collective-permute-start | bytes 786440 | tf_op jit(solution)/shard_map/ppermute | solution.py:248
  21.4 0.0 copy-start.5
  21.4 0.1 collective-permute-start.5
  21.5 0.0 collective-permute-done.3.right
  21.5 0.0 collective-permute-done.2.left
  21.5 3.2 %collective-permute-done.4.left_ends = f32[2,2,128,128]{3,2,1,0:T(8,128)S(1)} collective-permute-done((f32[2,2,128,128]{3,2,1,0:T(8,128)S(1)}, f32[2,2,128,128]{3,2,1,0:T(8,128)S(1)}, u32[]{:S(2)}, u32[]{:S(2)}) %collective-permute-start.4) | collective-permute-done | bytes 262176 | tf_op jit(solution)/shard_map/ppermute | solution.py:248
  24.6 2.9 %collective-permute-done.5.right_ends = f32[2,2,128,128]{3,2,1,0:T(8,128)S(1)} collective-permute-done((f32[2,2,128,128]{3,2,1,0:T(8,128)S(1)}, f32[2,2,128,128]{3,2,1,0:T(8,128)S(1)}, u32[]{:S(2)}, u32[]{:S(2)}) %collective-permute-start.5) | collective-permute-done | bytes 262176 | tf_op jit(solution)/shard_map/ppermute | solution.py:249
  27.5 0.0 copy-done.3
  27.5 0.0 copy-done.2
  27.6 0.0 copy-done.5
  27.6 9.6 %shard_map.77 = (f32[16,5,8,256]{3,2,1,0:T(8,128)S(1)}, f32[16,5,8,256]{3,2,1,0:T(8,128)S(1)}, f32[2,512,128]{2,1,0:T(8,128)S(1)}, f32[2,512,256]{2,1,0:T(8,128)S(1)}, f32[2,512,128]{2,1,0:T(8,128)S(1)}) custom-call(s32[2,4]{1,0:T(2,128)S(1)} %bitcast.20, s32[1]{0:T(128)} %bitcast.2.half, f32[2,256,256]{2,1,0:T(8,128)S(1)} %copy-done, ...), custom_call_target="tpu_custom_call" | custom-call | tf_op jit(solution)/shard_map/pallas_call | solution.py:186
  37.2 2.2 %collective-permute-start.8 = (f32[16,5,8,256]{3,2,1,0:T(8,128)S(1)}, f32[16,5,8,256]{3,2,1,0:T(8,128)S(1)}, u32[]{:S(2)}, u32[]{:S(2)}) collective-permute-start(f32[16,5,8,256]{3,2,1,0:T(8,128)S(1)} %get-tuple-element.20), channel_id=1, source_target_pairs={{0,1},{1,0},{2,3},{3,2},{4,5},{5,4},{6,7},{7,6},{8,9},{9,8},{10,11... | collective-permute-start | bytes 1966088 | tf_op jit(solution)/shard_map/ppermute | solution.py:252
  39.4 0.0 collective-permute-start.6
  39.5 0.5 collective-permute-start.7
  40.0 1.2 %collective-permute-done.8 = f32[16,5,8,256]{3,2,1,0:T(8,128)S(1)} collective-permute-done((f32[16,5,8,256]{3,2,1,0:T(8,128)S(1)}, f32[16,5,8,256]{3,2,1,0:T(8,128)S(1)}, u32[]{:S(2)}, u32[]{:S(2)}) %collective-permute-start.8) | collective-permute-done | bytes 655392 | tf_op jit(solution)/shard_map/ppermute | solution.py:252
  41.2 0.9 add.98
  42.1 6.9 %all-to-all-start = ((f32[16,5,8,256]{3,2,1,0:T(8,128)}), f32[16,5,8,256]{3,2,1,0:T(8,128)}, u32[]{:S(2)}, u32[]{:S(2)}) async-start(f32[16,5,8,256]{3,2,1,0:T(8,128)} %add.98), calls=%async_computation | async-start | bytes 1310720 | tf_op jit(solution)/shard_map/all_to_all | solution.py:255
  49.0 0.0 collective-permute-done.6
  49.0 0.0 collective-permute-done.7
  49.0 1.3 %maximum_add_fusion = f32[2,512,256]{2,1,0:T(8,128)S(1)} fusion(f32[2,512,256]{2,1,0:T(8,128)S(1)} %get-tuple-element.16, f32[2,512,128]{2,1,0:T(8,128)} %collective-permute-done.7, f32[2,512,128]{2,1,0:T(8,128)} %collective-permute-done.6), kind=kLoop, calls=%fused_computation | loop fusion | flops 524288 | bytes 3145728 | tf_op jit(solution)/shard_map/add | solution.py:257
  50.4 4.6 %collective-permute-start.9 = (f32[2,128,256]{2,1,0:T(8,128)S(1)}, f32[2,128,256]{2,1,0:T(8,128)S(1)}, u32[]{:S(2)}, u32[]{:S(2)}) collective-permute-start(f32[2,128,256]{2,1,0:T(8,128)S(1)} %get-tuple-element.27), channel_id=1, source_target_pairs={{16,0},{32,16},{48,32},{64,48},{80,64},{96,80},{112,96},{128,112},... | collective-permute-start | bytes 786440 | tf_op jit(solution)/shard_map/ppermute | solution.py:258
  55.0 9.3 %all-to-all-done = f32[16,5,8,256]{3,2,1,0:T(8,128)} async-done(((f32[16,5,8,256]{3,2,1,0:T(8,128)}), f32[16,5,8,256]{3,2,1,0:T(8,128)}, u32[]{:S(2)}, u32[]{:S(2)}) %all-to-all-start) | async-done | bytes 655392 | tf_op jit(solution)/shard_map/all_to_all | solution.py:255
  64.3 1.1 %fusion = f32[5,8,256]{2,1,0:T(8,128)S(1)} fusion(f32[16,5,8,256]{3,2,1,0:T(8,128)} %all-to-all-done), kind=kLoop, calls=%fused_computation.9 | loop fusion | flops 153600 | bytes 696320 | tf_op jit(solution)/shard_map/add | solution.py:256
  65.4 0.0 collective-permute-done.9
  65.4 3.8 %collective-permute-start.12 = (f32[5,8,256]{2,1,0:T(8,128)S(1)}, f32[5,8,256]{2,1,0:T(8,128)S(1)}, u32[]{:S(2)}, u32[]{:S(2)}) collective-permute-start(f32[5,8,256]{2,1,0:T(8,128)S(1)} %fusion), channel_id=1, source_target_pairs={{0,192},{32,224},{64,128},{96,160},{128,64},{160,96},{192,0},{224,... | collective-permute-start | bytes 122888 | tf_op jit(solution)/shard_map/ppermute | solution.py:261
  69.2 0.5 collective-permute-start.11
  69.7 1.7 %collective-permute-start.10 = (f32[5,8,256]{2,1,0:T(8,128)S(1)}, f32[5,8,256]{2,1,0:T(8,128)S(1)}, u32[]{:S(2)}, u32[]{:S(2)}) collective-permute-start(f32[5,8,256]{2,1,0:T(8,128)S(1)} %fusion), channel_id=1, source_target_pairs={{0,64},{32,96},{64,0},{96,32},{128,192},{160,224},{192,128},{224,1... | collective-permute-start | bytes 122888 | tf_op jit(solution)/shard_map/ppermute | solution.py:261
  71.4 1.2 %collective-permute-start.14 = (f32[2,128,256]{2,1,0:T(8,128)S(1)}, f32[2,128,256]{2,1,0:T(8,128)S(1)}, u32[]{:S(2)}, u32[]{:S(2)}) collective-permute-start(f32[2,128,256]{2,1,0:T(8,128)S(1)} %get-tuple-element.26), channel_id=1, source_target_pairs={{0,16},{16,32},{32,48},{48,64},{64,80},{80,96},{96,112},{112,128},... | collective-permute-start | bytes 786440 | tf_op jit(solution)/shard_map/ppermute | solution.py:260
  72.6 0.0 collective-permute-done.12
  72.6 3.6 %collective-permute-done.11 = f32[5,8,256]{2,1,0:T(8,128)S(1)} collective-permute-done((f32[5,8,256]{2,1,0:T(8,128)S(1)}, f32[5,8,256]{2,1,0:T(8,128)S(1)}, u32[]{:S(2)}, u32[]{:S(2)}) %collective-permute-start.11) | collective-permute-done | bytes 40992 | tf_op jit(solution)/shard_map/ppermute | solution.py:261
  76.2 0.0 collective-permute-done.10
  76.2 0.5 collective-permute-start.13
  76.8 2.7 %collective-permute-done.13 = f32[5,8,256]{2,1,0:T(8,128)S(1)} collective-permute-done((f32[5,8,256]{2,1,0:T(8,128)S(1)}, f32[5,8,256]{2,1,0:T(8,128)S(1)}, u32[]{:S(2)}, u32[]{:S(2)}) %collective-permute-start.13) | collective-permute-done | bytes 40992 | tf_op jit(solution)/shard_map/ppermute | solution.py:263
  79.5 0.1 collective-permute-done.14
  79.7 14.5 %all_to_all.10.own = f32[16,4,8,256]{3,2,1,0:T(8,128)S(1)} all-to-all(f32[16,4,8,256]{3,2,1,0:T(8,128)S(1)} %broadcast_in_dim.2), channel_id=1, replica_groups=mesh['z'=8,'xl'=2,'xh'=2,'y'=4,'co'=2] {'xh','xl','y'}, dimensions={0} | all-to-all | bytes 1048576 | tf_op jit(solution)/shard_map/all_to_all | solution.py:269
  94.2 5.4 %collective-permute-start.15 = (f32[16,4,8,256]{3,2,1,0:T(8,128)S(1)}, f32[16,4,8,256]{3,2,1,0:T(8,128)S(1)}, u32[]{:S(2)}, u32[]{:S(2)}) collective-permute-start(f32[16,4,8,256]{3,2,1,0:T(8,128)S(1)} %all_to_all.10.own), channel_id=1, source_target_pairs={{0,1},{1,0},{2,3},{3,2},{4,5},{5,4},{6,7},{7,6},{8,9},{9,8},{10,11... | collective-permute-start | bytes 1572872 | tf_op jit(solution)/shard_map/ppermute | solution.py:271
  99.6 0.9 slice_add_fusion
  100.4 0.7 collective-permute-done.15.swapped
  101.1 1.0 %shard_map.78 = f32[2,2,256,256]{3,2,1,0:T(8,128)} custom-call(s32[1]{0:T(128)} %bitcast.2.half, f32[16,4,8,256]{3,2,1,0:T(8,128)S(1)} %all_to_all.10.own, f32[16,4,8,256]{3,2,1,0:T(8,128)S(1)} %collective-permute-done.15.swapped), custom_call_target="tpu_custom_call" | custom-call | tf_op jit(solution)/shard_map/pallas_call | solution.py:227
  (17 shorter events, 0.2 us)
Async XLA Ops:
  0.6 8.6 %copy-start = (f32[2,256,256]{2,1,0:T(8,128)S(1)}, f32[2,256,256]{2,1,0:T(8,128)}, u32[]{:S(2)}) copy-start(f32[2,256,256]{2,1,0:T(8,128)} %tile) | copy-start | bytes 1572868
  1.8 12.4 %collective-permute-start.1 = (f32[2,128,256]{2,1,0:T(8,128)S(1)}, f32[2,128,256]{2,1,0:T(8,128)S(1)}, u32[]{:S(2)}, u32[]{:S(2)}) collective-permute-start(f32[2,128,256]{2,1,0:T(8,128)S(1)} %get-tuple-element.30), channel_id=1, source_target_pairs={{16,0},{32,16},{48,32},{64,48},{80,64},{96,80},{112,96},{128,112},... | collective-permute-start | bytes 786440 | tf_op jit(solution)/shard_map/ppermute | solution.py:245
  9.2 9.0 %collective-permute-start = (f32[2,128,256]{2,1,0:T(8,128)S(1)}, f32[2,128,256]{2,1,0:T(8,128)S(1)}, u32[]{:S(2)}, u32[]{:S(2)}) collective-permute-start(f32[2,128,256]{2,1,0:T(8,128)S(1)} %get-tuple-element.31), channel_id=1, source_target_pairs={{0,16},{16,32},{32,48},{48,64},{64,80},{80,96},{96,112},{112,128},... | collective-permute-start | bytes 786440 | tf_op jit(solution)/shard_map/ppermute | solution.py:244
  9.2 18.3 %copy-start.3 = (bf16[512,512]{1,0:T(8,128)(2,1)S(1)}, bf16[512,512]{1,0:T(8,128)(2,1)}, u32[]{:S(2)}) copy-start(bf16[512,512]{1,0:T(8,128)(2,1)} %constant.32.clone.bwd_hbm) | copy-start | bytes 1572868
  9.2 18.3 %copy-start.4 = (bf16[512,512]{1,0:T(8,128)(2,1)S(1)}, bf16[512,512]{1,0:T(8,128)(2,1)}, u32[]{:S(2)}) copy-start(bf16[512,512]{1,0:T(8,128)(2,1)} %constant.31.clone.fwd_hbm) | copy-start | bytes 1572868
  9.3 12.2 %collective-permute-start.3 = (f32[2,256,128]{2,1,0:T(8,128)S(1)}, f32[2,256,128]{2,1,0:T(8,128)S(1)}, u32[]{:S(2)}, u32[]{:S(2)}) collective-permute-start(f32[2,256,128]{2,1,0:T(8,128)S(1)} %get-tuple-element.28), channel_id=1, source_target_pairs={{1,0},{2,1},{3,2},{4,3},{5,4},{6,5},{7,6},{8,7},{9,8},{10,9},{11,1... | collective-permute-start | bytes 786440 | tf_op jit(solution)/shard_map/ppermute | solution.py:247
  10.3 17.3 %copy-start.1 = (f32[2,2,256,256]{3,2,1,0:T(8,128)S(1)}, f32[2,2,256,256]{3,2,1,0:T(8,128)}, u32[]{:S(2)}) copy-start(f32[2,2,256,256]{3,2,1,0:T(8,128)} %probe.1) | copy-start | bytes 3145732
  10.3 17.3 %copy-start.2 = (f32[4,1,256,256]{3,2,1,0:T(8,128)S(1)}, f32[4,1,256,256]{3,2,1,0:T(8,128)}, u32[]{:S(2)}) copy-start(f32[4,1,256,256]{3,2,1,0:T(8,128)} %amp.1) | copy-start | bytes 3145732
  10.3 11.2 %collective-permute-start.2 = (f32[2,256,128]{2,1,0:T(8,128)S(1)}, f32[2,256,128]{2,1,0:T(8,128)S(1)}, u32[]{:S(2)}, u32[]{:S(2)}) collective-permute-start(f32[2,256,128]{2,1,0:T(8,128)S(1)} %get-tuple-element.29), channel_id=1, source_target_pairs={{0,1},{1,2},{2,3},{3,4},{4,5},{5,6},{6,7},{7,8},{8,9},{9,10},{10,1... | collective-permute-start | bytes 786440 | tf_op jit(solution)/shard_map/ppermute | solution.py:246
  18.3 6.4 %collective-permute-start.4 = (f32[2,2,128,128]{3,2,1,0:T(8,128)S(1)}, f32[2,2,128,128]{3,2,1,0:T(8,128)S(1)}, u32[]{:S(2)}, u32[]{:S(2)}) collective-permute-start(f32[2,2,128,128]{3,2,1,0:T(8,128)S(1)} %pad_maximum_fusion), channel_id=1, source_target_pairs={{0,1},{1,2},{2,3},{3,4},{4,5},{5,6},{6,7},{7,8},{8,9},{9,10},{10,1... | collective-permute-start | bytes 786440 | tf_op jit(solution)/shard_map/ppermute | solution.py:248
  21.4 6.2 %copy-start.5 = (s32[4,1,2]{0,2,1:T(2,128)S(1)}, s32[4,1,2]{0,2,1:T(2,128)}, u32[]{:S(2)}) copy-start(s32[4,1,2]{0,2,1:T(2,128)} %param.9) | copy-start | bytes 100
  21.4 6.2 %collective-permute-start.5 = (f32[2,2,128,128]{3,2,1,0:T(8,128)S(1)}, f32[2,2,128,128]{3,2,1,0:T(8,128)S(1)}, u32[]{:S(2)}, u32[]{:S(2)}) collective-permute-start(f32[2,2,128,128]{3,2,1,0:T(8,128)S(1)} %pad_maximum_fusion.1), channel_id=1, source_target_pairs={{1,0},{2,1},{3,2},{4,3},{5,4},{6,5},{7,6},{8,7},{9,8},{10,9},{11,1... | collective-permute-start | bytes 786440 | tf_op jit(solution)/shard_map/ppermute | solution.py:249
  37.2 4.0 %collective-permute-start.8 = (f32[16,5,8,256]{3,2,1,0:T(8,128)S(1)}, f32[16,5,8,256]{3,2,1,0:T(8,128)S(1)}, u32[]{:S(2)}, u32[]{:S(2)}) collective-permute-start(f32[16,5,8,256]{3,2,1,0:T(8,128)S(1)} %get-tuple-element.20), channel_id=1, source_target_pairs={{0,1},{1,0},{2,3},{3,2},{4,5},{5,4},{6,7},{7,6},{8,9},{9,8},{10,11... | collective-permute-start | bytes 1966088 | tf_op jit(solution)/shard_map/ppermute | solution.py:252
  39.4 9.6 %collective-permute-start.6 = (f32[2,512,128]{2,1,0:T(8,128)S(1)}, f32[2,512,128]{2,1,0:T(8,128)}, u32[]{:S(2)}, u32[]{:S(2)}) collective-permute-start(f32[2,512,128]{2,1,0:T(8,128)S(1)} %get-tuple-element.17), channel_id=1, source_target_pairs={{0,1},{1,2},{2,3},{3,4},{4,5},{5,6},{6,7},{7,8},{8,9},{9,10},{10,1... | collective-permute-start | bytes 1572872 | tf_op jit(solution)/shard_map/ppermute | solution.py:254
  39.5 9.6 %collective-permute-start.7 = (f32[2,512,128]{2,1,0:T(8,128)S(1)}, f32[2,512,128]{2,1,0:T(8,128)}, u32[]{:S(2)}, u32[]{:S(2)}) collective-permute-start(f32[2,512,128]{2,1,0:T(8,128)S(1)} %get-tuple-element.18), channel_id=1, source_target_pairs={{1,0},{2,1},{3,2},{4,3},{5,4},{6,5},{7,6},{8,7},{9,8},{10,9},{11,1... | collective-permute-start | bytes 1572872 | tf_op jit(solution)/shard_map/ppermute | solution.py:253
  42.1 22.2 %all-to-all-start = ((f32[16,5,8,256]{3,2,1,0:T(8,128)}), f32[16,5,8,256]{3,2,1,0:T(8,128)}, u32[]{:S(2)}, u32[]{:S(2)}) async-start(f32[16,5,8,256]{3,2,1,0:T(8,128)} %add.98), calls=%async_computation | async-start | bytes 1310720 | tf_op jit(solution)/shard_map/all_to_all | solution.py:255
  50.4 15.0 %collective-permute-start.9 = (f32[2,128,256]{2,1,0:T(8,128)S(1)}, f32[2,128,256]{2,1,0:T(8,128)S(1)}, u32[]{:S(2)}, u32[]{:S(2)}) collective-permute-start(f32[2,128,256]{2,1,0:T(8,128)S(1)} %get-tuple-element.27), channel_id=1, source_target_pairs={{16,0},{32,16},{48,32},{64,48},{80,64},{96,80},{112,96},{128,112},... | collective-permute-start | bytes 786440 | tf_op jit(solution)/shard_map/ppermute | solution.py:258
  65.4 7.2 %collective-permute-start.12 = (f32[5,8,256]{2,1,0:T(8,128)S(1)}, f32[5,8,256]{2,1,0:T(8,128)S(1)}, u32[]{:S(2)}, u32[]{:S(2)}) collective-permute-start(f32[5,8,256]{2,1,0:T(8,128)S(1)} %fusion), channel_id=1, source_target_pairs={{0,192},{32,224},{64,128},{96,160},{128,64},{160,96},{192,0},{224,... | collective-permute-start | bytes 122888 | tf_op jit(solution)/shard_map/ppermute | solution.py:261
  69.2 7.0 %collective-permute-start.11 = (f32[5,8,256]{2,1,0:T(8,128)S(1)}, f32[5,8,256]{2,1,0:T(8,128)S(1)}, u32[]{:S(2)}, u32[]{:S(2)}) collective-permute-start(f32[5,8,256]{2,1,0:T(8,128)S(1)} %fusion), channel_id=1, source_target_pairs={{0,128},{32,160},{64,192},{96,224},{128,0},{160,32},{192,64},{224,... | collective-permute-start | bytes 122888 | tf_op jit(solution)/shard_map/ppermute | solution.py:261
  69.7 6.5 %collective-permute-start.10 = (f32[5,8,256]{2,1,0:T(8,128)S(1)}, f32[5,8,256]{2,1,0:T(8,128)S(1)}, u32[]{:S(2)}, u32[]{:S(2)}) collective-permute-start(f32[5,8,256]{2,1,0:T(8,128)S(1)} %fusion), channel_id=1, source_target_pairs={{0,64},{32,96},{64,0},{96,32},{128,192},{160,224},{192,128},{224,1... | collective-permute-start | bytes 122888 | tf_op jit(solution)/shard_map/ppermute | solution.py:261
  71.4 8.2 %collective-permute-start.14 = (f32[2,128,256]{2,1,0:T(8,128)S(1)}, f32[2,128,256]{2,1,0:T(8,128)S(1)}, u32[]{:S(2)}, u32[]{:S(2)}) collective-permute-start(f32[2,128,256]{2,1,0:T(8,128)S(1)} %get-tuple-element.26), channel_id=1, source_target_pairs={{0,16},{16,32},{32,48},{48,64},{64,80},{80,96},{96,112},{112,128},... | collective-permute-start | bytes 786440 | tf_op jit(solution)/shard_map/ppermute | solution.py:260
  76.2 3.2 %collective-permute-start.13 = (f32[5,8,256]{2,1,0:T(8,128)S(1)}, f32[5,8,256]{2,1,0:T(8,128)S(1)}, u32[]{:S(2)}, u32[]{:S(2)}) collective-permute-start(f32[5,8,256]{2,1,0:T(8,128)S(1)} %add_add_fusion), channel_id=1, source_target_pairs={{0,32},{32,0},{64,96},{96,64},{128,160},{160,128},{192,224},{224,1... | collective-permute-start | bytes 122888 | tf_op jit(solution)/shard_map/ppermute | solution.py:263
  94.2 6.9 %collective-permute-start.15 = (f32[16,4,8,256]{3,2,1,0:T(8,128)S(1)}, f32[16,4,8,256]{3,2,1,0:T(8,128)S(1)}, u32[]{:S(2)}, u32[]{:S(2)}) collective-permute-start(f32[16,4,8,256]{3,2,1,0:T(8,128)S(1)} %all_to_all.10.own), channel_id=1, source_target_pairs={{0,1},{1,0},{2,3},{3,2},{4,5},{5,4},{6,7},{7,6},{8,9},{9,8},{10,11... | collective-permute-start | bytes 1572872 | tf_op jit(solution)/shard_map/ppermute | solution.py:271

commit v7 on v5

--- a/solution.py
+++ b/solution.py
@@ -152,7 +152,7 @@
         lax.fori_loop(0, W // CH, spread, 0, unroll=True)
         return carry
 
-    lax.fori_loop(0, POS, position, 0)
+    lax.fori_loop(0, POS, position, 0, unroll=True)
     for d in range(2):
         for i in range(2 * W // HALF):
             rows = pl.ds(i * HALF, HALF)

time: 102 us -> 101 us (level)
  Pallas kernels: 10.7 us -> 9.33 us
    pallas_call x1, Pallas kernels: 9.63 us -> 8.29 us  [correct(): pl.pallas_call(kernel, out_shape=(part, part, strip, jax.ShapeDtypeStruct...]
where the time goes in v7:
time: 101 us; the launch traced here: 100 us
  starting transfers between devices  36.5 us (36%)
  waiting for transfers between devices  32.7 us (32%)
  blocking collectives  15.4 us (15%)
  Pallas kernels  9.33 us (9%)
  other arithmetic  4.27 us (4%)
  local copies, waits for them, and re-layouts  1.3 us (1%)
    all_to_all x1, blocking collectives, body(): lax.all_to_all(jnp.broadcast_to(local[None], (16,) + local.shape), group,...  15.4 us
    all_to_all x1, waiting for transfers between devices, body(): pieces = lax.all_to_all(part, group, 0, 0, tiled=True)  10.3 us
    pallas_call x1, Pallas kernels, correct(): pl.pallas_call(kernel, out_shape=(part, part, strip, jax.ShapeDtypeStruct...  8.29 us
    ppermute x1, starting transfers between devices, body(): bot = lax.ppermute(object_field[:, first], GX, DOWN)  7.41 us
    all_to_all x1, starting transfers between devices, body(): pieces = lax.all_to_all(part, group, 0, 0, tiled=True)  6.9 us
    ppermute x3, starting transfers between devices, body(): lax.ppermute(part, 'z', [(i, i ^ step) for i in range(8)])  6.29 us
    ppermute x1, waiting for transfers between devices, body(): top = lax.ppermute(object_field[:, last], GX, UP)  3.97 us
    ppermute x1, starting transfers between devices, body(): from_below = lax.ppermute(folded[:, :HALF], GX, DOWN)  3.56 us
  transfers between devices with their start and end apart: 17, of which 11 were waited for; matrix products, arithmetic and copies ran while one was open for 3% of the time, Pallas kernels for 0%

profile of v7, /device:TPU:1, one launch (start us, length us, event | category | flops | bytes accessed | tf_op | source)
XLA Modules:
  0.0 100.3 jit_solution(7326066715599614891)
XLA Ops:
  0.6 0.0 copy-start
  0.7 1.1 %fusion.3 = (f32[2,128,256]{2,1,0:T(8,128)S(1)}, f32[2,128,256]{2,1,0:T(8,128)S(1)}) fusion(f32[2,256,256]{2,1,0:T(8,128)} %tile), kind=kLoop, calls=%fused_computation.30 | loop fusion | bytes 1048576 | tf_op jit(solution)/shard_map/slice | solution.py:245
  1.8 7.4 %collective-permute-start.1 = (f32[2,128,256]{2,1,0:T(8,128)S(1)}, f32[2,128,256]{2,1,0:T(8,128)S(1)}, u32[]{:S(2)}, u32[]{:S(2)}) collective-permute-start(f32[2,128,256]{2,1,0:T(8,128)S(1)} %get-tuple-element.32), channel_id=1, source_target_pairs={{16,0},{32,16},{48,32},{64,48},{80,64},{96,80},{112,96},{128,112},... | collective-permute-start | bytes 786440 | tf_op jit(solution)/shard_map/ppermute | solution.py:245
  9.2 0.0 collective-permute-start
  9.2 0.0 copy-done
  9.3 1.0 %collective-permute-start.3 = (f32[2,256,128]{2,1,0:T(8,128)S(1)}, f32[2,256,128]{2,1,0:T(8,128)S(1)}, u32[]{:S(2)}, u32[]{:S(2)}) collective-permute-start(f32[2,256,128]{2,1,0:T(8,128)S(1)} %get-tuple-element.30), channel_id=1, source_target_pairs={{1,0},{2,1},{3,2},{4,3},{5,4},{6,5},{7,6},{8,7},{9,8},{10,9},{11,1... | collective-permute-start | bytes 786440 | tf_op jit(solution)/shard_map/ppermute | solution.py:247
  10.3 1.3 %collective-permute-start.2 = (f32[2,256,128]{2,1,0:T(8,128)S(1)}, f32[2,256,128]{2,1,0:T(8,128)S(1)}, u32[]{:S(2)}, u32[]{:S(2)}) collective-permute-start(f32[2,256,128]{2,1,0:T(8,128)S(1)} %get-tuple-element.31), channel_id=1, source_target_pairs={{0,1},{1,2},{2,3},{3,4},{4,5},{5,6},{6,7},{7,8},{8,9},{9,10},{10,1... | collective-permute-start | bytes 786440 | tf_op jit(solution)/shard_map/ppermute | solution.py:246
  11.6 2.6 %collective-permute-done.1.bot = f32[2,128,256]{2,1,0:T(8,128)S(1)} collective-permute-done((f32[2,128,256]{2,1,0:T(8,128)S(1)}, f32[2,128,256]{2,1,0:T(8,128)S(1)}, u32[]{:S(2)}, u32[]{:S(2)}) %collective-permute-start.1) | collective-permute-done | bytes 262176 | tf_op jit(solution)/shard_map/ppermute | solution.py:245
  14.2 4.0 %collective-permute-done.top = f32[2,128,256]{2,1,0:T(8,128)S(1)} collective-permute-done((f32[2,128,256]{2,1,0:T(8,128)S(1)}, f32[2,128,256]{2,1,0:T(8,128)S(1)}, u32[]{:S(2)}, u32[]{:S(2)}) %collective-permute-start) | collective-permute-done | bytes 262176 | tf_op jit(solution)/shard_map/ppermute | solution.py:244
  18.3 3.1 %collective-permute-start.4 = (f32[2,2,128,128]{3,2,1,0:T(8,128)S(1)}, f32[2,2,128,128]{3,2,1,0:T(8,128)S(1)}, u32[]{:S(2)}, u32[]{:S(2)}) collective-permute-start(f32[2,2,128,128]{3,2,1,0:T(8,128)S(1)} %pad_maximum_fusion), channel_id=1, source_target_pairs={{0,1},{1,2},{2,3},{3,4},{4,5},{5,6},{6,7},{7,8},{8,9},{9,10},{10,1... | collective-permute-start | bytes 786440 | tf_op jit(solution)/shard_map/ppermute | solution.py:248
  21.4 0.0 copy-start.5
  21.4 0.1 collective-permute-start.5
  21.5 0.0 collective-permute-done.3.right
  21.5 0.0 collective-permute-done.2.left
  21.5 3.2 %collective-permute-done.4.left_ends = f32[2,2,128,128]{3,2,1,0:T(8,128)S(1)} collective-permute-done((f32[2,2,128,128]{3,2,1,0:T(8,128)S(1)}, f32[2,2,128,128]{3,2,1,0:T(8,128)S(1)}, u32[]{:S(2)}, u32[]{:S(2)}) %collective-permute-start.4) | collective-permute-done | bytes 262176 | tf_op jit(solution)/shard_map/ppermute | solution.py:248
  24.6 2.9 %collective-permute-done.5.right_ends = f32[2,2,128,128]{3,2,1,0:T(8,128)S(1)} collective-permute-done((f32[2,2,128,128]{3,2,1,0:T(8,128)S(1)}, f32[2,2,128,128]{3,2,1,0:T(8,128)S(1)}, u32[]{:S(2)}, u32[]{:S(2)}) %collective-permute-start.5) | collective-permute-done | bytes 262176 | tf_op jit(solution)/shard_map/ppermute | solution.py:249
  27.5 0.0 copy-done.3
  27.5 0.0 copy-done.4
  27.5 0.0 copy-done.1
  27.6 8.3 %shard_map.77 = (f32[16,5,8,256]{3,2,1,0:T(8,128)S(1)}, f32[16,5,8,256]{3,2,1,0:T(8,128)S(1)}, f32[2,512,128]{2,1,0:T(8,128)S(1)}, f32[2,512,256]{2,1,0:T(8,128)S(1)}, f32[2,512,128]{2,1,0:T(8,128)S(1)}) custom-call(s32[2,4]{1,0:T(2,128)S(1)} %bitcast.20, s32[1]{0:T(128)} %bitcast.2.half, f32[2,256,256]{2,1,0:T(8,128)S(1)} %copy-done, ...), custom_call_target="tpu_custom_call" | custom-call | tf_op jit(solution)/shard_map/pallas_call | solution.py:186
  35.9 2.2 %collective-permute-start.6 = (f32[16,5,8,256]{3,2,1,0:T(8,128)S(1)}, f32[16,5,8,256]{3,2,1,0:T(8,128)S(1)}, u32[]{:S(2)}, u32[]{:S(2)}) collective-permute-start(f32[16,5,8,256]{3,2,1,0:T(8,128)S(1)} %get-tuple-element.18), channel_id=1, source_target_pairs={{0,1},{1,0},{2,3},{3,2},{4,5},{5,4},{6,7},{7,6},{8,9},{9,8},{10,11... | collective-permute-start | bytes 1966088 | tf_op jit(solution)/shard_map/ppermute | solution.py:252
  38.1 0.0 collective-permute-start.7
  38.1 0.5 collective-permute-start.8
  38.6 1.2 %collective-permute-done.6 = f32[16,5,8,256]{3,2,1,0:T(8,128)S(1)} collective-permute-done((f32[16,5,8,256]{3,2,1,0:T(8,128)S(1)}, f32[16,5,8,256]{3,2,1,0:T(8,128)S(1)}, u32[]{:S(2)}, u32[]{:S(2)}) %collective-permute-start.6) | collective-permute-done | bytes 655392 | tf_op jit(solution)/shard_map/ppermute | solution.py:252
  39.8 0.9 add.97
  40.7 6.9 %all-to-all-start = ((f32[16,5,8,256]{3,2,1,0:T(8,128)}), f32[16,5,8,256]{3,2,1,0:T(8,128)}, u32[]{:S(2)}, u32[]{:S(2)}) async-start(f32[16,5,8,256]{3,2,1,0:T(8,128)} %add.97), calls=%async_computation | async-start | bytes 1310720 | tf_op jit(solution)/shard_map/all_to_all | solution.py:255
  47.6 0.0 collective-permute-done.7
  47.6 0.0 collective-permute-done.8
  47.6 1.3 %maximum_add_fusion = f32[2,512,256]{2,1,0:T(8,128)S(1)} fusion(f32[2,512,256]{2,1,0:T(8,128)S(1)} %get-tuple-element.19, f32[2,512,128]{2,1,0:T(8,128)} %collective-permute-done.8, f32[2,512,128]{2,1,0:T(8,128)} %collective-permute-done.7), kind=kLoop, calls=%fused_computation | loop fusion | flops 524288 | bytes 3145728 | tf_op jit(solution)/shard_map/add | solution.py:257
  48.9 10.3 %all-to-all-done = f32[16,5,8,256]{3,2,1,0:T(8,128)} async-done(((f32[16,5,8,256]{3,2,1,0:T(8,128)}), f32[16,5,8,256]{3,2,1,0:T(8,128)}, u32[]{:S(2)}, u32[]{:S(2)}) %all-to-all-start) | async-done | bytes 655392 | tf_op jit(solution)/shard_map/all_to_all | solution.py:255
  59.3 1.1 %fusion = f32[5,8,256]{2,1,0:T(8,128)S(1)} fusion(f32[16,5,8,256]{3,2,1,0:T(8,128)} %all-to-all-done), kind=kLoop, calls=%fused_computation.9 | loop fusion | flops 153600 | bytes 696320 | tf_op jit(solution)/shard_map/add | solution.py:256
  60.4 4.1 %collective-permute-start.11 = (f32[5,8,256]{2,1,0:T(8,128)S(1)}, f32[5,8,256]{2,1,0:T(8,128)S(1)}, u32[]{:S(2)}, u32[]{:S(2)}) collective-permute-start(f32[5,8,256]{2,1,0:T(8,128)S(1)} %fusion), channel_id=1, source_target_pairs={{0,192},{32,224},{64,128},{96,160},{128,64},{160,96},{192,0},{224,... | collective-permute-start | bytes 122888 | tf_op jit(solution)/shard_map/ppermute | solution.py:261
  64.5 0.1 collective-permute-start.10
  64.6 2.1 %collective-permute-start.9 = (f32[5,8,256]{2,1,0:T(8,128)S(1)}, f32[5,8,256]{2,1,0:T(8,128)S(1)}, u32[]{:S(2)}, u32[]{:S(2)}) collective-permute-start(f32[5,8,256]{2,1,0:T(8,128)S(1)} %fusion), channel_id=1, source_target_pairs={{0,64},{32,96},{64,0},{96,32},{128,192},{160,224},{192,128},{224,1... | collective-permute-start | bytes 122888 | tf_op jit(solution)/shard_map/ppermute | solution.py:261
  66.7 0.1 collective-permute-start.14
  66.8 3.6 %collective-permute-start.13 = (f32[2,128,256]{2,1,0:T(8,128)S(1)}, f32[2,128,256]{2,1,0:T(8,128)S(1)}, u32[]{:S(2)}, u32[]{:S(2)}) collective-permute-start(f32[2,128,256]{2,1,0:T(8,128)S(1)} %get-tuple-element.29), channel_id=1, source_target_pairs={{16,0},{32,16},{48,32},{64,48},{80,64},{96,80},{112,96},{128,112},... | collective-permute-start | bytes 786440 | tf_op jit(solution)/shard_map/ppermute | solution.py:259
  70.4 0.0 collective-permute-done.11
  70.4 0.9 collective-permute-done.10
  71.3 0.0 collective-permute-done.9
  71.3 0.8 collective-permute-start.12
  72.1 3.5 %collective-permute-done.12 = f32[5,8,256]{2,1,0:T(8,128)S(1)} collective-permute-done((f32[5,8,256]{2,1,0:T(8,128)S(1)}, f32[5,8,256]{2,1,0:T(8,128)S(1)}, u32[]{:S(2)}, u32[]{:S(2)}) %collective-permute-start.12) | collective-permute-done | bytes 40992 | tf_op jit(solution)/shard_map/ppermute | solution.py:263
  75.6 0.1 collective-permute-done.14
  75.7 3.4 %collective-permute-done.13 = f32[2,128,256]{2,1,0:T(8,128)S(1)} collective-permute-done((f32[2,128,256]{2,1,0:T(8,128)S(1)}, f32[2,128,256]{2,1,0:T(8,128)S(1)}, u32[]{:S(2)}, u32[]{:S(2)}) %collective-permute-start.13) | collective-permute-done | bytes 262176 | tf_op jit(solution)/shard_map/ppermute | solution.py:259
  79.1 15.4 %all_to_all.10.own = f32[16,4,8,256]{3,2,1,0:T(8,128)S(1)} all-to-all(f32[16,4,8,256]{3,2,1,0:T(8,128)S(1)} %broadcast_in_dim.2), channel_id=1, replica_groups=mesh['z'=8,'xl'=2,'xh'=2,'y'=4,'co'=2] {'xh','xl','y'}, dimensions={0} | all-to-all | bytes 1048576 | tf_op jit(solution)/shard_map/all_to_all | solution.py:269
  94.5 3.2 %collective-permute-start.15 = (f32[16,4,8,256]{3,2,1,0:T(8,128)S(1)}, f32[16,4,8,256]{3,2,1,0:T(8,128)S(1)}, u32[]{:S(2)}, u32[]{:S(2)}) collective-permute-start(f32[16,4,8,256]{3,2,1,0:T(8,128)S(1)} %all_to_all.10.own), channel_id=1, source_target_pairs={{0,1},{1,0},{2,3},{3,2},{4,5},{5,4},{6,7},{7,6},{8,9},{9,8},{10,11... | collective-permute-start | bytes 1572872 | tf_op jit(solution)/shard_map/ppermute | solution.py:271
  97.7 0.9 maximum_add_fusion.1
  98.6 0.7 collective-permute-done.15.swapped
  99.3 1.0 %shard_map.78 = f32[2,2,256,256]{3,2,1,0:T(8,128)} custom-call(s32[1]{0:T(128)} %bitcast.2.half, f32[16,4,8,256]{3,2,1,0:T(8,128)S(1)} %all_to_all.10.own, f32[16,4,8,256]{3,2,1,0:T(8,128)S(1)} %collective-permute-done.15.swapped), custom_call_target="tpu_custom_call" | custom-call | tf_op jit(solution)/shard_map/pallas_call | solution.py:227
  (17 shorter events, 0.2 us)
Async XLA Ops:
  0.6 8.6 %copy-start = (f32[2,256,256]{2,1,0:T(8,128)S(1)}, f32[2,256,256]{2,1,0:T(8,128)}, u32[]{:S(2)}) copy-start(f32[2,256,256]{2,1,0:T(8,128)} %tile) | copy-start | bytes 1572868
  1.8 12.4 %collective-permute-start.1 = (f32[2,128,256]{2,1,0:T(8,128)S(1)}, f32[2,128,256]{2,1,0:T(8,128)S(1)}, u32[]{:S(2)}, u32[]{:S(2)}) collective-permute-start(f32[2,128,256]{2,1,0:T(8,128)S(1)} %get-tuple-element.32), channel_id=1, source_target_pairs={{16,0},{32,16},{48,32},{64,48},{80,64},{96,80},{112,96},{128,112},... | collective-permute-start | bytes 786440 | tf_op jit(solution)/shard_map/ppermute | solution.py:245
  9.2 9.0 %collective-permute-start = (f32[2,128,256]{2,1,0:T(8,128)S(1)}, f32[2,128,256]{2,1,0:T(8,128)S(1)}, u32[]{:S(2)}, u32[]{:S(2)}) collective-permute-start(f32[2,128,256]{2,1,0:T(8,128)S(1)} %get-tuple-element.33), channel_id=1, source_target_pairs={{0,16},{16,32},{32,48},{48,64},{64,80},{80,96},{96,112},{112,128},... | collective-permute-start | bytes 786440 | tf_op jit(solution)/shard_map/ppermute | solution.py:244
  9.2 18.3 %copy-start.3 = (bf16[512,512]{1,0:T(8,128)(2,1)S(1)}, bf16[512,512]{1,0:T(8,128)(2,1)}, u32[]{:S(2)}) copy-start(bf16[512,512]{1,0:T(8,128)(2,1)} %constant.32.clone.bwd_hbm) | copy-start | bytes 1572868
  9.2 18.3 %copy-start.4 = (bf16[512,512]{1,0:T(8,128)(2,1)S(1)}, bf16[512,512]{1,0:T(8,128)(2,1)}, u32[]{:S(2)}) copy-start(bf16[512,512]{1,0:T(8,128)(2,1)} %constant.31.clone.fwd_hbm) | copy-start | bytes 1572868
  9.3 12.2 %collective-permute-start.3 = (f32[2,256,128]{2,1,0:T(8,128)S(1)}, f32[2,256,128]{2,1,0:T(8,128)S(1)}, u32[]{:S(2)}, u32[]{:S(2)}) collective-permute-start(f32[2,256,128]{2,1,0:T(8,128)S(1)} %get-tuple-element.30), channel_id=1, source_target_pairs={{1,0},{2,1},{3,2},{4,3},{5,4},{6,5},{7,6},{8,7},{9,8},{10,9},{11,1... | collective-permute-start | bytes 786440 | tf_op jit(solution)/shard_map/ppermute | solution.py:247
  10.3 17.3 %copy-start.1 = (f32[2,2,256,256]{3,2,1,0:T(8,128)S(1)}, f32[2,2,256,256]{3,2,1,0:T(8,128)}, u32[]{:S(2)}) copy-start(f32[2,2,256,256]{3,2,1,0:T(8,128)} %probe.1) | copy-start | bytes 3145732
  10.3 17.3 %copy-start.2 = (f32[4,1,256,256]{3,2,1,0:T(8,128)S(1)}, f32[4,1,256,256]{3,2,1,0:T(8,128)}, u32[]{:S(2)}) copy-start(f32[4,1,256,256]{3,2,1,0:T(8,128)} %amp.1) | copy-start | bytes 3145732
  10.3 11.2 %collective-permute-start.2 = (f32[2,256,128]{2,1,0:T(8,128)S(1)}, f32[2,256,128]{2,1,0:T(8,128)S(1)}, u32[]{:S(2)}, u32[]{:S(2)}) collective-permute-start(f32[2,256,128]{2,1,0:T(8,128)S(1)} %get-tuple-element.31), channel_id=1, source_target_pairs={{0,1},{1,2},{2,3},{3,4},{4,5},{5,6},{6,7},{7,8},{8,9},{9,10},{10,1... | collective-permute-start | bytes 786440 | tf_op jit(solution)/shard_map/ppermute | solution.py:246
  18.3 6.4 %collective-permute-start.4 = (f32[2,2,128,128]{3,2,1,0:T(8,128)S(1)}, f32[2,2,128,128]{3,2,1,0:T(8,128)S(1)}, u32[]{:S(2)}, u32[]{:S(2)}) collective-permute-start(f32[2,2,128,128]{3,2,1,0:T(8,128)S(1)} %pad_maximum_fusion), channel_id=1, source_target_pairs={{0,1},{1,2},{2,3},{3,4},{4,5},{5,6},{6,7},{7,8},{8,9},{9,10},{10,1... | collective-permute-start | bytes 786440 | tf_op jit(solution)/shard_map/ppermute | solution.py:248
  21.4 6.2 %copy-start.5 = (s32[4,1,2]{0,2,1:T(2,128)S(1)}, s32[4,1,2]{0,2,1:T(2,128)}, u32[]{:S(2)}) copy-start(s32[4,1,2]{0,2,1:T(2,128)} %param.9) | copy-start | bytes 100
  21.4 6.2 %collective-permute-start.5 = (f32[2,2,128,128]{3,2,1,0:T(8,128)S(1)}, f32[2,2,128,128]{3,2,1,0:T(8,128)S(1)}, u32[]{:S(2)}, u32[]{:S(2)}) collective-permute-start(f32[2,2,128,128]{3,2,1,0:T(8,128)S(1)} %pad_maximum_fusion.1), channel_id=1, source_target_pairs={{1,0},{2,1},{3,2},{4,3},{5,4},{6,5},{7,6},{8,7},{9,8},{10,9},{11,1... | collective-permute-start | bytes 786440 | tf_op jit(solution)/shard_map/ppermute | solution.py:249
  35.9 3.9 %collective-permute-start.6 = (f32[16,5,8,256]{3,2,1,0:T(8,128)S(1)}, f32[16,5,8,256]{3,2,1,0:T(8,128)S(1)}, u32[]{:S(2)}, u32[]{:S(2)}) collective-permute-start(f32[16,5,8,256]{3,2,1,0:T(8,128)S(1)} %get-tuple-element.18), channel_id=1, source_target_pairs={{0,1},{1,0},{2,3},{3,2},{4,5},{5,4},{6,7},{7,6},{8,9},{9,8},{10,11... | collective-permute-start | bytes 1966088 | tf_op jit(solution)/shard_map/ppermute | solution.py:252
  38.1 9.6 %collective-permute-start.7 = (f32[2,512,128]{2,1,0:T(8,128)S(1)}, f32[2,512,128]{2,1,0:T(8,128)}, u32[]{:S(2)}, u32[]{:S(2)}) collective-permute-start(f32[2,512,128]{2,1,0:T(8,128)S(1)} %get-tuple-element.20), channel_id=1, source_target_pairs={{0,1},{1,2},{2,3},{3,4},{4,5},{5,6},{6,7},{7,8},{8,9},{9,10},{10,1... | collective-permute-start | bytes 1572872 | tf_op jit(solution)/shard_map/ppermute | solution.py:254
  38.1 9.6 %collective-permute-start.8 = (f32[2,512,128]{2,1,0:T(8,128)S(1)}, f32[2,512,128]{2,1,0:T(8,128)}, u32[]{:S(2)}, u32[]{:S(2)}) collective-permute-start(f32[2,512,128]{2,1,0:T(8,128)S(1)} %get-tuple-element.21), channel_id=1, source_target_pairs={{1,0},{2,1},{3,2},{4,3},{5,4},{6,5},{7,6},{8,7},{9,8},{10,9},{11,1... | collective-permute-start | bytes 1572872 | tf_op jit(solution)/shard_map/ppermute | solution.py:253
  40.7 18.6 %all-to-all-start = ((f32[16,5,8,256]{3,2,1,0:T(8,128)}), f32[16,5,8,256]{3,2,1,0:T(8,128)}, u32[]{:S(2)}, u32[]{:S(2)}) async-start(f32[16,5,8,256]{3,2,1,0:T(8,128)} %add.97), calls=%async_computation | async-start | bytes 1310720 | tf_op jit(solution)/shard_map/all_to_all | solution.py:255
  60.4 10.0 %collective-permute-start.11 = (f32[5,8,256]{2,1,0:T(8,128)S(1)}, f32[5,8,256]{2,1,0:T(8,128)S(1)}, u32[]{:S(2)}, u32[]{:S(2)}) collective-permute-start(f32[5,8,256]{2,1,0:T(8,128)S(1)} %fusion), channel_id=1, source_target_pairs={{0,192},{32,224},{64,128},{96,160},{128,64},{160,96},{192,0},{224,... | collective-permute-start | bytes 122888 | tf_op jit(solution)/shard_map/ppermute | solution.py:261
  64.5 6.8 %collective-permute-start.10 = (f32[5,8,256]{2,1,0:T(8,128)S(1)}, f32[5,8,256]{2,1,0:T(8,128)S(1)}, u32[]{:S(2)}, u32[]{:S(2)}) collective-permute-start(f32[5,8,256]{2,1,0:T(8,128)S(1)} %fusion), channel_id=1, source_target_pairs={{0,128},{32,160},{64,192},{96,224},{128,0},{160,32},{192,64},{224,... | collective-permute-start | bytes 122888 | tf_op jit(solution)/shard_map/ppermute | solution.py:261
  64.6 6.6 %collective-permute-start.9 = (f32[5,8,256]{2,1,0:T(8,128)S(1)}, f32[5,8,256]{2,1,0:T(8,128)S(1)}, u32[]{:S(2)}, u32[]{:S(2)}) collective-permute-start(f32[5,8,256]{2,1,0:T(8,128)S(1)} %fusion), channel_id=1, source_target_pairs={{0,64},{32,96},{64,0},{96,32},{128,192},{160,224},{192,128},{224,1... | collective-permute-start | bytes 122888 | tf_op jit(solution)/shard_map/ppermute | solution.py:261
  66.7 8.9 %collective-permute-start.14 = (f32[2,128,256]{2,1,0:T(8,128)S(1)}, f32[2,128,256]{2,1,0:T(8,128)S(1)}, u32[]{:S(2)}, u32[]{:S(2)}) collective-permute-start(f32[2,128,256]{2,1,0:T(8,128)S(1)} %get-tuple-element.28), channel_id=1, source_target_pairs={{0,16},{16,32},{32,48},{48,64},{64,80},{80,96},{96,112},{112,128},... | collective-permute-start | bytes 786440 | tf_op jit(solution)/shard_map/ppermute | solution.py:260
  66.8 12.2 %collective-permute-start.13 = (f32[2,128,256]{2,1,0:T(8,128)S(1)}, f32[2,128,256]{2,1,0:T(8,128)S(1)}, u32[]{:S(2)}, u32[]{:S(2)}) collective-permute-start(f32[2,128,256]{2,1,0:T(8,128)S(1)} %get-tuple-element.29), channel_id=1, source_target_pairs={{16,0},{32,16},{48,32},{64,48},{80,64},{96,80},{112,96},{128,112},... | collective-permute-start | bytes 786440 | tf_op jit(solution)/shard_map/ppermute | solution.py:259
  71.3 4.3 %collective-permute-start.12 = (f32[5,8,256]{2,1,0:T(8,128)S(1)}, f32[5,8,256]{2,1,0:T(8,128)S(1)}, u32[]{:S(2)}, u32[]{:S(2)}) collective-permute-start(f32[5,8,256]{2,1,0:T(8,128)S(1)} %add_add_fusion), channel_id=1, source_target_pairs={{0,32},{32,0},{64,96},{96,64},{128,160},{160,128},{192,224},{224,1... | collective-permute-start | bytes 122888 | tf_op jit(solution)/shard_map/ppermute | solution.py:263
  94.5 4.8 %collective-permute-start.15 = (f32[16,4,8,256]{3,2,1,0:T(8,128)S(1)}, f32[16,4,8,256]{3,2,1,0:T(8,128)S(1)}, u32[]{:S(2)}, u32[]{:S(2)}) collective-permute-start(f32[16,4,8,256]{3,2,1,0:T(8,128)S(1)} %all_to_all.10.own), channel_id=1, source_target_pairs={{0,1},{1,0},{2,3},{3,2},{4,5},{5,4},{6,7},{7,6},{8,9},{9,8},{10,11... | collective-permute-start | bytes 1572872 | tf_op jit(solution)/shard_map/ppermute | solution.py:271

commit v8 on v7

--- a/solution.py
+++ b/solution.py
@@ -32,41 +32,38 @@
     return fwd, bwd
 
 
+SMEM = pl.BlockSpec(memory_space=pltpu.SMEM)
+VMEM = pl.BlockSpec(memory_space=pltpu.VMEM)
+HBM = pl.BlockSpec(memory_space=pltpu.HBM)
+
+
+def spot(number, unit):
+    return pl.ds(pl.multiple_of(number * unit, unit), HALF)
+
+
 def kernel(
-    offs, half, tile, top, bot, left, right, left_ends, right_ends, probe, amp, fwd_hbm, bwd_hbm,
-    mine, other, out_left, out_mid, out_right,
-    ext, acc, win, stack, side, far, weight, grads, power, fwd, bwd, sems,
+    offs, flags, rows_in, rows_out, cols_in, cols_out, ends_in, ends_out, tile, probe, amp, power, inverse, fwd, bwd,
+    mine, other, back_in, back_out, out_mid,
+    ext, acc, win, stack, side, far, weight, grads,
 ):
-    copies = [
-        pltpu.make_async_copy(fwd_hbm, fwd, sems.at[0]),
-        pltpu.make_async_copy(bwd_hbm, bwd, sems.at[1]),
-    ]
-    for copy in copies:
-        copy.start()
+    co, xl = flags[0], flags[1]
+    q_in, q_out = 3 * (1 - co), 3 * co
+    at_in, at_out = spot(1 - xl, W + HALF), spot(xl, W + HALF)
+    middle = pl.ds(HALF, W)
     lanes = lax.broadcasted_iota(jnp.int32, (CH, HALF), 1)
     for q in range(2):
         cols = pl.ds(q * HALF, HALF)
-        ext[:, q + 1, 0:HALF, :] = top[:, :, cols]
-        ext[:, q + 1, HALF : HALF + W, :] = tile[:, :, cols]
-        ext[:, q + 1, HALF + W :, :] = bot[:, :, cols]
-    for q, middle, ends in ((0, left, left_ends), (3, right, right_ends)):
-        ext[:, q, 0:HALF, :] = ends[0]
-        ext[:, q, HALF : HALF + W, :] = middle[...]
-        ext[:, q, HALF + W :, :] = ends[1]
+        ext[:, q + 1, middle, :] = tile[:, :, cols]
+        ext[:, q + 1, at_in, :] = rows_in[:, :, cols]
+        ext[:, q + 1, at_out, :] = rows_out[:, :, cols]
+    for q, cols, ends in ((q_in, cols_in, ends_in), (q_out, cols_out, ends_out)):
+        ext[:, q, middle, :] = cols[...]
+        ext[:, q, at_in, :] = ends[0]
+        ext[:, q, at_out, :] = ends[1]
     acc[...] = jnp.zeros_like(acc)
     weight[...] = jnp.zeros_like(weight)
     grads[...] = jnp.zeros_like(grads)
-    top_power = jnp.zeros((CH, W), F32)
-    for i in range(W // CH):
-        rows = pl.ds(i * CH, CH)
-        total = jnp.zeros((CH, W), F32)
-        for k in range(MODES):
-            total += probe[k, 0, rows, :] * probe[k, 0, rows, :] + probe[k, 1, rows, :] * probe[k, 1, rows, :]
-        power[rows, :] = total
-        top_power = jnp.maximum(top_power, total)
-    scale = 1.0 / (jnp.max(top_power, axis=(0, 1), keepdims=True) + 1e-06)
-    for copy in copies:
-        copy.wait()
+    scale = inverse[0:1, :]
 
     def position(p, carry):
         r = offs[0, p] + HALF
@@ -156,16 +153,15 @@
     for d in range(2):
         for i in range(2 * W // HALF):
             rows = pl.ds(i * HALF, HALF)
-            out_left[d, rows, :] = acc[d, 0, rows, :] * scale
-            out_right[d, rows, :] = acc[d, 3, rows, :] * scale
+            back_in[d, rows, :] = acc[d, q_in, rows, :] * scale
+            back_out[d, rows, :] = acc[d, q_out, rows, :] * scale
             for q in range(2):
                 cols = pl.ds(q * HALF, HALF)
                 step = acc[d, q + 1, rows, :] * scale
                 if 1 <= i <= 2:
                     step += tile[d, pl.ds((i - 1) * HALF, HALF), cols]
                 out_mid[d, rows, cols] = step
-    h = half[0]
-    for out, side_of in ((mine, h), (other, 1 - h)):
+    for out, side_of in ((mine, co), (other, 1 - co)):
 
         def flush(i, carry):
             rows = pl.ds(pl.multiple_of(side_of * HALF + i * 8, 8), 8)
@@ -177,17 +173,14 @@
         lax.fori_loop(0, 16, flush, 0)
 
 
-def correct(offsets, half, border, probe, amplitude):
-    fwd, bwd = dft_matrices()
-    vmem = pl.BlockSpec(memory_space=pltpu.VMEM)
-    smem = pl.BlockSpec(memory_space=pltpu.SMEM)
+def correct(offsets, flags, border, staged):
     part = jax.ShapeDtypeStruct((16, 2 * MODES + 1, 8, W), F32)
     strip = jax.ShapeDtypeStruct((2, 2 * W, HALF), F32)
     return pl.pallas_call(
         kernel,
-        out_shape=(part, part, strip, jax.ShapeDtypeStruct((2, 2 * W, W), F32), strip),
-        in_specs=[smem, smem] + [vmem] * 9 + [pl.BlockSpec(memory_space=pl.ANY)] * 2,
-        out_specs=(vmem,) * 5,
+        out_shape=(part, part, strip, strip, jax.ShapeDtypeStruct((2, 2 * W, W), F32)),
+        in_specs=[SMEM, SMEM] + [VMEM] * 13,
+        out_specs=(VMEM,) * 5,
         scratch_shapes=[
             pltpu.VMEM((2, 4, 2 * W, HALF), F32),
             pltpu.VMEM((2, 4, 2 * W, HALF), F32),
@@ -197,78 +190,172 @@
             pltpu.VMEM((MODES, W, 2 * W), F32),
             pltpu.VMEM((W, W), F32),
             pltpu.VMEM((2 * MODES, W, W), F32),
-            pltpu.VMEM((W, W), F32),
-            pltpu.VMEM((2 * W, 2 * W), BF),
-            pltpu.VMEM((2 * W, 2 * W), BF),
-            pltpu.SemaphoreType.DMA((2,)),
         ],
         compiler_params=pltpu.CompilerParams(vmem_limit_bytes=20 << 20),
-    )(offsets, half, *border, probe, amplitude, jnp.asarray(fwd), jnp.asarray(bwd))
+    )(offsets, flags, *border, *staged)
 
 
 GX = ("z", "xl")
 GY = ("xh", "y", "co")
-UP = [(i, (i + 1) % 16) for i in range(16)]
-DOWN = [(j, i) for i, j in UP]
-SWAP = [(0, 1), (1, 0)]
-
-
-def arrange_kernel(half, own, swapped, out):
-    h = half[0]
-    for source, side_of in ((own, h), (swapped, 1 - h)):
-        for i in range(16):
-            rows = pl.ds(pl.multiple_of(side_of * HALF + i * 8, 8), 8)
-            for n in range(2 * MODES):
-                out[n // 2, n % 2, rows, :] = source[i, n]
-
-
-def arrange(half, own, swapped):
-    vmem = pl.BlockSpec(memory_space=pltpu.VMEM)
+NEAR = [(0, 1), (1, 0)]
+FAR = [(i, (i + 1) % 16 if i % 2 else (i - 1) % 16) for i in range(16)]
+
+
+def small_call(body, shapes, in_specs, scratch=()):
     return pl.pallas_call(
-        arrange_kernel,
-        out_shape=jax.ShapeDtypeStruct((MODES, 2, W, W), F32),
-        in_specs=[pl.BlockSpec(memory_space=pltpu.SMEM), vmem, vmem],
-        out_specs=vmem,
-        compiler_params=pltpu.CompilerParams(vmem_limit_bytes=4 << 20),
-    )(half, own, swapped)
+        body,
+        out_shape=tuple(jax.ShapeDtypeStruct(shape, dtype) for shape, dtype in shapes),
+        in_specs=in_specs,
+        out_specs=(VMEM,) * len(shapes),
+        scratch_shapes=scratch,
+        compiler_params=pltpu.CompilerParams(vmem_limit_bytes=6 << 20),
+    )
+
+
+def cut_borders(flags, tile):
+    def run(flags, tile, rows_in, rows_out, cols_in, cols_out, sems):
+        co, xl = flags[0], flags[1]
+        copies = [
+            pltpu.make_async_copy(tile.at[:, spot(1 - xl, HALF), :], rows_in, sems.at[0]),
+            pltpu.make_async_copy(tile.at[:, spot(xl, HALF), :], rows_out, sems.at[1]),
+            pltpu.make_async_copy(tile.at[:, :, spot(1 - co, HALF)], cols_in, sems.at[2]),
+            pltpu.make_async_copy(tile.at[:, :, spot(co, HALF)], cols_out, sems.at[3]),
+        ]
+        for copy in copies:
+            copy.start()
+        for copy in copies:
+            copy.wait()
+
+    return small_call(
+        run,
+        [((2, HALF, W), F32)] * 2 + [((2, W, HALF), F32)] * 2,
+        [SMEM, HBM],
+        [pltpu.SemaphoreType.DMA((4,))],
+    )(flags, tile)
+
+
+def stage(offsets, tile, probe, amplitude, after):
+    fwd, bwd = (jnp.asarray(matrix) for matrix in dft_matrices())
+    arrays = (tile, probe, amplitude, fwd, bwd)
+
+    def run(offs, tile, probe, amp, fwd, bwd, after, offs_s, tile_v, probe_v, amp_v, power, inverse, fwd_v, bwd_v, sems):
+        pairs = ((probe, probe_v), (tile, tile_v), (fwd, fwd_v), (bwd, bwd_v), (amp, amp_v))
+        copies = [pltpu.make_async_copy(a, b, sems.at[n]) for n, (a, b) in enumerate(pairs)]
+        for copy in copies:
+            copy.start()
+        for i in range(2):
+            for p in range(POS):
+                offs_s[i, p] = offs[i, p]
+        copies[0].wait()
+        largest = jnp.zeros((CH, W), F32)
+        for i in range(W // CH):
+            rows = pl.ds(i * CH, CH)
+            total = jnp.zeros((CH, W), F32)
+            for k in range(MODES):
+                total += probe_v[k, 0, rows, :] * probe_v[k, 0, rows, :] + probe_v[k, 1, rows, :] * probe_v[k, 1, rows, :]
+            power[rows, :] = total
+            largest = jnp.maximum(largest, total)
+        scale = 1.0 / (jnp.max(largest, axis=(0, 1), keepdims=True) + 1e-06)
+        inverse[...] = jnp.broadcast_to(scale, inverse.shape)
+        for copy in copies[1:]:
+            copy.wait()
+
+    shapes = [(a.shape, a.dtype) for a in arrays[:3]] + [((W, W), F32), ((8, HALF), F32)]
+    shapes += [(a.shape, a.dtype) for a in arrays[3:]]
+    return pl.pallas_call(
+        run,
+        out_shape=[jax.ShapeDtypeStruct(offsets.shape, jnp.int32)] + [jax.ShapeDtypeStruct(*a) for a in shapes],
+        in_specs=[SMEM] + [HBM] * 5 + [pl.BlockSpec(memory_space=pl.ANY)],
+        out_specs=[SMEM] + [VMEM] * 7,
+        scratch_shapes=[pltpu.SemaphoreType.DMA((5,))],
+        compiler_params=pltpu.CompilerParams(vmem_limit_bytes=6 << 20),
+    )(offsets, *arrays, after)
+
+
+def cut_ends(flags, rows_in, rows_out):
+    def run(flags, rows_in, rows_out, ends_in, ends_out):
+        co = flags[0]
+        for n, rows in enumerate((rows_in, rows_out)):
+            ends_in[n] = rows[:, :, spot(1 - co, HALF)]
+            ends_out[n] = rows[:, :, spot(co, HALF)]
+
+    return small_call(run, [((2, 2, HALF, HALF), F32)] * 2, [SMEM, VMEM, VMEM])(flags, rows_in, rows_out)
+
+
+def fold(flags, middle, from_in, from_out):
+    def run(flags, middle, from_in, from_out, back_in, back_out, center):
+        co, xl = flags[0], flags[1]
+        for c in range(2):
+
+            @pl.when(co == c)
+            def _():
+                for q, extra in ((1 - c, from_in), (c, from_out)):
+                    cols = pl.ds(q * HALF, HALF)
+                    for dst, at in ((back_in, spot(1 - xl, W + HALF)), (back_out, spot(xl, W + HALF)), (center, pl.ds(HALF, W))):
+                        dst[:, :, cols] = middle[:, at, cols] + extra[:, at, :]
+
+    return small_call(run, [((2, HALF, W), F32)] * 2 + [((2, W, W), F32)], [SMEM] + [VMEM] * 3)(flags, middle, from_in, from_out)
+
+
+def finish(flags, center, from_in, from_out):
+    def run(flags, center, from_in, from_out, out):
+        xl = flags[1]
+        for at, extra in ((spot(1 - xl, HALF), from_in), (spot(xl, HALF), from_out)):
+            out[:, at, :] = center[:, at, :] + extra[...]
+
+    return small_call(run, [((2, W, W), F32)], [SMEM] + [VMEM] * 3)(flags, center, from_in, from_out)[0]
+
+
+def arrange(flags, own, swapped):
+    def run(flags, own, swapped, out):
+        co = flags[0]
+        for source, side_of in ((own, co), (swapped, 1 - co)):
+            for i in range(16):
+                rows = pl.ds(pl.multiple_of(side_of * HALF + i * 8, 8), 8)
+                for n in range(2 * MODES):
+                    out[n // 2, n % 2, rows, :] = source[i, n]
+
+    return small_call(run, [((MODES, 2, W, W), F32)], [SMEM, VMEM, VMEM])(flags, own, swapped)[0]
 
 
 def body(object_field, probe_field, amplitude, offsets):
     group = ("xh", "xl", "y")
     co = lax.axis_index("co")
-    half = co.reshape(1)
+    flags = jnp.stack([co, lax.axis_index("xl")])
     block = (co * 16 + lax.axis_index(group)) * 8
     offs = offsets.transpose(1, 2, 0).reshape(2, POS)
-    object_field, half, block = lax.optimization_barrier((object_field, half, block))
-    first, last = slice(0, HALF), slice(HALF, W)
-    top = lax.ppermute(object_field[:, last], GX, UP)
-    bot = lax.ppermute(object_field[:, first], GX, DOWN)
-    left = lax.ppermute(object_field[:, :, last], GY, UP)
-    right = lax.ppermute(object_field[:, :, first], GY, DOWN)
-    left_ends = lax.ppermute(jnp.stack([top[:, :, last], bot[:, :, last]]), GY, UP)
-    right_ends = lax.ppermute(jnp.stack([top[:, :, first], bot[:, :, first]]), GY, DOWN)
-    border = (object_field, top, bot, left, right, left_ends, right_ends)
-    mine, other, out_left, out_mid, out_right = correct(offs, half, border, probe_field, amplitude)
-    part = mine + lax.ppermute(other, "co", SWAP)
-    from_right = lax.ppermute(out_left, GY, DOWN)
-    from_left = lax.ppermute(out_right, GY, UP)
+    object_field, flags, block = lax.optimization_barrier((object_field, flags, block))
+    rows_in, rows_out, cols_in, cols_out = cut_borders(flags, object_field)
+    rows_out = lax.ppermute(rows_out, GX, FAR)
+    rows_in = lax.ppermute(rows_in, "xl", NEAR)
+    cols_out = lax.ppermute(cols_out, GY, FAR)
+    cols_in = lax.ppermute(cols_in, "co", NEAR)
+    ends_in, ends_out = cut_ends(flags, rows_in, rows_out)
+    ends_out = lax.ppermute(ends_out, GY, FAR)
+    ends_in = lax.ppermute(ends_in, "co", NEAR)
+    offs, *staged = stage(offs, object_field, probe_field, amplitude, cols_in)
+    border = (rows_in, rows_out, cols_in, cols_out, ends_in, ends_out)
+    mine, other, back_in, back_out, middle = correct(offs, flags, border, staged)
+    from_out = lax.ppermute(back_out, GY, FAR)
+    from_in = lax.ppermute(back_in, "co", NEAR)
+    part = mine + lax.ppermute(other, "co", NEAR)
     pieces = lax.all_to_all(part, group, 0, 0, tiled=True)
     part = sum(pieces[i] for i in range(16))
-    folded = out_mid + jnp.concatenate([from_left, from_right], 2)
-    part, folded = lax.optimization_barrier((part, folded))
-    from_below = lax.ppermute(folded[:, :HALF], GX, DOWN)
-    from_above = lax.ppermute(folded[:, HALF + W :], GX, UP)
+    back_in, back_out, center = fold(flags, middle, from_in, from_out)
+    part, back_in, back_out = lax.optimization_barrier((part, back_in, back_out))
+    from_out = lax.ppermute(back_out, GX, FAR)
+    from_in = lax.ppermute(back_in, "xl", NEAR)
     peers = [lax.ppermute(part, "z", [(i, i ^ step) for i in range(8)]) for step in (2, 4, 6)]
     part = (part + peers[0]) + (peers[1] + peers[2])
     part = part + lax.ppermute(part, "z", [(i, i ^ 1) for i in range(8)])
-    part, from_below, from_above = lax.optimization_barrier((part, from_below, from_above))
+    part, from_in, from_out = lax.optimization_barrier((part, from_in, from_out))
     planes = probe_field.reshape(2 * MODES, W, W)
     local = lax.dynamic_slice_in_dim(planes, block, 8, 1)
     weight = part[2 * MODES]
     local = local + (part[: 2 * MODES] - local * weight) / (weight + 1e-05)
     gathered = lax.all_to_all(jnp.broadcast_to(local[None], (16,) + local.shape), group, 0, 0, tiled=True)
-    updated_object = folded[:, HALF : HALF + W] + jnp.concatenate([from_above, from_below], 1)
-    updated_probe = arrange(half, gathered, lax.ppermute(gathered, "co", SWAP))
+    updated_object = finish(flags, center, from_in, from_out)
+    updated_probe = arrange(flags, gathered, lax.ppermute(gathered, "co", NEAR))
     return (updated_object, updated_probe)
 
 

time: 101 us -> 108 us (1.069)
  waiting for transfers between devices: 32.7 us -> 22.7 us
  starting transfers between devices: 36.5 us -> 43.4 us
  Pallas kernels: 9.33 us -> 15.3 us
  blocking collectives: 15.4 us -> 18.9 us
  local copies, waits for them, and re-layouts: 1.3 us -> 4.58 us
  other arithmetic: 4.27 us -> 1.92 us
    all_to_all x1, waiting for transfers between devices: 10.3 us -> 0.01 us  [body(): pieces = lax.all_to_all(part, group, 0, 0, tiled=True)]
    ppermute x12, starting transfers between devices: 22.5 us -> 28.7 us  [the longest x1 5.55 us: body(): rows_out = lax.ppermute(rows_out, GX, FAR)]
    pallas_call x2 -> x7, Pallas kernels: 9.33 us -> 15.3 us  [the longest x1 8.71 us: correct(): pl.pallas_call(kernel, out_shape=(part, part, strip, strip, jax.ShapeDtyp...]
    unnamed x12 -> x14, local copies, waits for them, and re-layouts: 0.03 us -> 4.54 us
    all_to_all x1, blocking collectives: 15.4 us -> 18.9 us  [body(): lax.all_to_all(jnp.broadcast_to(local[None], (16,) + local.shape), group,...]
    add x3 -> x1, other arithmetic: 3.08 us -> 0.92 us  [body(): part = mine + lax.ppermute(other, 'co', NEAR)]
    ppermute x3, starting transfers between devices: 6.29 us -> 8.29 us  [body(): lax.ppermute(part, 'z', [(i, i ^ step) for i in range(8)])]
    all_to_all x1, starting transfers between devices: 6.9 us -> 5.55 us  [body(): pieces = lax.all_to_all(part, group, 0, 0, tiled=True)]
  transfers between devices with their start and end apart: 17 -> 17, of which waited for: 11 -> 8; matrix products, arithmetic and copies ran while one was open for 3% -> 0% of each run, Pallas kernels for 0% -> 4%
where the time goes in v8:
time: 108 us; the launch traced here: 107 us
  starting transfers between devices  43.4 us (40%)
  waiting for transfers between devices  22.7 us (21%)
  blocking collectives  18.9 us (17%)
  Pallas kernels  15.3 us (14%)
  local copies, waits for them, and re-layouts  4.58 us (4%)
  other arithmetic  1.92 us (2%)
    all_to_all x1, blocking collectives, body(): lax.all_to_all(jnp.broadcast_to(local[None], (16,) + local.shape), group,...  18.9 us
    ppermute x1, waiting for transfers between devices, body(): from_out = lax.ppermute(back_out, GY, FAR)  13.2 us
    pallas_call x1, Pallas kernels, correct(): pl.pallas_call(kernel, out_shape=(part, part, strip, strip, jax.ShapeDtyp...  8.71 us
    ppermute x3, starting transfers between devices, body(): lax.ppermute(part, 'z', [(i, i ^ step) for i in range(8)])  8.29 us
    all_to_all x1, starting transfers between devices, body(): pieces = lax.all_to_all(part, group, 0, 0, tiled=True)  5.55 us
    ppermute x1, starting transfers between devices, body(): rows_out = lax.ppermute(rows_out, GX, FAR)  5.55 us
    ppermute x1, starting transfers between devices, body(): part = mine + lax.ppermute(other, 'co', NEAR)  5.51 us
    unnamed x14, local copies, waits for them, and re-layouts  4.54 us
  transfers between devices with their start and end apart: 17, of which 8 were waited for; matrix products, arithmetic and copies ran while one was open for 0% of the time, Pallas kernels for 4%

profile of v8, /device:TPU:1, one launch (start us, length us, event | category | flops | bytes accessed | tf_op | source)
XLA Modules:
  0.0 107.5 jit_solution(7193252819922763725)
XLA Ops:
  0.6 0.1 pad_add_fusion.flags
  0.7 1.0 copy-done
  1.8 0.7 shard_map.77
  2.4 2.1 %collective-permute-start.1 = (f32[2,128,256]{2,1,0:T(8,128)S(1)}, f32[2,128,256]{2,1,0:T(8,128)S(1)}, u32[]{:S(2)}, u32[]{:S(2)}) collective-permute-start(f32[2,128,256]{2,1,0:T(8,128)S(1)} %get-tuple-element.37), channel_id=1, source_target_pairs={{0,16},{16,0},{1,17},{17,1},{2,18},{18,2},{3,19},{19,3},{4,20},{20... | collective-permute-start | bytes 786440 | tf_op jit(solution)/shard_map/ppermute | solution.py:330
  4.6 5.5 %collective-permute-start.2 = (f32[2,128,256]{2,1,0:T(8,128)S(1)}, f32[2,128,256]{2,1,0:T(8,128)S(1)}, u32[]{:S(2)}, u32[]{:S(2)}) collective-permute-start(f32[2,128,256]{2,1,0:T(8,128)S(1)} %get-tuple-element.38), channel_id=1, source_target_pairs={{0,240},{16,32},{32,16},{48,64},{64,48},{80,96},{96,80},{112,128},... | collective-permute-start | bytes 786440 | tf_op jit(solution)/shard_map/ppermute | solution.py:329
  10.1 1.2 %collective-permute-start = (f32[2,256,128]{2,1,0:T(8,128)S(1)}, f32[2,256,128]{2,1,0:T(8,128)S(1)}, u32[]{:S(2)}, u32[]{:S(2)}) collective-permute-start(f32[2,256,128]{2,1,0:T(8,128)S(1)} %get-tuple-element.35), channel_id=1, source_target_pairs={{0,1},{1,0},{2,3},{3,2},{4,5},{5,4},{6,7},{7,6},{8,9},{9,8},{10,11... | collective-permute-start | bytes 786440 | tf_op jit(solution)/shard_map/ppermute | solution.py:332
  11.3 1.2 %collective-permute-start.3 = (f32[2,256,128]{2,1,0:T(8,128)S(1)}, f32[2,256,128]{2,1,0:T(8,128)S(1)}, u32[]{:S(2)}, u32[]{:S(2)}) collective-permute-start(f32[2,256,128]{2,1,0:T(8,128)S(1)} %get-tuple-element.39), channel_id=1, source_target_pairs={{0,15},{1,2},{2,1},{3,4},{4,3},{5,6},{6,5},{7,8},{8,7},{9,10},{10,... | collective-permute-start | bytes 786440 | tf_op jit(solution)/shard_map/ppermute | solution.py:331
  12.5 2.3 %collective-permute-done.1.rows_in = f32[2,128,256]{2,1,0:T(8,128)S(1)} collective-permute-done((f32[2,128,256]{2,1,0:T(8,128)S(1)}, f32[2,128,256]{2,1,0:T(8,128)S(1)}, u32[]{:S(2)}, u32[]{:S(2)}) %collective-permute-start.1) | collective-permute-done | bytes 262176 | tf_op jit(solution)/shard_map/ppermute | solution.py:330
  14.9 1.0 collective-permute-done.2.rows_out
  15.9 0.6 shard_map.79
  16.4 2.0 %collective-permute-start.4 = (f32[2,2,128,128]{3,2,1,0:T(8,128)S(1)}, f32[2,2,128,128]{3,2,1,0:T(8,128)S(1)}, u32[]{:S(2)}, u32[]{:S(2)}) collective-permute-start(f32[2,2,128,128]{3,2,1,0:T(8,128)S(1)} %get-tuple-element.40), channel_id=1, source_target_pairs={{0,1},{1,0},{2,3},{3,2},{4,5},{5,4},{6,7},{7,6},{8,9},{9,8},{10,11... | collective-permute-start | bytes 786440 | tf_op jit(solution)/shard_map/ppermute | solution.py:335
  18.4 1.2 %collective-permute-start.5 = (f32[2,2,128,128]{3,2,1,0:T(8,128)S(1)}, f32[2,2,128,128]{3,2,1,0:T(8,128)S(1)}, u32[]{:S(2)}, u32[]{:S(2)}) collective-permute-start(f32[2,2,128,128]{3,2,1,0:T(8,128)S(1)} %get-tuple-element.41), channel_id=1, source_target_pairs={{0,15},{1,2},{2,1},{3,4},{4,3},{5,6},{6,5},{7,8},{8,7},{9,10},{10,... | collective-permute-start | bytes 786440 | tf_op jit(solution)/shard_map/ppermute | solution.py:334
  19.7 0.0 collective-permute-done.after.cols_in
  19.7 0.0 copy-start.2
  19.7 1.2 %copy-done.2 = f32[2,2,256,256]{3,2,1,0:T(8,128)S(1)} copy-done((f32[2,2,256,256]{3,2,1,0:T(8,128)S(1)}, f32[2,2,256,256]{3,2,1,0:T(8,128)}, u32[]{:S(2)}) %copy-start.2) | copy-done | bytes 1048600
  20.9 1.2 %copy-done.3 = f32[4,1,256,256]{3,2,1,0:T(8,128)S(1)} copy-done((f32[4,1,256,256]{3,2,1,0:T(8,128)S(1)}, f32[4,1,256,256]{3,2,1,0:T(8,128)}, u32[]{:S(2)}) %copy-start.3) | copy-done | bytes 1048600
  22.1 1.0 copy-done.5
  23.2 1.7 %shard_map.78 = (s32[2,4]{1,0:T(2,128)S(1)}, f32[2,256,256]{2,1,0:T(8,128)S(1)}, f32[2,2,256,256]{3,2,1,0:T(8,128)S(1)}, f32[4,1,256,256]{3,2,1,0:T(8,128)S(1)},...) custom-call(s32[2,4]{1,0:T(2,128)S(1)} %bitcast.13, ...), custom_call_target="tpu_custom_call" | custom-call | tf_op jit(solution)/shard_map/pallas_call | solution.py:265
  24.8 0.0 collective-permute-done.3.cols_out
  24.9 0.0 collective-permute-done.5.ends_out
  24.9 8.7 %shard_map.80 = (f32[16,5,8,256]{3,2,1,0:T(8,128)S(1)}, f32[16,5,8,256]{3,2,1,0:T(8,128)S(1)}, f32[2,512,128]{2,1,0:T(8,128)S(1)}, f32[2,512,128]{2,1,0:T(8,128)S(1)}, f32[2,512,256]{2,1,0:T(8,128)S(1)}) custom-call(s32[2,4]{1,0:T(2,128)S(1)} %get-tuple-element.36.offs, s32[2]{0:T(128)S(1)} %pad_add_fusion.flags, ...), custom_call_target="tpu_custom_call" | custom-call | tf_op jit(solution)/shard_map/pallas_call | solution.py:179
  33.6 5.5 %collective-permute-start.8 = (f32[16,5,8,256]{3,2,1,0:T(8,128)S(1)}, f32[16,5,8,256]{3,2,1,0:T(8,128)S(1)}, u32[]{:S(2)}, u32[]{:S(2)}) collective-permute-start(f32[16,5,8,256]{3,2,1,0:T(8,128)S(1)} %get-tuple-element.54), channel_id=1, source_target_pairs={{0,1},{1,0},{2,3},{3,2},{4,5},{5,4},{6,7},{7,6},{8,9},{9,8},{10,11... | collective-permute-start | bytes 1966088 | tf_op jit(solution)/shard_map/ppermute | solution.py:341
  39.1 1.7 %collective-permute-done.8 = f32[16,5,8,256]{3,2,1,0:T(8,128)S(1)} collective-permute-done((f32[16,5,8,256]{3,2,1,0:T(8,128)S(1)}, f32[16,5,8,256]{3,2,1,0:T(8,128)S(1)}, u32[]{:S(2)}, u32[]{:S(2)}) %collective-permute-start.8) | collective-permute-done | bytes 655392 | tf_op jit(solution)/shard_map/ppermute | solution.py:341
  40.8 0.9 add.91
  41.8 5.5 %all-to-all-start = ((f32[16,5,8,256]{3,2,1,0:T(8,128)}), f32[16,5,8,256]{3,2,1,0:T(8,128)S(1)}, u32[]{:S(2)}, u32[]{:S(2)}) async-start(f32[16,5,8,256]{3,2,1,0:T(8,128)} %add.91), calls=%async_computation | async-start | bytes 1310720 | tf_op jit(solution)/shard_map/all_to_all | solution.py:342
  47.3 0.5 collective-permute-start.6
  47.8 1.7 %collective-permute-start.7 = (f32[2,512,128]{2,1,0:T(8,128)S(1)}, f32[2,512,128]{2,1,0:T(8,128)S(1)}, u32[]{:S(2)}, u32[]{:S(2)}) collective-permute-start(f32[2,512,128]{2,1,0:T(8,128)S(1)} %get-tuple-element.51), channel_id=1, source_target_pairs={{0,15},{1,2},{2,1},{3,4},{4,3},{5,6},{6,5},{7,8},{8,7},{9,10},{10,... | collective-permute-start | bytes 1572872 | tf_op jit(solution)/shard_map/ppermute | solution.py:339
  49.6 0.0 collective-permute-done.6.from_in
  49.6 13.2 %collective-permute-done.7.from_out = f32[2,512,128]{2,1,0:T(8,128)S(1)} collective-permute-done((f32[2,512,128]{2,1,0:T(8,128)S(1)}, f32[2,512,128]{2,1,0:T(8,128)S(1)}, u32[]{:S(2)}, u32[]{:S(2)}) %collective-permute-start.7) | collective-permute-done | bytes 524320 | tf_op jit(solution)/shard_map/ppermute | solution.py:339
  62.8 0.7 shard_map.81
  63.6 6.1 %collective-permute-start.11 = (f32[5,8,256]{2,1,0:T(8,128)S(1)}, f32[5,8,256]{2,1,0:T(8,128)S(1)}, u32[]{:S(2)}, u32[]{:S(2)}) collective-permute-start(f32[5,8,256]{2,1,0:T(8,128)S(1)} %fusion), channel_id=1, source_target_pairs={{0,192},{32,224},{64,128},{96,160},{128,64},{160,96},{192,0},{224,... | collective-permute-start | bytes 122888 | tf_op jit(solution)/shard_map/ppermute | solution.py:348
  69.7 1.0 collective-permute-start.10
  70.6 1.2 %collective-permute-start.9 = (f32[5,8,256]{2,1,0:T(8,128)S(1)}, f32[5,8,256]{2,1,0:T(8,128)S(1)}, u32[]{:S(2)}, u32[]{:S(2)}) collective-permute-start(f32[5,8,256]{2,1,0:T(8,128)S(1)} %fusion), channel_id=1, source_target_pairs={{0,64},{32,96},{64,0},{96,32},{128,192},{160,224},{192,128},{224,1... | collective-permute-start | bytes 122888 | tf_op jit(solution)/shard_map/ppermute | solution.py:348
  71.8 1.2 %collective-permute-start.13 = (f32[2,128,256]{2,1,0:T(8,128)S(1)}, f32[2,128,256]{2,1,0:T(8,128)S(1)}, u32[]{:S(2)}, u32[]{:S(2)}) collective-permute-start(f32[2,128,256]{2,1,0:T(8,128)S(1)} %get-tuple-element.58), channel_id=1, source_target_pairs={{0,16},{16,0},{1,17},{17,1},{2,18},{18,2},{3,19},{19,3},{4,20},{20... | collective-permute-start | bytes 786440 | tf_op jit(solution)/shard_map/ppermute | solution.py:347
  73.0 3.1 %collective-permute-start.14 = (f32[2,128,256]{2,1,0:T(8,128)S(1)}, f32[2,128,256]{2,1,0:T(8,128)S(1)}, u32[]{:S(2)}, u32[]{:S(2)}) collective-permute-start(f32[2,128,256]{2,1,0:T(8,128)S(1)} %get-tuple-element.59), channel_id=1, source_target_pairs={{0,240},{16,32},{32,16},{48,64},{64,48},{80,96},{96,80},{112,128},... | collective-permute-start | bytes 786440 | tf_op jit(solution)/shard_map/ppermute | solution.py:346
  76.1 0.0 collective-permute-done.11
  76.1 0.6 collective-permute-done.10
  76.7 0.0 collective-permute-done.9
  76.7 0.8 collective-permute-start.12
  77.5 3.2 %collective-permute-done.12 = f32[5,8,256]{2,1,0:T(8,128)S(1)} collective-permute-done((f32[5,8,256]{2,1,0:T(8,128)S(1)}, f32[5,8,256]{2,1,0:T(8,128)S(1)}, u32[]{:S(2)}, u32[]{:S(2)}) %collective-permute-start.12) | collective-permute-done | bytes 40992 | tf_op jit(solution)/shard_map/ppermute | solution.py:350
  80.7 0.0 collective-permute-done.13.from_in
  80.8 0.4 collective-permute-done.14.from_out
  81.1 0.9 divide_add_fusion
  82.0 18.9 %all_to_all.10.own = f32[16,4,8,256]{3,2,1,0:T(8,128)S(1)} all-to-all(f32[16,4,8,256]{3,2,1,0:T(8,128)S(1)} %broadcast_in_dim.2), channel_id=1, replica_groups=mesh['z'=8,'xl'=2,'xh'=2,'y'=4,'co'=2] {'xh','xl','y'}, dimensions={0} | all-to-all | bytes 1048576 | tf_op jit(solution)/shard_map/all_to_all | solution.py:356
  100.9 3.5 %collective-permute-start.15 = (f32[16,4,8,256]{3,2,1,0:T(8,128)S(1)}, f32[16,4,8,256]{3,2,1,0:T(8,128)S(1)}, u32[]{:S(2)}, u32[]{:S(2)}) collective-permute-start(f32[16,4,8,256]{3,2,1,0:T(8,128)S(1)} %all_to_all.10.own), channel_id=1, source_target_pairs={{0,1},{1,0},{2,3},{3,2},{4,5},{5,4},{6,7},{7,6},{8,9},{9,8},{10,11... | collective-permute-start | bytes 1572872 | tf_op jit(solution)/shard_map/ppermute | solution.py:358
  104.4 1.4 %shard_map.82 = f32[2,256,256]{2,1,0:T(8,128)} custom-call(s32[2]{0:T(128)S(1)} %pad_add_fusion.flags, f32[2,256,256]{2,1,0:T(8,128)S(1)} %get-tuple-element.52.center, f32[2,128,256]{2,1,0:T(8,128)S(1)} %collective-permute-done.13.from_in, f32[2,128,256]{2,1,0:T(8,128)S(1)} %collective-permute-done.14.from_out), custom_call_target="tpu_custom_call" | custom-call | tf_op jit(solution)/shard_map/pallas_call | solution.py:306
  105.7 0.1 collective-permute-done.15.swapped
  105.9 1.6 %shard_map.83 = f32[2,2,256,256]{3,2,1,0:T(8,128)} custom-call(s32[2]{0:T(128)S(1)} %pad_add_fusion.flags, f32[16,4,8,256]{3,2,1,0:T(8,128)S(1)} %all_to_all.10.own, f32[16,4,8,256]{3,2,1,0:T(8,128)S(1)} %collective-permute-done.15.swapped), custom_call_target="tpu_custom_call" | custom-call | tf_op jit(solution)/shard_map/pallas_call | solution.py:318
  (16 shorter events, 0.1 us)
Async XLA Ops:
  0.7 1.0 copy-start
  1.8 17.9 %copy-start.1 = (f32[2,256,256]{2,1,0:T(8,128)S(1)}, f32[2,256,256]{2,1,0:T(8,128)}, u32[]{:S(2)}) copy-start(f32[2,256,256]{2,1,0:T(8,128)} %tile.1) | copy-start | bytes 1572868
  1.8 17.9 %copy-start.4 = (bf16[512,512]{1,0:T(8,128)(2,1)S(1)}, bf16[512,512]{1,0:T(8,128)(2,1)}, u32[]{:S(2)}) copy-start(bf16[512,512]{1,0:T(8,128)(2,1)} %constant.32.clone.bwd) | copy-start | bytes 1572868
  2.4 12.4 %collective-permute-start.1 = (f32[2,128,256]{2,1,0:T(8,128)S(1)}, f32[2,128,256]{2,1,0:T(8,128)S(1)}, u32[]{:S(2)}, u32[]{:S(2)}) collective-permute-start(f32[2,128,256]{2,1,0:T(8,128)S(1)} %get-tuple-element.37), channel_id=1, source_target_pairs={{0,16},{16,0},{1,17},{17,1},{2,18},{18,2},{3,19},{19,3},{4,20},{20... | collective-permute-start | bytes 786440 | tf_op jit(solution)/shard_map/ppermute | solution.py:330
  4.6 11.3 %collective-permute-start.2 = (f32[2,128,256]{2,1,0:T(8,128)S(1)}, f32[2,128,256]{2,1,0:T(8,128)S(1)}, u32[]{:S(2)}, u32[]{:S(2)}) collective-permute-start(f32[2,128,256]{2,1,0:T(8,128)S(1)} %get-tuple-element.38), channel_id=1, source_target_pairs={{0,240},{16,32},{32,16},{48,64},{64,48},{80,96},{96,80},{112,128},... | collective-permute-start | bytes 786440 | tf_op jit(solution)/shard_map/ppermute | solution.py:329
  10.1 9.6 %collective-permute-start = (f32[2,256,128]{2,1,0:T(8,128)S(1)}, f32[2,256,128]{2,1,0:T(8,128)S(1)}, u32[]{:S(2)}, u32[]{:S(2)}) collective-permute-start(f32[2,256,128]{2,1,0:T(8,128)S(1)} %get-tuple-element.35), channel_id=1, source_target_pairs={{0,1},{1,0},{2,3},{3,2},{4,5},{5,4},{6,7},{7,6},{8,9},{9,8},{10,11... | collective-permute-start | bytes 786440 | tf_op jit(solution)/shard_map/ppermute | solution.py:332
  11.3 13.5 %collective-permute-start.3 = (f32[2,256,128]{2,1,0:T(8,128)S(1)}, f32[2,256,128]{2,1,0:T(8,128)S(1)}, u32[]{:S(2)}, u32[]{:S(2)}) collective-permute-start(f32[2,256,128]{2,1,0:T(8,128)S(1)} %get-tuple-element.39), channel_id=1, source_target_pairs={{0,15},{1,2},{2,1},{3,4},{4,3},{5,6},{6,5},{7,8},{8,7},{9,10},{10,... | collective-permute-start | bytes 786440 | tf_op jit(solution)/shard_map/ppermute | solution.py:331
  16.4 8.4 %collective-permute-start.4 = (f32[2,2,128,128]{3,2,1,0:T(8,128)S(1)}, f32[2,2,128,128]{3,2,1,0:T(8,128)S(1)}, u32[]{:S(2)}, u32[]{:S(2)}) collective-permute-start(f32[2,2,128,128]{3,2,1,0:T(8,128)S(1)} %get-tuple-element.40), channel_id=1, source_target_pairs={{0,1},{1,0},{2,3},{3,2},{4,5},{5,4},{6,7},{7,6},{8,9},{9,8},{10,11... | collective-permute-start | bytes 786440 | tf_op jit(solution)/shard_map/ppermute | solution.py:335
  18.4 1.2 %copy-start.6 = (s32[4,1,2]{0,2,1:T(2,128)S(1)}, s32[4,1,2]{0,2,1:T(2,128)}, u32[]{:S(2)}) copy-start(s32[4,1,2]{0,2,1:T(2,128)} %param.9) | copy-start | bytes 100
  18.4 6.4 %collective-permute-start.5 = (f32[2,2,128,128]{3,2,1,0:T(8,128)S(1)}, f32[2,2,128,128]{3,2,1,0:T(8,128)S(1)}, u32[]{:S(2)}, u32[]{:S(2)}) collective-permute-start(f32[2,2,128,128]{3,2,1,0:T(8,128)S(1)} %get-tuple-element.41), channel_id=1, source_target_pairs={{0,15},{1,2},{2,1},{3,4},{4,3},{5,6},{6,5},{7,8},{8,7},{9,10},{10,... | collective-permute-start | bytes 786440 | tf_op jit(solution)/shard_map/ppermute | solution.py:334
  19.7 1.2 %copy-start.2 = (f32[2,2,256,256]{3,2,1,0:T(8,128)S(1)}, f32[2,2,256,256]{3,2,1,0:T(8,128)}, u32[]{:S(2)}) copy-start(f32[2,2,256,256]{3,2,1,0:T(8,128)} %probe.1) | copy-start | bytes 3145732
  20.9 1.2 %copy-start.3 = (f32[4,1,256,256]{3,2,1,0:T(8,128)S(1)}, f32[4,1,256,256]{3,2,1,0:T(8,128)}, u32[]{:S(2)}) copy-start(f32[4,1,256,256]{3,2,1,0:T(8,128)} %amp.1) | copy-start | bytes 3145732
  22.1 1.0 copy-start.5
  33.6 7.2 %collective-permute-start.8 = (f32[16,5,8,256]{3,2,1,0:T(8,128)S(1)}, f32[16,5,8,256]{3,2,1,0:T(8,128)S(1)}, u32[]{:S(2)}, u32[]{:S(2)}) collective-permute-start(f32[16,5,8,256]{3,2,1,0:T(8,128)S(1)} %get-tuple-element.54), channel_id=1, source_target_pairs={{0,1},{1,0},{2,3},{3,2},{4,5},{5,4},{6,7},{7,6},{8,9},{9,8},{10,11... | collective-permute-start | bytes 1966088 | tf_op jit(solution)/shard_map/ppermute | solution.py:341
  41.8 21.7 %all-to-all-start = ((f32[16,5,8,256]{3,2,1,0:T(8,128)}), f32[16,5,8,256]{3,2,1,0:T(8,128)S(1)}, u32[]{:S(2)}, u32[]{:S(2)}) async-start(f32[16,5,8,256]{3,2,1,0:T(8,128)} %add.91), calls=%async_computation | async-start | bytes 1310720 | tf_op jit(solution)/shard_map/all_to_all | solution.py:342
  47.3 2.2 %collective-permute-start.6 = (f32[2,512,128]{2,1,0:T(8,128)S(1)}, f32[2,512,128]{2,1,0:T(8,128)S(1)}, u32[]{:S(2)}, u32[]{:S(2)}) collective-permute-start(f32[2,512,128]{2,1,0:T(8,128)S(1)} %get-tuple-element.50), channel_id=1, source_target_pairs={{0,1},{1,0},{2,3},{3,2},{4,5},{5,4},{6,7},{7,6},{8,9},{9,8},{10,11... | collective-permute-start | bytes 1572872 | tf_op jit(solution)/shard_map/ppermute | solution.py:340
  47.8 15.0 %collective-permute-start.7 = (f32[2,512,128]{2,1,0:T(8,128)S(1)}, f32[2,512,128]{2,1,0:T(8,128)S(1)}, u32[]{:S(2)}, u32[]{:S(2)}) collective-permute-start(f32[2,512,128]{2,1,0:T(8,128)S(1)} %get-tuple-element.51), channel_id=1, source_target_pairs={{0,15},{1,2},{2,1},{3,4},{4,3},{5,6},{6,5},{7,8},{8,7},{9,10},{10,... | collective-permute-start | bytes 1572872 | tf_op jit(solution)/shard_map/ppermute | solution.py:339
  63.6 12.5 %collective-permute-start.11 = (f32[5,8,256]{2,1,0:T(8,128)S(1)}, f32[5,8,256]{2,1,0:T(8,128)S(1)}, u32[]{:S(2)}, u32[]{:S(2)}) collective-permute-start(f32[5,8,256]{2,1,0:T(8,128)S(1)} %fusion), channel_id=1, source_target_pairs={{0,192},{32,224},{64,128},{96,160},{128,64},{160,96},{192,0},{224,... | collective-permute-start | bytes 122888 | tf_op jit(solution)/shard_map/ppermute | solution.py:348
  69.7 7.0 %collective-permute-start.10 = (f32[5,8,256]{2,1,0:T(8,128)S(1)}, f32[5,8,256]{2,1,0:T(8,128)S(1)}, u32[]{:S(2)}, u32[]{:S(2)}) collective-permute-start(f32[5,8,256]{2,1,0:T(8,128)S(1)} %fusion), channel_id=1, source_target_pairs={{0,128},{32,160},{64,192},{96,224},{128,0},{160,32},{192,64},{224,... | collective-permute-start | bytes 122888 | tf_op jit(solution)/shard_map/ppermute | solution.py:348
  70.6 6.0 %collective-permute-start.9 = (f32[5,8,256]{2,1,0:T(8,128)S(1)}, f32[5,8,256]{2,1,0:T(8,128)S(1)}, u32[]{:S(2)}, u32[]{:S(2)}) collective-permute-start(f32[5,8,256]{2,1,0:T(8,128)S(1)} %fusion), channel_id=1, source_target_pairs={{0,64},{32,96},{64,0},{96,32},{128,192},{160,224},{192,128},{224,1... | collective-permute-start | bytes 122888 | tf_op jit(solution)/shard_map/ppermute | solution.py:348
  71.8 8.9 %collective-permute-start.13 = (f32[2,128,256]{2,1,0:T(8,128)S(1)}, f32[2,128,256]{2,1,0:T(8,128)S(1)}, u32[]{:S(2)}, u32[]{:S(2)}) collective-permute-start(f32[2,128,256]{2,1,0:T(8,128)S(1)} %get-tuple-element.58), channel_id=1, source_target_pairs={{0,16},{16,0},{1,17},{17,1},{2,18},{18,2},{3,19},{19,3},{4,20},{20... | collective-permute-start | bytes 786440 | tf_op jit(solution)/shard_map/ppermute | solution.py:347
  73.0 8.1 %collective-permute-start.14 = (f32[2,128,256]{2,1,0:T(8,128)S(1)}, f32[2,128,256]{2,1,0:T(8,128)S(1)}, u32[]{:S(2)}, u32[]{:S(2)}) collective-permute-start(f32[2,128,256]{2,1,0:T(8,128)S(1)} %get-tuple-element.59), channel_id=1, source_target_pairs={{0,240},{16,32},{32,16},{48,64},{64,48},{80,96},{96,80},{112,128},... | collective-permute-start | bytes 786440 | tf_op jit(solution)/shard_map/ppermute | solution.py:346
  76.7 4.0 %collective-permute-start.12 = (f32[5,8,256]{2,1,0:T(8,128)S(1)}, f32[5,8,256]{2,1,0:T(8,128)S(1)}, u32[]{:S(2)}, u32[]{:S(2)}) collective-permute-start(f32[5,8,256]{2,1,0:T(8,128)S(1)} %add_add_fusion), channel_id=1, source_target_pairs={{0,32},{32,0},{64,96},{96,64},{128,160},{160,128},{192,224},{224,1... | collective-permute-start | bytes 122888 | tf_op jit(solution)/shard_map/ppermute | solution.py:350
  100.9 5.0 %collective-permute-start.15 = (f32[16,4,8,256]{3,2,1,0:T(8,128)S(1)}, f32[16,4,8,256]{3,2,1,0:T(8,128)S(1)}, u32[]{:S(2)}, u32[]{:S(2)}) collective-permute-start(f32[16,4,8,256]{3,2,1,0:T(8,128)S(1)} %all_to_all.10.own), channel_id=1, source_target_pairs={{0,1},{1,0},{2,3},{3,2},{4,5},{5,4},{6,7},{7,6},{8,9},{9,8},{10,11... | collective-permute-start | bytes 1572872 | tf_op jit(solution)/shard_map/ppermute | solution.py:358

commit v9 on v8

--- a/solution.py
+++ b/solution.py
@@ -16,6 +16,7 @@
 POS = 4
 MODES = 2
 CH = 32
+FOLD_FLOPS = 4_000_000_000
 BF = jnp.bfloat16
 F32 = jnp.float32
 
@@ -191,6 +192,7 @@
             pltpu.VMEM((W, W), F32),
             pltpu.VMEM((2 * MODES, W, W), F32),
         ],
+        cost_estimate=cost([((8 << 20,), jnp.int8)], 4 * MODES * POS * 2 * (2 * W) ** 2 * W),
         compiler_params=pltpu.CompilerParams(vmem_limit_bytes=20 << 20),
     )(offsets, flags, *border, *staged)
 
@@ -201,14 +203,20 @@
 FAR = [(i, (i + 1) % 16 if i % 2 else (i - 1) % 16) for i in range(16)]
 
 
-def small_call(body, shapes, in_specs, scratch=()):
+def cost(shapes, flops=0):
+    size = sum(2 * math.prod(shape) * jnp.dtype(dtype).itemsize for shape, dtype in shapes)
+    return pl.CostEstimate(flops=flops, bytes_accessed=size, transcendentals=0)
+
+
+def small_call(body, shapes, in_specs, scratch=(), limit=6 << 20, flops=0):
     return pl.pallas_call(
         body,
         out_shape=tuple(jax.ShapeDtypeStruct(shape, dtype) for shape, dtype in shapes),
         in_specs=in_specs,
         out_specs=(VMEM,) * len(shapes),
         scratch_shapes=scratch,
-        compiler_params=pltpu.CompilerParams(vmem_limit_bytes=6 << 20),
+        cost_estimate=cost(shapes, flops),
+        compiler_params=pltpu.CompilerParams(vmem_limit_bytes=limit),
     )
 
 
@@ -231,14 +239,15 @@
         [((2, HALF, W), F32)] * 2 + [((2, W, HALF), F32)] * 2,
         [SMEM, HBM],
         [pltpu.SemaphoreType.DMA((4,))],
+        125 << 19,
     )(flags, tile)
 
 
-def stage(offsets, tile, probe, amplitude, after):
+def stage(offsets, flags, tile, probe, amplitude):
     fwd, bwd = (jnp.asarray(matrix) for matrix in dft_matrices())
     arrays = (tile, probe, amplitude, fwd, bwd)
 
-    def run(offs, tile, probe, amp, fwd, bwd, after, offs_s, tile_v, probe_v, amp_v, power, inverse, fwd_v, bwd_v, sems):
+    def run(offs, flags, tile, probe, amp, fwd, bwd, offs_s, own, tile_v, probe_v, amp_v, power, inverse, fwd_v, bwd_v, sems):
         pairs = ((probe, probe_v), (tile, tile_v), (fwd, fwd_v), (bwd, bwd_v), (amp, amp_v))
         copies = [pltpu.make_async_copy(a, b, sems.at[n]) for n, (a, b) in enumerate(pairs)]
         for copy in copies:
@@ -255,21 +264,24 @@
                 total += probe_v[k, 0, rows, :] * probe_v[k, 0, rows, :] + probe_v[k, 1, rows, :] * probe_v[k, 1, rows, :]
             power[rows, :] = total
             largest = jnp.maximum(largest, total)
+        for n in range(2 * MODES):
+            own[n] = probe_v[n // 2, n % 2, pl.ds(pl.multiple_of(flags[2], 8), 8), :]
         scale = 1.0 / (jnp.max(largest, axis=(0, 1), keepdims=True) + 1e-06)
         inverse[...] = jnp.broadcast_to(scale, inverse.shape)
         for copy in copies[1:]:
             copy.wait()
 
-    shapes = [(a.shape, a.dtype) for a in arrays[:3]] + [((W, W), F32), ((8, HALF), F32)]
+    shapes = [((2 * MODES, 8, W), F32)] + [(a.shape, a.dtype) for a in arrays[:3]] + [((W, W), F32), ((8, HALF), F32)]
     shapes += [(a.shape, a.dtype) for a in arrays[3:]]
     return pl.pallas_call(
         run,
         out_shape=[jax.ShapeDtypeStruct(offsets.shape, jnp.int32)] + [jax.ShapeDtypeStruct(*a) for a in shapes],
-        in_specs=[SMEM] + [HBM] * 5 + [pl.BlockSpec(memory_space=pl.ANY)],
-        out_specs=[SMEM] + [VMEM] * 7,
+        in_specs=[SMEM, SMEM] + [HBM] * 5,
+        out_specs=[SMEM] + [VMEM] * 8,
         scratch_shapes=[pltpu.SemaphoreType.DMA((5,))],
+        cost_estimate=cost(shapes),
         compiler_params=pltpu.CompilerParams(vmem_limit_bytes=6 << 20),
-    )(offsets, *arrays, after)
+    )(offsets, flags, *arrays)
 
 
 def cut_ends(flags, rows_in, rows_out):
@@ -294,7 +306,8 @@
                     for dst, at in ((back_in, spot(1 - xl, W + HALF)), (back_out, spot(xl, W + HALF)), (center, pl.ds(HALF, W))):
                         dst[:, :, cols] = middle[:, at, cols] + extra[:, at, :]
 
-    return small_call(run, [((2, HALF, W), F32)] * 2 + [((2, W, W), F32)], [SMEM] + [VMEM] * 3)(flags, middle, from_in, from_out)
+    shapes = [((2, HALF, W), F32)] * 2 + [((2, W, W), F32)]
+    return small_call(run, shapes, [SMEM] + [VMEM] * 3, flops=FOLD_FLOPS)(flags, middle, from_in, from_out)
 
 
 def finish(flags, center, from_in, from_out):
@@ -321,19 +334,20 @@
 def body(object_field, probe_field, amplitude, offsets):
     group = ("xh", "xl", "y")
     co = lax.axis_index("co")
-    flags = jnp.stack([co, lax.axis_index("xl")])
-    block = (co * 16 + lax.axis_index(group)) * 8
+    flags = jnp.stack([co, lax.axis_index("xl"), (co * 16 + lax.axis_index(group)) * 8])
     offs = offsets.transpose(1, 2, 0).reshape(2, POS)
-    object_field, flags, block = lax.optimization_barrier((object_field, flags, block))
+    object_field, flags = lax.optimization_barrier((object_field, flags))
     rows_in, rows_out, cols_in, cols_out = cut_borders(flags, object_field)
     rows_out = lax.ppermute(rows_out, GX, FAR)
     rows_in = lax.ppermute(rows_in, "xl", NEAR)
     cols_out = lax.ppermute(cols_out, GY, FAR)
     cols_in = lax.ppermute(cols_in, "co", NEAR)
+    staged = stage(offs, flags, object_field, probe_field, amplitude)
+    rows_in, rows_out, staged = lax.optimization_barrier((rows_in, rows_out, staged))
+    offs, local, *staged = staged
     ends_in, ends_out = cut_ends(flags, rows_in, rows_out)
     ends_out = lax.ppermute(ends_out, GY, FAR)
     ends_in = lax.ppermute(ends_in, "co", NEAR)
-    offs, *staged = stage(offs, object_field, probe_field, amplitude, cols_in)
     border = (rows_in, rows_out, cols_in, cols_out, ends_in, ends_out)
     mine, other, back_in, back_out, middle = correct(offs, flags, border, staged)
     from_out = lax.ppermute(back_out, GY, FAR)
@@ -349,8 +363,6 @@
     part = (part + peers[0]) + (peers[1] + peers[2])
     part = part + lax.ppermute(part, "z", [(i, i ^ 1) for i in range(8)])
     part, from_in, from_out = lax.optimization_barrier((part, from_in, from_out))
-    planes = probe_field.reshape(2 * MODES, W, W)
-    local = lax.dynamic_slice_in_dim(planes, block, 8, 1)
     weight = part[2 * MODES]
     local = local + (part[: 2 * MODES] - local * weight) / (weight + 1e-05)
     gathered = lax.all_to_all(jnp.broadcast_to(local[None], (16,) + local.shape), group, 0, 0, tiled=True)

time: 108 us -> 104 us (0.963)
  starting transfers between devices: 43.4 us -> 35.3 us
  waiting for transfers between devices: 22.7 us -> 29.6 us
  blocking collectives: 18.9 us -> 13.3 us
  Pallas kernels: 15.3 us -> 17.4 us
    ppermute x1, waiting for transfers between devices: 13.2 us -> 1.16 us  [body(): from_out = lax.ppermute(back_out, GY, FAR)]
    all_to_all x1, waiting for transfers between devices: 0.01 us -> 11.6 us  [body(): pieces = lax.all_to_all(part, group, 0, 0, tiled=True)]
    all_to_all x1, blocking collectives: 18.9 us -> 13.3 us  [body(): lax.all_to_all(jnp.broadcast_to(local[None], (16,) + local.shape), group,...]
    ppermute x1, waiting for transfers between devices: 0.01 us -> 4.63 us  [body(): ends_out = lax.ppermute(ends_out, GY, FAR)]
    ppermute x1, waiting for transfers between devices: 0.01 us -> 2.99 us  [body(): from_in = lax.ppermute(back_in, 'xl', NEAR)]
    ppermute x1, waiting for transfers between devices: 3.24 us -> 5.97 us  [body(): part = part + lax.ppermute(part, 'z', [(i, i ^ 1) for i in range(8)])]
    ppermute x3, starting transfers between devices: 8.29 us -> 5.74 us  [body(): lax.ppermute(part, 'z', [(i, i ^ step) for i in range(8)])]
    ppermute x1, starting transfers between devices: 1.98 us -> 4.49 us  [body(): ends_in = lax.ppermute(ends_in, 'co', NEAR)]
  transfers between devices with their start and end apart: 17 -> 17, of which waited for: 8 -> 9; matrix products, arithmetic and copies ran while one was open for 0% -> 1% of each run, Pallas kernels for 4% -> 4%
where the time goes in v9:
time: 104 us
  starting transfers between devices  35.3 us (34%)
  waiting for transfers between devices  29.6 us (28%)
  Pallas kernels  17.4 us (17%)
  blocking collectives  13.3 us (13%)
  local copies, waits for them, and re-layouts  4.59 us (4%)
  other arithmetic  2.73 us (3%)
    all_to_all x1, blocking collectives, body(): lax.all_to_all(jnp.broadcast_to(local[None], (16,) + local.shape), group,...  13.3 us
    all_to_all x1, waiting for transfers between devices, body(): pieces = lax.all_to_all(part, group, 0, 0, tiled=True)  11.6 us
    pallas_call x1, Pallas kernels, correct(): pl.pallas_call(kernel, out_shape=(part, part, strip, strip, jax.ShapeDtyp...  8.68 us
    ppermute x1, waiting for transfers between devices, body(): part = part + lax.ppermute(part, 'z', [(i, i ^ 1) for i in range(8)])  5.97 us
    ppermute x3, starting transfers between devices, body(): lax.ppermute(part, 'z', [(i, i ^ step) for i in range(8)])  5.74 us
    ppermute x1, starting transfers between devices, body(): rows_out = lax.ppermute(rows_out, GX, FAR)  5.55 us
    all_to_all x1, starting transfers between devices, body(): pieces = lax.all_to_all(part, group, 0, 0, tiled=True)  5.18 us
    ppermute x1, waiting for transfers between devices, body(): ends_out = lax.ppermute(ends_out, GY, FAR)  4.63 us
  transfers between devices with their start and end apart: 17, of which 9 were waited for; matrix products, arithmetic and copies ran while one was open for 1% of the time, Pallas kernels for 4%

profile of v9, /device:TPU:1, one launch (start us, length us, event | category | flops | bytes accessed | tf_op | source)
XLA Modules:
  0.0 103.7 jit_solution(8569684040170318445)
XLA Ops:
  0.6 0.0 copy-start
  0.7 0.7 pad_add_fusion.flags
  1.3 2.9 %shard_map.77 = (f32[2,128,256]{2,1,0:T(8,128)}, f32[2,128,256]{2,1,0:T(8,128)}, f32[2,256,128]{2,1,0:T(8,128)}, f32[2,256,128]{2,1,0:T(8,128)}) custom-call(s32[3]{0:T(128)} %pad_add_fusion.flags, f32[2,256,256]{2,1,0:T(8,128)} %tile.1), custom_call_target="tpu_custom_call" | custom-call | bytes 2097152 | tf_op jit(solution)/shard_map/pallas_call | solution.py:237
  4.2 2.1 %collective-permute-start = (f32[2,128,256]{2,1,0:T(8,128)}, f32[2,128,256]{2,1,0:T(8,128)S(1)}, u32[]{:S(2)}, u32[]{:S(2)}) collective-permute-start(f32[2,128,256]{2,1,0:T(8,128)} %get-tuple-element.46), channel_id=1, source_target_pairs={{0,16},{16,0},{1,17},{17,1},{2,18},{18,2},{3,19},{19,3},{4,20},{20... | collective-permute-start | bytes 786440 | tf_op jit(solution)/shard_map/ppermute | solution.py:342
  6.3 5.5 %collective-permute-start.1 = (f32[2,128,256]{2,1,0:T(8,128)}, f32[2,128,256]{2,1,0:T(8,128)S(1)}, u32[]{:S(2)}, u32[]{:S(2)}) collective-permute-start(f32[2,128,256]{2,1,0:T(8,128)} %get-tuple-element.47), channel_id=1, source_target_pairs={{0,240},{16,32},{32,16},{48,64},{64,48},{80,96},{96,80},{112,128},... | collective-permute-start | bytes 786440 | tf_op jit(solution)/shard_map/ppermute | solution.py:341
  11.9 1.2 %collective-permute-start.2 = (f32[2,256,128]{2,1,0:T(8,128)}, f32[2,256,128]{2,1,0:T(8,128)S(1)}, u32[]{:S(2)}, u32[]{:S(2)}) collective-permute-start(f32[2,256,128]{2,1,0:T(8,128)} %get-tuple-element.60), channel_id=1, source_target_pairs={{0,1},{1,0},{2,3},{3,2},{4,5},{5,4},{6,7},{7,6},{8,9},{9,8},{10,11... | collective-permute-start | bytes 786440 | tf_op jit(solution)/shard_map/ppermute | solution.py:344
  13.1 1.2 %collective-permute-start.3 = (f32[2,256,128]{2,1,0:T(8,128)}, f32[2,256,128]{2,1,0:T(8,128)S(1)}, u32[]{:S(2)}, u32[]{:S(2)}) collective-permute-start(f32[2,256,128]{2,1,0:T(8,128)} %get-tuple-element.61), channel_id=1, source_target_pairs={{0,15},{1,2},{2,1},{3,4},{4,3},{5,6},{6,5},{7,8},{8,7},{9,10},{10,... | collective-permute-start | bytes 786440 | tf_op jit(solution)/shard_map/ppermute | solution.py:343
  14.3 1.2 %copy-done.1 = f32[2,2,256,256]{3,2,1,0:T(8,128)S(1)} copy-done((f32[2,2,256,256]{3,2,1,0:T(8,128)S(1)}, f32[2,2,256,256]{3,2,1,0:T(8,128)}, u32[]{:S(2)}) %copy-start.1) | copy-done | bytes 1048600
  15.5 1.2 %copy-done.2 = f32[4,1,256,256]{3,2,1,0:T(8,128)S(1)} copy-done((f32[4,1,256,256]{3,2,1,0:T(8,128)S(1)}, f32[4,1,256,256]{3,2,1,0:T(8,128)}, u32[]{:S(2)}) %copy-start.2) | copy-done | bytes 1048600
  16.7 1.0 %copy-done.3 = bf16[512,512]{1,0:T(8,128)(2,1)S(1)} copy-done((bf16[512,512]{1,0:T(8,128)(2,1)S(1)}, bf16[512,512]{1,0:T(8,128)(2,1)}, u32[]{:S(2)}) %copy-start.3) | copy-done | bytes 524312
  17.8 1.0 %copy-done.4 = bf16[512,512]{1,0:T(8,128)(2,1)S(1)} copy-done((bf16[512,512]{1,0:T(8,128)(2,1)S(1)}, bf16[512,512]{1,0:T(8,128)(2,1)}, u32[]{:S(2)}) %copy-start.4) | copy-done | bytes 524312
  18.8 1.7 %shard_map.78 = (s32[2,4]{1,0:T(2,128)S(1)}, f32[4,8,256]{2,1,0:T(8,128)S(1)}, f32[2,256,256]{2,1,0:T(8,128)S(1)}, f32[2,2,256,256]{3,2,1,0:T(8,128)S(1)}, f32[4...) custom-call(s32[2,4]{1,0:T(2,128)S(1)} %bitcast.12, ...), custom_call_target="tpu_custom_call" | custom-call | bytes 7938048 | tf_op jit(solution)/shard_map/pallas_call | solution.py:276
  20.5 0.0 collective-permute-done.rows_in
  20.5 0.0 collective-permute-done.1.rows_out
  20.5 0.6 shard_map.79
  21.1 4.5 %collective-permute-start.4 = (f32[2,2,128,128]{3,2,1,0:T(8,128)S(1)}, f32[2,2,128,128]{3,2,1,0:T(8,128)S(1)}, u32[]{:S(2)}, u32[]{:S(2)}) collective-permute-start(f32[2,2,128,128]{3,2,1,0:T(8,128)S(1)} %get-tuple-element.62), channel_id=1, source_target_pairs={{0,1},{1,0},{2,3},{3,2},{4,5},{5,4},{6,7},{7,6},{8,9},{9,8},{10,11... | collective-permute-start | bytes 786440 | tf_op jit(solution)/shard_map/ppermute | solution.py:350
  25.6 0.0 collective-permute-start.5
  25.6 0.0 collective-permute-done.2.cols_in
  25.6 0.0 collective-permute-done.3.cols_out
  25.6 1.1 %collective-permute-done.4.ends_in = f32[2,2,128,128]{3,2,1,0:T(8,128)S(1)} collective-permute-done((f32[2,2,128,128]{3,2,1,0:T(8,128)S(1)}, f32[2,2,128,128]{3,2,1,0:T(8,128)S(1)}, u32[]{:S(2)}, u32[]{:S(2)}) %collective-permute-start.4) | collective-permute-done | bytes 262176 | tf_op jit(solution)/shard_map/ppermute | solution.py:350
  26.8 4.6 %collective-permute-done.5.ends_out = f32[2,2,128,128]{3,2,1,0:T(8,128)S(1)} collective-permute-done((f32[2,2,128,128]{3,2,1,0:T(8,128)S(1)}, f32[2,2,128,128]{3,2,1,0:T(8,128)S(1)}, u32[]{:S(2)}, u32[]{:S(2)}) %collective-permute-start.5) | collective-permute-done | bytes 262176 | tf_op jit(solution)/shard_map/ppermute | solution.py:349
  31.4 8.7 %shard_map.80 = (f32[16,5,8,256]{3,2,1,0:T(8,128)S(1)}, f32[16,5,8,256]{3,2,1,0:T(8,128)S(1)}, f32[2,512,128]{2,1,0:T(8,128)S(1)}, f32[2,512,128]{2,1,0:T(8,128)S(1)}, f32[2,512,256]{2,1,0:T(8,128)S(1)}) custom-call(s32[2,4]{1,0:T(2,128)S(1)} %get-tuple-element.57.offs, s32[3]{0:T(128)S(1)} %copy-done.5, f32[2,128,256]{2,1,0:T(8,128)S(1)} %collective-permute-done.rows_in, ...), custom_call_target="tpu_custom_call" | custom-call | flops 4294967296 | bytes 16777216 | tf_op jit(solution)/shard_map/pallas_call | solution.py:180
  40.1 3.8 %collective-permute-start.8 = (f32[16,5,8,256]{3,2,1,0:T(8,128)S(1)}, f32[16,5,8,256]{3,2,1,0:T(8,128)S(1)}, u32[]{:S(2)}, u32[]{:S(2)}) collective-permute-start(f32[16,5,8,256]{3,2,1,0:T(8,128)S(1)} %get-tuple-element.76), channel_id=1, source_target_pairs={{0,1},{1,0},{2,3},{3,2},{4,5},{5,4},{6,7},{7,6},{8,9},{9,8},{10,11... | collective-permute-start | bytes 1966088 | tf_op jit(solution)/shard_map/ppermute | solution.py:355
  43.9 0.1 collective-permute-start.6
  44.0 0.0 collective-permute-start.7
  44.0 1.6 %collective-permute-done.8 = f32[16,5,8,256]{3,2,1,0:T(8,128)S(1)} collective-permute-done((f32[16,5,8,256]{3,2,1,0:T(8,128)S(1)}, f32[16,5,8,256]{3,2,1,0:T(8,128)S(1)}, u32[]{:S(2)}, u32[]{:S(2)}) %collective-permute-start.8) | collective-permute-done | bytes 655392 | tf_op jit(solution)/shard_map/ppermute | solution.py:355
  45.6 0.9 add.88
  46.5 5.2 %all-to-all-start = ((f32[16,5,8,256]{3,2,1,0:T(8,128)}), f32[16,5,8,256]{3,2,1,0:T(8,128)}, u32[]{:S(2)}, u32[]{:S(2)}) async-start(f32[16,5,8,256]{3,2,1,0:T(8,128)} %add.88), calls=%async_computation | async-start | bytes 1310720 | tf_op jit(solution)/shard_map/all_to_all | solution.py:356
  51.7 0.0 collective-permute-done.6.from_in
  51.7 1.2 %collective-permute-done.7.from_out = f32[2,512,128]{2,1,0:T(8,128)S(1)} collective-permute-done((f32[2,512,128]{2,1,0:T(8,128)S(1)}, f32[2,512,128]{2,1,0:T(8,128)S(1)}, u32[]{:S(2)}, u32[]{:S(2)}) %collective-permute-start.7) | collective-permute-done | bytes 524320 | tf_op jit(solution)/shard_map/ppermute | solution.py:353
  52.9 0.7 shard_map.81
  53.6 11.6 %all-to-all-done = f32[16,5,8,256]{3,2,1,0:T(8,128)} async-done(((f32[16,5,8,256]{3,2,1,0:T(8,128)}), f32[16,5,8,256]{3,2,1,0:T(8,128)}, u32[]{:S(2)}, u32[]{:S(2)}) %all-to-all-start) | async-done | bytes 655392 | tf_op jit(solution)/shard_map/all_to_all | solution.py:356
  65.2 1.1 %fusion = f32[5,8,256]{2,1,0:T(8,128)S(1)} fusion(f32[16,5,8,256]{3,2,1,0:T(8,128)} %all-to-all-done), kind=kLoop, calls=%fused_computation.1 | loop fusion | flops 153600 | bytes 696320 | tf_op jit(solution)/shard_map/add | solution.py:357
  66.3 1.0 collective-permute-start.11
  67.3 1.0 collective-permute-start.10
  68.3 3.7 %collective-permute-start.9 = (f32[5,8,256]{2,1,0:T(8,128)S(1)}, f32[5,8,256]{2,1,0:T(8,128)S(1)}, u32[]{:S(2)}, u32[]{:S(2)}) collective-permute-start(f32[5,8,256]{2,1,0:T(8,128)S(1)} %fusion), channel_id=1, source_target_pairs={{0,64},{32,96},{64,0},{96,32},{128,192},{160,224},{192,128},{224,1... | collective-permute-start | bytes 122888 | tf_op jit(solution)/shard_map/ppermute | solution.py:362
  72.1 1.7 %collective-permute-start.14 = (f32[2,128,256]{2,1,0:T(8,128)S(1)}, f32[2,128,256]{2,1,0:T(8,128)S(1)}, u32[]{:S(2)}, u32[]{:S(2)}) collective-permute-start(f32[2,128,256]{2,1,0:T(8,128)S(1)} %get-tuple-element.81), channel_id=1, source_target_pairs={{0,240},{16,32},{32,16},{48,64},{64,48},{80,96},{96,80},{112,128},... | collective-permute-start | bytes 786440 | tf_op jit(solution)/shard_map/ppermute | solution.py:360
  73.7 0.0 collective-permute-done.11
  73.7 0.3 collective-permute-done.10
  74.1 1.0 collective-permute-start.12
  75.0 6.0 %collective-permute-done.12 = f32[5,8,256]{2,1,0:T(8,128)S(1)} collective-permute-done((f32[5,8,256]{2,1,0:T(8,128)S(1)}, f32[5,8,256]{2,1,0:T(8,128)S(1)}, u32[]{:S(2)}, u32[]{:S(2)}) %collective-permute-start.12) | collective-permute-done | bytes 40992 | tf_op jit(solution)/shard_map/ppermute | solution.py:364
  81.0 3.0 %collective-permute-done.13.from_in = f32[2,128,256]{2,1,0:T(8,128)S(1)} collective-permute-done((f32[2,128,256]{2,1,0:T(8,128)S(1)}, f32[2,128,256]{2,1,0:T(8,128)S(1)}, u32[]{:S(2)}, u32[]{:S(2)}) %collective-permute-start.13) | collective-permute-done | bytes 262176 | tf_op jit(solution)/shard_map/ppermute | solution.py:361
  84.0 0.0 collective-permute-done.14.from_out
  84.1 13.3 %all_to_all.10.own = f32[16,4,8,256]{3,2,1,0:T(8,128)S(1)} all-to-all(f32[16,4,8,256]{3,2,1,0:T(8,128)S(1)} %broadcast_in_dim.2), channel_id=1, replica_groups=mesh['z'=8,'xl'=2,'xh'=2,'y'=4,'co'=2] {'xh','xl','y'}, dimensions={0} | all-to-all | bytes 1048576 | tf_op jit(solution)/shard_map/all_to_all | solution.py:368
  97.3 3.3 %collective-permute-start.15 = (f32[16,4,8,256]{3,2,1,0:T(8,128)S(1)}, f32[16,4,8,256]{3,2,1,0:T(8,128)S(1)}, u32[]{:S(2)}, u32[]{:S(2)}) collective-permute-start(f32[16,4,8,256]{3,2,1,0:T(8,128)S(1)} %all_to_all.10.own), channel_id=1, source_target_pairs={{0,1},{1,0},{2,3},{3,2},{4,5},{5,4},{6,7},{7,6},{8,9},{9,8},{10,11... | collective-permute-start | bytes 1572872 | tf_op jit(solution)/shard_map/ppermute | solution.py:370
  100.6 1.4 %shard_map.82 = f32[2,256,256]{2,1,0:T(8,128)} custom-call(s32[3]{0:T(128)S(1)} %copy-done.5, f32[2,256,256]{2,1,0:T(8,128)S(1)} %get-tuple-element.74.center, f32[2,128,256]{2,1,0:T(8,128)S(1)} %collective-permute-done.13.from_in, f32[2,128,256]{2,1,0:T(8,128)S(1)} %collective-permute-done.14.from_out), custom_call_target="tpu_custom_call" | custom-call | bytes 1048576 | tf_op jit(solution)/shard_map/pallas_call | solution.py:319
  102.0 0.1 collective-permute-done.15.swapped
  102.1 1.6 %shard_map.83 = f32[2,2,256,256]{3,2,1,0:T(8,128)} custom-call(s32[3]{0:T(128)S(1)} %copy-done.5, f32[16,4,8,256]{3,2,1,0:T(8,128)S(1)} %all_to_all.10.own, f32[16,4,8,256]{3,2,1,0:T(8,128)S(1)} %collective-permute-done.15.swapped), custom_call_target="tpu_custom_call" | custom-call | bytes 2097152 | tf_op jit(solution)/shard_map/pallas_call | solution.py:331
  (16 shorter events, 0.1 us)
Async XLA Ops:
  0.6 13.7 %copy-start = (f32[2,256,256]{2,1,0:T(8,128)S(1)}, f32[2,256,256]{2,1,0:T(8,128)}, u32[]{:S(2)}) copy-start(f32[2,256,256]{2,1,0:T(8,128)} %tile.1) | copy-start | bytes 1572868
  4.2 16.3 %collective-permute-start = (f32[2,128,256]{2,1,0:T(8,128)}, f32[2,128,256]{2,1,0:T(8,128)S(1)}, u32[]{:S(2)}, u32[]{:S(2)}) collective-permute-start(f32[2,128,256]{2,1,0:T(8,128)} %get-tuple-element.46), channel_id=1, source_target_pairs={{0,16},{16,0},{1,17},{17,1},{2,18},{18,2},{3,19},{19,3},{4,20},{20... | collective-permute-start | bytes 786440 | tf_op jit(solution)/shard_map/ppermute | solution.py:342
  6.3 14.2 %collective-permute-start.1 = (f32[2,128,256]{2,1,0:T(8,128)}, f32[2,128,256]{2,1,0:T(8,128)S(1)}, u32[]{:S(2)}, u32[]{:S(2)}) collective-permute-start(f32[2,128,256]{2,1,0:T(8,128)} %get-tuple-element.47), channel_id=1, source_target_pairs={{0,240},{16,32},{32,16},{48,64},{64,48},{80,96},{96,80},{112,128},... | collective-permute-start | bytes 786440 | tf_op jit(solution)/shard_map/ppermute | solution.py:341
  11.9 13.7 %collective-permute-start.2 = (f32[2,256,128]{2,1,0:T(8,128)}, f32[2,256,128]{2,1,0:T(8,128)S(1)}, u32[]{:S(2)}, u32[]{:S(2)}) collective-permute-start(f32[2,256,128]{2,1,0:T(8,128)} %get-tuple-element.60), channel_id=1, source_target_pairs={{0,1},{1,0},{2,3},{3,2},{4,5},{5,4},{6,7},{7,6},{8,9},{9,8},{10,11... | collective-permute-start | bytes 786440 | tf_op jit(solution)/shard_map/ppermute | solution.py:344
  13.1 1.2 %copy-start.5 = (s32[3]{0:T(128)S(1)}, s32[3]{0:T(128)}, u32[]{:S(2)}) copy-start(s32[3]{0:T(128)} %pad_add_fusion.flags) | copy-start | bytes 40
  13.1 1.2 %copy-start.6 = (s32[4,1,2]{0,2,1:T(2,128)S(1)}, s32[4,1,2]{0,2,1:T(2,128)}, u32[]{:S(2)}) copy-start(s32[4,1,2]{0,2,1:T(2,128)} %param.9) | copy-start | bytes 100
  13.1 12.5 %collective-permute-start.3 = (f32[2,256,128]{2,1,0:T(8,128)}, f32[2,256,128]{2,1,0:T(8,128)S(1)}, u32[]{:S(2)}, u32[]{:S(2)}) collective-permute-start(f32[2,256,128]{2,1,0:T(8,128)} %get-tuple-element.61), channel_id=1, source_target_pairs={{0,15},{1,2},{2,1},{3,4},{4,3},{5,6},{6,5},{7,8},{8,7},{9,10},{10,... | collective-permute-start | bytes 786440 | tf_op jit(solution)/shard_map/ppermute | solution.py:343
  14.3 1.2 %copy-start.1 = (f32[2,2,256,256]{3,2,1,0:T(8,128)S(1)}, f32[2,2,256,256]{3,2,1,0:T(8,128)}, u32[]{:S(2)}) copy-start(f32[2,2,256,256]{3,2,1,0:T(8,128)} %probe.1) | copy-start | bytes 3145732
  15.5 1.2 %copy-start.2 = (f32[4,1,256,256]{3,2,1,0:T(8,128)S(1)}, f32[4,1,256,256]{3,2,1,0:T(8,128)}, u32[]{:S(2)}) copy-start(f32[4,1,256,256]{3,2,1,0:T(8,128)} %amp.1) | copy-start | bytes 3145732
  16.7 1.0 %copy-start.3 = (bf16[512,512]{1,0:T(8,128)(2,1)S(1)}, bf16[512,512]{1,0:T(8,128)(2,1)}, u32[]{:S(2)}) copy-start(bf16[512,512]{1,0:T(8,128)(2,1)} %constant.28.clone.bwd) | copy-start | bytes 1572868
  17.8 1.0 %copy-start.4 = (bf16[512,512]{1,0:T(8,128)(2,1)S(1)}, bf16[512,512]{1,0:T(8,128)(2,1)}, u32[]{:S(2)}) copy-start(bf16[512,512]{1,0:T(8,128)(2,1)} %constant.27.clone.fwd) | copy-start | bytes 1572868
  21.1 5.7 %collective-permute-start.4 = (f32[2,2,128,128]{3,2,1,0:T(8,128)S(1)}, f32[2,2,128,128]{3,2,1,0:T(8,128)S(1)}, u32[]{:S(2)}, u32[]{:S(2)}) collective-permute-start(f32[2,2,128,128]{3,2,1,0:T(8,128)S(1)} %get-tuple-element.62), channel_id=1, source_target_pairs={{0,1},{1,0},{2,3},{3,2},{4,5},{5,4},{6,7},{7,6},{8,9},{9,8},{10,11... | collective-permute-start | bytes 786440 | tf_op jit(solution)/shard_map/ppermute | solution.py:350
  25.6 5.8 %collective-permute-start.5 = (f32[2,2,128,128]{3,2,1,0:T(8,128)S(1)}, f32[2,2,128,128]{3,2,1,0:T(8,128)S(1)}, u32[]{:S(2)}, u32[]{:S(2)}) collective-permute-start(f32[2,2,128,128]{3,2,1,0:T(8,128)S(1)} %get-tuple-element.63), channel_id=1, source_target_pairs={{0,15},{1,2},{2,1},{3,4},{4,3},{5,6},{6,5},{7,8},{8,7},{9,10},{10,... | collective-permute-start | bytes 786440 | tf_op jit(solution)/shard_map/ppermute | solution.py:349
  40.1 5.5 %collective-permute-start.8 = (f32[16,5,8,256]{3,2,1,0:T(8,128)S(1)}, f32[16,5,8,256]{3,2,1,0:T(8,128)S(1)}, u32[]{:S(2)}, u32[]{:S(2)}) collective-permute-start(f32[16,5,8,256]{3,2,1,0:T(8,128)S(1)} %get-tuple-element.76), channel_id=1, source_target_pairs={{0,1},{1,0},{2,3},{3,2},{4,5},{5,4},{6,7},{7,6},{8,9},{9,8},{10,11... | collective-permute-start | bytes 1966088 | tf_op jit(solution)/shard_map/ppermute | solution.py:355
  43.9 7.8 %collective-permute-start.6 = (f32[2,512,128]{2,1,0:T(8,128)S(1)}, f32[2,512,128]{2,1,0:T(8,128)S(1)}, u32[]{:S(2)}, u32[]{:S(2)}) collective-permute-start(f32[2,512,128]{2,1,0:T(8,128)S(1)} %get-tuple-element.72), channel_id=1, source_target_pairs={{0,1},{1,0},{2,3},{3,2},{4,5},{5,4},{6,7},{7,6},{8,9},{9,8},{10,11... | collective-permute-start | bytes 1572872 | tf_op jit(solution)/shard_map/ppermute | solution.py:354
  44.0 8.9 %collective-permute-start.7 = (f32[2,512,128]{2,1,0:T(8,128)S(1)}, f32[2,512,128]{2,1,0:T(8,128)S(1)}, u32[]{:S(2)}, u32[]{:S(2)}) collective-permute-start(f32[2,512,128]{2,1,0:T(8,128)S(1)} %get-tuple-element.73), channel_id=1, source_target_pairs={{0,15},{1,2},{2,1},{3,4},{4,3},{5,6},{6,5},{7,8},{8,7},{9,10},{10,... | collective-permute-start | bytes 1572872 | tf_op jit(solution)/shard_map/ppermute | solution.py:353
  46.5 18.7 %all-to-all-start = ((f32[16,5,8,256]{3,2,1,0:T(8,128)}), f32[16,5,8,256]{3,2,1,0:T(8,128)}, u32[]{:S(2)}, u32[]{:S(2)}) async-start(f32[16,5,8,256]{3,2,1,0:T(8,128)} %add.88), calls=%async_computation | async-start | bytes 1310720 | tf_op jit(solution)/shard_map/all_to_all | solution.py:356
  66.3 7.4 %collective-permute-start.11 = (f32[5,8,256]{2,1,0:T(8,128)S(1)}, f32[5,8,256]{2,1,0:T(8,128)S(1)}, u32[]{:S(2)}, u32[]{:S(2)}) collective-permute-start(f32[5,8,256]{2,1,0:T(8,128)S(1)} %fusion), channel_id=1, source_target_pairs={{0,192},{32,224},{64,128},{96,160},{128,64},{160,96},{192,0},{224,... | collective-permute-start | bytes 122888 | tf_op jit(solution)/shard_map/ppermute | solution.py:362
  67.3 6.8 %collective-permute-start.10 = (f32[5,8,256]{2,1,0:T(8,128)S(1)}, f32[5,8,256]{2,1,0:T(8,128)S(1)}, u32[]{:S(2)}, u32[]{:S(2)}) collective-permute-start(f32[5,8,256]{2,1,0:T(8,128)S(1)} %fusion), channel_id=1, source_target_pairs={{0,128},{32,160},{64,192},{96,224},{128,0},{160,32},{192,64},{224,... | collective-permute-start | bytes 122888 | tf_op jit(solution)/shard_map/ppermute | solution.py:362
  68.3 5.7 %collective-permute-start.9 = (f32[5,8,256]{2,1,0:T(8,128)S(1)}, f32[5,8,256]{2,1,0:T(8,128)S(1)}, u32[]{:S(2)}, u32[]{:S(2)}) collective-permute-start(f32[5,8,256]{2,1,0:T(8,128)S(1)} %fusion), channel_id=1, source_target_pairs={{0,64},{32,96},{64,0},{96,32},{128,192},{160,224},{192,128},{224,1... | collective-permute-start | bytes 122888 | tf_op jit(solution)/shard_map/ppermute | solution.py:362
  72.1 11.9 %collective-permute-start.13 = (f32[2,128,256]{2,1,0:T(8,128)S(1)}, f32[2,128,256]{2,1,0:T(8,128)S(1)}, u32[]{:S(2)}, u32[]{:S(2)}) collective-permute-start(f32[2,128,256]{2,1,0:T(8,128)S(1)} %get-tuple-element.80), channel_id=1, source_target_pairs={{0,16},{16,0},{1,17},{17,1},{2,18},{18,2},{3,19},{19,3},{4,20},{20... | collective-permute-start | bytes 786440 | tf_op jit(solution)/shard_map/ppermute | solution.py:361
  72.1 11.9 %collective-permute-start.14 = (f32[2,128,256]{2,1,0:T(8,128)S(1)}, f32[2,128,256]{2,1,0:T(8,128)S(1)}, u32[]{:S(2)}, u32[]{:S(2)}) collective-permute-start(f32[2,128,256]{2,1,0:T(8,128)S(1)} %get-tuple-element.81), channel_id=1, source_target_pairs={{0,240},{16,32},{32,16},{48,64},{64,48},{80,96},{96,80},{112,128},... | collective-permute-start | bytes 786440 | tf_op jit(solution)/shard_map/ppermute | solution.py:360
  74.1 6.9 %collective-permute-start.12 = (f32[5,8,256]{2,1,0:T(8,128)S(1)}, f32[5,8,256]{2,1,0:T(8,128)S(1)}, u32[]{:S(2)}, u32[]{:S(2)}) collective-permute-start(f32[5,8,256]{2,1,0:T(8,128)S(1)} %add_add_fusion), channel_id=1, source_target_pairs={{0,32},{32,0},{64,96},{96,64},{128,160},{160,128},{192,224},{224,1... | collective-permute-start | bytes 122888 | tf_op jit(solution)/shard_map/ppermute | solution.py:364
  97.3 4.8 %collective-permute-start.15 = (f32[16,4,8,256]{3,2,1,0:T(8,128)S(1)}, f32[16,4,8,256]{3,2,1,0:T(8,128)S(1)}, u32[]{:S(2)}, u32[]{:S(2)}) collective-permute-start(f32[16,4,8,256]{3,2,1,0:T(8,128)S(1)} %all_to_all.10.own), channel_id=1, source_target_pairs={{0,1},{1,0},{2,3},{3,2},{4,5},{5,4},{6,7},{7,6},{8,9},{9,8},{10,11... | collective-permute-start | bytes 1572872 | tf_op jit(solution)/shard_map/ppermute | solution.py:370

commit v10 on v7

--- a/solution.py
+++ b/solution.py
@@ -32,9 +32,13 @@
     return fwd, bwd
 
 
+def spot(number, unit):
+    return pl.ds(pl.multiple_of(number * unit, unit), HALF)
+
+
 def kernel(
-    offs, half, tile, top, bot, left, right, left_ends, right_ends, probe, amp, fwd_hbm, bwd_hbm,
-    mine, other, out_left, out_mid, out_right,
+    offs, flags, tile, rows_in, rows_out, cols_in, cols_out, ends_in, ends_out, probe, amp, fwd_hbm, bwd_hbm,
+    mine, other, back_in, back_out, out_mid,
     ext, acc, win, stack, side, far, weight, grads, power, fwd, bwd, sems,
 ):
     copies = [
@@ -43,16 +47,20 @@
     ]
     for copy in copies:
         copy.start()
+    co, xl = flags[0], flags[1]
+    q_in, q_out = 3 * (1 - co), 3 * co
+    at_in, at_out = spot(1 - xl, W + HALF), spot(xl, W + HALF)
+    middle = pl.ds(HALF, W)
     lanes = lax.broadcasted_iota(jnp.int32, (CH, HALF), 1)
     for q in range(2):
         cols = pl.ds(q * HALF, HALF)
-        ext[:, q + 1, 0:HALF, :] = top[:, :, cols]
-        ext[:, q + 1, HALF : HALF + W, :] = tile[:, :, cols]
-        ext[:, q + 1, HALF + W :, :] = bot[:, :, cols]
-    for q, middle, ends in ((0, left, left_ends), (3, right, right_ends)):
-        ext[:, q, 0:HALF, :] = ends[0]
-        ext[:, q, HALF : HALF + W, :] = middle[...]
-        ext[:, q, HALF + W :, :] = ends[1]
+        ext[:, q + 1, middle, :] = tile[:, :, cols]
+        ext[:, q + 1, at_in, :] = rows_in[:, :, cols]
+        ext[:, q + 1, at_out, :] = rows_out[:, :, cols]
+    for q, cols, ends in ((q_in, cols_in, ends_in), (q_out, cols_out, ends_out)):
+        ext[:, q, middle, :] = cols[...]
+        ext[:, q, at_in, :] = ends[0]
+        ext[:, q, at_out, :] = ends[1]
     acc[...] = jnp.zeros_like(acc)
     weight[...] = jnp.zeros_like(weight)
     grads[...] = jnp.zeros_like(grads)
@@ -156,16 +164,15 @@
     for d in range(2):
         for i in range(2 * W // HALF):
             rows = pl.ds(i * HALF, HALF)
-            out_left[d, rows, :] = acc[d, 0, rows, :] * scale
-            out_right[d, rows, :] = acc[d, 3, rows, :] * scale
+            back_in[d, rows, :] = acc[d, q_in, rows, :] * scale
+            back_out[d, rows, :] = acc[d, q_out, rows, :] * scale
             for q in range(2):
                 cols = pl.ds(q * HALF, HALF)
                 step = acc[d, q + 1, rows, :] * scale
                 if 1 <= i <= 2:
                     step += tile[d, pl.ds((i - 1) * HALF, HALF), cols]
                 out_mid[d, rows, cols] = step
-    h = half[0]
-    for out, side_of in ((mine, h), (other, 1 - h)):
+    for out, side_of in ((mine, co), (other, 1 - co)):
 
         def flush(i, carry):
             rows = pl.ds(pl.multiple_of(side_of * HALF + i * 8, 8), 8)
@@ -177,7 +184,7 @@
         lax.fori_loop(0, 16, flush, 0)
 
 
-def correct(offsets, half, border, probe, amplitude):
+def correct(offsets, flags, border, probe, amplitude):
     fwd, bwd = dft_matrices()
     vmem = pl.BlockSpec(memory_space=pltpu.VMEM)
     smem = pl.BlockSpec(memory_space=pltpu.SMEM)
@@ -185,7 +192,7 @@
     strip = jax.ShapeDtypeStruct((2, 2 * W, HALF), F32)
     return pl.pallas_call(
         kernel,
-        out_shape=(part, part, strip, jax.ShapeDtypeStruct((2, 2 * W, W), F32), strip),
+        out_shape=(part, part, strip, strip, jax.ShapeDtypeStruct((2, 2 * W, W), F32)),
         in_specs=[smem, smem] + [vmem] * 9 + [pl.BlockSpec(memory_space=pl.ANY)] * 2,
         out_specs=(vmem,) * 5,
         scratch_shapes=[
@@ -203,14 +210,13 @@
             pltpu.SemaphoreType.DMA((2,)),
         ],
         compiler_params=pltpu.CompilerParams(vmem_limit_bytes=20 << 20),
-    )(offsets, half, *border, probe, amplitude, jnp.asarray(fwd), jnp.asarray(bwd))
+    )(offsets, flags, *border, probe, amplitude, jnp.asarray(fwd), jnp.asarray(bwd))
 
 
 GX = ("z", "xl")
 GY = ("xh", "y", "co")
-UP = [(i, (i + 1) % 16) for i in range(16)]
-DOWN = [(j, i) for i, j in UP]
-SWAP = [(0, 1), (1, 0)]
+NEAR = [(0, 1), (1, 0)]
+FAR = [(i, (i + 1) % 16 if i % 2 else (i - 1) % 16) for i in range(16)]
 
 
 def arrange_kernel(half, own, swapped, out):
@@ -233,42 +239,50 @@
     )(half, own, swapped)
 
 
+def in_order(number, near, far, axis):
+    first = number == 0
+    return jnp.concatenate([jnp.where(first, far, near), jnp.where(first, near, far)], axis)
+
+
 def body(object_field, probe_field, amplitude, offsets):
     group = ("xh", "xl", "y")
-    co = lax.axis_index("co")
-    half = co.reshape(1)
+    co, xl = lax.axis_index("co"), lax.axis_index("xl")
     block = (co * 16 + lax.axis_index(group)) * 8
     offs = offsets.transpose(1, 2, 0).reshape(2, POS)
-    object_field, half, block = lax.optimization_barrier((object_field, half, block))
-    first, last = slice(0, HALF), slice(HALF, W)
-    top = lax.ppermute(object_field[:, last], GX, UP)
-    bot = lax.ppermute(object_field[:, first], GX, DOWN)
-    left = lax.ppermute(object_field[:, :, last], GY, UP)
-    right = lax.ppermute(object_field[:, :, first], GY, DOWN)
-    left_ends = lax.ppermute(jnp.stack([top[:, :, last], bot[:, :, last]]), GY, UP)
-    right_ends = lax.ppermute(jnp.stack([top[:, :, first], bot[:, :, first]]), GY, DOWN)
-    border = (object_field, top, bot, left, right, left_ends, right_ends)
-    mine, other, out_left, out_mid, out_right = correct(offs, half, border, probe_field, amplitude)
-    part = mine + lax.ppermute(other, "co", SWAP)
-    from_right = lax.ppermute(out_left, GY, DOWN)
-    from_left = lax.ppermute(out_right, GY, UP)
+    half_in, half_out = (1 - co) * HALF, co * HALF
+    rows_at_in, rows_at_out = (1 - xl) * HALF, xl * HALF
+    scalars = (co, xl, block, half_in, half_out, rows_at_in, rows_at_out, 3 * rows_at_in, 3 * rows_at_out)
+    flags = jnp.stack([co, xl])
+    object_field, flags, *scalars = lax.optimization_barrier((object_field, flags, *scalars))
+    co, xl, block, half_in, half_out, rows_at_in, rows_at_out, ends_at_in, ends_at_out = scalars
+    cut = lax.dynamic_slice_in_dim
+    rows_out = lax.ppermute(cut(object_field, rows_at_out, HALF, 1), GX, FAR)
+    rows_in = lax.ppermute(cut(object_field, rows_at_in, HALF, 1), "xl", NEAR)
+    cols_out = lax.ppermute(cut(object_field, half_out, HALF, 2), GY, FAR)
+    cols_in = lax.ppermute(cut(object_field, half_in, HALF, 2), "co", NEAR)
+    ends_out = lax.ppermute(jnp.stack([cut(rows, half_out, HALF, 2) for rows in (rows_in, rows_out)]), GY, FAR)
+    ends_in = lax.ppermute(jnp.stack([cut(rows, half_in, HALF, 2) for rows in (rows_in, rows_out)]), "co", NEAR)
+    border = (object_field, rows_in, rows_out, cols_in, cols_out, ends_in, ends_out)
+    mine, other, back_in, back_out, middle = correct(offs, flags, border, probe_field, amplitude)
+    from_out = lax.ppermute(back_out, GY, FAR)
+    from_in = lax.ppermute(back_in, "co", NEAR)
+    part = mine + lax.ppermute(other, "co", NEAR)
     pieces = lax.all_to_all(part, group, 0, 0, tiled=True)
     part = sum(pieces[i] for i in range(16))
-    folded = out_mid + jnp.concatenate([from_left, from_right], 2)
+    folded = middle + in_order(co, from_in, from_out, 2)
     part, folded = lax.optimization_barrier((part, folded))
-    from_below = lax.ppermute(folded[:, :HALF], GX, DOWN)
-    from_above = lax.ppermute(folded[:, HALF + W :], GX, UP)
+    from_out = lax.ppermute(cut(folded, ends_at_out, HALF, 1), GX, FAR)
+    from_in = lax.ppermute(cut(folded, ends_at_in, HALF, 1), "xl", NEAR)
     peers = [lax.ppermute(part, "z", [(i, i ^ step) for i in range(8)]) for step in (2, 4, 6)]
     part = (part + peers[0]) + (peers[1] + peers[2])
     part = part + lax.ppermute(part, "z", [(i, i ^ 1) for i in range(8)])
-    part, from_below, from_above = lax.optimization_barrier((part, from_below, from_above))
-    planes = probe_field.reshape(2 * MODES, W, W)
-    local = lax.dynamic_slice_in_dim(planes, block, 8, 1)
+    part, from_in, from_out = lax.optimization_barrier((part, from_in, from_out))
+    local = cut(probe_field.reshape(2 * MODES, W, W), block, 8, 1)
     weight = part[2 * MODES]
     local = local + (part[: 2 * MODES] - local * weight) / (weight + 1e-05)
     gathered = lax.all_to_all(jnp.broadcast_to(local[None], (16,) + local.shape), group, 0, 0, tiled=True)
-    updated_object = folded[:, HALF : HALF + W] + jnp.concatenate([from_above, from_below], 1)
-    updated_probe = arrange(half, gathered, lax.ppermute(gathered, "co", SWAP))
+    updated_object = folded[:, HALF : HALF + W] + in_order(xl, from_in, from_out, 1)
+    updated_probe = arrange(flags, gathered, lax.ppermute(gathered, "co", NEAR))
     return (updated_object, updated_probe)
 
 

time: 101 us -> 107 us (1.059)
  waiting for transfers between devices: 32.7 us -> 35.2 us
  Pallas kernels: 9.33 us -> 11.4 us
    ppermute x12, starting transfers between devices: 22.5 us -> 27.1 us  [the longest x1 7.43 us: body(): rows_out = lax.ppermute(cut(object_field, rows_at_out, HALF, 1), GX, FAR)]
    all_to_all x1, starting transfers between devices: 6.9 us -> 4.26 us  [body(): pieces = lax.all_to_all(part, group, 0, 0, tiled=True)]
    ppermute x3, waiting for transfers between devices: 0.9 us -> 3.03 us  [body(): lax.ppermute(part, 'z', [(i, i ^ step) for i in range(8)])]
    pallas_call x1, Pallas kernels: 8.29 us -> 9.78 us  [correct(): pl.pallas_call(kernel, out_shape=(part, part, strip, strip, jax.ShapeDtyp...]
    dynamic_slice x0 -> x3, local copies, waits for them, and re-layouts: none -> 1.41 us  [the longest x1 1.14 us: body(): rows_out = lax.ppermute(cut(object_field, rows_at_out, HALF, 1), GX, FAR)]
    select_n x0 -> x2, other arithmetic: none -> 1.31 us  [in_order(): jnp.where(first, far, near)]
    ppermute x12, waiting for transfers between devices: 18 us -> 16.7 us  [the longest x1 6.16 us: body(): rows_in = lax.ppermute(cut(object_field, rows_at_in, HALF, 1), 'xl', NEAR)]
    slice x3 -> x0, local copies, waits for them, and re-layouts: 1.2 us -> none  [the longest x1 1.13 us: body(): bot = lax.ppermute(object_field[:, first], GX, DOWN)]
  transfers between devices with their start and end apart: 17 -> 17, of which waited for: 11 -> 8; matrix products, arithmetic and copies ran while one was open for 3% -> 4% of each run, Pallas kernels for 0% -> 0%
where the time goes in v10:
time: 107 us
  starting transfers between devices  37.5 us (35%)
  waiting for transfers between devices  35.2 us (33%)
  blocking collectives  15.6 us (15%)
  Pallas kernels  11.4 us (11%)
  other arithmetic  4.47 us (4%)
  local copies, waits for them, and re-layouts  1.76 us (2%)
    all_to_all x1, blocking collectives, body(): lax.all_to_all(jnp.broadcast_to(local[None], (16,) + local.shape), group,...  15.6 us
    all_to_all x1, waiting for transfers between devices, body(): pieces = lax.all_to_all(part, group, 0, 0, tiled=True)  11.5 us
    pallas_call x1, Pallas kernels, correct(): pl.pallas_call(kernel, out_shape=(part, part, strip, strip, jax.ShapeDtyp...  9.78 us
    ppermute x1, starting transfers between devices, body(): rows_out = lax.ppermute(cut(object_field, rows_at_out, HALF, 1), GX, FAR)  7.43 us
    ppermute x1, waiting for transfers between devices, body(): rows_in = lax.ppermute(cut(object_field, rows_at_in, HALF, 1), 'xl', NEAR)  6.16 us
    ppermute x3, starting transfers between devices, body(): lax.ppermute(part, 'z', [(i, i ^ step) for i in range(8)])  5.74 us
    ppermute x1, starting transfers between devices, body(): from_in = lax.ppermute(back_in, 'co', NEAR)  5.43 us
    ppermute x1, waiting for transfers between devices, body(): from_in = lax.ppermute(cut(folded, ends_at_in, HALF, 1), 'xl', NEAR)  4.84 us
  transfers between devices with their start and end apart: 17, of which 8 were waited for; matrix products, arithmetic and copies ran while one was open for 4% of the time, Pallas kernels for 0%

profile of v10, /device:TPU:1, one launch (start us, length us, event | category | flops | bytes accessed | tf_op | source)
XLA Modules:
  0.0 106.7 jit_solution(4038690695555050572)
XLA Ops:
  0.6 0.1 pad_add_fusion.flags.half
  0.7 1.1 %constant_dynamic-slice_fusion.4 = (f32[2,128,256]{2,1,0:T(8,128)S(1)}, f32[2,128,256]{2,1,0:T(8,128)S(1)}) fusion(f32[2,256,256]{2,1,0:T(8,128)} %tile, s32[]{:T(128)S(6)} %select_n.50, s32[]{:T(128)S(6)} %select_n.49), kind=kLoop, calls=%fused_computation.36 | loop fusion | bytes 1048584 | tf_op jit(solution)/shard_map/dynamic_slice | solution.py:259
  1.9 7.4 %collective-permute-start.1 = (f32[2,128,256]{2,1,0:T(8,128)S(1)}, f32[2,128,256]{2,1,0:T(8,128)S(1)}, u32[]{:S(2)}, u32[]{:S(2)}) collective-permute-start(f32[2,128,256]{2,1,0:T(8,128)S(1)} %get-tuple-element.52), channel_id=1, source_target_pairs={{0,240},{16,32},{32,16},{48,64},{64,48},{80,96},{96,80},{112,128},... | collective-permute-start | bytes 786440 | tf_op jit(solution)/shard_map/ppermute | solution.py:259
  9.3 0.0 collective-permute-start
  9.3 0.2 constant_dynamic-slice_fusion.2
  9.5 2.2 %collective-permute-start.3 = (f32[2,256,128]{2,1,0:T(8,128)S(1)}, f32[2,256,128]{2,1,0:T(8,128)S(1)}, u32[]{:S(2)}, u32[]{:S(2)}) collective-permute-start(f32[2,256,128]{2,1,0:T(8,128)S(1)} %get-tuple-element.50), channel_id=1, source_target_pairs={{0,15},{1,2},{2,1},{3,4},{4,3},{5,6},{6,5},{7,8},{8,7},{9,10},{10,... | collective-permute-start | bytes 786440 | tf_op jit(solution)/shard_map/ppermute | solution.py:261
  11.8 3.2 %collective-permute-start.2 = (f32[2,256,128]{2,1,0:T(8,128)S(1)}, f32[2,256,128]{2,1,0:T(8,128)S(1)}, u32[]{:S(2)}, u32[]{:S(2)}) collective-permute-start(f32[2,256,128]{2,1,0:T(8,128)S(1)} %get-tuple-element.51), channel_id=1, source_target_pairs={{0,1},{1,0},{2,3},{3,2},{4,5},{5,4},{6,7},{7,6},{8,9},{9,8},{10,11... | collective-permute-start | bytes 786440 | tf_op jit(solution)/shard_map/ppermute | solution.py:262
  14.9 0.4 collective-permute-done.1.rows_out
  15.4 0.1 dynamic-slice_bitcast_fusion
  15.5 6.2 %collective-permute-done.rows_in = f32[2,128,256]{2,1,0:T(8,128)S(1)} collective-permute-done((f32[2,128,256]{2,1,0:T(8,128)S(1)}, f32[2,128,256]{2,1,0:T(8,128)S(1)}, u32[]{:S(2)}, u32[]{:S(2)}) %collective-permute-start) | collective-permute-done | bytes 262176 | tf_op jit(solution)/shard_map/ppermute | solution.py:260
  21.7 0.1 dynamic-slice_bitcast_fusion.1
  21.9 0.6 collective-permute-start.4
  22.5 0.0 copy-start.5
  22.5 1.3 %collective-permute-start.5 = (f32[2,2,128,128]{3,2,1,0:T(8,128)S(1)}, f32[2,2,128,128]{3,2,1,0:T(8,128)S(1)}, u32[]{:S(2)}, u32[]{:S(2)}) collective-permute-start(f32[2,2,128,128]{3,2,1,0:T(8,128)S(1)} %pad_maximum_fusion.1), channel_id=1, source_target_pairs={{0,15},{1,2},{2,1},{3,4},{4,3},{5,6},{6,5},{7,8},{8,7},{9,10},{10,... | collective-permute-start | bytes 786440 | tf_op jit(solution)/shard_map/ppermute | solution.py:263
  23.8 0.0 collective-permute-done.3.cols_out
  23.8 0.0 collective-permute-done.2.cols_in
  23.8 0.0 collective-permute-done.4.ends_in
  23.8 4.6 %collective-permute-done.5.ends_out = f32[2,2,128,128]{3,2,1,0:T(8,128)S(1)} collective-permute-done((f32[2,2,128,128]{3,2,1,0:T(8,128)S(1)}, f32[2,2,128,128]{3,2,1,0:T(8,128)S(1)}, u32[]{:S(2)}, u32[]{:S(2)}) %collective-permute-start.5) | collective-permute-done | bytes 262176 | tf_op jit(solution)/shard_map/ppermute | solution.py:263
  28.4 9.8 %shard_map.77 = (f32[16,5,8,256]{3,2,1,0:T(8,128)S(1)}, f32[16,5,8,256]{3,2,1,0:T(8,128)S(1)}, f32[2,512,128]{2,1,0:T(8,128)}, f32[2,512,128]{2,1,0:T(8,128)}, f32[2,512,256]{2,1,0:T(8,128)S(1)}) custom-call(s32[2,4]{1,0:T(2,128)S(1)} %bitcast.21, s32[2]{0:T(128)S(1)} %pad_add_fusion.flags.half, f32[2,256,256]{2,1,0:T(8,128)S(1)} %copy-done, ...), custom_call_target="tpu_custom_call" | custom-call | tf_op jit(solution)/shard_map/pallas_call | solution.py:193
  38.2 3.7 %collective-permute-start.6 = (f32[16,5,8,256]{3,2,1,0:T(8,128)S(1)}, f32[16,5,8,256]{3,2,1,0:T(8,128)S(1)}, u32[]{:S(2)}, u32[]{:S(2)}) collective-permute-start(f32[16,5,8,256]{3,2,1,0:T(8,128)S(1)} %get-tuple-element.30), channel_id=1, source_target_pairs={{0,1},{1,0},{2,3},{3,2},{4,5},{5,4},{6,7},{7,6},{8,9},{9,8},{10,11... | collective-permute-start | bytes 1966088 | tf_op jit(solution)/shard_map/ppermute | solution.py:269
  41.9 0.0 collective-permute-start.7
  41.9 5.4 %collective-permute-start.8 = (f32[2,512,128]{2,1,0:T(8,128)}, f32[2,512,128]{2,1,0:T(8,128)}, u32[]{:S(2)}, u32[]{:S(2)}) collective-permute-start(f32[2,512,128]{2,1,0:T(8,128)} %get-tuple-element.34), channel_id=1, source_target_pairs={{0,1},{1,0},{2,3},{3,2},{4,5},{5,4},{6,7},{7,6},{8,9},{9,8},{10,11... | collective-permute-start | bytes 1572872 | tf_op jit(solution)/shard_map/ppermute | solution.py:268
  47.4 0.0 collective-permute-done.6
  47.4 0.9 add.123
  48.3 4.3 %all-to-all-start = ((f32[16,5,8,256]{3,2,1,0:T(8,128)}), f32[16,5,8,256]{3,2,1,0:T(8,128)}, u32[]{:S(2)}, u32[]{:S(2)}) async-start(f32[16,5,8,256]{3,2,1,0:T(8,128)} %add.123), calls=%async_computation | async-start | bytes 1310720 | tf_op jit(solution)/shard_map/all_to_all | solution.py:270
  52.6 0.0 collective-permute-done.7
  52.6 0.0 collective-permute-done.8
  52.6 1.3 %broadcast_select_fusion.1 = (f32[2,512,128]{2,1,0:T(8,128)S(1)}, f32[2,512,128]{2,1,0:T(8,128)S(1)}) fusion(f32[2,512,128]{2,1,0:T(8,128)} %collective-permute-done.7, f32[2,512,128]{2,1,0:T(8,128)} %collective-permute-done.8, pred[]{:T(512)S(6)} %eq.6), kind=kLoop, calls=%fused_computation.5 | loop fusion | flops 262144 | bytes 2097153 | tf_op jit(solution)/shard_map/jit(_where)/select_n | solution.py:244
  53.9 0.1 maximum_add_fusion
  54.0 11.5 %all-to-all-done = f32[16,5,8,256]{3,2,1,0:T(8,128)} async-done(((f32[16,5,8,256]{3,2,1,0:T(8,128)}), f32[16,5,8,256]{3,2,1,0:T(8,128)}, u32[]{:S(2)}, u32[]{:S(2)}) %all-to-all-start) | async-done | bytes 655392 | tf_op jit(solution)/shard_map/all_to_all | solution.py:270
  65.5 1.1 %fusion = f32[5,8,256]{2,1,0:T(8,128)S(1)} fusion(f32[16,5,8,256]{3,2,1,0:T(8,128)} %all-to-all-done), kind=kLoop, calls=%fused_computation.13 | loop fusion | flops 153600 | bytes 696320 | tf_op jit(solution)/shard_map/add | solution.py:271
  66.6 2.3 %collective-permute-start.11 = (f32[5,8,256]{2,1,0:T(8,128)S(1)}, f32[5,8,256]{2,1,0:T(8,128)S(1)}, u32[]{:S(2)}, u32[]{:S(2)}) collective-permute-start(f32[5,8,256]{2,1,0:T(8,128)S(1)} %fusion), channel_id=1, source_target_pairs={{0,192},{32,224},{64,128},{96,160},{128,64},{160,96},{192,0},{224,... | collective-permute-start | bytes 122888 | tf_op jit(solution)/shard_map/ppermute | solution.py:276
  68.8 1.9 %collective-permute-start.10 = (f32[5,8,256]{2,1,0:T(8,128)S(1)}, f32[5,8,256]{2,1,0:T(8,128)S(1)}, u32[]{:S(2)}, u32[]{:S(2)}) collective-permute-start(f32[5,8,256]{2,1,0:T(8,128)S(1)} %fusion), channel_id=1, source_target_pairs={{0,128},{32,160},{64,192},{96,224},{128,0},{160,32},{192,64},{224,... | collective-permute-start | bytes 122888 | tf_op jit(solution)/shard_map/ppermute | solution.py:276
  70.8 1.5 %collective-permute-start.9 = (f32[5,8,256]{2,1,0:T(8,128)S(1)}, f32[5,8,256]{2,1,0:T(8,128)S(1)}, u32[]{:S(2)}, u32[]{:S(2)}) collective-permute-start(f32[5,8,256]{2,1,0:T(8,128)S(1)} %fusion), channel_id=1, source_target_pairs={{0,64},{32,96},{64,0},{96,32},{128,192},{160,224},{192,128},{224,1... | collective-permute-start | bytes 122888 | tf_op jit(solution)/shard_map/ppermute | solution.py:276
  72.3 0.1 constant_dynamic-slice_fusion
  72.4 0.7 collective-permute-start.14
  73.1 0.0 collective-permute-start.13
  73.1 0.0 collective-permute-done.11
  73.1 3.0 %collective-permute-done.10 = f32[5,8,256]{2,1,0:T(8,128)S(1)} collective-permute-done((f32[5,8,256]{2,1,0:T(8,128)S(1)}, f32[5,8,256]{2,1,0:T(8,128)S(1)}, u32[]{:S(2)}, u32[]{:S(2)}) %collective-permute-start.10) | collective-permute-done | bytes 40992 | tf_op jit(solution)/shard_map/ppermute | solution.py:276
  76.1 0.0 collective-permute-done.9
  76.2 0.4 collective-permute-start.12
  76.5 4.0 %collective-permute-done.12 = f32[5,8,256]{2,1,0:T(8,128)S(1)} collective-permute-done((f32[5,8,256]{2,1,0:T(8,128)S(1)}, f32[5,8,256]{2,1,0:T(8,128)S(1)}, u32[]{:S(2)}, u32[]{:S(2)}) %collective-permute-start.12) | collective-permute-done | bytes 40992 | tf_op jit(solution)/shard_map/ppermute | solution.py:278
  80.6 4.8 %collective-permute-done.13 = f32[2,128,256]{2,1,0:T(8,128)S(1)} collective-permute-done((f32[2,128,256]{2,1,0:T(8,128)S(1)}, f32[2,128,256]{2,1,0:T(8,128)S(1)}, u32[]{:S(2)}, u32[]{:S(2)}) %collective-permute-start.13) | collective-permute-done | bytes 262176 | tf_op jit(solution)/shard_map/ppermute | solution.py:275
  85.5 15.6 %all_to_all.10.own = f32[16,4,8,256]{3,2,1,0:T(8,128)S(1)} all-to-all(f32[16,4,8,256]{3,2,1,0:T(8,128)S(1)} %broadcast_in_dim.2), channel_id=1, replica_groups=mesh['z'=8,'xl'=2,'xh'=2,'y'=4,'co'=2] {'xh','xl','y'}, dimensions={0} | all-to-all | bytes 1048576 | tf_op jit(solution)/shard_map/all_to_all | solution.py:283
  101.1 2.5 %collective-permute-start.15 = (f32[16,4,8,256]{3,2,1,0:T(8,128)S(1)}, f32[16,4,8,256]{3,2,1,0:T(8,128)S(1)}, u32[]{:S(2)}, u32[]{:S(2)}) collective-permute-start(f32[16,4,8,256]{3,2,1,0:T(8,128)S(1)} %all_to_all.10.own), channel_id=1, source_target_pairs={{0,1},{1,0},{2,3},{3,2},{4,5},{5,4},{6,7},{7,6},{8,9},{9,8},{10,11... | collective-permute-start | bytes 1572872 | tf_op jit(solution)/shard_map/ppermute | solution.py:285
  103.6 0.9 maximum_add_fusion.1
  104.5 0.6 collective-permute-done.15.swapped
  105.1 1.6 %shard_map.78 = f32[2,2,256,256]{3,2,1,0:T(8,128)} custom-call(s32[2]{0:T(128)S(1)} %pad_add_fusion.flags.half, f32[16,4,8,256]{3,2,1,0:T(8,128)S(1)} %all_to_all.10.own, f32[16,4,8,256]{3,2,1,0:T(8,128)S(1)} %collective-permute-done.15.swapped), custom_call_target="tpu_custom_call" | custom-call | tf_op jit(solution)/shard_map/pallas_call | solution.py:233
  (20 shorter events, 0.2 us)
Async XLA Ops:
  0.7 8.6 %copy-start = (f32[2,256,256]{2,1,0:T(8,128)S(1)}, f32[2,256,256]{2,1,0:T(8,128)}, u32[]{:S(2)}) copy-start(f32[2,256,256]{2,1,0:T(8,128)} %tile) | copy-start | bytes 1572868
  1.9 13.5 %collective-permute-start.1 = (f32[2,128,256]{2,1,0:T(8,128)S(1)}, f32[2,128,256]{2,1,0:T(8,128)S(1)}, u32[]{:S(2)}, u32[]{:S(2)}) collective-permute-start(f32[2,128,256]{2,1,0:T(8,128)S(1)} %get-tuple-element.52), channel_id=1, source_target_pairs={{0,240},{16,32},{32,16},{48,64},{64,48},{80,96},{96,80},{112,128},... | collective-permute-start | bytes 786440 | tf_op jit(solution)/shard_map/ppermute | solution.py:259
  9.3 12.4 %collective-permute-start = (f32[2,128,256]{2,1,0:T(8,128)S(1)}, f32[2,128,256]{2,1,0:T(8,128)S(1)}, u32[]{:S(2)}, u32[]{:S(2)}) collective-permute-start(f32[2,128,256]{2,1,0:T(8,128)S(1)} %get-tuple-element.53), channel_id=1, source_target_pairs={{0,16},{16,0},{1,17},{17,1},{2,18},{18,2},{3,19},{19,3},{4,20},{20... | collective-permute-start | bytes 786440 | tf_op jit(solution)/shard_map/ppermute | solution.py:260
  9.3 19.1 %copy-start.3 = (bf16[512,512]{1,0:T(8,128)(2,1)S(1)}, bf16[512,512]{1,0:T(8,128)(2,1)}, u32[]{:S(2)}) copy-start(bf16[512,512]{1,0:T(8,128)(2,1)} %constant.42.clone.bwd_hbm) | copy-start | bytes 1572868
  9.3 19.1 %copy-start.4 = (bf16[512,512]{1,0:T(8,128)(2,1)S(1)}, bf16[512,512]{1,0:T(8,128)(2,1)}, u32[]{:S(2)}) copy-start(bf16[512,512]{1,0:T(8,128)(2,1)} %constant.41.clone.fwd_hbm) | copy-start | bytes 1572868
  9.5 14.2 %collective-permute-start.3 = (f32[2,256,128]{2,1,0:T(8,128)S(1)}, f32[2,256,128]{2,1,0:T(8,128)S(1)}, u32[]{:S(2)}, u32[]{:S(2)}) collective-permute-start(f32[2,256,128]{2,1,0:T(8,128)S(1)} %get-tuple-element.50), channel_id=1, source_target_pairs={{0,15},{1,2},{2,1},{3,4},{4,3},{5,6},{6,5},{7,8},{8,7},{9,10},{10,... | collective-permute-start | bytes 786440 | tf_op jit(solution)/shard_map/ppermute | solution.py:261
  11.8 16.6 %copy-start.1 = (f32[2,2,256,256]{3,2,1,0:T(8,128)S(1)}, f32[2,2,256,256]{3,2,1,0:T(8,128)}, u32[]{:S(2)}) copy-start(f32[2,2,256,256]{3,2,1,0:T(8,128)} %probe.1) | copy-start | bytes 3145732
  11.8 16.6 %copy-start.2 = (f32[4,1,256,256]{3,2,1,0:T(8,128)S(1)}, f32[4,1,256,256]{3,2,1,0:T(8,128)}, u32[]{:S(2)}) copy-start(f32[4,1,256,256]{3,2,1,0:T(8,128)} %amp.1) | copy-start | bytes 3145732
  11.8 12.0 %collective-permute-start.2 = (f32[2,256,128]{2,1,0:T(8,128)S(1)}, f32[2,256,128]{2,1,0:T(8,128)S(1)}, u32[]{:S(2)}, u32[]{:S(2)}) collective-permute-start(f32[2,256,128]{2,1,0:T(8,128)S(1)} %get-tuple-element.51), channel_id=1, source_target_pairs={{0,1},{1,0},{2,3},{3,2},{4,5},{5,4},{6,7},{7,6},{8,9},{9,8},{10,11... | collective-permute-start | bytes 786440 | tf_op jit(solution)/shard_map/ppermute | solution.py:262
  21.9 1.9 %collective-permute-start.4 = (f32[2,2,128,128]{3,2,1,0:T(8,128)S(1)}, f32[2,2,128,128]{3,2,1,0:T(8,128)S(1)}, u32[]{:S(2)}, u32[]{:S(2)}) collective-permute-start(f32[2,2,128,128]{3,2,1,0:T(8,128)S(1)} %pad_maximum_fusion), channel_id=1, source_target_pairs={{0,1},{1,0},{2,3},{3,2},{4,5},{5,4},{6,7},{7,6},{8,9},{9,8},{10,11... | collective-permute-start | bytes 786440 | tf_op jit(solution)/shard_map/ppermute | solution.py:264
  22.5 5.9 %copy-start.5 = (s32[4,1,2]{0,2,1:T(2,128)S(1)}, s32[4,1,2]{0,2,1:T(2,128)}, u32[]{:S(2)}) copy-start(s32[4,1,2]{0,2,1:T(2,128)} %param.9) | copy-start | bytes 100
  22.5 5.9 %collective-permute-start.5 = (f32[2,2,128,128]{3,2,1,0:T(8,128)S(1)}, f32[2,2,128,128]{3,2,1,0:T(8,128)S(1)}, u32[]{:S(2)}, u32[]{:S(2)}) collective-permute-start(f32[2,2,128,128]{3,2,1,0:T(8,128)S(1)} %pad_maximum_fusion.1), channel_id=1, source_target_pairs={{0,15},{1,2},{2,1},{3,4},{4,3},{5,6},{6,5},{7,8},{8,7},{9,10},{10,... | collective-permute-start | bytes 786440 | tf_op jit(solution)/shard_map/ppermute | solution.py:263
  38.2 9.2 %collective-permute-start.6 = (f32[16,5,8,256]{3,2,1,0:T(8,128)S(1)}, f32[16,5,8,256]{3,2,1,0:T(8,128)S(1)}, u32[]{:S(2)}, u32[]{:S(2)}) collective-permute-start(f32[16,5,8,256]{3,2,1,0:T(8,128)S(1)} %get-tuple-element.30), channel_id=1, source_target_pairs={{0,1},{1,0},{2,3},{3,2},{4,5},{5,4},{6,7},{7,6},{8,9},{9,8},{10,11... | collective-permute-start | bytes 1966088 | tf_op jit(solution)/shard_map/ppermute | solution.py:269
  41.9 10.6 %collective-permute-start.7 = (f32[2,512,128]{2,1,0:T(8,128)}, f32[2,512,128]{2,1,0:T(8,128)}, u32[]{:S(2)}, u32[]{:S(2)}) collective-permute-start(f32[2,512,128]{2,1,0:T(8,128)} %get-tuple-element.33), channel_id=1, source_target_pairs={{0,15},{1,2},{2,1},{3,4},{4,3},{5,6},{6,5},{7,8},{8,7},{9,10},{10,... | collective-permute-start | bytes 1572872 | tf_op jit(solution)/shard_map/ppermute | solution.py:267
  41.9 10.6 %collective-permute-start.8 = (f32[2,512,128]{2,1,0:T(8,128)}, f32[2,512,128]{2,1,0:T(8,128)}, u32[]{:S(2)}, u32[]{:S(2)}) collective-permute-start(f32[2,512,128]{2,1,0:T(8,128)} %get-tuple-element.34), channel_id=1, source_target_pairs={{0,1},{1,0},{2,3},{3,2},{4,5},{5,4},{6,7},{7,6},{8,9},{9,8},{10,11... | collective-permute-start | bytes 1572872 | tf_op jit(solution)/shard_map/ppermute | solution.py:268
  48.3 17.2 %all-to-all-start = ((f32[16,5,8,256]{3,2,1,0:T(8,128)}), f32[16,5,8,256]{3,2,1,0:T(8,128)}, u32[]{:S(2)}, u32[]{:S(2)}) async-start(f32[16,5,8,256]{3,2,1,0:T(8,128)} %add.123), calls=%async_computation | async-start | bytes 1310720 | tf_op jit(solution)/shard_map/all_to_all | solution.py:270
  66.6 6.5 %collective-permute-start.11 = (f32[5,8,256]{2,1,0:T(8,128)S(1)}, f32[5,8,256]{2,1,0:T(8,128)S(1)}, u32[]{:S(2)}, u32[]{:S(2)}) collective-permute-start(f32[5,8,256]{2,1,0:T(8,128)S(1)} %fusion), channel_id=1, source_target_pairs={{0,192},{32,224},{64,128},{96,160},{128,64},{160,96},{192,0},{224,... | collective-permute-start | bytes 122888 | tf_op jit(solution)/shard_map/ppermute | solution.py:276
  68.8 7.3 %collective-permute-start.10 = (f32[5,8,256]{2,1,0:T(8,128)S(1)}, f32[5,8,256]{2,1,0:T(8,128)S(1)}, u32[]{:S(2)}, u32[]{:S(2)}) collective-permute-start(f32[5,8,256]{2,1,0:T(8,128)S(1)} %fusion), channel_id=1, source_target_pairs={{0,128},{32,160},{64,192},{96,224},{128,0},{160,32},{192,64},{224,... | collective-permute-start | bytes 122888 | tf_op jit(solution)/shard_map/ppermute | solution.py:276
  70.8 5.4 %collective-permute-start.9 = (f32[5,8,256]{2,1,0:T(8,128)S(1)}, f32[5,8,256]{2,1,0:T(8,128)S(1)}, u32[]{:S(2)}, u32[]{:S(2)}) collective-permute-start(f32[5,8,256]{2,1,0:T(8,128)S(1)} %fusion), channel_id=1, source_target_pairs={{0,64},{32,96},{64,0},{96,32},{128,192},{160,224},{192,128},{224,1... | collective-permute-start | bytes 122888 | tf_op jit(solution)/shard_map/ppermute | solution.py:276
  72.4 8.2 %collective-permute-start.14 = (f32[2,128,256]{2,1,0:T(8,128)S(1)}, f32[2,128,256]{2,1,0:T(8,128)S(1)}, u32[]{:S(2)}, u32[]{:S(2)}) collective-permute-start(f32[2,128,256]{2,1,0:T(8,128)S(1)} %get-tuple-element.44), channel_id=1, source_target_pairs={{0,240},{16,32},{32,16},{48,64},{64,48},{80,96},{96,80},{112,128},... | collective-permute-start | bytes 786440 | tf_op jit(solution)/shard_map/ppermute | solution.py:274
  73.1 12.3 %collective-permute-start.13 = (f32[2,128,256]{2,1,0:T(8,128)S(1)}, f32[2,128,256]{2,1,0:T(8,128)S(1)}, u32[]{:S(2)}, u32[]{:S(2)}) collective-permute-start(f32[2,128,256]{2,1,0:T(8,128)S(1)} %get-tuple-element.45), channel_id=1, source_target_pairs={{0,16},{16,0},{1,17},{17,1},{2,18},{18,2},{3,19},{19,3},{4,20},{20... | collective-permute-start | bytes 786440 | tf_op jit(solution)/shard_map/ppermute | solution.py:275
  76.2 4.4 %collective-permute-start.12 = (f32[5,8,256]{2,1,0:T(8,128)S(1)}, f32[5,8,256]{2,1,0:T(8,128)S(1)}, u32[]{:S(2)}, u32[]{:S(2)}) collective-permute-start(f32[5,8,256]{2,1,0:T(8,128)S(1)} %add_add_fusion), channel_id=1, source_target_pairs={{0,32},{32,0},{64,96},{96,64},{128,160},{160,128},{192,224},{224,1... | collective-permute-start | bytes 122888 | tf_op jit(solution)/shard_map/ppermute | solution.py:278
  101.1 4.1 %collective-permute-start.15 = (f32[16,4,8,256]{3,2,1,0:T(8,128)S(1)}, f32[16,4,8,256]{3,2,1,0:T(8,128)S(1)}, u32[]{:S(2)}, u32[]{:S(2)}) collective-permute-start(f32[16,4,8,256]{3,2,1,0:T(8,128)S(1)} %all_to_all.10.own), channel_id=1, source_target_pairs={{0,1},{1,0},{2,3},{3,2},{4,5},{5,4},{6,7},{7,6},{8,9},{9,8},{10,11... | collective-permute-start | bytes 1572872 | tf_op jit(solution)/shard_map/ppermute | solution.py:285

commit v11 on v10

--- a/solution.py
+++ b/solution.py
@@ -38,7 +38,7 @@
 
 def kernel(
     offs, flags, tile, rows_in, rows_out, cols_in, cols_out, ends_in, ends_out, probe, amp, fwd_hbm, bwd_hbm,
-    mine, other, back_in, back_out, out_mid,
+    mine, other, out_left, out_right, out_mid,
     ext, acc, win, stack, side, far, weight, grads, power, fwd, bwd, sems,
 ):
     copies = [
@@ -59,8 +59,8 @@
         ext[:, q + 1, at_out, :] = rows_out[:, :, cols]
     for q, cols, ends in ((q_in, cols_in, ends_in), (q_out, cols_out, ends_out)):
         ext[:, q, middle, :] = cols[...]
-        ext[:, q, at_in, :] = ends[0]
-        ext[:, q, at_out, :] = ends[1]
+        ext[:, q, at_out, :] = ends[0]
+        ext[:, q, at_in, :] = ends[1]
     acc[...] = jnp.zeros_like(acc)
     weight[...] = jnp.zeros_like(weight)
     grads[...] = jnp.zeros_like(grads)
@@ -164,8 +164,8 @@
     for d in range(2):
         for i in range(2 * W // HALF):
             rows = pl.ds(i * HALF, HALF)
-            back_in[d, rows, :] = acc[d, q_in, rows, :] * scale
-            back_out[d, rows, :] = acc[d, q_out, rows, :] * scale
+            out_left[d, rows, :] = acc[d, 0, rows, :] * scale
+            out_right[d, rows, :] = acc[d, 3, rows, :] * scale
             for q in range(2):
                 cols = pl.ds(q * HALF, HALF)
                 step = acc[d, q + 1, rows, :] * scale
@@ -216,6 +216,8 @@
 GX = ("z", "xl")
 GY = ("xh", "y", "co")
 NEAR = [(0, 1), (1, 0)]
+UP = [(i, (i + 1) % 16) for i in range(16)]
+DOWN = [(j, i) for i, j in UP]
 FAR = [(i, (i + 1) % 16 if i % 2 else (i - 1) % 16) for i in range(16)]
 
 
@@ -239,11 +241,6 @@
     )(half, own, swapped)
 
 
-def in_order(number, near, far, axis):
-    first = number == 0
-    return jnp.concatenate([jnp.where(first, far, near), jnp.where(first, near, far)], axis)
-
-
 def body(object_field, probe_field, amplitude, offsets):
     group = ("xh", "xl", "y")
     co, xl = lax.axis_index("co"), lax.axis_index("xl")
@@ -251,37 +248,38 @@
     offs = offsets.transpose(1, 2, 0).reshape(2, POS)
     half_in, half_out = (1 - co) * HALF, co * HALF
     rows_at_in, rows_at_out = (1 - xl) * HALF, xl * HALF
-    scalars = (co, xl, block, half_in, half_out, rows_at_in, rows_at_out, 3 * rows_at_in, 3 * rows_at_out)
+    scalars = (co, block, half_in, half_out, rows_at_in, rows_at_out)
     flags = jnp.stack([co, xl])
     object_field, flags, *scalars = lax.optimization_barrier((object_field, flags, *scalars))
-    co, xl, block, half_in, half_out, rows_at_in, rows_at_out, ends_at_in, ends_at_out = scalars
+    co, block, half_in, half_out, rows_at_in, rows_at_out = scalars
     cut = lax.dynamic_slice_in_dim
+    rows_in = lax.ppermute(cut(object_field, rows_at_in, HALF, 1), "xl", NEAR)
     rows_out = lax.ppermute(cut(object_field, rows_at_out, HALF, 1), GX, FAR)
-    rows_in = lax.ppermute(cut(object_field, rows_at_in, HALF, 1), "xl", NEAR)
+    cols_in = lax.ppermute(cut(object_field, half_in, HALF, 2), "co", NEAR)
     cols_out = lax.ppermute(cut(object_field, half_out, HALF, 2), GY, FAR)
-    cols_in = lax.ppermute(cut(object_field, half_in, HALF, 2), "co", NEAR)
-    ends_out = lax.ppermute(jnp.stack([cut(rows, half_out, HALF, 2) for rows in (rows_in, rows_out)]), GY, FAR)
-    ends_in = lax.ppermute(jnp.stack([cut(rows, half_in, HALF, 2) for rows in (rows_in, rows_out)]), "co", NEAR)
+    rows_out, rows_in = lax.optimization_barrier((rows_out, rows_in))
+    ends_in = lax.ppermute(jnp.stack([cut(rows, half_in, HALF, 2) for rows in (rows_out, rows_in)]), "co", NEAR)
+    ends_out = lax.ppermute(jnp.stack([cut(rows, half_out, HALF, 2) for rows in (rows_out, rows_in)]), GY, FAR)
     border = (object_field, rows_in, rows_out, cols_in, cols_out, ends_in, ends_out)
-    mine, other, back_in, back_out, middle = correct(offs, flags, border, probe_field, amplitude)
-    from_out = lax.ppermute(back_out, GY, FAR)
-    from_in = lax.ppermute(back_in, "co", NEAR)
+    mine, other, out_left, out_right, middle = correct(offs, flags, border, probe_field, amplitude)
+    from_right = lax.ppermute(out_left, GY, DOWN)
+    from_left = lax.ppermute(out_right, GY, UP)
     part = mine + lax.ppermute(other, "co", NEAR)
     pieces = lax.all_to_all(part, group, 0, 0, tiled=True)
     part = sum(pieces[i] for i in range(16))
-    folded = middle + in_order(co, from_in, from_out, 2)
+    folded = middle + jnp.concatenate([from_left, from_right], 2)
     part, folded = lax.optimization_barrier((part, folded))
-    from_out = lax.ppermute(cut(folded, ends_at_out, HALF, 1), GX, FAR)
-    from_in = lax.ppermute(cut(folded, ends_at_in, HALF, 1), "xl", NEAR)
+    from_below = lax.ppermute(folded[:, :HALF], GX, DOWN)
+    from_above = lax.ppermute(folded[:, HALF + W :], GX, UP)
     peers = [lax.ppermute(part, "z", [(i, i ^ step) for i in range(8)]) for step in (2, 4, 6)]
     part = (part + peers[0]) + (peers[1] + peers[2])
     part = part + lax.ppermute(part, "z", [(i, i ^ 1) for i in range(8)])
-    part, from_in, from_out = lax.optimization_barrier((part, from_in, from_out))
+    part, from_below, from_above = lax.optimization_barrier((part, from_below, from_above))
     local = cut(probe_field.reshape(2 * MODES, W, W), block, 8, 1)
     weight = part[2 * MODES]
     local = local + (part[: 2 * MODES] - local * weight) / (weight + 1e-05)
     gathered = lax.all_to_all(jnp.broadcast_to(local[None], (16,) + local.shape), group, 0, 0, tiled=True)
-    updated_object = folded[:, HALF : HALF + W] + in_order(xl, from_in, from_out, 1)
+    updated_object = folded[:, HALF : HALF + W] + jnp.concatenate([from_above, from_below], 1)
     updated_probe = arrange(flags, gathered, lax.ppermute(gathered, "co", NEAR))
     return (updated_object, updated_probe)
 

time: 107 us -> 103 us (0.963)
  waiting for transfers between devices: 35.2 us -> 25.3 us
  starting transfers between devices: 37.5 us -> 44.2 us
    ppermute x1, waiting for transfers between devices: 6.16 us -> 0.01 us  [body(): rows_in = lax.ppermute(cut(object_field, rows_at_in, HALF, 1), 'xl', NEAR)]
    ppermute x3, starting transfers between devices: 5.74 us -> 8.3 us  [body(): lax.ppermute(part, 'z', [(i, i ^ step) for i in range(8)])]
    all_to_all x1, starting transfers between devices: 4.26 us -> 6.81 us  [body(): pieces = lax.all_to_all(part, group, 0, 0, tiled=True)]
    ppermute x1, starting transfers between devices: 0.01 us -> 2.12 us  [body(): rows_in = lax.ppermute(cut(object_field, rows_at_in, HALF, 1), 'xl', NEAR)]
    ppermute x3, waiting for transfers between devices: 3.03 us -> 1.14 us  [body(): lax.ppermute(part, 'z', [(i, i ^ step) for i in range(8)])]
    ppermute x1, starting transfers between devices: 7.43 us -> 5.55 us  [body(): rows_out = lax.ppermute(cut(object_field, rows_at_out, HALF, 1), GX, FAR)]
    select_n x2 -> x0, other arithmetic: 1.31 us -> none  [in_order(): jnp.where(first, far, near)]
    add x2, other arithmetic: 0.97 us -> 2.2 us  [the longest x1 1.34 us: body(): folded = middle + jnp.concatenate([from_left, from_right], 2)]
where the time goes in v11:
time: 103 us
  starting transfers between devices  44.2 us (43%)
  waiting for transfers between devices  25.3 us (25%)
  blocking collectives  15.3 us (15%)
  Pallas kernels  11.4 us (11%)
  other arithmetic  4.38 us (4%)
  local copies, waits for them, and re-layouts  1.67 us (2%)
    all_to_all x1, blocking collectives, body(): lax.all_to_all(jnp.broadcast_to(local[None], (16,) + local.shape), group,...  15.3 us
    all_to_all x1, waiting for transfers between devices, body(): pieces = lax.all_to_all(part, group, 0, 0, tiled=True)  10.3 us
    pallas_call x1, Pallas kernels, correct(): pl.pallas_call(kernel, out_shape=(part, part, strip, strip, jax.ShapeDtyp...  9.78 us
    ppermute x3, starting transfers between devices, body(): lax.ppermute(part, 'z', [(i, i ^ step) for i in range(8)])  8.3 us
    all_to_all x1, starting transfers between devices, body(): pieces = lax.all_to_all(part, group, 0, 0, tiled=True)  6.81 us
    ppermute x1, starting transfers between devices, body(): rows_out = lax.ppermute(cut(object_field, rows_at_out, HALF, 1), GX, FAR)  5.55 us
    ppermute x1, waiting for transfers between devices, body(): lax.ppermute(jnp.stack([cut(rows, half_out, HALF, 2) for rows in (rows_ou...  4.94 us
    ppermute x1, starting transfers between devices, body(): part = mine + lax.ppermute(other, 'co', NEAR)  4.65 us
  transfers between devices with their start and end apart: 17, of which 8 were waited for; matrix products, arithmetic and copies ran while one was open for 4% of the time, Pallas kernels for 0%

profile of v11, /device:TPU:1, one launch (start us, length us, event | category | flops | bytes accessed | tf_op | source)
XLA Modules:
  0.0 103.0 jit_solution(4198371307507151947)
XLA Ops:
  0.6 0.1 pad_add_fusion.flags.half
  0.7 1.2 %constant_dynamic-slice_fusion.2 = (f32[2,128,256]{2,1,0:T(8,128)S(1)}, f32[2,128,256]{2,1,0:T(8,128)S(1)}) fusion(f32[2,256,256]{2,1,0:T(8,128)} %tile, s32[]{:T(128)S(6)} %select_n.20, s32[]{:T(128)S(6)} %select_n.19), kind=kLoop, calls=%fused_computation.30 | loop fusion | bytes 1048584 | tf_op jit(solution)/shard_map/dynamic_slice | solution.py:256
  1.9 2.1 %collective-permute-start.1 = (f32[2,128,256]{2,1,0:T(8,128)S(1)}, f32[2,128,256]{2,1,0:T(8,128)S(1)}, u32[]{:S(2)}, u32[]{:S(2)}) collective-permute-start(f32[2,128,256]{2,1,0:T(8,128)S(1)} %get-tuple-element.44), channel_id=1, source_target_pairs={{0,16},{16,0},{1,17},{17,1},{2,18},{18,2},{3,19},{19,3},{4,20},{20... | collective-permute-start | bytes 786440 | tf_op jit(solution)/shard_map/ppermute | solution.py:256
  4.0 5.6 %collective-permute-start = (f32[2,128,256]{2,1,0:T(8,128)S(1)}, f32[2,128,256]{2,1,0:T(8,128)S(1)}, u32[]{:S(2)}, u32[]{:S(2)}) collective-permute-start(f32[2,128,256]{2,1,0:T(8,128)S(1)} %get-tuple-element.45), channel_id=1, source_target_pairs={{0,240},{16,32},{32,16},{48,64},{64,48},{80,96},{96,80},{112,128},... | collective-permute-start | bytes 786440 | tf_op jit(solution)/shard_map/ppermute | solution.py:257
  9.6 0.2 constant_dynamic-slice_fusion
  9.8 2.5 %collective-permute-start.3 = (f32[2,256,128]{2,1,0:T(8,128)S(1)}, f32[2,256,128]{2,1,0:T(8,128)S(1)}, u32[]{:S(2)}, u32[]{:S(2)}) collective-permute-start(f32[2,256,128]{2,1,0:T(8,128)S(1)} %get-tuple-element.42), channel_id=1, source_target_pairs={{0,15},{1,2},{2,1},{3,4},{4,3},{5,6},{6,5},{7,8},{8,7},{9,10},{10,... | collective-permute-start | bytes 786440 | tf_op jit(solution)/shard_map/ppermute | solution.py:259
  12.3 3.2 %collective-permute-start.2 = (f32[2,256,128]{2,1,0:T(8,128)S(1)}, f32[2,256,128]{2,1,0:T(8,128)S(1)}, u32[]{:S(2)}, u32[]{:S(2)}) collective-permute-start(f32[2,256,128]{2,1,0:T(8,128)S(1)} %get-tuple-element.43), channel_id=1, source_target_pairs={{0,1},{1,0},{2,3},{3,2},{4,5},{5,4},{6,7},{7,6},{8,9},{9,8},{10,11... | collective-permute-start | bytes 786440 | tf_op jit(solution)/shard_map/ppermute | solution.py:258
  15.5 0.0 collective-permute-done.1.rows_in
  15.5 0.0 collective-permute-done.rows_out
  15.5 0.2 dynamic-slice_bitcast_fusion
  15.7 1.8 %collective-permute-start.4 = (f32[2,2,128,128]{3,2,1,0:T(8,128)S(1)}, f32[2,2,128,128]{3,2,1,0:T(8,128)S(1)}, u32[]{:S(2)}, u32[]{:S(2)}) collective-permute-start(f32[2,2,128,128]{3,2,1,0:T(8,128)S(1)} %pad_maximum_fusion), channel_id=1, source_target_pairs={{0,1},{1,0},{2,3},{3,2},{4,5},{5,4},{6,7},{7,6},{8,9},{9,8},{10,11... | collective-permute-start | bytes 786440 | tf_op jit(solution)/shard_map/ppermute | solution.py:261
  17.6 0.0 copy-start.5
  17.6 1.2 %collective-permute-start.5 = (f32[2,2,128,128]{3,2,1,0:T(8,128)S(1)}, f32[2,2,128,128]{3,2,1,0:T(8,128)S(1)}, u32[]{:S(2)}, u32[]{:S(2)}) collective-permute-start(f32[2,2,128,128]{3,2,1,0:T(8,128)S(1)} %pad_maximum_fusion.1), channel_id=1, source_target_pairs={{0,15},{1,2},{2,1},{3,4},{4,3},{5,6},{6,5},{7,8},{8,7},{9,10},{10,... | collective-permute-start | bytes 786440 | tf_op jit(solution)/shard_map/ppermute | solution.py:262
  18.8 0.0 collective-permute-done.3.cols_out
  18.8 0.0 collective-permute-done.2.cols_in
  18.8 0.0 collective-permute-done.4.ends_in
  18.8 4.9 %collective-permute-done.5.ends_out = f32[2,2,128,128]{3,2,1,0:T(8,128)S(1)} collective-permute-done((f32[2,2,128,128]{3,2,1,0:T(8,128)S(1)}, f32[2,2,128,128]{3,2,1,0:T(8,128)S(1)}, u32[]{:S(2)}, u32[]{:S(2)}) %collective-permute-start.5) | collective-permute-done | bytes 262176 | tf_op jit(solution)/shard_map/ppermute | solution.py:262
  23.8 0.0 copy-done.1
  23.8 0.0 copy-done.2
  23.8 9.8 %shard_map.77 = (f32[16,5,8,256]{3,2,1,0:T(8,128)S(1)}, f32[16,5,8,256]{3,2,1,0:T(8,128)S(1)}, f32[2,512,128]{2,1,0:T(8,128)}, f32[2,512,128]{2,1,0:T(8,128)}, f32[2,512,256]{2,1,0:T(8,128)S(1)}) custom-call(s32[2,4]{1,0:T(2,128)S(1)} %bitcast.21, s32[2]{0:T(128)S(1)} %pad_add_fusion.flags.half, f32[2,256,256]{2,1,0:T(8,128)S(1)} %copy-done, ...), custom_call_target="tpu_custom_call" | custom-call | tf_op jit(solution)/shard_map/pallas_call | solution.py:193
  33.6 4.6 %collective-permute-start.6 = (f32[16,5,8,256]{3,2,1,0:T(8,128)S(1)}, f32[16,5,8,256]{3,2,1,0:T(8,128)S(1)}, u32[]{:S(2)}, u32[]{:S(2)}) collective-permute-start(f32[16,5,8,256]{3,2,1,0:T(8,128)S(1)} %get-tuple-element.30), channel_id=1, source_target_pairs={{0,1},{1,0},{2,3},{3,2},{4,5},{5,4},{6,7},{7,6},{8,9},{9,8},{10,11... | collective-permute-start | bytes 1966088 | tf_op jit(solution)/shard_map/ppermute | solution.py:267
  38.2 0.0 collective-permute-start.7
  38.2 0.5 collective-permute-start.8
  38.7 1.2 %collective-permute-done.6 = f32[16,5,8,256]{3,2,1,0:T(8,128)S(1)} collective-permute-done((f32[16,5,8,256]{3,2,1,0:T(8,128)S(1)}, f32[16,5,8,256]{3,2,1,0:T(8,128)S(1)}, u32[]{:S(2)}, u32[]{:S(2)}) %collective-permute-start.6) | collective-permute-done | bytes 655392 | tf_op jit(solution)/shard_map/ppermute | solution.py:267
  39.9 0.9 add.117
  40.9 6.8 %all-to-all-start = ((f32[16,5,8,256]{3,2,1,0:T(8,128)}), f32[16,5,8,256]{3,2,1,0:T(8,128)}, u32[]{:S(2)}, u32[]{:S(2)}) async-start(f32[16,5,8,256]{3,2,1,0:T(8,128)} %add.117), calls=%async_computation | async-start | bytes 1310720 | tf_op jit(solution)/shard_map/all_to_all | solution.py:268
  47.7 0.0 collective-permute-done.7
  47.7 0.0 collective-permute-done.8
  47.7 1.3 %maximum_add_fusion = f32[2,512,256]{2,1,0:T(8,128)S(1)} fusion(f32[2,512,256]{2,1,0:T(8,128)S(1)} %get-tuple-element.31, f32[2,512,128]{2,1,0:T(8,128)} %collective-permute-done.8, f32[2,512,128]{2,1,0:T(8,128)} %collective-permute-done.7), kind=kLoop, calls=%fused_computation | loop fusion | flops 524288 | bytes 3145728 | tf_op jit(solution)/shard_map/add | solution.py:270
  49.0 10.3 %all-to-all-done = f32[16,5,8,256]{3,2,1,0:T(8,128)} async-done(((f32[16,5,8,256]{3,2,1,0:T(8,128)}), f32[16,5,8,256]{3,2,1,0:T(8,128)}, u32[]{:S(2)}, u32[]{:S(2)}) %all-to-all-start) | async-done | bytes 655392 | tf_op jit(solution)/shard_map/all_to_all | solution.py:268
  59.4 1.1 %fusion = f32[5,8,256]{2,1,0:T(8,128)S(1)} fusion(f32[16,5,8,256]{3,2,1,0:T(8,128)} %all-to-all-done), kind=kLoop, calls=%fused_computation.9 | loop fusion | flops 153600 | bytes 696320 | tf_op jit(solution)/shard_map/add | solution.py:269
  60.5 6.1 %collective-permute-start.11 = (f32[5,8,256]{2,1,0:T(8,128)S(1)}, f32[5,8,256]{2,1,0:T(8,128)S(1)}, u32[]{:S(2)}, u32[]{:S(2)}) collective-permute-start(f32[5,8,256]{2,1,0:T(8,128)S(1)} %fusion), channel_id=1, source_target_pairs={{0,192},{32,224},{64,128},{96,160},{128,64},{160,96},{192,0},{224,... | collective-permute-start | bytes 122888 | tf_op jit(solution)/shard_map/ppermute | solution.py:274
  66.6 1.0 collective-permute-start.10
  67.6 1.2 %collective-permute-start.9 = (f32[5,8,256]{2,1,0:T(8,128)S(1)}, f32[5,8,256]{2,1,0:T(8,128)S(1)}, u32[]{:S(2)}, u32[]{:S(2)}) collective-permute-start(f32[5,8,256]{2,1,0:T(8,128)S(1)} %fusion), channel_id=1, source_target_pairs={{0,64},{32,96},{64,0},{96,32},{128,192},{160,224},{192,128},{224,1... | collective-permute-start | bytes 122888 | tf_op jit(solution)/shard_map/ppermute | solution.py:274
  68.8 0.1 collective-permute-start.14
  68.9 3.6 %collective-permute-start.13 = (f32[2,128,256]{2,1,0:T(8,128)S(1)}, f32[2,128,256]{2,1,0:T(8,128)S(1)}, u32[]{:S(2)}, u32[]{:S(2)}) collective-permute-start(f32[2,128,256]{2,1,0:T(8,128)S(1)} %get-tuple-element.41), channel_id=1, source_target_pairs={{16,0},{32,16},{48,32},{64,48},{80,64},{96,80},{112,96},{128,112},... | collective-permute-start | bytes 786440 | tf_op jit(solution)/shard_map/ppermute | solution.py:272
  72.5 0.0 collective-permute-done.11
  72.5 1.1 %collective-permute-done.10 = f32[5,8,256]{2,1,0:T(8,128)S(1)} collective-permute-done((f32[5,8,256]{2,1,0:T(8,128)S(1)}, f32[5,8,256]{2,1,0:T(8,128)S(1)}, u32[]{:S(2)}, u32[]{:S(2)}) %collective-permute-start.10) | collective-permute-done | bytes 40992 | tf_op jit(solution)/shard_map/ppermute | solution.py:274
  73.6 0.0 collective-permute-done.9
  73.6 0.6 collective-permute-start.12
  74.3 3.2 %collective-permute-done.12 = f32[5,8,256]{2,1,0:T(8,128)S(1)} collective-permute-done((f32[5,8,256]{2,1,0:T(8,128)S(1)}, f32[5,8,256]{2,1,0:T(8,128)S(1)}, u32[]{:S(2)}, u32[]{:S(2)}) %collective-permute-start.12) | collective-permute-done | bytes 40992 | tf_op jit(solution)/shard_map/ppermute | solution.py:276
  77.5 0.6 collective-permute-done.14
  78.1 3.1 %collective-permute-done.13 = f32[2,128,256]{2,1,0:T(8,128)S(1)} collective-permute-done((f32[2,128,256]{2,1,0:T(8,128)S(1)}, f32[2,128,256]{2,1,0:T(8,128)S(1)}, u32[]{:S(2)}, u32[]{:S(2)}) %collective-permute-start.13) | collective-permute-done | bytes 262176 | tf_op jit(solution)/shard_map/ppermute | solution.py:272
  81.3 15.3 %all_to_all.10.own = f32[16,4,8,256]{3,2,1,0:T(8,128)S(1)} all-to-all(f32[16,4,8,256]{3,2,1,0:T(8,128)S(1)} %broadcast_in_dim.2), channel_id=1, replica_groups=mesh['z'=8,'xl'=2,'xh'=2,'y'=4,'co'=2] {'xh','xl','y'}, dimensions={0} | all-to-all | bytes 1048576 | tf_op jit(solution)/shard_map/all_to_all | solution.py:281
  96.6 3.2 %collective-permute-start.15 = (f32[16,4,8,256]{3,2,1,0:T(8,128)S(1)}, f32[16,4,8,256]{3,2,1,0:T(8,128)S(1)}, u32[]{:S(2)}, u32[]{:S(2)}) collective-permute-start(f32[16,4,8,256]{3,2,1,0:T(8,128)S(1)} %all_to_all.10.own), channel_id=1, source_target_pairs={{0,1},{1,0},{2,3},{3,2},{4,5},{5,4},{6,7},{7,6},{8,9},{9,8},{10,11... | collective-permute-start | bytes 1572872 | tf_op jit(solution)/shard_map/ppermute | solution.py:283
  99.9 0.9 maximum_add_fusion.1
  100.7 0.7 collective-permute-done.15.swapped
  101.4 1.6 %shard_map.78 = f32[2,2,256,256]{3,2,1,0:T(8,128)} custom-call(s32[2]{0:T(128)S(1)} %pad_add_fusion.flags.half, f32[16,4,8,256]{3,2,1,0:T(8,128)S(1)} %all_to_all.10.own, f32[16,4,8,256]{3,2,1,0:T(8,128)S(1)} %collective-permute-done.15.swapped), custom_call_target="tpu_custom_call" | custom-call | tf_op jit(solution)/shard_map/pallas_call | solution.py:235
  (17 shorter events, 0.2 us)
Async XLA Ops:
  0.7 8.8 %copy-start = (f32[2,256,256]{2,1,0:T(8,128)S(1)}, f32[2,256,256]{2,1,0:T(8,128)}, u32[]{:S(2)}) copy-start(f32[2,256,256]{2,1,0:T(8,128)} %tile) | copy-start | bytes 1572868
  1.9 13.6 %collective-permute-start.1 = (f32[2,128,256]{2,1,0:T(8,128)S(1)}, f32[2,128,256]{2,1,0:T(8,128)S(1)}, u32[]{:S(2)}, u32[]{:S(2)}) collective-permute-start(f32[2,128,256]{2,1,0:T(8,128)S(1)} %get-tuple-element.44), channel_id=1, source_target_pairs={{0,16},{16,0},{1,17},{17,1},{2,18},{18,2},{3,19},{19,3},{4,20},{20... | collective-permute-start | bytes 786440 | tf_op jit(solution)/shard_map/ppermute | solution.py:256
  4.0 11.5 %collective-permute-start = (f32[2,128,256]{2,1,0:T(8,128)S(1)}, f32[2,128,256]{2,1,0:T(8,128)S(1)}, u32[]{:S(2)}, u32[]{:S(2)}) collective-permute-start(f32[2,128,256]{2,1,0:T(8,128)S(1)} %get-tuple-element.45), channel_id=1, source_target_pairs={{0,240},{16,32},{32,16},{48,64},{64,48},{80,96},{96,80},{112,128},... | collective-permute-start | bytes 786440 | tf_op jit(solution)/shard_map/ppermute | solution.py:257
  9.6 14.2 %copy-start.3 = (bf16[512,512]{1,0:T(8,128)(2,1)S(1)}, bf16[512,512]{1,0:T(8,128)(2,1)}, u32[]{:S(2)}) copy-start(bf16[512,512]{1,0:T(8,128)(2,1)} %constant.36.clone.bwd_hbm) | copy-start | bytes 1572868
  9.6 14.2 %copy-start.4 = (bf16[512,512]{1,0:T(8,128)(2,1)S(1)}, bf16[512,512]{1,0:T(8,128)(2,1)}, u32[]{:S(2)}) copy-start(bf16[512,512]{1,0:T(8,128)(2,1)} %constant.35.clone.fwd_hbm) | copy-start | bytes 1572868
  9.8 9.0 %collective-permute-start.3 = (f32[2,256,128]{2,1,0:T(8,128)S(1)}, f32[2,256,128]{2,1,0:T(8,128)S(1)}, u32[]{:S(2)}, u32[]{:S(2)}) collective-permute-start(f32[2,256,128]{2,1,0:T(8,128)S(1)} %get-tuple-element.42), channel_id=1, source_target_pairs={{0,15},{1,2},{2,1},{3,4},{4,3},{5,6},{6,5},{7,8},{8,7},{9,10},{10,... | collective-permute-start | bytes 786440 | tf_op jit(solution)/shard_map/ppermute | solution.py:259
  12.3 11.5 %copy-start.1 = (f32[2,2,256,256]{3,2,1,0:T(8,128)S(1)}, f32[2,2,256,256]{3,2,1,0:T(8,128)}, u32[]{:S(2)}) copy-start(f32[2,2,256,256]{3,2,1,0:T(8,128)} %probe.1) | copy-start | bytes 3145732
  12.3 11.5 %copy-start.2 = (f32[4,1,256,256]{3,2,1,0:T(8,128)S(1)}, f32[4,1,256,256]{3,2,1,0:T(8,128)}, u32[]{:S(2)}) copy-start(f32[4,1,256,256]{3,2,1,0:T(8,128)} %amp.1) | copy-start | bytes 3145732
  12.3 6.5 %collective-permute-start.2 = (f32[2,256,128]{2,1,0:T(8,128)S(1)}, f32[2,256,128]{2,1,0:T(8,128)S(1)}, u32[]{:S(2)}, u32[]{:S(2)}) collective-permute-start(f32[2,256,128]{2,1,0:T(8,128)S(1)} %get-tuple-element.43), channel_id=1, source_target_pairs={{0,1},{1,0},{2,3},{3,2},{4,5},{5,4},{6,7},{7,6},{8,9},{9,8},{10,11... | collective-permute-start | bytes 786440 | tf_op jit(solution)/shard_map/ppermute | solution.py:258
  15.7 3.1 %collective-permute-start.4 = (f32[2,2,128,128]{3,2,1,0:T(8,128)S(1)}, f32[2,2,128,128]{3,2,1,0:T(8,128)S(1)}, u32[]{:S(2)}, u32[]{:S(2)}) collective-permute-start(f32[2,2,128,128]{3,2,1,0:T(8,128)S(1)} %pad_maximum_fusion), channel_id=1, source_target_pairs={{0,1},{1,0},{2,3},{3,2},{4,5},{5,4},{6,7},{7,6},{8,9},{9,8},{10,11... | collective-permute-start | bytes 786440 | tf_op jit(solution)/shard_map/ppermute | solution.py:261
  17.6 6.2 %copy-start.5 = (s32[4,1,2]{0,2,1:T(2,128)S(1)}, s32[4,1,2]{0,2,1:T(2,128)}, u32[]{:S(2)}) copy-start(s32[4,1,2]{0,2,1:T(2,128)} %param.9) | copy-start | bytes 100
  17.6 6.2 %collective-permute-start.5 = (f32[2,2,128,128]{3,2,1,0:T(8,128)S(1)}, f32[2,2,128,128]{3,2,1,0:T(8,128)S(1)}, u32[]{:S(2)}, u32[]{:S(2)}) collective-permute-start(f32[2,2,128,128]{3,2,1,0:T(8,128)S(1)} %pad_maximum_fusion.1), channel_id=1, source_target_pairs={{0,15},{1,2},{2,1},{3,4},{4,3},{5,6},{6,5},{7,8},{8,7},{9,10},{10,... | collective-permute-start | bytes 786440 | tf_op jit(solution)/shard_map/ppermute | solution.py:262
  33.6 6.4 %collective-permute-start.6 = (f32[16,5,8,256]{3,2,1,0:T(8,128)S(1)}, f32[16,5,8,256]{3,2,1,0:T(8,128)S(1)}, u32[]{:S(2)}, u32[]{:S(2)}) collective-permute-start(f32[16,5,8,256]{3,2,1,0:T(8,128)S(1)} %get-tuple-element.30), channel_id=1, source_target_pairs={{0,1},{1,0},{2,3},{3,2},{4,5},{5,4},{6,7},{7,6},{8,9},{9,8},{10,11... | collective-permute-start | bytes 1966088 | tf_op jit(solution)/shard_map/ppermute | solution.py:267
  38.2 9.5 %collective-permute-start.7 = (f32[2,512,128]{2,1,0:T(8,128)}, f32[2,512,128]{2,1,0:T(8,128)}, u32[]{:S(2)}, u32[]{:S(2)}) collective-permute-start(f32[2,512,128]{2,1,0:T(8,128)} %get-tuple-element.32), channel_id=1, source_target_pairs={{0,1},{1,2},{2,3},{3,4},{4,5},{5,6},{6,7},{7,8},{8,9},{9,10},{10,1... | collective-permute-start | bytes 1572872 | tf_op jit(solution)/shard_map/ppermute | solution.py:266
  38.2 9.5 %collective-permute-start.8 = (f32[2,512,128]{2,1,0:T(8,128)}, f32[2,512,128]{2,1,0:T(8,128)}, u32[]{:S(2)}, u32[]{:S(2)}) collective-permute-start(f32[2,512,128]{2,1,0:T(8,128)} %get-tuple-element.33), channel_id=1, source_target_pairs={{1,0},{2,1},{3,2},{4,3},{5,4},{6,5},{7,6},{8,7},{9,8},{10,9},{11,1... | collective-permute-start | bytes 1572872 | tf_op jit(solution)/shard_map/ppermute | solution.py:265
  40.9 18.5 %all-to-all-start = ((f32[16,5,8,256]{3,2,1,0:T(8,128)}), f32[16,5,8,256]{3,2,1,0:T(8,128)}, u32[]{:S(2)}, u32[]{:S(2)}) async-start(f32[16,5,8,256]{3,2,1,0:T(8,128)} %add.117), calls=%async_computation | async-start | bytes 1310720 | tf_op jit(solution)/shard_map/all_to_all | solution.py:268
  60.5 12.0 %collective-permute-start.11 = (f32[5,8,256]{2,1,0:T(8,128)S(1)}, f32[5,8,256]{2,1,0:T(8,128)S(1)}, u32[]{:S(2)}, u32[]{:S(2)}) collective-permute-start(f32[5,8,256]{2,1,0:T(8,128)S(1)} %fusion), channel_id=1, source_target_pairs={{0,192},{32,224},{64,128},{96,160},{128,64},{160,96},{192,0},{224,... | collective-permute-start | bytes 122888 | tf_op jit(solution)/shard_map/ppermute | solution.py:274
  66.6 7.0 %collective-permute-start.10 = (f32[5,8,256]{2,1,0:T(8,128)S(1)}, f32[5,8,256]{2,1,0:T(8,128)S(1)}, u32[]{:S(2)}, u32[]{:S(2)}) collective-permute-start(f32[5,8,256]{2,1,0:T(8,128)S(1)} %fusion), channel_id=1, source_target_pairs={{0,128},{32,160},{64,192},{96,224},{128,0},{160,32},{192,64},{224,... | collective-permute-start | bytes 122888 | tf_op jit(solution)/shard_map/ppermute | solution.py:274
  67.6 6.0 %collective-permute-start.9 = (f32[5,8,256]{2,1,0:T(8,128)S(1)}, f32[5,8,256]{2,1,0:T(8,128)S(1)}, u32[]{:S(2)}, u32[]{:S(2)}) collective-permute-start(f32[5,8,256]{2,1,0:T(8,128)S(1)} %fusion), channel_id=1, source_target_pairs={{0,64},{32,96},{64,0},{96,32},{128,192},{160,224},{192,128},{224,1... | collective-permute-start | bytes 122888 | tf_op jit(solution)/shard_map/ppermute | solution.py:274
  68.8 9.3 %collective-permute-start.14 = (f32[2,128,256]{2,1,0:T(8,128)S(1)}, f32[2,128,256]{2,1,0:T(8,128)S(1)}, u32[]{:S(2)}, u32[]{:S(2)}) collective-permute-start(f32[2,128,256]{2,1,0:T(8,128)S(1)} %get-tuple-element.40), channel_id=1, source_target_pairs={{0,16},{16,32},{32,48},{48,64},{64,80},{80,96},{96,112},{112,128},... | collective-permute-start | bytes 786440 | tf_op jit(solution)/shard_map/ppermute | solution.py:273
  68.9 12.3 %collective-permute-start.13 = (f32[2,128,256]{2,1,0:T(8,128)S(1)}, f32[2,128,256]{2,1,0:T(8,128)S(1)}, u32[]{:S(2)}, u32[]{:S(2)}) collective-permute-start(f32[2,128,256]{2,1,0:T(8,128)S(1)} %get-tuple-element.41), channel_id=1, source_target_pairs={{16,0},{32,16},{48,32},{64,48},{80,64},{96,80},{112,96},{128,112},... | collective-permute-start | bytes 786440 | tf_op jit(solution)/shard_map/ppermute | solution.py:272
  73.6 3.8 %collective-permute-start.12 = (f32[5,8,256]{2,1,0:T(8,128)S(1)}, f32[5,8,256]{2,1,0:T(8,128)S(1)}, u32[]{:S(2)}, u32[]{:S(2)}) collective-permute-start(f32[5,8,256]{2,1,0:T(8,128)S(1)} %add_add_fusion), channel_id=1, source_target_pairs={{0,32},{32,0},{64,96},{96,64},{128,160},{160,128},{192,224},{224,1... | collective-permute-start | bytes 122888 | tf_op jit(solution)/shard_map/ppermute | solution.py:276
  96.6 4.8 %collective-permute-start.15 = (f32[16,4,8,256]{3,2,1,0:T(8,128)S(1)}, f32[16,4,8,256]{3,2,1,0:T(8,128)S(1)}, u32[]{:S(2)}, u32[]{:S(2)}) collective-permute-start(f32[16,4,8,256]{3,2,1,0:T(8,128)S(1)} %all_to_all.10.own), channel_id=1, source_target_pairs={{0,1},{1,0},{2,3},{3,2},{4,5},{5,4},{6,7},{7,6},{8,9},{9,8},{10,11... | collective-permute-start | bytes 1572872 | tf_op jit(solution)/shard_map/ppermute | solution.py:283

commit v12 on v11

--- a/solution.py
+++ b/solution.py
@@ -32,12 +32,8 @@
     return fwd, bwd
 
 
-def spot(number, unit):
-    return pl.ds(pl.multiple_of(number * unit, unit), HALF)
-
-
 def kernel(
-    offs, flags, tile, rows_in, rows_out, cols_in, cols_out, ends_in, ends_out, probe, amp, fwd_hbm, bwd_hbm,
+    offs, core, x_low, tile, rows_in, rows_out, cols_in, cols_out, ends_in, ends_out, probe, amp, fwd_hbm, bwd_hbm,
     mine, other, out_left, out_right, out_mid,
     ext, acc, win, stack, side, far, weight, grads, power, fwd, bwd, sems,
 ):
@@ -47,20 +43,29 @@
     ]
     for copy in copies:
         copy.start()
-    co, xl = flags[0], flags[1]
-    q_in, q_out = 3 * (1 - co), 3 * co
-    at_in, at_out = spot(1 - xl, W + HALF), spot(xl, W + HALF)
+    co = core[0]
     middle = pl.ds(HALF, W)
     lanes = lax.broadcasted_iota(jnp.int32, (CH, HALF), 1)
     for q in range(2):
-        cols = pl.ds(q * HALF, HALF)
-        ext[:, q + 1, middle, :] = tile[:, :, cols]
-        ext[:, q + 1, at_in, :] = rows_in[:, :, cols]
-        ext[:, q + 1, at_out, :] = rows_out[:, :, cols]
-    for q, cols, ends in ((q_in, cols_in, ends_in), (q_out, cols_out, ends_out)):
-        ext[:, q, middle, :] = cols[...]
-        ext[:, q, at_out, :] = ends[0]
-        ext[:, q, at_in, :] = ends[1]
+        ext[:, q + 1, middle, :] = tile[:, :, q * HALF : (q + 1) * HALF]
+    before, after = pl.ds(0, HALF), pl.ds(HALF + W, HALF)
+    for x, at_in, at_out in ((0, after, before), (1, before, after)):
+
+        @pl.when(x_low[0] == x)
+        def _():
+            for q in range(2):
+                ext[:, q + 1, at_in, :] = rows_in[:, :, q * HALF : (q + 1) * HALF]
+                ext[:, q + 1, at_out, :] = rows_out[:, :, q * HALF : (q + 1) * HALF]
+
+        for c, q_in, q_out in ((0, 3, 0), (1, 0, 3)):
+
+            @pl.when((x_low[0] == x) & (co == c))
+            def _():
+                for q, cols, ends in ((q_in, cols_in, ends_in), (q_out, cols_out, ends_out)):
+                    ext[:, q, middle, :] = cols[...]
+                    ext[:, q, at_out, :] = ends[0]
+                    ext[:, q, at_in, :] = ends[1]
+
     acc[...] = jnp.zeros_like(acc)
     weight[...] = jnp.zeros_like(weight)
     grads[...] = jnp.zeros_like(grads)
@@ -73,10 +78,8 @@
         power[rows, :] = total
         top_power = jnp.maximum(top_power, total)
     scale = 1.0 / (jnp.max(top_power, axis=(0, 1), keepdims=True) + 1e-06)
-    for copy in copies:
-        copy.wait()
-
-    def position(p, carry):
+
+    def position(p):
         r = offs[0, p] + HALF
         c = offs[1, p] + HALF
         q = c // HALF
@@ -104,6 +107,9 @@
             return carry
 
         lax.fori_loop(0, W // CH, cut, 0, unroll=True)
+        if p == 0:
+            for copy in copies:
+                copy.wait()
         for k in range(MODES):
             rows_f = jnp.dot(fwd[...], stack[k], preferred_element_type=F32)
             side[k, :, 0:W] = rows_f[0:W].astype(BF)
@@ -158,9 +164,9 @@
             return carry
 
         lax.fori_loop(0, W // CH, spread, 0, unroll=True)
-        return carry
-
-    lax.fori_loop(0, POS, position, 0, unroll=True)
+
+    for p in range(POS):
+        position(p)
     for d in range(2):
         for i in range(2 * W // HALF):
             rows = pl.ds(i * HALF, HALF)
@@ -184,7 +190,7 @@
         lax.fori_loop(0, 16, flush, 0)
 
 
-def correct(offsets, flags, border, probe, amplitude):
+def correct(offsets, place, border, probe, amplitude):
     fwd, bwd = dft_matrices()
     vmem = pl.BlockSpec(memory_space=pltpu.VMEM)
     smem = pl.BlockSpec(memory_space=pltpu.SMEM)
@@ -193,7 +199,7 @@
     return pl.pallas_call(
         kernel,
         out_shape=(part, part, strip, strip, jax.ShapeDtypeStruct((2, 2 * W, W), F32)),
-        in_specs=[smem, smem] + [vmem] * 9 + [pl.BlockSpec(memory_space=pl.ANY)] * 2,
+        in_specs=[smem] * 3 + [vmem] * 9 + [pl.BlockSpec(memory_space=pl.ANY)] * 2,
         out_specs=(vmem,) * 5,
         scratch_shapes=[
             pltpu.VMEM((2, 4, 2 * W, HALF), F32),
@@ -210,7 +216,7 @@
             pltpu.SemaphoreType.DMA((2,)),
         ],
         compiler_params=pltpu.CompilerParams(vmem_limit_bytes=20 << 20),
-    )(offsets, flags, *border, probe, amplitude, jnp.asarray(fwd), jnp.asarray(bwd))
+    )(offsets, *place, *border, probe, amplitude, jnp.asarray(fwd), jnp.asarray(bwd))
 
 
 GX = ("z", "xl")
@@ -249,8 +255,8 @@
     half_in, half_out = (1 - co) * HALF, co * HALF
     rows_at_in, rows_at_out = (1 - xl) * HALF, xl * HALF
     scalars = (co, block, half_in, half_out, rows_at_in, rows_at_out)
-    flags = jnp.stack([co, xl])
-    object_field, flags, *scalars = lax.optimization_barrier((object_field, flags, *scalars))
+    place = (co.reshape(1), xl.reshape(1))
+    object_field, place, *scalars = lax.optimization_barrier((object_field, place, *scalars))
     co, block, half_in, half_out, rows_at_in, rows_at_out = scalars
     cut = lax.dynamic_slice_in_dim
     rows_in = lax.ppermute(cut(object_field, rows_at_in, HALF, 1), "xl", NEAR)
@@ -261,7 +267,7 @@
     ends_in = lax.ppermute(jnp.stack([cut(rows, half_in, HALF, 2) for rows in (rows_out, rows_in)]), "co", NEAR)
     ends_out = lax.ppermute(jnp.stack([cut(rows, half_out, HALF, 2) for rows in (rows_out, rows_in)]), GY, FAR)
     border = (object_field, rows_in, rows_out, cols_in, cols_out, ends_in, ends_out)
-    mine, other, out_left, out_right, middle = correct(offs, flags, border, probe_field, amplitude)
+    mine, other, out_left, out_right, middle = correct(offs, place, border, probe_field, amplitude)
     from_right = lax.ppermute(out_left, GY, DOWN)
     from_left = lax.ppermute(out_right, GY, UP)
     part = mine + lax.ppermute(other, "co", NEAR)
@@ -280,7 +286,7 @@
     local = local + (part[: 2 * MODES] - local * weight) / (weight + 1e-05)
     gathered = lax.all_to_all(jnp.broadcast_to(local[None], (16,) + local.shape), group, 0, 0, tiled=True)
     updated_object = folded[:, HALF : HALF + W] + jnp.concatenate([from_above, from_below], 1)
-    updated_probe = arrange(flags, gathered, lax.ppermute(gathered, "co", NEAR))
+    updated_probe = arrange(place[0], gathered, lax.ppermute(gathered, "co", NEAR))
     return (updated_object, updated_probe)
 
 

time: 103 us -> 102 us (level)
  Pallas kernels: 11.4 us -> 10.3 us
  transfers between devices with their start and end apart: 17 -> 17, of which waited for: 8 -> 7; matrix products, arithmetic and copies ran while one was open for 4% -> 4% of each run, Pallas kernels for 0% -> 0%
where the time goes in v12:
time: 102 us
  starting transfers between devices  44.3 us (43%)
  waiting for transfers between devices  25.1 us (25%)
  blocking collectives  15.4 us (15%)
  Pallas kernels  10.3 us (10%)
  other arithmetic  4.27 us (4%)
  local copies, waits for them, and re-layouts  1.68 us (2%)
    all_to_all x1, blocking collectives, body(): lax.all_to_all(jnp.broadcast_to(local[None], (16,) + local.shape), group,...  15.4 us
    all_to_all x1, waiting for transfers between devices, body(): pieces = lax.all_to_all(part, group, 0, 0, tiled=True)  10.3 us
    pallas_call x1, Pallas kernels, correct(): pl.pallas_call(kernel, out_shape=(part, part, strip, strip, jax.ShapeDtyp...  9.22 us
    ppermute x3, starting transfers between devices, body(): lax.ppermute(part, 'z', [(i, i ^ step) for i in range(8)])  8.44 us
    all_to_all x1, starting transfers between devices, body(): pieces = lax.all_to_all(part, group, 0, 0, tiled=True)  6.69 us
    ppermute x1, starting transfers between devices, body(): rows_out = lax.ppermute(cut(object_field, rows_at_out, HALF, 1), GX, FAR)  5.55 us
    ppermute x1, waiting for transfers between devices, body(): lax.ppermute(jnp.stack([cut(rows, half_out, HALF, 2) for rows in (rows_ou...  4.94 us
    ppermute x1, starting transfers between devices, body(): part = mine + lax.ppermute(other, 'co', NEAR)  4.67 us
  transfers between devices with their start and end apart: 17, of which 7 were waited for; matrix products, arithmetic and copies ran while one was open for 4% of the time, Pallas kernels for 0%

profile of v12, /device:TPU:1, one launch (start us, length us, event | category | flops | bytes accessed | tf_op | source)
XLA Modules:
  0.0 101.8 jit_solution(13332036987629745061)
XLA Ops:
  0.6 0.0 copy-start
  0.7 1.2 %constant_dynamic-slice_fusion.2 = (f32[2,128,256]{2,1,0:T(8,128)S(1)}, f32[2,128,256]{2,1,0:T(8,128)S(1)}) fusion(f32[2,256,256]{2,1,0:T(8,128)} %tile, s32[]{:T(128)S(6)} %select_n.20, s32[]{:T(128)S(6)} %select_n.19), kind=kLoop, calls=%fused_computation.30 | loop fusion | bytes 1048584 | tf_op jit(solution)/shard_map/dynamic_slice | solution.py:262
  1.8 2.1 %collective-permute-start.1 = (f32[2,128,256]{2,1,0:T(8,128)S(1)}, f32[2,128,256]{2,1,0:T(8,128)S(1)}, u32[]{:S(2)}, u32[]{:S(2)}) collective-permute-start(f32[2,128,256]{2,1,0:T(8,128)S(1)} %get-tuple-element.46), channel_id=1, source_target_pairs={{0,16},{16,0},{1,17},{17,1},{2,18},{18,2},{3,19},{19,3},{4,20},{20... | collective-permute-start | bytes 786440 | tf_op jit(solution)/shard_map/ppermute | solution.py:262
  3.9 5.5 %collective-permute-start = (f32[2,128,256]{2,1,0:T(8,128)S(1)}, f32[2,128,256]{2,1,0:T(8,128)S(1)}, u32[]{:S(2)}, u32[]{:S(2)}) collective-permute-start(f32[2,128,256]{2,1,0:T(8,128)S(1)} %get-tuple-element.47), channel_id=1, source_target_pairs={{0,240},{16,32},{32,16},{48,64},{64,48},{80,96},{96,80},{112,128},... | collective-permute-start | bytes 786440 | tf_op jit(solution)/shard_map/ppermute | solution.py:263
  9.5 0.0 copy-done
  9.5 0.2 constant_dynamic-slice_fusion
  9.7 2.5 %collective-permute-start.3 = (f32[2,256,128]{2,1,0:T(8,128)S(1)}, f32[2,256,128]{2,1,0:T(8,128)S(1)}, u32[]{:S(2)}, u32[]{:S(2)}) collective-permute-start(f32[2,256,128]{2,1,0:T(8,128)S(1)} %get-tuple-element.44), channel_id=1, source_target_pairs={{0,15},{1,2},{2,1},{3,4},{4,3},{5,6},{6,5},{7,8},{8,7},{9,10},{10,... | collective-permute-start | bytes 786440 | tf_op jit(solution)/shard_map/ppermute | solution.py:265
  12.2 3.2 %collective-permute-start.2 = (f32[2,256,128]{2,1,0:T(8,128)S(1)}, f32[2,256,128]{2,1,0:T(8,128)S(1)}, u32[]{:S(2)}, u32[]{:S(2)}) collective-permute-start(f32[2,256,128]{2,1,0:T(8,128)S(1)} %get-tuple-element.45), channel_id=1, source_target_pairs={{0,1},{1,0},{2,3},{3,2},{4,5},{5,4},{6,7},{7,6},{8,9},{9,8},{10,11... | collective-permute-start | bytes 786440 | tf_op jit(solution)/shard_map/ppermute | solution.py:264
  15.4 0.0 collective-permute-done.1.rows_in
  15.4 0.0 collective-permute-done.rows_out
  15.4 0.2 dynamic-slice_bitcast_fusion
  15.6 1.8 %collective-permute-start.4 = (f32[2,2,128,128]{3,2,1,0:T(8,128)S(1)}, f32[2,2,128,128]{3,2,1,0:T(8,128)S(1)}, u32[]{:S(2)}, u32[]{:S(2)}) collective-permute-start(f32[2,2,128,128]{3,2,1,0:T(8,128)S(1)} %pad_maximum_fusion), channel_id=1, source_target_pairs={{0,1},{1,0},{2,3},{3,2},{4,5},{5,4},{6,7},{7,6},{8,9},{9,8},{10,11... | collective-permute-start | bytes 786440 | tf_op jit(solution)/shard_map/ppermute | solution.py:267
  17.5 0.0 copy-start.5
  17.5 1.2 %collective-permute-start.5 = (f32[2,2,128,128]{3,2,1,0:T(8,128)S(1)}, f32[2,2,128,128]{3,2,1,0:T(8,128)S(1)}, u32[]{:S(2)}, u32[]{:S(2)}) collective-permute-start(f32[2,2,128,128]{3,2,1,0:T(8,128)S(1)} %pad_maximum_fusion.1), channel_id=1, source_target_pairs={{0,15},{1,2},{2,1},{3,4},{4,3},{5,6},{6,5},{7,8},{8,7},{9,10},{10,... | collective-permute-start | bytes 786440 | tf_op jit(solution)/shard_map/ppermute | solution.py:268
  18.7 0.0 collective-permute-done.3.cols_out
  18.7 0.0 collective-permute-done.2.cols_in
  18.7 0.0 collective-permute-done.4.ends_in
  18.7 4.9 %collective-permute-done.5.ends_out = f32[2,2,128,128]{3,2,1,0:T(8,128)S(1)} collective-permute-done((f32[2,2,128,128]{3,2,1,0:T(8,128)S(1)}, f32[2,2,128,128]{3,2,1,0:T(8,128)S(1)}, u32[]{:S(2)}, u32[]{:S(2)}) %collective-permute-start.5) | collective-permute-done | bytes 262176 | tf_op jit(solution)/shard_map/ppermute | solution.py:268
  23.7 0.0 copy-done.3
  23.7 9.2 %shard_map.77 = (f32[16,5,8,256]{3,2,1,0:T(8,128)S(1)}, f32[16,5,8,256]{3,2,1,0:T(8,128)S(1)}, f32[2,512,128]{2,1,0:T(8,128)}, f32[2,512,128]{2,1,0:T(8,128)}, f32[2,512,256]{2,1,0:T(8,128)S(1)}) custom-call(s32[2,4]{1,0:T(2,128)S(1)} %bitcast.21, s32[1]{0:T(128)} %bitcast.2.core.half, s32[1]{0:T(128)} %bitcast.3.x_low, f32[2,256,256]{2,1,0:T(8,128)S(1)} %copy-done, ...), custom_call_target="tpu_custom_call" | custom-call | tf_op jit(solution)/shard_map/pallas_call | solution.py:199
  32.9 4.7 %collective-permute-start.6 = (f32[16,5,8,256]{3,2,1,0:T(8,128)S(1)}, f32[16,5,8,256]{3,2,1,0:T(8,128)S(1)}, u32[]{:S(2)}, u32[]{:S(2)}) collective-permute-start(f32[16,5,8,256]{3,2,1,0:T(8,128)S(1)} %get-tuple-element.32), channel_id=1, source_target_pairs={{0,1},{1,0},{2,3},{3,2},{4,5},{5,4},{6,7},{7,6},{8,9},{9,8},{10,11... | collective-permute-start | bytes 1966088 | tf_op jit(solution)/shard_map/ppermute | solution.py:273
  37.6 0.0 collective-permute-start.7
  37.6 0.5 collective-permute-start.8
  38.1 1.2 %collective-permute-done.6 = f32[16,5,8,256]{3,2,1,0:T(8,128)S(1)} collective-permute-done((f32[16,5,8,256]{3,2,1,0:T(8,128)S(1)}, f32[16,5,8,256]{3,2,1,0:T(8,128)S(1)}, u32[]{:S(2)}, u32[]{:S(2)}) %collective-permute-start.6) | collective-permute-done | bytes 655392 | tf_op jit(solution)/shard_map/ppermute | solution.py:273
  39.3 0.9 add.117
  40.2 6.7 %all-to-all-start = ((f32[16,5,8,256]{3,2,1,0:T(8,128)}), f32[16,5,8,256]{3,2,1,0:T(8,128)}, u32[]{:S(2)}, u32[]{:S(2)}) async-start(f32[16,5,8,256]{3,2,1,0:T(8,128)} %add.117), calls=%async_computation | async-start | bytes 1310720 | tf_op jit(solution)/shard_map/all_to_all | solution.py:274
  46.9 0.0 collective-permute-done.7
  47.0 0.0 collective-permute-done.8
  47.0 1.3 %maximum_add_fusion = f32[2,512,256]{2,1,0:T(8,128)S(1)} fusion(f32[2,512,256]{2,1,0:T(8,128)S(1)} %get-tuple-element.33, f32[2,512,128]{2,1,0:T(8,128)} %collective-permute-done.8, f32[2,512,128]{2,1,0:T(8,128)} %collective-permute-done.7), kind=kLoop, calls=%fused_computation | loop fusion | flops 524288 | bytes 3145728 | tf_op jit(solution)/shard_map/add | solution.py:276
  48.3 10.3 %all-to-all-done = f32[16,5,8,256]{3,2,1,0:T(8,128)} async-done(((f32[16,5,8,256]{3,2,1,0:T(8,128)}), f32[16,5,8,256]{3,2,1,0:T(8,128)}, u32[]{:S(2)}, u32[]{:S(2)}) %all-to-all-start) | async-done | bytes 655392 | tf_op jit(solution)/shard_map/all_to_all | solution.py:274
  58.6 1.1 %fusion = f32[5,8,256]{2,1,0:T(8,128)S(1)} fusion(f32[16,5,8,256]{3,2,1,0:T(8,128)} %all-to-all-done), kind=kLoop, calls=%fused_computation.9 | loop fusion | flops 153600 | bytes 696320 | tf_op jit(solution)/shard_map/add | solution.py:275
  59.7 6.3 %collective-permute-start.11 = (f32[5,8,256]{2,1,0:T(8,128)S(1)}, f32[5,8,256]{2,1,0:T(8,128)S(1)}, u32[]{:S(2)}, u32[]{:S(2)}) collective-permute-start(f32[5,8,256]{2,1,0:T(8,128)S(1)} %fusion), channel_id=1, source_target_pairs={{0,192},{32,224},{64,128},{96,160},{128,64},{160,96},{192,0},{224,... | collective-permute-start | bytes 122888 | tf_op jit(solution)/shard_map/ppermute | solution.py:280
  66.0 1.0 collective-permute-start.10
  66.9 1.2 %collective-permute-start.9 = (f32[5,8,256]{2,1,0:T(8,128)S(1)}, f32[5,8,256]{2,1,0:T(8,128)S(1)}, u32[]{:S(2)}, u32[]{:S(2)}) collective-permute-start(f32[5,8,256]{2,1,0:T(8,128)S(1)} %fusion), channel_id=1, source_target_pairs={{0,64},{32,96},{64,0},{96,32},{128,192},{160,224},{192,128},{224,1... | collective-permute-start | bytes 122888 | tf_op jit(solution)/shard_map/ppermute | solution.py:280
  68.2 0.1 collective-permute-start.14
  68.3 3.6 %collective-permute-start.13 = (f32[2,128,256]{2,1,0:T(8,128)S(1)}, f32[2,128,256]{2,1,0:T(8,128)S(1)}, u32[]{:S(2)}, u32[]{:S(2)}) collective-permute-start(f32[2,128,256]{2,1,0:T(8,128)S(1)} %get-tuple-element.43), channel_id=1, source_target_pairs={{16,0},{32,16},{48,32},{64,48},{80,64},{96,80},{112,96},{128,112},... | collective-permute-start | bytes 786440 | tf_op jit(solution)/shard_map/ppermute | solution.py:278
  71.9 0.0 collective-permute-done.11
  71.9 1.1 %collective-permute-done.10 = f32[5,8,256]{2,1,0:T(8,128)S(1)} collective-permute-done((f32[5,8,256]{2,1,0:T(8,128)S(1)}, f32[5,8,256]{2,1,0:T(8,128)S(1)}, u32[]{:S(2)}, u32[]{:S(2)}) %collective-permute-start.10) | collective-permute-done | bytes 40992 | tf_op jit(solution)/shard_map/ppermute | solution.py:280
  73.0 0.0 collective-permute-done.9
  73.0 0.6 collective-permute-start.12
  73.7 3.4 %collective-permute-done.12 = f32[5,8,256]{2,1,0:T(8,128)S(1)} collective-permute-done((f32[5,8,256]{2,1,0:T(8,128)S(1)}, f32[5,8,256]{2,1,0:T(8,128)S(1)}, u32[]{:S(2)}, u32[]{:S(2)}) %collective-permute-start.12) | collective-permute-done | bytes 40992 | tf_op jit(solution)/shard_map/ppermute | solution.py:282
  77.1 0.0 collective-permute-done.14
  77.1 3.3 %collective-permute-done.13 = f32[2,128,256]{2,1,0:T(8,128)S(1)} collective-permute-done((f32[2,128,256]{2,1,0:T(8,128)S(1)}, f32[2,128,256]{2,1,0:T(8,128)S(1)}, u32[]{:S(2)}, u32[]{:S(2)}) %collective-permute-start.13) | collective-permute-done | bytes 262176 | tf_op jit(solution)/shard_map/ppermute | solution.py:278
  80.5 15.4 %all_to_all.10.own = f32[16,4,8,256]{3,2,1,0:T(8,128)S(1)} all-to-all(f32[16,4,8,256]{3,2,1,0:T(8,128)S(1)} %broadcast_in_dim.2), channel_id=1, replica_groups=mesh['z'=8,'xl'=2,'xh'=2,'y'=4,'co'=2] {'xh','xl','y'}, dimensions={0} | all-to-all | bytes 1048576 | tf_op jit(solution)/shard_map/all_to_all | solution.py:287
  96.0 3.2 %collective-permute-start.15 = (f32[16,4,8,256]{3,2,1,0:T(8,128)S(1)}, f32[16,4,8,256]{3,2,1,0:T(8,128)S(1)}, u32[]{:S(2)}, u32[]{:S(2)}) collective-permute-start(f32[16,4,8,256]{3,2,1,0:T(8,128)S(1)} %all_to_all.10.own), channel_id=1, source_target_pairs={{0,1},{1,0},{2,3},{3,2},{4,5},{5,4},{6,7},{7,6},{8,9},{9,8},{10,11... | collective-permute-start | bytes 1572872 | tf_op jit(solution)/shard_map/ppermute | solution.py:289
  99.2 0.9 maximum_add_fusion.1
  100.1 0.7 collective-permute-done.15.swapped
  100.7 1.0 %shard_map.78 = f32[2,2,256,256]{3,2,1,0:T(8,128)} custom-call(s32[1]{0:T(128)} %bitcast.2.core.half, f32[16,4,8,256]{3,2,1,0:T(8,128)S(1)} %all_to_all.10.own, f32[16,4,8,256]{3,2,1,0:T(8,128)S(1)} %collective-permute-done.15.swapped), custom_call_target="tpu_custom_call" | custom-call | tf_op jit(solution)/shard_map/pallas_call | solution.py:241
  (16 shorter events, 0.2 us)
Async XLA Ops:
  0.6 8.8 %copy-start = (f32[2,256,256]{2,1,0:T(8,128)S(1)}, f32[2,256,256]{2,1,0:T(8,128)}, u32[]{:S(2)}) copy-start(f32[2,256,256]{2,1,0:T(8,128)} %tile) | copy-start | bytes 1572868
  1.8 13.6 %collective-permute-start.1 = (f32[2,128,256]{2,1,0:T(8,128)S(1)}, f32[2,128,256]{2,1,0:T(8,128)S(1)}, u32[]{:S(2)}, u32[]{:S(2)}) collective-permute-start(f32[2,128,256]{2,1,0:T(8,128)S(1)} %get-tuple-element.46), channel_id=1, source_target_pairs={{0,16},{16,0},{1,17},{17,1},{2,18},{18,2},{3,19},{19,3},{4,20},{20... | collective-permute-start | bytes 786440 | tf_op jit(solution)/shard_map/ppermute | solution.py:262
  3.9 11.5 %collective-permute-start = (f32[2,128,256]{2,1,0:T(8,128)S(1)}, f32[2,128,256]{2,1,0:T(8,128)S(1)}, u32[]{:S(2)}, u32[]{:S(2)}) collective-permute-start(f32[2,128,256]{2,1,0:T(8,128)S(1)} %get-tuple-element.47), channel_id=1, source_target_pairs={{0,240},{16,32},{32,16},{48,64},{64,48},{80,96},{96,80},{112,128},... | collective-permute-start | bytes 786440 | tf_op jit(solution)/shard_map/ppermute | solution.py:263
  9.5 14.2 %copy-start.3 = (bf16[512,512]{1,0:T(8,128)(2,1)S(1)}, bf16[512,512]{1,0:T(8,128)(2,1)}, u32[]{:S(2)}) copy-start(bf16[512,512]{1,0:T(8,128)(2,1)} %constant.36.clone.bwd_hbm) | copy-start | bytes 1572868
  9.5 14.2 %copy-start.4 = (bf16[512,512]{1,0:T(8,128)(2,1)S(1)}, bf16[512,512]{1,0:T(8,128)(2,1)}, u32[]{:S(2)}) copy-start(bf16[512,512]{1,0:T(8,128)(2,1)} %constant.35.clone.fwd_hbm) | copy-start | bytes 1572868
  9.7 9.0 %collective-permute-start.3 = (f32[2,256,128]{2,1,0:T(8,128)S(1)}, f32[2,256,128]{2,1,0:T(8,128)S(1)}, u32[]{:S(2)}, u32[]{:S(2)}) collective-permute-start(f32[2,256,128]{2,1,0:T(8,128)S(1)} %get-tuple-element.44), channel_id=1, source_target_pairs={{0,15},{1,2},{2,1},{3,4},{4,3},{5,6},{6,5},{7,8},{8,7},{9,10},{10,... | collective-permute-start | bytes 786440 | tf_op jit(solution)/shard_map/ppermute | solution.py:265
  12.2 11.5 %copy-start.1 = (f32[2,2,256,256]{3,2,1,0:T(8,128)S(1)}, f32[2,2,256,256]{3,2,1,0:T(8,128)}, u32[]{:S(2)}) copy-start(f32[2,2,256,256]{3,2,1,0:T(8,128)} %probe.1) | copy-start | bytes 3145732
  12.2 11.5 %copy-start.2 = (f32[4,1,256,256]{3,2,1,0:T(8,128)S(1)}, f32[4,1,256,256]{3,2,1,0:T(8,128)}, u32[]{:S(2)}) copy-start(f32[4,1,256,256]{3,2,1,0:T(8,128)} %amp.1) | copy-start | bytes 3145732
  12.2 6.5 %collective-permute-start.2 = (f32[2,256,128]{2,1,0:T(8,128)S(1)}, f32[2,256,128]{2,1,0:T(8,128)S(1)}, u32[]{:S(2)}, u32[]{:S(2)}) collective-permute-start(f32[2,256,128]{2,1,0:T(8,128)S(1)} %get-tuple-element.45), channel_id=1, source_target_pairs={{0,1},{1,0},{2,3},{3,2},{4,5},{5,4},{6,7},{7,6},{8,9},{9,8},{10,11... | collective-permute-start | bytes 786440 | tf_op jit(solution)/shard_map/ppermute | solution.py:264
  15.6 3.1 %collective-permute-start.4 = (f32[2,2,128,128]{3,2,1,0:T(8,128)S(1)}, f32[2,2,128,128]{3,2,1,0:T(8,128)S(1)}, u32[]{:S(2)}, u32[]{:S(2)}) collective-permute-start(f32[2,2,128,128]{3,2,1,0:T(8,128)S(1)} %pad_maximum_fusion), channel_id=1, source_target_pairs={{0,1},{1,0},{2,3},{3,2},{4,5},{5,4},{6,7},{7,6},{8,9},{9,8},{10,11... | collective-permute-start | bytes 786440 | tf_op jit(solution)/shard_map/ppermute | solution.py:267
  17.5 6.2 %copy-start.5 = (s32[4,1,2]{0,2,1:T(2,128)S(1)}, s32[4,1,2]{0,2,1:T(2,128)}, u32[]{:S(2)}) copy-start(s32[4,1,2]{0,2,1:T(2,128)} %param.9) | copy-start | bytes 100
  17.5 6.2 %collective-permute-start.5 = (f32[2,2,128,128]{3,2,1,0:T(8,128)S(1)}, f32[2,2,128,128]{3,2,1,0:T(8,128)S(1)}, u32[]{:S(2)}, u32[]{:S(2)}) collective-permute-start(f32[2,2,128,128]{3,2,1,0:T(8,128)S(1)} %pad_maximum_fusion.1), channel_id=1, source_target_pairs={{0,15},{1,2},{2,1},{3,4},{4,3},{5,6},{6,5},{7,8},{8,7},{9,10},{10,... | collective-permute-start | bytes 786440 | tf_op jit(solution)/shard_map/ppermute | solution.py:268
  32.9 6.4 %collective-permute-start.6 = (f32[16,5,8,256]{3,2,1,0:T(8,128)S(1)}, f32[16,5,8,256]{3,2,1,0:T(8,128)S(1)}, u32[]{:S(2)}, u32[]{:S(2)}) collective-permute-start(f32[16,5,8,256]{3,2,1,0:T(8,128)S(1)} %get-tuple-element.32), channel_id=1, source_target_pairs={{0,1},{1,0},{2,3},{3,2},{4,5},{5,4},{6,7},{7,6},{8,9},{9,8},{10,11... | collective-permute-start | bytes 1966088 | tf_op jit(solution)/shard_map/ppermute | solution.py:273
  37.6 9.3 %collective-permute-start.7 = (f32[2,512,128]{2,1,0:T(8,128)}, f32[2,512,128]{2,1,0:T(8,128)}, u32[]{:S(2)}, u32[]{:S(2)}) collective-permute-start(f32[2,512,128]{2,1,0:T(8,128)} %get-tuple-element.34), channel_id=1, source_target_pairs={{0,1},{1,2},{2,3},{3,4},{4,5},{5,6},{6,7},{7,8},{8,9},{9,10},{10,1... | collective-permute-start | bytes 1572872 | tf_op jit(solution)/shard_map/ppermute | solution.py:272
  37.6 9.4 %collective-permute-start.8 = (f32[2,512,128]{2,1,0:T(8,128)}, f32[2,512,128]{2,1,0:T(8,128)}, u32[]{:S(2)}, u32[]{:S(2)}) collective-permute-start(f32[2,512,128]{2,1,0:T(8,128)} %get-tuple-element.35), channel_id=1, source_target_pairs={{1,0},{2,1},{3,2},{4,3},{5,4},{6,5},{7,6},{8,7},{9,8},{10,9},{11,1... | collective-permute-start | bytes 1572872 | tf_op jit(solution)/shard_map/ppermute | solution.py:271
  40.2 18.4 %all-to-all-start = ((f32[16,5,8,256]{3,2,1,0:T(8,128)}), f32[16,5,8,256]{3,2,1,0:T(8,128)}, u32[]{:S(2)}, u32[]{:S(2)}) async-start(f32[16,5,8,256]{3,2,1,0:T(8,128)} %add.117), calls=%async_computation | async-start | bytes 1310720 | tf_op jit(solution)/shard_map/all_to_all | solution.py:274
  59.7 12.1 %collective-permute-start.11 = (f32[5,8,256]{2,1,0:T(8,128)S(1)}, f32[5,8,256]{2,1,0:T(8,128)S(1)}, u32[]{:S(2)}, u32[]{:S(2)}) collective-permute-start(f32[5,8,256]{2,1,0:T(8,128)S(1)} %fusion), channel_id=1, source_target_pairs={{0,192},{32,224},{64,128},{96,160},{128,64},{160,96},{192,0},{224,... | collective-permute-start | bytes 122888 | tf_op jit(solution)/shard_map/ppermute | solution.py:280
  66.0 7.0 %collective-permute-start.10 = (f32[5,8,256]{2,1,0:T(8,128)S(1)}, f32[5,8,256]{2,1,0:T(8,128)S(1)}, u32[]{:S(2)}, u32[]{:S(2)}) collective-permute-start(f32[5,8,256]{2,1,0:T(8,128)S(1)} %fusion), channel_id=1, source_target_pairs={{0,128},{32,160},{64,192},{96,224},{128,0},{160,32},{192,64},{224,... | collective-permute-start | bytes 122888 | tf_op jit(solution)/shard_map/ppermute | solution.py:280
  66.9 6.1 %collective-permute-start.9 = (f32[5,8,256]{2,1,0:T(8,128)S(1)}, f32[5,8,256]{2,1,0:T(8,128)S(1)}, u32[]{:S(2)}, u32[]{:S(2)}) collective-permute-start(f32[5,8,256]{2,1,0:T(8,128)S(1)} %fusion), channel_id=1, source_target_pairs={{0,64},{32,96},{64,0},{96,32},{128,192},{160,224},{192,128},{224,1... | collective-permute-start | bytes 122888 | tf_op jit(solution)/shard_map/ppermute | solution.py:280
  68.2 8.9 %collective-permute-start.14 = (f32[2,128,256]{2,1,0:T(8,128)S(1)}, f32[2,128,256]{2,1,0:T(8,128)S(1)}, u32[]{:S(2)}, u32[]{:S(2)}) collective-permute-start(f32[2,128,256]{2,1,0:T(8,128)S(1)} %get-tuple-element.42), channel_id=1, source_target_pairs={{0,16},{16,32},{32,48},{48,64},{64,80},{80,96},{96,112},{112,128},... | collective-permute-start | bytes 786440 | tf_op jit(solution)/shard_map/ppermute | solution.py:279
  68.3 12.2 %collective-permute-start.13 = (f32[2,128,256]{2,1,0:T(8,128)S(1)}, f32[2,128,256]{2,1,0:T(8,128)S(1)}, u32[]{:S(2)}, u32[]{:S(2)}) collective-permute-start(f32[2,128,256]{2,1,0:T(8,128)S(1)} %get-tuple-element.43), channel_id=1, source_target_pairs={{16,0},{32,16},{48,32},{64,48},{80,64},{96,80},{112,96},{128,112},... | collective-permute-start | bytes 786440 | tf_op jit(solution)/shard_map/ppermute | solution.py:278
  73.0 4.1 %collective-permute-start.12 = (f32[5,8,256]{2,1,0:T(8,128)S(1)}, f32[5,8,256]{2,1,0:T(8,128)S(1)}, u32[]{:S(2)}, u32[]{:S(2)}) collective-permute-start(f32[5,8,256]{2,1,0:T(8,128)S(1)} %add_add_fusion), channel_id=1, source_target_pairs={{0,32},{32,0},{64,96},{96,64},{128,160},{160,128},{192,224},{224,1... | collective-permute-start | bytes 122888 | tf_op jit(solution)/shard_map/ppermute | solution.py:282
  96.0 4.8 %collective-permute-start.15 = (f32[16,4,8,256]{3,2,1,0:T(8,128)S(1)}, f32[16,4,8,256]{3,2,1,0:T(8,128)S(1)}, u32[]{:S(2)}, u32[]{:S(2)}) collective-permute-start(f32[16,4,8,256]{3,2,1,0:T(8,128)S(1)} %all_to_all.10.own), channel_id=1, source_target_pairs={{0,1},{1,0},{2,3},{3,2},{4,5},{5,4},{6,7},{7,6},{8,9},{9,8},{10,11... | collective-permute-start | bytes 1572872 | tf_op jit(solution)/shard_map/ppermute | solution.py:289

commit v13 on v7

--- a/solution.py
+++ b/solution.py
@@ -65,10 +65,8 @@
         power[rows, :] = total
         top_power = jnp.maximum(top_power, total)
     scale = 1.0 / (jnp.max(top_power, axis=(0, 1), keepdims=True) + 1e-06)
-    for copy in copies:
-        copy.wait()
-
-    def position(p, carry):
+
+    def position(p):
         r = offs[0, p] + HALF
         c = offs[1, p] + HALF
         q = c // HALF
@@ -96,6 +94,9 @@
             return carry
 
         lax.fori_loop(0, W // CH, cut, 0, unroll=True)
+        if p == 0:
+            for copy in copies:
+                copy.wait()
         for k in range(MODES):
             rows_f = jnp.dot(fwd[...], stack[k], preferred_element_type=F32)
             side[k, :, 0:W] = rows_f[0:W].astype(BF)
@@ -150,9 +151,9 @@
             return carry
 
         lax.fori_loop(0, W // CH, spread, 0, unroll=True)
-        return carry
-
-    lax.fori_loop(0, POS, position, 0, unroll=True)
+
+    for p in range(POS):
+        position(p)
     for d in range(2):
         for i in range(2 * W // HALF):
             rows = pl.ds(i * HALF, HALF)
@@ -245,6 +246,7 @@
     bot = lax.ppermute(object_field[:, first], GX, DOWN)
     left = lax.ppermute(object_field[:, :, last], GY, UP)
     right = lax.ppermute(object_field[:, :, first], GY, DOWN)
+    bot, top = lax.optimization_barrier((bot, top))
     left_ends = lax.ppermute(jnp.stack([top[:, :, last], bot[:, :, last]]), GY, UP)
     right_ends = lax.ppermute(jnp.stack([top[:, :, first], bot[:, :, first]]), GY, DOWN)
     border = (object_field, top, bot, left, right, left_ends, right_ends)

time: 101 us -> 101 us (level)
  waiting for transfers between devices: 32.7 us -> 30.7 us
  starting transfers between devices: 36.5 us -> 37.9 us
    ppermute x1, starting transfers between devices: 0.01 us -> 2.12 us  [body(): top = lax.ppermute(object_field[:, last], GX, UP)]
    ppermute x1, starting transfers between devices: 7.41 us -> 5.38 us  [body(): bot = lax.ppermute(object_field[:, first], GX, DOWN)]
    ppermute x1, waiting for transfers between devices: 2.63 us -> 1.05 us  [body(): bot = lax.ppermute(object_field[:, first], GX, DOWN)]
    ppermute x3, starting transfers between devices: 6.29 us -> 7.84 us  [body(): lax.ppermute(part, 'z', [(i, i ^ step) for i in range(8)])]
  transfers between devices with their start and end apart: 17 -> 17, of which waited for: 11 -> 10; matrix products, arithmetic and copies ran while one was open for 3% -> 3% of each run, Pallas kernels for 0% -> 0%
where the time goes in v13:
time: 101 us; the launch traced here: 100 us
  starting transfers between devices  37.9 us (38%)
  waiting for transfers between devices  30.7 us (30%)
  blocking collectives  16.2 us (16%)
  Pallas kernels  9.15 us (9%)
  other arithmetic  4.27 us (4%)
  local copies, waits for them, and re-layouts  1.3 us (1%)
    all_to_all x1, blocking collectives, body(): lax.all_to_all(jnp.broadcast_to(local[None], (16,) + local.shape), group,...  16.2 us
    all_to_all x1, waiting for transfers between devices, body(): pieces = lax.all_to_all(part, group, 0, 0, tiled=True)  9.69 us
    pallas_call x1, Pallas kernels, correct(): pl.pallas_call(kernel, out_shape=(part, part, strip, jax.ShapeDtypeStruct...  8.1 us
    ppermute x3, starting transfers between devices, body(): lax.ppermute(part, 'z', [(i, i ^ step) for i in range(8)])  7.84 us
    all_to_all x1, starting transfers between devices, body(): pieces = lax.all_to_all(part, group, 0, 0, tiled=True)  6.92 us
    ppermute x1, starting transfers between devices, body(): bot = lax.ppermute(object_field[:, first], GX, DOWN)  5.38 us
    ppermute x1, waiting for transfers between devices, body(): part = part + lax.ppermute(part, 'z', [(i, i ^ 1) for i in range(8)])  3.88 us
    ppermute x1, waiting for transfers between devices, body(): top = lax.ppermute(object_field[:, last], GX, UP)  3.61 us
  transfers between devices with their start and end apart: 17, of which 10 were waited for; matrix products, arithmetic and copies ran while one was open for 3% of the time, Pallas kernels for 0%

profile of v13, /device:TPU:1, one launch (start us, length us, event | category | flops | bytes accessed | tf_op | source)
XLA Modules:
  0.0 100.4 jit_solution(13970001913330225845)
XLA Ops:
  0.6 0.0 copy-start
  0.7 1.1 %fusion.3 = (f32[2,128,256]{2,1,0:T(8,128)S(1)}, f32[2,128,256]{2,1,0:T(8,128)S(1)}) fusion(f32[2,256,256]{2,1,0:T(8,128)} %tile), kind=kLoop, calls=%fused_computation.30 | loop fusion | bytes 1048576 | tf_op jit(solution)/shard_map/slice | solution.py:245
  1.8 2.1 %collective-permute-start.1 = (f32[2,128,256]{2,1,0:T(8,128)S(1)}, f32[2,128,256]{2,1,0:T(8,128)S(1)}, u32[]{:S(2)}, u32[]{:S(2)}) collective-permute-start(f32[2,128,256]{2,1,0:T(8,128)S(1)} %get-tuple-element.36), channel_id=1, source_target_pairs={{0,16},{16,32},{32,48},{48,64},{64,80},{80,96},{96,112},{112,128},... | collective-permute-start | bytes 786440 | tf_op jit(solution)/shard_map/ppermute | solution.py:245
  3.9 5.4 %collective-permute-start = (f32[2,128,256]{2,1,0:T(8,128)S(1)}, f32[2,128,256]{2,1,0:T(8,128)S(1)}, u32[]{:S(2)}, u32[]{:S(2)}) collective-permute-start(f32[2,128,256]{2,1,0:T(8,128)S(1)} %get-tuple-element.37), channel_id=1, source_target_pairs={{16,0},{32,16},{48,32},{64,48},{80,64},{96,80},{112,96},{128,112},... | collective-permute-start | bytes 786440 | tf_op jit(solution)/shard_map/ppermute | solution.py:246
  9.3 0.0 copy-done
  9.3 1.0 %collective-permute-start.3 = (f32[2,256,128]{2,1,0:T(8,128)S(1)}, f32[2,256,128]{2,1,0:T(8,128)S(1)}, u32[]{:S(2)}, u32[]{:S(2)}) collective-permute-start(f32[2,256,128]{2,1,0:T(8,128)S(1)} %get-tuple-element.34), channel_id=1, source_target_pairs={{1,0},{2,1},{3,2},{4,3},{5,4},{6,5},{7,6},{8,7},{9,8},{10,9},{11,1... | collective-permute-start | bytes 786440 | tf_op jit(solution)/shard_map/ppermute | solution.py:248
  10.4 1.3 %collective-permute-start.2 = (f32[2,256,128]{2,1,0:T(8,128)S(1)}, f32[2,256,128]{2,1,0:T(8,128)S(1)}, u32[]{:S(2)}, u32[]{:S(2)}) collective-permute-start(f32[2,256,128]{2,1,0:T(8,128)S(1)} %get-tuple-element.35), channel_id=1, source_target_pairs={{0,1},{1,2},{2,3},{3,4},{4,5},{5,6},{6,7},{7,8},{8,9},{9,10},{10,1... | collective-permute-start | bytes 786440 | tf_op jit(solution)/shard_map/ppermute | solution.py:247
  11.7 3.6 %collective-permute-done.1.top = f32[2,128,256]{2,1,0:T(8,128)S(1)} collective-permute-done((f32[2,128,256]{2,1,0:T(8,128)S(1)}, f32[2,128,256]{2,1,0:T(8,128)S(1)}, u32[]{:S(2)}, u32[]{:S(2)}) %collective-permute-start.1) | collective-permute-done | bytes 262176 | tf_op jit(solution)/shard_map/ppermute | solution.py:245
  15.3 1.1 %collective-permute-done.bot = f32[2,128,256]{2,1,0:T(8,128)S(1)} collective-permute-done((f32[2,128,256]{2,1,0:T(8,128)S(1)}, f32[2,128,256]{2,1,0:T(8,128)S(1)}, u32[]{:S(2)}, u32[]{:S(2)}) %collective-permute-start) | collective-permute-done | bytes 262176 | tf_op jit(solution)/shard_map/ppermute | solution.py:246
  16.4 3.3 %collective-permute-start.4 = (f32[2,2,128,128]{3,2,1,0:T(8,128)S(1)}, f32[2,2,128,128]{3,2,1,0:T(8,128)S(1)}, u32[]{:S(2)}, u32[]{:S(2)}) collective-permute-start(f32[2,2,128,128]{3,2,1,0:T(8,128)S(1)} %pad_maximum_fusion), channel_id=1, source_target_pairs={{0,1},{1,2},{2,3},{3,4},{4,5},{5,6},{6,7},{7,8},{8,9},{9,10},{10,1... | collective-permute-start | bytes 786440 | tf_op jit(solution)/shard_map/ppermute | solution.py:250
  19.7 0.0 copy-start.5
  19.7 0.1 collective-permute-start.5
  19.8 0.0 collective-permute-done.3.right
  19.8 0.0 collective-permute-done.2.left
  19.9 3.2 %collective-permute-done.4.left_ends = f32[2,2,128,128]{3,2,1,0:T(8,128)S(1)} collective-permute-done((f32[2,2,128,128]{3,2,1,0:T(8,128)S(1)}, f32[2,2,128,128]{3,2,1,0:T(8,128)S(1)}, u32[]{:S(2)}, u32[]{:S(2)}) %collective-permute-start.4) | collective-permute-done | bytes 262176 | tf_op jit(solution)/shard_map/ppermute | solution.py:250
  23.0 2.9 %collective-permute-done.5.right_ends = f32[2,2,128,128]{3,2,1,0:T(8,128)S(1)} collective-permute-done((f32[2,2,128,128]{3,2,1,0:T(8,128)S(1)}, f32[2,2,128,128]{3,2,1,0:T(8,128)S(1)}, u32[]{:S(2)}, u32[]{:S(2)}) %collective-permute-start.5) | collective-permute-done | bytes 262176 | tf_op jit(solution)/shard_map/ppermute | solution.py:251
  25.9 0.0 copy-done.3
  25.9 0.0 copy-done.4
  25.9 0.0 copy-done.1
  25.9 8.1 %shard_map.77 = (f32[16,5,8,256]{3,2,1,0:T(8,128)S(1)}, f32[16,5,8,256]{3,2,1,0:T(8,128)S(1)}, f32[2,512,128]{2,1,0:T(8,128)S(1)}, f32[2,512,256]{2,1,0:T(8,128)S(1)}, f32[2,512,128]{2,1,0:T(8,128)S(1)}) custom-call(s32[2,4]{1,0:T(2,128)S(1)} %bitcast.20, s32[1]{0:T(128)} %bitcast.2.half, f32[2,256,256]{2,1,0:T(8,128)S(1)} %copy-done, ...), custom_call_target="tpu_custom_call" | custom-call | tf_op jit(solution)/shard_map/pallas_call | solution.py:187
  34.1 2.2 %collective-permute-start.6 = (f32[16,5,8,256]{3,2,1,0:T(8,128)S(1)}, f32[16,5,8,256]{3,2,1,0:T(8,128)S(1)}, u32[]{:S(2)}, u32[]{:S(2)}) collective-permute-start(f32[16,5,8,256]{3,2,1,0:T(8,128)S(1)} %get-tuple-element.22), channel_id=1, source_target_pairs={{0,1},{1,0},{2,3},{3,2},{4,5},{5,4},{6,7},{7,6},{8,9},{9,8},{10,11... | collective-permute-start | bytes 1966088 | tf_op jit(solution)/shard_map/ppermute | solution.py:254
  36.2 0.0 collective-permute-start.7
  36.2 0.5 collective-permute-start.8
  36.7 1.2 %collective-permute-done.6 = f32[16,5,8,256]{3,2,1,0:T(8,128)S(1)} collective-permute-done((f32[16,5,8,256]{3,2,1,0:T(8,128)S(1)}, f32[16,5,8,256]{3,2,1,0:T(8,128)S(1)}, u32[]{:S(2)}, u32[]{:S(2)}) %collective-permute-start.6) | collective-permute-done | bytes 655392 | tf_op jit(solution)/shard_map/ppermute | solution.py:254
  37.9 0.9 add.97
  38.9 6.9 %all-to-all-start = ((f32[16,5,8,256]{3,2,1,0:T(8,128)}), f32[16,5,8,256]{3,2,1,0:T(8,128)}, u32[]{:S(2)}, u32[]{:S(2)}) async-start(f32[16,5,8,256]{3,2,1,0:T(8,128)} %add.97), calls=%async_computation | async-start | bytes 1310720 | tf_op jit(solution)/shard_map/all_to_all | solution.py:257
  45.8 0.0 collective-permute-done.7
  45.8 0.0 collective-permute-done.8
  45.8 1.3 %maximum_add_fusion = f32[2,512,256]{2,1,0:T(8,128)S(1)} fusion(f32[2,512,256]{2,1,0:T(8,128)S(1)} %get-tuple-element.23, f32[2,512,128]{2,1,0:T(8,128)} %collective-permute-done.8, f32[2,512,128]{2,1,0:T(8,128)} %collective-permute-done.7), kind=kLoop, calls=%fused_computation | loop fusion | flops 524288 | bytes 3145728 | tf_op jit(solution)/shard_map/add | solution.py:259
  47.1 9.7 %all-to-all-done = f32[16,5,8,256]{3,2,1,0:T(8,128)} async-done(((f32[16,5,8,256]{3,2,1,0:T(8,128)}), f32[16,5,8,256]{3,2,1,0:T(8,128)}, u32[]{:S(2)}, u32[]{:S(2)}) %all-to-all-start) | async-done | bytes 655392 | tf_op jit(solution)/shard_map/all_to_all | solution.py:257
  56.8 1.1 %fusion = f32[5,8,256]{2,1,0:T(8,128)S(1)} fusion(f32[16,5,8,256]{3,2,1,0:T(8,128)} %all-to-all-done), kind=kLoop, calls=%fused_computation.9 | loop fusion | flops 153600 | bytes 696320 | tf_op jit(solution)/shard_map/add | solution.py:258
  57.9 5.7 %collective-permute-start.11 = (f32[5,8,256]{2,1,0:T(8,128)S(1)}, f32[5,8,256]{2,1,0:T(8,128)S(1)}, u32[]{:S(2)}, u32[]{:S(2)}) collective-permute-start(f32[5,8,256]{2,1,0:T(8,128)S(1)} %fusion), channel_id=1, source_target_pairs={{0,192},{32,224},{64,128},{96,160},{128,64},{160,96},{192,0},{224,... | collective-permute-start | bytes 122888 | tf_op jit(solution)/shard_map/ppermute | solution.py:263
  63.6 1.9 %collective-permute-start.10 = (f32[5,8,256]{2,1,0:T(8,128)S(1)}, f32[5,8,256]{2,1,0:T(8,128)S(1)}, u32[]{:S(2)}, u32[]{:S(2)}) collective-permute-start(f32[5,8,256]{2,1,0:T(8,128)S(1)} %fusion), channel_id=1, source_target_pairs={{0,128},{32,160},{64,192},{96,224},{128,0},{160,32},{192,64},{224,... | collective-permute-start | bytes 122888 | tf_op jit(solution)/shard_map/ppermute | solution.py:263
  65.5 0.3 collective-permute-start.9
  65.8 0.1 collective-permute-start.14
  65.9 3.6 %collective-permute-start.13 = (f32[2,128,256]{2,1,0:T(8,128)S(1)}, f32[2,128,256]{2,1,0:T(8,128)S(1)}, u32[]{:S(2)}, u32[]{:S(2)}) collective-permute-start(f32[2,128,256]{2,1,0:T(8,128)S(1)} %get-tuple-element.33), channel_id=1, source_target_pairs={{16,0},{32,16},{48,32},{64,48},{80,64},{96,80},{112,96},{128,112},... | collective-permute-start | bytes 786440 | tf_op jit(solution)/shard_map/ppermute | solution.py:261
  69.5 0.0 collective-permute-done.11
  69.5 1.3 %collective-permute-done.10 = f32[5,8,256]{2,1,0:T(8,128)S(1)} collective-permute-done((f32[5,8,256]{2,1,0:T(8,128)S(1)}, f32[5,8,256]{2,1,0:T(8,128)S(1)}, u32[]{:S(2)}, u32[]{:S(2)}) %collective-permute-start.10) | collective-permute-done | bytes 40992 | tf_op jit(solution)/shard_map/ppermute | solution.py:263
  70.8 0.0 collective-permute-done.9
  70.8 0.4 collective-permute-start.12
  71.2 3.9 %collective-permute-done.12 = f32[5,8,256]{2,1,0:T(8,128)S(1)} collective-permute-done((f32[5,8,256]{2,1,0:T(8,128)S(1)}, f32[5,8,256]{2,1,0:T(8,128)S(1)}, u32[]{:S(2)}, u32[]{:S(2)}) %collective-permute-start.12) | collective-permute-done | bytes 40992 | tf_op jit(solution)/shard_map/ppermute | solution.py:265
  75.1 0.0 collective-permute-done.14
  75.1 3.2 %collective-permute-done.13 = f32[2,128,256]{2,1,0:T(8,128)S(1)} collective-permute-done((f32[2,128,256]{2,1,0:T(8,128)S(1)}, f32[2,128,256]{2,1,0:T(8,128)S(1)}, u32[]{:S(2)}, u32[]{:S(2)}) %collective-permute-start.13) | collective-permute-done | bytes 262176 | tf_op jit(solution)/shard_map/ppermute | solution.py:261
  78.4 16.2 %all_to_all.10.own = f32[16,4,8,256]{3,2,1,0:T(8,128)S(1)} all-to-all(f32[16,4,8,256]{3,2,1,0:T(8,128)S(1)} %broadcast_in_dim.2), channel_id=1, replica_groups=mesh['z'=8,'xl'=2,'xh'=2,'y'=4,'co'=2] {'xh','xl','y'}, dimensions={0} | all-to-all | bytes 1048576 | tf_op jit(solution)/shard_map/all_to_all | solution.py:271
  94.6 3.2 %collective-permute-start.15 = (f32[16,4,8,256]{3,2,1,0:T(8,128)S(1)}, f32[16,4,8,256]{3,2,1,0:T(8,128)S(1)}, u32[]{:S(2)}, u32[]{:S(2)}) collective-permute-start(f32[16,4,8,256]{3,2,1,0:T(8,128)S(1)} %all_to_all.10.own), channel_id=1, source_target_pairs={{0,1},{1,0},{2,3},{3,2},{4,5},{5,4},{6,7},{7,6},{8,9},{9,8},{10,11... | collective-permute-start | bytes 1572872 | tf_op jit(solution)/shard_map/ppermute | solution.py:273
  97.8 0.9 maximum_add_fusion.1
  98.7 0.7 collective-permute-done.15.swapped
  99.4 1.0 %shard_map.78 = f32[2,2,256,256]{3,2,1,0:T(8,128)} custom-call(s32[1]{0:T(128)} %bitcast.2.half, f32[16,4,8,256]{3,2,1,0:T(8,128)S(1)} %all_to_all.10.own, f32[16,4,8,256]{3,2,1,0:T(8,128)S(1)} %collective-permute-done.15.swapped), custom_call_target="tpu_custom_call" | custom-call | tf_op jit(solution)/shard_map/pallas_call | solution.py:228
  (16 shorter events, 0.2 us)
Async XLA Ops:
  0.6 8.6 %copy-start = (f32[2,256,256]{2,1,0:T(8,128)S(1)}, f32[2,256,256]{2,1,0:T(8,128)}, u32[]{:S(2)}) copy-start(f32[2,256,256]{2,1,0:T(8,128)} %tile) | copy-start | bytes 1572868
  1.8 13.5 %collective-permute-start.1 = (f32[2,128,256]{2,1,0:T(8,128)S(1)}, f32[2,128,256]{2,1,0:T(8,128)S(1)}, u32[]{:S(2)}, u32[]{:S(2)}) collective-permute-start(f32[2,128,256]{2,1,0:T(8,128)S(1)} %get-tuple-element.36), channel_id=1, source_target_pairs={{0,16},{16,32},{32,48},{48,64},{64,80},{80,96},{96,112},{112,128},... | collective-permute-start | bytes 786440 | tf_op jit(solution)/shard_map/ppermute | solution.py:245
  3.9 12.4 %collective-permute-start = (f32[2,128,256]{2,1,0:T(8,128)S(1)}, f32[2,128,256]{2,1,0:T(8,128)S(1)}, u32[]{:S(2)}, u32[]{:S(2)}) collective-permute-start(f32[2,128,256]{2,1,0:T(8,128)S(1)} %get-tuple-element.37), channel_id=1, source_target_pairs={{16,0},{32,16},{48,32},{64,48},{80,64},{96,80},{112,96},{128,112},... | collective-permute-start | bytes 786440 | tf_op jit(solution)/shard_map/ppermute | solution.py:246
  9.3 16.6 %copy-start.3 = (bf16[512,512]{1,0:T(8,128)(2,1)S(1)}, bf16[512,512]{1,0:T(8,128)(2,1)}, u32[]{:S(2)}) copy-start(bf16[512,512]{1,0:T(8,128)(2,1)} %constant.32.clone.bwd_hbm) | copy-start | bytes 1572868
  9.3 16.6 %copy-start.4 = (bf16[512,512]{1,0:T(8,128)(2,1)S(1)}, bf16[512,512]{1,0:T(8,128)(2,1)}, u32[]{:S(2)}) copy-start(bf16[512,512]{1,0:T(8,128)(2,1)} %constant.31.clone.fwd_hbm) | copy-start | bytes 1572868
  9.3 10.5 %collective-permute-start.3 = (f32[2,256,128]{2,1,0:T(8,128)S(1)}, f32[2,256,128]{2,1,0:T(8,128)S(1)}, u32[]{:S(2)}, u32[]{:S(2)}) collective-permute-start(f32[2,256,128]{2,1,0:T(8,128)S(1)} %get-tuple-element.34), channel_id=1, source_target_pairs={{1,0},{2,1},{3,2},{4,3},{5,4},{6,5},{7,6},{8,7},{9,8},{10,9},{11,1... | collective-permute-start | bytes 786440 | tf_op jit(solution)/shard_map/ppermute | solution.py:248
  10.4 15.6 %copy-start.1 = (f32[2,2,256,256]{3,2,1,0:T(8,128)S(1)}, f32[2,2,256,256]{3,2,1,0:T(8,128)}, u32[]{:S(2)}) copy-start(f32[2,2,256,256]{3,2,1,0:T(8,128)} %probe.1) | copy-start | bytes 3145732
  10.4 15.6 %copy-start.2 = (f32[4,1,256,256]{3,2,1,0:T(8,128)S(1)}, f32[4,1,256,256]{3,2,1,0:T(8,128)}, u32[]{:S(2)}) copy-start(f32[4,1,256,256]{3,2,1,0:T(8,128)} %amp.1) | copy-start | bytes 3145732
  10.4 9.5 %collective-permute-start.2 = (f32[2,256,128]{2,1,0:T(8,128)S(1)}, f32[2,256,128]{2,1,0:T(8,128)S(1)}, u32[]{:S(2)}, u32[]{:S(2)}) collective-permute-start(f32[2,256,128]{2,1,0:T(8,128)S(1)} %get-tuple-element.35), channel_id=1, source_target_pairs={{0,1},{1,2},{2,3},{3,4},{4,5},{5,6},{6,7},{7,8},{8,9},{9,10},{10,1... | collective-permute-start | bytes 786440 | tf_op jit(solution)/shard_map/ppermute | solution.py:247
  16.4 6.6 %collective-permute-start.4 = (f32[2,2,128,128]{3,2,1,0:T(8,128)S(1)}, f32[2,2,128,128]{3,2,1,0:T(8,128)S(1)}, u32[]{:S(2)}, u32[]{:S(2)}) collective-permute-start(f32[2,2,128,128]{3,2,1,0:T(8,128)S(1)} %pad_maximum_fusion), channel_id=1, source_target_pairs={{0,1},{1,2},{2,3},{3,4},{4,5},{5,6},{6,7},{7,8},{8,9},{9,10},{10,1... | collective-permute-start | bytes 786440 | tf_op jit(solution)/shard_map/ppermute | solution.py:250
  19.7 6.2 %copy-start.5 = (s32[4,1,2]{0,2,1:T(2,128)S(1)}, s32[4,1,2]{0,2,1:T(2,128)}, u32[]{:S(2)}) copy-start(s32[4,1,2]{0,2,1:T(2,128)} %param.9) | copy-start | bytes 100
  19.7 6.2 %collective-permute-start.5 = (f32[2,2,128,128]{3,2,1,0:T(8,128)S(1)}, f32[2,2,128,128]{3,2,1,0:T(8,128)S(1)}, u32[]{:S(2)}, u32[]{:S(2)}) collective-permute-start(f32[2,2,128,128]{3,2,1,0:T(8,128)S(1)} %pad_maximum_fusion.1), channel_id=1, source_target_pairs={{1,0},{2,1},{3,2},{4,3},{5,4},{6,5},{7,6},{8,7},{9,8},{10,9},{11,1... | collective-permute-start | bytes 786440 | tf_op jit(solution)/shard_map/ppermute | solution.py:251
  34.1 3.9 %collective-permute-start.6 = (f32[16,5,8,256]{3,2,1,0:T(8,128)S(1)}, f32[16,5,8,256]{3,2,1,0:T(8,128)S(1)}, u32[]{:S(2)}, u32[]{:S(2)}) collective-permute-start(f32[16,5,8,256]{3,2,1,0:T(8,128)S(1)} %get-tuple-element.22), channel_id=1, source_target_pairs={{0,1},{1,0},{2,3},{3,2},{4,5},{5,4},{6,7},{7,6},{8,9},{9,8},{10,11... | collective-permute-start | bytes 1966088 | tf_op jit(solution)/shard_map/ppermute | solution.py:254
  36.2 9.6 %collective-permute-start.7 = (f32[2,512,128]{2,1,0:T(8,128)S(1)}, f32[2,512,128]{2,1,0:T(8,128)}, u32[]{:S(2)}, u32[]{:S(2)}) collective-permute-start(f32[2,512,128]{2,1,0:T(8,128)S(1)} %get-tuple-element.24), channel_id=1, source_target_pairs={{0,1},{1,2},{2,3},{3,4},{4,5},{5,6},{6,7},{7,8},{8,9},{9,10},{10,1... | collective-permute-start | bytes 1572872 | tf_op jit(solution)/shard_map/ppermute | solution.py:256
  36.2 9.6 %collective-permute-start.8 = (f32[2,512,128]{2,1,0:T(8,128)S(1)}, f32[2,512,128]{2,1,0:T(8,128)}, u32[]{:S(2)}, u32[]{:S(2)}) collective-permute-start(f32[2,512,128]{2,1,0:T(8,128)S(1)} %get-tuple-element.25), channel_id=1, source_target_pairs={{1,0},{2,1},{3,2},{4,3},{5,4},{6,5},{7,6},{8,7},{9,8},{10,9},{11,1... | collective-permute-start | bytes 1572872 | tf_op jit(solution)/shard_map/ppermute | solution.py:255
  38.9 18.0 %all-to-all-start = ((f32[16,5,8,256]{3,2,1,0:T(8,128)}), f32[16,5,8,256]{3,2,1,0:T(8,128)}, u32[]{:S(2)}, u32[]{:S(2)}) async-start(f32[16,5,8,256]{3,2,1,0:T(8,128)} %add.97), calls=%async_computation | async-start | bytes 1310720 | tf_op jit(solution)/shard_map/all_to_all | solution.py:257
  57.9 11.5 %collective-permute-start.11 = (f32[5,8,256]{2,1,0:T(8,128)S(1)}, f32[5,8,256]{2,1,0:T(8,128)S(1)}, u32[]{:S(2)}, u32[]{:S(2)}) collective-permute-start(f32[5,8,256]{2,1,0:T(8,128)S(1)} %fusion), channel_id=1, source_target_pairs={{0,192},{32,224},{64,128},{96,160},{128,64},{160,96},{192,0},{224,... | collective-permute-start | bytes 122888 | tf_op jit(solution)/shard_map/ppermute | solution.py:263
  63.6 7.2 %collective-permute-start.10 = (f32[5,8,256]{2,1,0:T(8,128)S(1)}, f32[5,8,256]{2,1,0:T(8,128)S(1)}, u32[]{:S(2)}, u32[]{:S(2)}) collective-permute-start(f32[5,8,256]{2,1,0:T(8,128)S(1)} %fusion), channel_id=1, source_target_pairs={{0,128},{32,160},{64,192},{96,224},{128,0},{160,32},{192,64},{224,... | collective-permute-start | bytes 122888 | tf_op jit(solution)/shard_map/ppermute | solution.py:263
  65.5 5.3 %collective-permute-start.9 = (f32[5,8,256]{2,1,0:T(8,128)S(1)}, f32[5,8,256]{2,1,0:T(8,128)S(1)}, u32[]{:S(2)}, u32[]{:S(2)}) collective-permute-start(f32[5,8,256]{2,1,0:T(8,128)S(1)} %fusion), channel_id=1, source_target_pairs={{0,64},{32,96},{64,0},{96,32},{128,192},{160,224},{192,128},{224,1... | collective-permute-start | bytes 122888 | tf_op jit(solution)/shard_map/ppermute | solution.py:263
  65.8 9.3 %collective-permute-start.14 = (f32[2,128,256]{2,1,0:T(8,128)S(1)}, f32[2,128,256]{2,1,0:T(8,128)S(1)}, u32[]{:S(2)}, u32[]{:S(2)}) collective-permute-start(f32[2,128,256]{2,1,0:T(8,128)S(1)} %get-tuple-element.32), channel_id=1, source_target_pairs={{0,16},{16,32},{32,48},{48,64},{64,80},{80,96},{96,112},{112,128},... | collective-permute-start | bytes 786440 | tf_op jit(solution)/shard_map/ppermute | solution.py:262
  65.9 12.4 %collective-permute-start.13 = (f32[2,128,256]{2,1,0:T(8,128)S(1)}, f32[2,128,256]{2,1,0:T(8,128)S(1)}, u32[]{:S(2)}, u32[]{:S(2)}) collective-permute-start(f32[2,128,256]{2,1,0:T(8,128)S(1)} %get-tuple-element.33), channel_id=1, source_target_pairs={{16,0},{32,16},{48,32},{64,48},{80,64},{96,80},{112,96},{128,112},... | collective-permute-start | bytes 786440 | tf_op jit(solution)/shard_map/ppermute | solution.py:261
  70.8 4.3 %collective-permute-start.12 = (f32[5,8,256]{2,1,0:T(8,128)S(1)}, f32[5,8,256]{2,1,0:T(8,128)S(1)}, u32[]{:S(2)}, u32[]{:S(2)}) collective-permute-start(f32[5,8,256]{2,1,0:T(8,128)S(1)} %add_add_fusion), channel_id=1, source_target_pairs={{0,32},{32,0},{64,96},{96,64},{128,160},{160,128},{192,224},{224,1... | collective-permute-start | bytes 122888 | tf_op jit(solution)/shard_map/ppermute | solution.py:265
  94.6 4.8 %collective-permute-start.15 = (f32[16,4,8,256]{3,2,1,0:T(8,128)S(1)}, f32[16,4,8,256]{3,2,1,0:T(8,128)S(1)}, u32[]{:S(2)}, u32[]{:S(2)}) collective-permute-start(f32[16,4,8,256]{3,2,1,0:T(8,128)S(1)} %all_to_all.10.own), channel_id=1, source_target_pairs={{0,1},{1,0},{2,3},{3,2},{4,5},{5,4},{6,7},{7,6},{8,9},{9,8},{10,11... | collective-permute-start | bytes 1572872 | tf_op jit(solution)/shard_map/ppermute | solution.py:273

commit v14 on v13

--- a/solution.py
+++ b/solution.py
@@ -260,9 +260,9 @@
     part, folded = lax.optimization_barrier((part, folded))
     from_below = lax.ppermute(folded[:, :HALF], GX, DOWN)
     from_above = lax.ppermute(folded[:, HALF + W :], GX, UP)
-    peers = [lax.ppermute(part, "z", [(i, i ^ step) for i in range(8)]) for step in (2, 4, 6)]
+    peers = [lax.ppermute(part, "z", [(i, i ^ step) for i in range(8)]) for step in (1, 2, 3)]
     part = (part + peers[0]) + (peers[1] + peers[2])
-    part = part + lax.ppermute(part, "z", [(i, i ^ 1) for i in range(8)])
+    part = part + lax.ppermute(part, "z", [(i, i ^ 4) for i in range(8)])
     part, from_below, from_above = lax.optimization_barrier((part, from_below, from_above))
     planes = probe_field.reshape(2 * MODES, W, W)
     local = lax.dynamic_slice_in_dim(planes, block, 8, 1)

time: 101 us -> 97.2 us (0.962)
  waiting for transfers between devices: 30.7 us -> 25 us
  starting transfers between devices: 37.9 us -> 41.5 us
  blocking collectives: 16.2 us -> 14.8 us
    ppermute x1, starting transfers between devices: 0.38 us -> 6.4 us  [body(): part = part + lax.ppermute(part, 'z', [(i, i ^ 4) for i in range(8)])]
    ppermute x3, starting transfers between devices: 7.84 us -> 4.29 us  [body(): lax.ppermute(part, 'z', [(i, i ^ step) for i in range(8)])]
    ppermute x1, waiting for transfers between devices: 3.88 us -> 1.39 us  [body(): part = part + lax.ppermute(part, 'z', [(i, i ^ 4) for i in range(8)])]
    ppermute x1, waiting for transfers between devices: 3.2 us -> 1.32 us  [body(): from_below = lax.ppermute(folded[:, :HALF], GX, DOWN)]
    all_to_all x1, blocking collectives: 16.2 us -> 14.8 us  [body(): lax.all_to_all(jnp.broadcast_to(local[None], (16,) + local.shape), group,...]
    ppermute x3, waiting for transfers between devices: 1.34 us -> 0.01 us  [body(): lax.ppermute(part, 'z', [(i, i ^ step) for i in range(8)])]
  transfers between devices with their start and end apart: 17 -> 17, of which waited for: 10 -> 9; matrix products, arithmetic and copies ran while one was open for 3% -> 3% of each run, Pallas kernels for 0% -> 0%
where the time goes in v14:
time: 97.2 us; the launch traced here: 96.9 us
  starting transfers between devices  41.5 us (43%)
  waiting for transfers between devices  25 us (26%)
  blocking collectives  14.8 us (15%)
  Pallas kernels  9.21 us (9%)
  other arithmetic  4.28 us (4%)
  local copies, waits for them, and re-layouts  1.3 us (1%)
    all_to_all x1, blocking collectives, body(): lax.all_to_all(jnp.broadcast_to(local[None], (16,) + local.shape), group,...  14.8 us
    all_to_all x1, waiting for transfers between devices, body(): pieces = lax.all_to_all(part, group, 0, 0, tiled=True)  9.69 us
    pallas_call x1, Pallas kernels, correct(): pl.pallas_call(kernel, out_shape=(part, part, strip, jax.ShapeDtypeStruct...  8.17 us
    all_to_all x1, starting transfers between devices, body(): pieces = lax.all_to_all(part, group, 0, 0, tiled=True)  6.91 us
    ppermute x1, starting transfers between devices, body(): part = part + lax.ppermute(part, 'z', [(i, i ^ 4) for i in range(8)])  6.4 us
    ppermute x1, starting transfers between devices, body(): bot = lax.ppermute(object_field[:, first], GX, DOWN)  5.38 us
    ppermute x3, starting transfers between devices, body(): lax.ppermute(part, 'z', [(i, i ^ step) for i in range(8)])  4.29 us
    ppermute x1, starting transfers between devices, body(): updated_probe = arrange(half, gathered, lax.ppermute(gathered, 'co', SWAP))  4.02 us
  transfers between devices with their start and end apart: 17, of which 9 were waited for; matrix products, arithmetic and copies ran while one was open for 3% of the time, Pallas kernels for 0%

profile of v14, /device:TPU:1, one launch (start us, length us, event | category | flops | bytes accessed | tf_op | source)
XLA Modules:
  0.0 96.9 jit_solution(362004309114764507)
XLA Ops:
  0.6 0.0 copy-start
  0.7 1.1 %fusion.3 = (f32[2,128,256]{2,1,0:T(8,128)S(1)}, f32[2,128,256]{2,1,0:T(8,128)S(1)}) fusion(f32[2,256,256]{2,1,0:T(8,128)} %tile), kind=kLoop, calls=%fused_computation.30 | loop fusion | bytes 1048576 | tf_op jit(solution)/shard_map/slice | solution.py:245
  1.8 2.1 %collective-permute-start.1 = (f32[2,128,256]{2,1,0:T(8,128)S(1)}, f32[2,128,256]{2,1,0:T(8,128)S(1)}, u32[]{:S(2)}, u32[]{:S(2)}) collective-permute-start(f32[2,128,256]{2,1,0:T(8,128)S(1)} %get-tuple-element.36), channel_id=1, source_target_pairs={{0,16},{16,32},{32,48},{48,64},{64,80},{80,96},{96,112},{112,128},... | collective-permute-start | bytes 786440 | tf_op jit(solution)/shard_map/ppermute | solution.py:245
  3.9 5.4 %collective-permute-start = (f32[2,128,256]{2,1,0:T(8,128)S(1)}, f32[2,128,256]{2,1,0:T(8,128)S(1)}, u32[]{:S(2)}, u32[]{:S(2)}) collective-permute-start(f32[2,128,256]{2,1,0:T(8,128)S(1)} %get-tuple-element.37), channel_id=1, source_target_pairs={{16,0},{32,16},{48,32},{64,48},{80,64},{96,80},{112,96},{128,112},... | collective-permute-start | bytes 786440 | tf_op jit(solution)/shard_map/ppermute | solution.py:246
  9.3 0.0 copy-done
  9.3 1.0 %collective-permute-start.3 = (f32[2,256,128]{2,1,0:T(8,128)S(1)}, f32[2,256,128]{2,1,0:T(8,128)S(1)}, u32[]{:S(2)}, u32[]{:S(2)}) collective-permute-start(f32[2,256,128]{2,1,0:T(8,128)S(1)} %get-tuple-element.34), channel_id=1, source_target_pairs={{1,0},{2,1},{3,2},{4,3},{5,4},{6,5},{7,6},{8,7},{9,8},{10,9},{11,1... | collective-permute-start | bytes 786440 | tf_op jit(solution)/shard_map/ppermute | solution.py:248
  10.4 1.3 %collective-permute-start.2 = (f32[2,256,128]{2,1,0:T(8,128)S(1)}, f32[2,256,128]{2,1,0:T(8,128)S(1)}, u32[]{:S(2)}, u32[]{:S(2)}) collective-permute-start(f32[2,256,128]{2,1,0:T(8,128)S(1)} %get-tuple-element.35), channel_id=1, source_target_pairs={{0,1},{1,2},{2,3},{3,4},{4,5},{5,6},{6,7},{7,8},{8,9},{9,10},{10,1... | collective-permute-start | bytes 786440 | tf_op jit(solution)/shard_map/ppermute | solution.py:247
  11.7 3.6 %collective-permute-done.1.top = f32[2,128,256]{2,1,0:T(8,128)S(1)} collective-permute-done((f32[2,128,256]{2,1,0:T(8,128)S(1)}, f32[2,128,256]{2,1,0:T(8,128)S(1)}, u32[]{:S(2)}, u32[]{:S(2)}) %collective-permute-start.1) | collective-permute-done | bytes 262176 | tf_op jit(solution)/shard_map/ppermute | solution.py:245
  15.3 1.1 %collective-permute-done.bot = f32[2,128,256]{2,1,0:T(8,128)S(1)} collective-permute-done((f32[2,128,256]{2,1,0:T(8,128)S(1)}, f32[2,128,256]{2,1,0:T(8,128)S(1)}, u32[]{:S(2)}, u32[]{:S(2)}) %collective-permute-start) | collective-permute-done | bytes 262176 | tf_op jit(solution)/shard_map/ppermute | solution.py:246
  16.4 3.3 %collective-permute-start.4 = (f32[2,2,128,128]{3,2,1,0:T(8,128)S(1)}, f32[2,2,128,128]{3,2,1,0:T(8,128)S(1)}, u32[]{:S(2)}, u32[]{:S(2)}) collective-permute-start(f32[2,2,128,128]{3,2,1,0:T(8,128)S(1)} %pad_maximum_fusion), channel_id=1, source_target_pairs={{0,1},{1,2},{2,3},{3,4},{4,5},{5,6},{6,7},{7,8},{8,9},{9,10},{10,1... | collective-permute-start | bytes 786440 | tf_op jit(solution)/shard_map/ppermute | solution.py:250
  19.7 0.0 copy-start.5
  19.7 0.1 collective-permute-start.5
  19.8 0.0 collective-permute-done.3.right
  19.8 0.0 collective-permute-done.2.left
  19.9 3.2 %collective-permute-done.4.left_ends = f32[2,2,128,128]{3,2,1,0:T(8,128)S(1)} collective-permute-done((f32[2,2,128,128]{3,2,1,0:T(8,128)S(1)}, f32[2,2,128,128]{3,2,1,0:T(8,128)S(1)}, u32[]{:S(2)}, u32[]{:S(2)}) %collective-permute-start.4) | collective-permute-done | bytes 262176 | tf_op jit(solution)/shard_map/ppermute | solution.py:250
  23.0 2.9 %collective-permute-done.5.right_ends = f32[2,2,128,128]{3,2,1,0:T(8,128)S(1)} collective-permute-done((f32[2,2,128,128]{3,2,1,0:T(8,128)S(1)}, f32[2,2,128,128]{3,2,1,0:T(8,128)S(1)}, u32[]{:S(2)}, u32[]{:S(2)}) %collective-permute-start.5) | collective-permute-done | bytes 262176 | tf_op jit(solution)/shard_map/ppermute | solution.py:251
  25.9 0.0 copy-done.3
  25.9 0.0 copy-done.2
  25.9 0.0 copy-done.5
  25.9 8.2 %shard_map.77 = (f32[16,5,8,256]{3,2,1,0:T(8,128)S(1)}, f32[16,5,8,256]{3,2,1,0:T(8,128)S(1)}, f32[2,512,128]{2,1,0:T(8,128)S(1)}, f32[2,512,256]{2,1,0:T(8,128)S(1)}, f32[2,512,128]{2,1,0:T(8,128)S(1)}) custom-call(s32[2,4]{1,0:T(2,128)S(1)} %bitcast.20, s32[1]{0:T(128)} %bitcast.2.half, f32[2,256,256]{2,1,0:T(8,128)S(1)} %copy-done, ...), custom_call_target="tpu_custom_call" | custom-call | tf_op jit(solution)/shard_map/pallas_call | solution.py:187
  34.1 2.1 %collective-permute-start.6 = (f32[16,5,8,256]{3,2,1,0:T(8,128)S(1)}, f32[16,5,8,256]{3,2,1,0:T(8,128)S(1)}, u32[]{:S(2)}, u32[]{:S(2)}) collective-permute-start(f32[16,5,8,256]{3,2,1,0:T(8,128)S(1)} %get-tuple-element.22), channel_id=1, source_target_pairs={{0,1},{1,0},{2,3},{3,2},{4,5},{5,4},{6,7},{7,6},{8,9},{9,8},{10,11... | collective-permute-start | bytes 1966088 | tf_op jit(solution)/shard_map/ppermute | solution.py:254
  36.3 0.0 collective-permute-start.7
  36.3 0.5 collective-permute-start.8
  36.8 1.2 %collective-permute-done.6 = f32[16,5,8,256]{3,2,1,0:T(8,128)S(1)} collective-permute-done((f32[16,5,8,256]{3,2,1,0:T(8,128)S(1)}, f32[16,5,8,256]{3,2,1,0:T(8,128)S(1)}, u32[]{:S(2)}, u32[]{:S(2)}) %collective-permute-start.6) | collective-permute-done | bytes 655392 | tf_op jit(solution)/shard_map/ppermute | solution.py:254
  38.0 0.9 add.97
  38.9 6.9 %all-to-all-start = ((f32[16,5,8,256]{3,2,1,0:T(8,128)}), f32[16,5,8,256]{3,2,1,0:T(8,128)}, u32[]{:S(2)}, u32[]{:S(2)}) async-start(f32[16,5,8,256]{3,2,1,0:T(8,128)} %add.97), calls=%async_computation | async-start | bytes 1310720 | tf_op jit(solution)/shard_map/all_to_all | solution.py:257
  45.8 0.0 collective-permute-done.7
  45.8 0.0 collective-permute-done.8
  45.8 1.3 %maximum_add_fusion = f32[2,512,256]{2,1,0:T(8,128)S(1)} fusion(f32[2,512,256]{2,1,0:T(8,128)S(1)} %get-tuple-element.23, f32[2,512,128]{2,1,0:T(8,128)} %collective-permute-done.8, f32[2,512,128]{2,1,0:T(8,128)} %collective-permute-done.7), kind=kLoop, calls=%fused_computation | loop fusion | flops 524288 | bytes 3145728 | tf_op jit(solution)/shard_map/add | solution.py:259
  47.1 9.7 %all-to-all-done = f32[16,5,8,256]{3,2,1,0:T(8,128)} async-done(((f32[16,5,8,256]{3,2,1,0:T(8,128)}), f32[16,5,8,256]{3,2,1,0:T(8,128)}, u32[]{:S(2)}, u32[]{:S(2)}) %all-to-all-start) | async-done | bytes 655392 | tf_op jit(solution)/shard_map/all_to_all | solution.py:257
  56.8 1.1 %fusion = f32[5,8,256]{2,1,0:T(8,128)S(1)} fusion(f32[16,5,8,256]{3,2,1,0:T(8,128)} %all-to-all-done), kind=kLoop, calls=%fused_computation.9 | loop fusion | flops 153600 | bytes 696320 | tf_op jit(solution)/shard_map/add | solution.py:258
  58.0 3.9 %collective-permute-start.11 = (f32[5,8,256]{2,1,0:T(8,128)S(1)}, f32[5,8,256]{2,1,0:T(8,128)S(1)}, u32[]{:S(2)}, u32[]{:S(2)}) collective-permute-start(f32[5,8,256]{2,1,0:T(8,128)S(1)} %fusion), channel_id=1, source_target_pairs={{0,96},{32,64},{64,32},{96,0},{128,224},{160,192},{192,160},{224,1... | collective-permute-start | bytes 122888 | tf_op jit(solution)/shard_map/ppermute | solution.py:263
  61.9 0.0 collective-permute-start.10
  61.9 0.4 collective-permute-start.9
  62.3 0.1 collective-permute-start.14
  62.4 3.9 %collective-permute-start.13 = (f32[2,128,256]{2,1,0:T(8,128)S(1)}, f32[2,128,256]{2,1,0:T(8,128)S(1)}, u32[]{:S(2)}, u32[]{:S(2)}) collective-permute-start(f32[2,128,256]{2,1,0:T(8,128)S(1)} %get-tuple-element.33), channel_id=1, source_target_pairs={{16,0},{32,16},{48,32},{64,48},{80,64},{96,80},{112,96},{128,112},... | collective-permute-start | bytes 786440 | tf_op jit(solution)/shard_map/ppermute | solution.py:261
  66.3 0.0 collective-permute-done.11
  66.3 0.0 collective-permute-done.10
  66.3 0.0 collective-permute-done.9
  66.3 6.4 %collective-permute-start.12 = (f32[5,8,256]{2,1,0:T(8,128)S(1)}, f32[5,8,256]{2,1,0:T(8,128)S(1)}, u32[]{:S(2)}, u32[]{:S(2)}) collective-permute-start(f32[5,8,256]{2,1,0:T(8,128)S(1)} %add_add_fusion), channel_id=1, source_target_pairs={{0,128},{32,160},{64,192},{96,224},{128,0},{160,32},{192,64},{224,... | collective-permute-start | bytes 122888 | tf_op jit(solution)/shard_map/ppermute | solution.py:265
  72.7 1.4 %collective-permute-done.12 = f32[5,8,256]{2,1,0:T(8,128)S(1)} collective-permute-done((f32[5,8,256]{2,1,0:T(8,128)S(1)}, f32[5,8,256]{2,1,0:T(8,128)S(1)}, u32[]{:S(2)}, u32[]{:S(2)}) %collective-permute-start.12) | collective-permute-done | bytes 40992 | tf_op jit(solution)/shard_map/ppermute | solution.py:265
  74.1 0.0 collective-permute-done.14
  74.1 1.3 %collective-permute-done.13 = f32[2,128,256]{2,1,0:T(8,128)S(1)} collective-permute-done((f32[2,128,256]{2,1,0:T(8,128)S(1)}, f32[2,128,256]{2,1,0:T(8,128)S(1)}, u32[]{:S(2)}, u32[]{:S(2)}) %collective-permute-start.13) | collective-permute-done | bytes 262176 | tf_op jit(solution)/shard_map/ppermute | solution.py:261
  75.5 14.8 %all_to_all.10.own = f32[16,4,8,256]{3,2,1,0:T(8,128)S(1)} all-to-all(f32[16,4,8,256]{3,2,1,0:T(8,128)S(1)} %broadcast_in_dim.2), channel_id=1, replica_groups=mesh['z'=8,'xl'=2,'xh'=2,'y'=4,'co'=2] {'xh','xl','y'}, dimensions={0} | all-to-all | bytes 1048576 | tf_op jit(solution)/shard_map/all_to_all | solution.py:271
  90.3 4.0 %collective-permute-start.15 = (f32[16,4,8,256]{3,2,1,0:T(8,128)S(1)}, f32[16,4,8,256]{3,2,1,0:T(8,128)S(1)}, u32[]{:S(2)}, u32[]{:S(2)}) collective-permute-start(f32[16,4,8,256]{3,2,1,0:T(8,128)S(1)} %all_to_all.10.own), channel_id=1, source_target_pairs={{0,1},{1,0},{2,3},{3,2},{4,5},{5,4},{6,7},{7,6},{8,9},{9,8},{10,11... | collective-permute-start | bytes 1572872 | tf_op jit(solution)/shard_map/ppermute | solution.py:273
  94.3 0.9 maximum_add_fusion.1
  95.2 0.7 collective-permute-done.15.swapped
  95.8 1.0 %shard_map.78 = f32[2,2,256,256]{3,2,1,0:T(8,128)} custom-call(s32[1]{0:T(128)} %bitcast.2.half, f32[16,4,8,256]{3,2,1,0:T(8,128)S(1)} %all_to_all.10.own, f32[16,4,8,256]{3,2,1,0:T(8,128)S(1)} %collective-permute-done.15.swapped), custom_call_target="tpu_custom_call" | custom-call | tf_op jit(solution)/shard_map/pallas_call | solution.py:228
  (16 shorter events, 0.2 us)
Async XLA Ops:
  0.6 8.6 %copy-start = (f32[2,256,256]{2,1,0:T(8,128)S(1)}, f32[2,256,256]{2,1,0:T(8,128)}, u32[]{:S(2)}) copy-start(f32[2,256,256]{2,1,0:T(8,128)} %tile) | copy-start | bytes 1572868
  1.8 13.5 %collective-permute-start.1 = (f32[2,128,256]{2,1,0:T(8,128)S(1)}, f32[2,128,256]{2,1,0:T(8,128)S(1)}, u32[]{:S(2)}, u32[]{:S(2)}) collective-permute-start(f32[2,128,256]{2,1,0:T(8,128)S(1)} %get-tuple-element.36), channel_id=1, source_target_pairs={{0,16},{16,32},{32,48},{48,64},{64,80},{80,96},{96,112},{112,128},... | collective-permute-start | bytes 786440 | tf_op jit(solution)/shard_map/ppermute | solution.py:245
  3.9 12.4 %collective-permute-start = (f32[2,128,256]{2,1,0:T(8,128)S(1)}, f32[2,128,256]{2,1,0:T(8,128)S(1)}, u32[]{:S(2)}, u32[]{:S(2)}) collective-permute-start(f32[2,128,256]{2,1,0:T(8,128)S(1)} %get-tuple-element.37), channel_id=1, source_target_pairs={{16,0},{32,16},{48,32},{64,48},{80,64},{96,80},{112,96},{128,112},... | collective-permute-start | bytes 786440 | tf_op jit(solution)/shard_map/ppermute | solution.py:246
  9.3 16.6 %copy-start.3 = (bf16[512,512]{1,0:T(8,128)(2,1)S(1)}, bf16[512,512]{1,0:T(8,128)(2,1)}, u32[]{:S(2)}) copy-start(bf16[512,512]{1,0:T(8,128)(2,1)} %constant.32.clone.bwd_hbm) | copy-start | bytes 1572868
  9.3 16.6 %copy-start.4 = (bf16[512,512]{1,0:T(8,128)(2,1)S(1)}, bf16[512,512]{1,0:T(8,128)(2,1)}, u32[]{:S(2)}) copy-start(bf16[512,512]{1,0:T(8,128)(2,1)} %constant.31.clone.fwd_hbm) | copy-start | bytes 1572868
  9.3 10.5 %collective-permute-start.3 = (f32[2,256,128]{2,1,0:T(8,128)S(1)}, f32[2,256,128]{2,1,0:T(8,128)S(1)}, u32[]{:S(2)}, u32[]{:S(2)}) collective-permute-start(f32[2,256,128]{2,1,0:T(8,128)S(1)} %get-tuple-element.34), channel_id=1, source_target_pairs={{1,0},{2,1},{3,2},{4,3},{5,4},{6,5},{7,6},{8,7},{9,8},{10,9},{11,1... | collective-permute-start | bytes 786440 | tf_op jit(solution)/shard_map/ppermute | solution.py:248
  10.4 15.6 %copy-start.1 = (f32[2,2,256,256]{3,2,1,0:T(8,128)S(1)}, f32[2,2,256,256]{3,2,1,0:T(8,128)}, u32[]{:S(2)}) copy-start(f32[2,2,256,256]{3,2,1,0:T(8,128)} %probe.1) | copy-start | bytes 3145732
  10.4 15.6 %copy-start.2 = (f32[4,1,256,256]{3,2,1,0:T(8,128)S(1)}, f32[4,1,256,256]{3,2,1,0:T(8,128)}, u32[]{:S(2)}) copy-start(f32[4,1,256,256]{3,2,1,0:T(8,128)} %amp.1) | copy-start | bytes 3145732
  10.4 9.5 %collective-permute-start.2 = (f32[2,256,128]{2,1,0:T(8,128)S(1)}, f32[2,256,128]{2,1,0:T(8,128)S(1)}, u32[]{:S(2)}, u32[]{:S(2)}) collective-permute-start(f32[2,256,128]{2,1,0:T(8,128)S(1)} %get-tuple-element.35), channel_id=1, source_target_pairs={{0,1},{1,2},{2,3},{3,4},{4,5},{5,6},{6,7},{7,8},{8,9},{9,10},{10,1... | collective-permute-start | bytes 786440 | tf_op jit(solution)/shard_map/ppermute | solution.py:247
  16.4 6.6 %collective-permute-start.4 = (f32[2,2,128,128]{3,2,1,0:T(8,128)S(1)}, f32[2,2,128,128]{3,2,1,0:T(8,128)S(1)}, u32[]{:S(2)}, u32[]{:S(2)}) collective-permute-start(f32[2,2,128,128]{3,2,1,0:T(8,128)S(1)} %pad_maximum_fusion), channel_id=1, source_target_pairs={{0,1},{1,2},{2,3},{3,4},{4,5},{5,6},{6,7},{7,8},{8,9},{9,10},{10,1... | collective-permute-start | bytes 786440 | tf_op jit(solution)/shard_map/ppermute | solution.py:250
  19.7 6.2 %copy-start.5 = (s32[4,1,2]{0,2,1:T(2,128)S(1)}, s32[4,1,2]{0,2,1:T(2,128)}, u32[]{:S(2)}) copy-start(s32[4,1,2]{0,2,1:T(2,128)} %param.9) | copy-start | bytes 100
  19.7 6.2 %collective-permute-start.5 = (f32[2,2,128,128]{3,2,1,0:T(8,128)S(1)}, f32[2,2,128,128]{3,2,1,0:T(8,128)S(1)}, u32[]{:S(2)}, u32[]{:S(2)}) collective-permute-start(f32[2,2,128,128]{3,2,1,0:T(8,128)S(1)} %pad_maximum_fusion.1), channel_id=1, source_target_pairs={{1,0},{2,1},{3,2},{4,3},{5,4},{6,5},{7,6},{8,7},{9,8},{10,9},{11,1... | collective-permute-start | bytes 786440 | tf_op jit(solution)/shard_map/ppermute | solution.py:251
  34.1 3.9 %collective-permute-start.6 = (f32[16,5,8,256]{3,2,1,0:T(8,128)S(1)}, f32[16,5,8,256]{3,2,1,0:T(8,128)S(1)}, u32[]{:S(2)}, u32[]{:S(2)}) collective-permute-start(f32[16,5,8,256]{3,2,1,0:T(8,128)S(1)} %get-tuple-element.22), channel_id=1, source_target_pairs={{0,1},{1,0},{2,3},{3,2},{4,5},{5,4},{6,7},{7,6},{8,9},{9,8},{10,11... | collective-permute-start | bytes 1966088 | tf_op jit(solution)/shard_map/ppermute | solution.py:254
  36.3 9.6 %collective-permute-start.7 = (f32[2,512,128]{2,1,0:T(8,128)S(1)}, f32[2,512,128]{2,1,0:T(8,128)}, u32[]{:S(2)}, u32[]{:S(2)}) collective-permute-start(f32[2,512,128]{2,1,0:T(8,128)S(1)} %get-tuple-element.24), channel_id=1, source_target_pairs={{0,1},{1,2},{2,3},{3,4},{4,5},{5,6},{6,7},{7,8},{8,9},{9,10},{10,1... | collective-permute-start | bytes 1572872 | tf_op jit(solution)/shard_map/ppermute | solution.py:256
  36.3 9.6 %collective-permute-start.8 = (f32[2,512,128]{2,1,0:T(8,128)S(1)}, f32[2,512,128]{2,1,0:T(8,128)}, u32[]{:S(2)}, u32[]{:S(2)}) collective-permute-start(f32[2,512,128]{2,1,0:T(8,128)S(1)} %get-tuple-element.25), channel_id=1, source_target_pairs={{1,0},{2,1},{3,2},{4,3},{5,4},{6,5},{7,6},{8,7},{9,8},{10,9},{11,1... | collective-permute-start | bytes 1572872 | tf_op jit(solution)/shard_map/ppermute | solution.py:255
  38.9 17.9 %all-to-all-start = ((f32[16,5,8,256]{3,2,1,0:T(8,128)}), f32[16,5,8,256]{3,2,1,0:T(8,128)}, u32[]{:S(2)}, u32[]{:S(2)}) async-start(f32[16,5,8,256]{3,2,1,0:T(8,128)} %add.97), calls=%async_computation | async-start | bytes 1310720 | tf_op jit(solution)/shard_map/all_to_all | solution.py:257
  58.0 8.3 %collective-permute-start.11 = (f32[5,8,256]{2,1,0:T(8,128)S(1)}, f32[5,8,256]{2,1,0:T(8,128)S(1)}, u32[]{:S(2)}, u32[]{:S(2)}) collective-permute-start(f32[5,8,256]{2,1,0:T(8,128)S(1)} %fusion), channel_id=1, source_target_pairs={{0,96},{32,64},{64,32},{96,0},{128,224},{160,192},{192,160},{224,1... | collective-permute-start | bytes 122888 | tf_op jit(solution)/shard_map/ppermute | solution.py:263
  61.9 4.4 %collective-permute-start.10 = (f32[5,8,256]{2,1,0:T(8,128)S(1)}, f32[5,8,256]{2,1,0:T(8,128)S(1)}, u32[]{:S(2)}, u32[]{:S(2)}) collective-permute-start(f32[5,8,256]{2,1,0:T(8,128)S(1)} %fusion), channel_id=1, source_target_pairs={{0,64},{32,96},{64,0},{96,32},{128,192},{160,224},{192,128},{224,1... | collective-permute-start | bytes 122888 | tf_op jit(solution)/shard_map/ppermute | solution.py:263
  61.9 4.4 %collective-permute-start.9 = (f32[5,8,256]{2,1,0:T(8,128)S(1)}, f32[5,8,256]{2,1,0:T(8,128)S(1)}, u32[]{:S(2)}, u32[]{:S(2)}) collective-permute-start(f32[5,8,256]{2,1,0:T(8,128)S(1)} %fusion), channel_id=1, source_target_pairs={{0,32},{32,0},{64,96},{96,64},{128,160},{160,128},{192,224},{224,1... | collective-permute-start | bytes 122888 | tf_op jit(solution)/shard_map/ppermute | solution.py:263
  62.3 11.8 %collective-permute-start.14 = (f32[2,128,256]{2,1,0:T(8,128)S(1)}, f32[2,128,256]{2,1,0:T(8,128)S(1)}, u32[]{:S(2)}, u32[]{:S(2)}) collective-permute-start(f32[2,128,256]{2,1,0:T(8,128)S(1)} %get-tuple-element.32), channel_id=1, source_target_pairs={{0,16},{16,32},{32,48},{48,64},{64,80},{80,96},{96,112},{112,128},... | collective-permute-start | bytes 786440 | tf_op jit(solution)/shard_map/ppermute | solution.py:262
  62.4 13.0 %collective-permute-start.13 = (f32[2,128,256]{2,1,0:T(8,128)S(1)}, f32[2,128,256]{2,1,0:T(8,128)S(1)}, u32[]{:S(2)}, u32[]{:S(2)}) collective-permute-start(f32[2,128,256]{2,1,0:T(8,128)S(1)} %get-tuple-element.33), channel_id=1, source_target_pairs={{16,0},{32,16},{48,32},{64,48},{80,64},{96,80},{112,96},{128,112},... | collective-permute-start | bytes 786440 | tf_op jit(solution)/shard_map/ppermute | solution.py:261
  66.3 7.8 %collective-permute-start.12 = (f32[5,8,256]{2,1,0:T(8,128)S(1)}, f32[5,8,256]{2,1,0:T(8,128)S(1)}, u32[]{:S(2)}, u32[]{:S(2)}) collective-permute-start(f32[5,8,256]{2,1,0:T(8,128)S(1)} %add_add_fusion), channel_id=1, source_target_pairs={{0,128},{32,160},{64,192},{96,224},{128,0},{160,32},{192,64},{224,... | collective-permute-start | bytes 122888 | tf_op jit(solution)/shard_map/ppermute | solution.py:265
  90.3 5.6 %collective-permute-start.15 = (f32[16,4,8,256]{3,2,1,0:T(8,128)S(1)}, f32[16,4,8,256]{3,2,1,0:T(8,128)S(1)}, u32[]{:S(2)}, u32[]{:S(2)}) collective-permute-start(f32[16,4,8,256]{3,2,1,0:T(8,128)S(1)} %all_to_all.10.own), channel_id=1, source_target_pairs={{0,1},{1,0},{2,3},{3,2},{4,5},{5,4},{6,7},{7,6},{8,9},{9,8},{10,11... | collective-permute-start | bytes 1572872 | tf_op jit(solution)/shard_map/ppermute | solution.py:273

commit v15 on v14

--- a/solution.py
+++ b/solution.py
@@ -260,7 +260,7 @@
     part, folded = lax.optimization_barrier((part, folded))
     from_below = lax.ppermute(folded[:, :HALF], GX, DOWN)
     from_above = lax.ppermute(folded[:, HALF + W :], GX, UP)
-    peers = [lax.ppermute(part, "z", [(i, i ^ step) for i in range(8)]) for step in (1, 2, 3)]
+    peers = [lax.ppermute(part, "z", [(i, i ^ step) for i in range(8)]) for step in (3, 2, 1)]
     part = (part + peers[0]) + (peers[1] + peers[2])
     part = part + lax.ppermute(part, "z", [(i, i ^ 4) for i in range(8)])
     part, from_below, from_above = lax.optimization_barrier((part, from_below, from_above))

time: 97.2 us -> 97.3 us (level)
  blocking collectives: 14.8 us -> 16.2 us
  starting transfers between devices: 41.5 us -> 40.4 us
    all_to_all x1, blocking collectives: 14.8 us -> 16.2 us  [body(): lax.all_to_all(jnp.broadcast_to(local[None], (16,) + local.shape), group,...]
    ppermute x1, waiting for transfers between devices: 1.32 us -> 0.01 us  [body(): from_below = lax.ppermute(folded[:, :HALF], GX, DOWN)]
    ppermute x3, waiting for transfers between devices: 0.01 us -> 1.03 us  [body(): lax.ppermute(part, 'z', [(i, i ^ step) for i in range(8)])]
where the time goes in v15:
time: 97.3 us; the launch traced here: 97 us
  starting transfers between devices  40.4 us (42%)
  waiting for transfers between devices  24.8 us (25%)
  blocking collectives  16.2 us (17%)
  Pallas kernels  9.19 us (9%)
  other arithmetic  4.28 us (4%)
  local copies, waits for them, and re-layouts  1.3 us (1%)
    all_to_all x1, blocking collectives, body(): lax.all_to_all(jnp.broadcast_to(local[None], (16,) + local.shape), group,...  16.2 us
    all_to_all x1, waiting for transfers between devices, body(): pieces = lax.all_to_all(part, group, 0, 0, tiled=True)  9.69 us
    pallas_call x1, Pallas kernels, correct(): pl.pallas_call(kernel, out_shape=(part, part, strip, jax.ShapeDtypeStruct...  8.14 us
    all_to_all x1, starting transfers between devices, body(): pieces = lax.all_to_all(part, group, 0, 0, tiled=True)  6.91 us
    ppermute x1, starting transfers between devices, body(): part = part + lax.ppermute(part, 'z', [(i, i ^ 4) for i in range(8)])  5.43 us
    ppermute x1, starting transfers between devices, body(): bot = lax.ppermute(object_field[:, first], GX, DOWN)  5.38 us
    ppermute x3, starting transfers between devices, body(): lax.ppermute(part, 'z', [(i, i ^ step) for i in range(8)])  4.28 us
    ppermute x1, starting transfers between devices, body(): from_below = lax.ppermute(folded[:, :HALF], GX, DOWN)  3.94 us
  transfers between devices with their start and end apart: 17, of which 9 were waited for; matrix products, arithmetic and copies ran while one was open for 3% of the time, Pallas kernels for 0%

profile of v15, /device:TPU:1, one launch (start us, length us, event | category | flops | bytes accessed | tf_op | source)
XLA Modules:
  0.0 97.0 jit_solution(587207008009430581)
XLA Ops:
  0.6 0.0 copy-start
  0.7 1.1 %fusion.3 = (f32[2,128,256]{2,1,0:T(8,128)S(1)}, f32[2,128,256]{2,1,0:T(8,128)S(1)}) fusion(f32[2,256,256]{2,1,0:T(8,128)} %tile), kind=kLoop, calls=%fused_computation.30 | loop fusion | bytes 1048576 | tf_op jit(solution)/shard_map/slice | solution.py:245
  1.8 2.1 %collective-permute-start.1 = (f32[2,128,256]{2,1,0:T(8,128)S(1)}, f32[2,128,256]{2,1,0:T(8,128)S(1)}, u32[]{:S(2)}, u32[]{:S(2)}) collective-permute-start(f32[2,128,256]{2,1,0:T(8,128)S(1)} %get-tuple-element.36), channel_id=1, source_target_pairs={{0,16},{16,32},{32,48},{48,64},{64,80},{80,96},{96,112},{112,128},... | collective-permute-start | bytes 786440 | tf_op jit(solution)/shard_map/ppermute | solution.py:245
  3.9 5.4 %collective-permute-start = (f32[2,128,256]{2,1,0:T(8,128)S(1)}, f32[2,128,256]{2,1,0:T(8,128)S(1)}, u32[]{:S(2)}, u32[]{:S(2)}) collective-permute-start(f32[2,128,256]{2,1,0:T(8,128)S(1)} %get-tuple-element.37), channel_id=1, source_target_pairs={{16,0},{32,16},{48,32},{64,48},{80,64},{96,80},{112,96},{128,112},... | collective-permute-start | bytes 786440 | tf_op jit(solution)/shard_map/ppermute | solution.py:246
  9.3 0.0 copy-done
  9.3 1.0 %collective-permute-start.3 = (f32[2,256,128]{2,1,0:T(8,128)S(1)}, f32[2,256,128]{2,1,0:T(8,128)S(1)}, u32[]{:S(2)}, u32[]{:S(2)}) collective-permute-start(f32[2,256,128]{2,1,0:T(8,128)S(1)} %get-tuple-element.34), channel_id=1, source_target_pairs={{1,0},{2,1},{3,2},{4,3},{5,4},{6,5},{7,6},{8,7},{9,8},{10,9},{11,1... | collective-permute-start | bytes 786440 | tf_op jit(solution)/shard_map/ppermute | solution.py:248
  10.4 1.3 %collective-permute-start.2 = (f32[2,256,128]{2,1,0:T(8,128)S(1)}, f32[2,256,128]{2,1,0:T(8,128)S(1)}, u32[]{:S(2)}, u32[]{:S(2)}) collective-permute-start(f32[2,256,128]{2,1,0:T(8,128)S(1)} %get-tuple-element.35), channel_id=1, source_target_pairs={{0,1},{1,2},{2,3},{3,4},{4,5},{5,6},{6,7},{7,8},{8,9},{9,10},{10,1... | collective-permute-start | bytes 786440 | tf_op jit(solution)/shard_map/ppermute | solution.py:247
  11.7 3.6 %collective-permute-done.1.top = f32[2,128,256]{2,1,0:T(8,128)S(1)} collective-permute-done((f32[2,128,256]{2,1,0:T(8,128)S(1)}, f32[2,128,256]{2,1,0:T(8,128)S(1)}, u32[]{:S(2)}, u32[]{:S(2)}) %collective-permute-start.1) | collective-permute-done | bytes 262176 | tf_op jit(solution)/shard_map/ppermute | solution.py:245
  15.3 1.1 %collective-permute-done.bot = f32[2,128,256]{2,1,0:T(8,128)S(1)} collective-permute-done((f32[2,128,256]{2,1,0:T(8,128)S(1)}, f32[2,128,256]{2,1,0:T(8,128)S(1)}, u32[]{:S(2)}, u32[]{:S(2)}) %collective-permute-start) | collective-permute-done | bytes 262176 | tf_op jit(solution)/shard_map/ppermute | solution.py:246
  16.4 3.3 %collective-permute-start.4 = (f32[2,2,128,128]{3,2,1,0:T(8,128)S(1)}, f32[2,2,128,128]{3,2,1,0:T(8,128)S(1)}, u32[]{:S(2)}, u32[]{:S(2)}) collective-permute-start(f32[2,2,128,128]{3,2,1,0:T(8,128)S(1)} %pad_maximum_fusion), channel_id=1, source_target_pairs={{0,1},{1,2},{2,3},{3,4},{4,5},{5,6},{6,7},{7,8},{8,9},{9,10},{10,1... | collective-permute-start | bytes 786440 | tf_op jit(solution)/shard_map/ppermute | solution.py:250
  19.7 0.0 copy-start.5
  19.7 0.1 collective-permute-start.5
  19.8 0.0 collective-permute-done.3.right
  19.8 0.0 collective-permute-done.2.left
  19.9 3.2 %collective-permute-done.4.left_ends = f32[2,2,128,128]{3,2,1,0:T(8,128)S(1)} collective-permute-done((f32[2,2,128,128]{3,2,1,0:T(8,128)S(1)}, f32[2,2,128,128]{3,2,1,0:T(8,128)S(1)}, u32[]{:S(2)}, u32[]{:S(2)}) %collective-permute-start.4) | collective-permute-done | bytes 262176 | tf_op jit(solution)/shard_map/ppermute | solution.py:250
  23.0 2.9 %collective-permute-done.5.right_ends = f32[2,2,128,128]{3,2,1,0:T(8,128)S(1)} collective-permute-done((f32[2,2,128,128]{3,2,1,0:T(8,128)S(1)}, f32[2,2,128,128]{3,2,1,0:T(8,128)S(1)}, u32[]{:S(2)}, u32[]{:S(2)}) %collective-permute-start.5) | collective-permute-done | bytes 262176 | tf_op jit(solution)/shard_map/ppermute | solution.py:251
  25.9 0.0 copy-done.3
  25.9 0.0 copy-done.4
  25.9 0.0 copy-done.1
  25.9 8.1 %shard_map.77 = (f32[16,5,8,256]{3,2,1,0:T(8,128)S(1)}, f32[16,5,8,256]{3,2,1,0:T(8,128)S(1)}, f32[2,512,128]{2,1,0:T(8,128)S(1)}, f32[2,512,256]{2,1,0:T(8,128)S(1)}, f32[2,512,128]{2,1,0:T(8,128)S(1)}) custom-call(s32[2,4]{1,0:T(2,128)S(1)} %bitcast.20, s32[1]{0:T(128)} %bitcast.2.half, f32[2,256,256]{2,1,0:T(8,128)S(1)} %copy-done, ...), custom_call_target="tpu_custom_call" | custom-call | tf_op jit(solution)/shard_map/pallas_call | solution.py:187
  34.1 2.1 %collective-permute-start.6 = (f32[16,5,8,256]{3,2,1,0:T(8,128)S(1)}, f32[16,5,8,256]{3,2,1,0:T(8,128)S(1)}, u32[]{:S(2)}, u32[]{:S(2)}) collective-permute-start(f32[16,5,8,256]{3,2,1,0:T(8,128)S(1)} %get-tuple-element.22), channel_id=1, source_target_pairs={{0,1},{1,0},{2,3},{3,2},{4,5},{5,4},{6,7},{7,6},{8,9},{9,8},{10,11... | collective-permute-start | bytes 1966088 | tf_op jit(solution)/shard_map/ppermute | solution.py:254
  36.2 0.0 collective-permute-start.7
  36.2 0.5 collective-permute-start.8
  36.7 1.2 %collective-permute-done.6 = f32[16,5,8,256]{3,2,1,0:T(8,128)S(1)} collective-permute-done((f32[16,5,8,256]{3,2,1,0:T(8,128)S(1)}, f32[16,5,8,256]{3,2,1,0:T(8,128)S(1)}, u32[]{:S(2)}, u32[]{:S(2)}) %collective-permute-start.6) | collective-permute-done | bytes 655392 | tf_op jit(solution)/shard_map/ppermute | solution.py:254
  37.9 0.9 add.97
  38.9 6.9 %all-to-all-start = ((f32[16,5,8,256]{3,2,1,0:T(8,128)}), f32[16,5,8,256]{3,2,1,0:T(8,128)}, u32[]{:S(2)}, u32[]{:S(2)}) async-start(f32[16,5,8,256]{3,2,1,0:T(8,128)} %add.97), calls=%async_computation | async-start | bytes 1310720 | tf_op jit(solution)/shard_map/all_to_all | solution.py:257
  45.8 0.0 collective-permute-done.7
  45.8 0.0 collective-permute-done.8
  45.8 1.3 %maximum_add_fusion = f32[2,512,256]{2,1,0:T(8,128)S(1)} fusion(f32[2,512,256]{2,1,0:T(8,128)S(1)} %get-tuple-element.23, f32[2,512,128]{2,1,0:T(8,128)} %collective-permute-done.8, f32[2,512,128]{2,1,0:T(8,128)} %collective-permute-done.7), kind=kLoop, calls=%fused_computation | loop fusion | flops 524288 | bytes 3145728 | tf_op jit(solution)/shard_map/add | solution.py:259
  47.1 9.7 %all-to-all-done = f32[16,5,8,256]{3,2,1,0:T(8,128)} async-done(((f32[16,5,8,256]{3,2,1,0:T(8,128)}), f32[16,5,8,256]{3,2,1,0:T(8,128)}, u32[]{:S(2)}, u32[]{:S(2)}) %all-to-all-start) | async-done | bytes 655392 | tf_op jit(solution)/shard_map/all_to_all | solution.py:257
  56.8 1.1 %fusion = f32[5,8,256]{2,1,0:T(8,128)S(1)} fusion(f32[16,5,8,256]{3,2,1,0:T(8,128)} %all-to-all-done), kind=kLoop, calls=%fused_computation.9 | loop fusion | flops 153600 | bytes 696320 | tf_op jit(solution)/shard_map/add | solution.py:258
  57.9 1.3 %collective-permute-start.11 = (f32[5,8,256]{2,1,0:T(8,128)S(1)}, f32[5,8,256]{2,1,0:T(8,128)S(1)}, u32[]{:S(2)}, u32[]{:S(2)}) collective-permute-start(f32[5,8,256]{2,1,0:T(8,128)S(1)} %fusion), channel_id=1, source_target_pairs={{0,32},{32,0},{64,96},{96,64},{128,160},{160,128},{192,224},{224,1... | collective-permute-start | bytes 122888 | tf_op jit(solution)/shard_map/ppermute | solution.py:263
  59.2 3.0 %collective-permute-start.10 = (f32[5,8,256]{2,1,0:T(8,128)S(1)}, f32[5,8,256]{2,1,0:T(8,128)S(1)}, u32[]{:S(2)}, u32[]{:S(2)}) collective-permute-start(f32[5,8,256]{2,1,0:T(8,128)S(1)} %fusion), channel_id=1, source_target_pairs={{0,64},{32,96},{64,0},{96,32},{128,192},{160,224},{192,128},{224,1... | collective-permute-start | bytes 122888 | tf_op jit(solution)/shard_map/ppermute | solution.py:263
  62.2 0.0 collective-permute-start.9
  62.2 0.1 collective-permute-start.14
  62.3 3.9 %collective-permute-start.13 = (f32[2,128,256]{2,1,0:T(8,128)S(1)}, f32[2,128,256]{2,1,0:T(8,128)S(1)}, u32[]{:S(2)}, u32[]{:S(2)}) collective-permute-start(f32[2,128,256]{2,1,0:T(8,128)S(1)} %get-tuple-element.33), channel_id=1, source_target_pairs={{16,0},{32,16},{48,32},{64,48},{80,64},{96,80},{112,96},{128,112},... | collective-permute-start | bytes 786440 | tf_op jit(solution)/shard_map/ppermute | solution.py:261
  66.3 0.0 collective-permute-done.11
  66.3 0.0 collective-permute-done.10
  66.3 1.0 %collective-permute-done.9 = f32[5,8,256]{2,1,0:T(8,128)S(1)} collective-permute-done((f32[5,8,256]{2,1,0:T(8,128)S(1)}, f32[5,8,256]{2,1,0:T(8,128)S(1)}, u32[]{:S(2)}, u32[]{:S(2)}) %collective-permute-start.9) | collective-permute-done | bytes 40992 | tf_op jit(solution)/shard_map/ppermute | solution.py:263
  67.3 5.4 %collective-permute-start.12 = (f32[5,8,256]{2,1,0:T(8,128)S(1)}, f32[5,8,256]{2,1,0:T(8,128)S(1)}, u32[]{:S(2)}, u32[]{:S(2)}) collective-permute-start(f32[5,8,256]{2,1,0:T(8,128)S(1)} %add_add_fusion), channel_id=1, source_target_pairs={{0,128},{32,160},{64,192},{96,224},{128,0},{160,32},{192,64},{224,... | collective-permute-start | bytes 122888 | tf_op jit(solution)/shard_map/ppermute | solution.py:265
  72.7 1.4 %collective-permute-done.12 = f32[5,8,256]{2,1,0:T(8,128)S(1)} collective-permute-done((f32[5,8,256]{2,1,0:T(8,128)S(1)}, f32[5,8,256]{2,1,0:T(8,128)S(1)}, u32[]{:S(2)}, u32[]{:S(2)}) %collective-permute-start.12) | collective-permute-done | bytes 40992 | tf_op jit(solution)/shard_map/ppermute | solution.py:265
  74.2 0.0 collective-permute-done.14
  74.2 0.0 collective-permute-done.13
  74.3 16.2 %all_to_all.10.own = f32[16,4,8,256]{3,2,1,0:T(8,128)S(1)} all-to-all(f32[16,4,8,256]{3,2,1,0:T(8,128)S(1)} %broadcast_in_dim.2), channel_id=1, replica_groups=mesh['z'=8,'xl'=2,'xh'=2,'y'=4,'co'=2] {'xh','xl','y'}, dimensions={0} | all-to-all | bytes 1048576 | tf_op jit(solution)/shard_map/all_to_all | solution.py:271
  90.5 3.9 %collective-permute-start.15 = (f32[16,4,8,256]{3,2,1,0:T(8,128)S(1)}, f32[16,4,8,256]{3,2,1,0:T(8,128)S(1)}, u32[]{:S(2)}, u32[]{:S(2)}) collective-permute-start(f32[16,4,8,256]{3,2,1,0:T(8,128)S(1)} %all_to_all.10.own), channel_id=1, source_target_pairs={{0,1},{1,0},{2,3},{3,2},{4,5},{5,4},{6,7},{7,6},{8,9},{9,8},{10,11... | collective-permute-start | bytes 1572872 | tf_op jit(solution)/shard_map/ppermute | solution.py:273
  94.4 0.9 maximum_add_fusion.1
  95.2 0.7 collective-permute-done.15.swapped
  95.9 1.0 %shard_map.78 = f32[2,2,256,256]{3,2,1,0:T(8,128)} custom-call(s32[1]{0:T(128)} %bitcast.2.half, f32[16,4,8,256]{3,2,1,0:T(8,128)S(1)} %all_to_all.10.own, f32[16,4,8,256]{3,2,1,0:T(8,128)S(1)} %collective-permute-done.15.swapped), custom_call_target="tpu_custom_call" | custom-call | tf_op jit(solution)/shard_map/pallas_call | solution.py:228
  (16 shorter events, 0.2 us)
Async XLA Ops:
  0.6 8.6 %copy-start = (f32[2,256,256]{2,1,0:T(8,128)S(1)}, f32[2,256,256]{2,1,0:T(8,128)}, u32[]{:S(2)}) copy-start(f32[2,256,256]{2,1,0:T(8,128)} %tile) | copy-start | bytes 1572868
  1.8 13.5 %collective-permute-start.1 = (f32[2,128,256]{2,1,0:T(8,128)S(1)}, f32[2,128,256]{2,1,0:T(8,128)S(1)}, u32[]{:S(2)}, u32[]{:S(2)}) collective-permute-start(f32[2,128,256]{2,1,0:T(8,128)S(1)} %get-tuple-element.36), channel_id=1, source_target_pairs={{0,16},{16,32},{32,48},{48,64},{64,80},{80,96},{96,112},{112,128},... | collective-permute-start | bytes 786440 | tf_op jit(solution)/shard_map/ppermute | solution.py:245
  3.9 12.4 %collective-permute-start = (f32[2,128,256]{2,1,0:T(8,128)S(1)}, f32[2,128,256]{2,1,0:T(8,128)S(1)}, u32[]{:S(2)}, u32[]{:S(2)}) collective-permute-start(f32[2,128,256]{2,1,0:T(8,128)S(1)} %get-tuple-element.37), channel_id=1, source_target_pairs={{16,0},{32,16},{48,32},{64,48},{80,64},{96,80},{112,96},{128,112},... | collective-permute-start | bytes 786440 | tf_op jit(solution)/shard_map/ppermute | solution.py:246
  9.3 16.6 %copy-start.3 = (bf16[512,512]{1,0:T(8,128)(2,1)S(1)}, bf16[512,512]{1,0:T(8,128)(2,1)}, u32[]{:S(2)}) copy-start(bf16[512,512]{1,0:T(8,128)(2,1)} %constant.32.clone.bwd_hbm) | copy-start | bytes 1572868
  9.3 16.6 %copy-start.4 = (bf16[512,512]{1,0:T(8,128)(2,1)S(1)}, bf16[512,512]{1,0:T(8,128)(2,1)}, u32[]{:S(2)}) copy-start(bf16[512,512]{1,0:T(8,128)(2,1)} %constant.31.clone.fwd_hbm) | copy-start | bytes 1572868
  9.3 10.5 %collective-permute-start.3 = (f32[2,256,128]{2,1,0:T(8,128)S(1)}, f32[2,256,128]{2,1,0:T(8,128)S(1)}, u32[]{:S(2)}, u32[]{:S(2)}) collective-permute-start(f32[2,256,128]{2,1,0:T(8,128)S(1)} %get-tuple-element.34), channel_id=1, source_target_pairs={{1,0},{2,1},{3,2},{4,3},{5,4},{6,5},{7,6},{8,7},{9,8},{10,9},{11,1... | collective-permute-start | bytes 786440 | tf_op jit(solution)/shard_map/ppermute | solution.py:248
  10.4 15.6 %copy-start.1 = (f32[2,2,256,256]{3,2,1,0:T(8,128)S(1)}, f32[2,2,256,256]{3,2,1,0:T(8,128)}, u32[]{:S(2)}) copy-start(f32[2,2,256,256]{3,2,1,0:T(8,128)} %probe.1) | copy-start | bytes 3145732
  10.4 15.6 %copy-start.2 = (f32[4,1,256,256]{3,2,1,0:T(8,128)S(1)}, f32[4,1,256,256]{3,2,1,0:T(8,128)}, u32[]{:S(2)}) copy-start(f32[4,1,256,256]{3,2,1,0:T(8,128)} %amp.1) | copy-start | bytes 3145732
  10.4 9.5 %collective-permute-start.2 = (f32[2,256,128]{2,1,0:T(8,128)S(1)}, f32[2,256,128]{2,1,0:T(8,128)S(1)}, u32[]{:S(2)}, u32[]{:S(2)}) collective-permute-start(f32[2,256,128]{2,1,0:T(8,128)S(1)} %get-tuple-element.35), channel_id=1, source_target_pairs={{0,1},{1,2},{2,3},{3,4},{4,5},{5,6},{6,7},{7,8},{8,9},{9,10},{10,1... | collective-permute-start | bytes 786440 | tf_op jit(solution)/shard_map/ppermute | solution.py:247
  16.4 6.6 %collective-permute-start.4 = (f32[2,2,128,128]{3,2,1,0:T(8,128)S(1)}, f32[2,2,128,128]{3,2,1,0:T(8,128)S(1)}, u32[]{:S(2)}, u32[]{:S(2)}) collective-permute-start(f32[2,2,128,128]{3,2,1,0:T(8,128)S(1)} %pad_maximum_fusion), channel_id=1, source_target_pairs={{0,1},{1,2},{2,3},{3,4},{4,5},{5,6},{6,7},{7,8},{8,9},{9,10},{10,1... | collective-permute-start | bytes 786440 | tf_op jit(solution)/shard_map/ppermute | solution.py:250
  19.7 6.2 %copy-start.5 = (s32[4,1,2]{0,2,1:T(2,128)S(1)}, s32[4,1,2]{0,2,1:T(2,128)}, u32[]{:S(2)}) copy-start(s32[4,1,2]{0,2,1:T(2,128)} %param.9) | copy-start | bytes 100
  19.7 6.2 %collective-permute-start.5 = (f32[2,2,128,128]{3,2,1,0:T(8,128)S(1)}, f32[2,2,128,128]{3,2,1,0:T(8,128)S(1)}, u32[]{:S(2)}, u32[]{:S(2)}) collective-permute-start(f32[2,2,128,128]{3,2,1,0:T(8,128)S(1)} %pad_maximum_fusion.1), channel_id=1, source_target_pairs={{1,0},{2,1},{3,2},{4,3},{5,4},{6,5},{7,6},{8,7},{9,8},{10,9},{11,1... | collective-permute-start | bytes 786440 | tf_op jit(solution)/shard_map/ppermute | solution.py:251
  34.1 3.8 %collective-permute-start.6 = (f32[16,5,8,256]{3,2,1,0:T(8,128)S(1)}, f32[16,5,8,256]{3,2,1,0:T(8,128)S(1)}, u32[]{:S(2)}, u32[]{:S(2)}) collective-permute-start(f32[16,5,8,256]{3,2,1,0:T(8,128)S(1)} %get-tuple-element.22), channel_id=1, source_target_pairs={{0,1},{1,0},{2,3},{3,2},{4,5},{5,4},{6,7},{7,6},{8,9},{9,8},{10,11... | collective-permute-start | bytes 1966088 | tf_op jit(solution)/shard_map/ppermute | solution.py:254
  36.2 9.6 %collective-permute-start.7 = (f32[2,512,128]{2,1,0:T(8,128)S(1)}, f32[2,512,128]{2,1,0:T(8,128)}, u32[]{:S(2)}, u32[]{:S(2)}) collective-permute-start(f32[2,512,128]{2,1,0:T(8,128)S(1)} %get-tuple-element.24), channel_id=1, source_target_pairs={{0,1},{1,2},{2,3},{3,4},{4,5},{5,6},{6,7},{7,8},{8,9},{9,10},{10,1... | collective-permute-start | bytes 1572872 | tf_op jit(solution)/shard_map/ppermute | solution.py:256
  36.2 9.6 %collective-permute-start.8 = (f32[2,512,128]{2,1,0:T(8,128)S(1)}, f32[2,512,128]{2,1,0:T(8,128)}, u32[]{:S(2)}, u32[]{:S(2)}) collective-permute-start(f32[2,512,128]{2,1,0:T(8,128)S(1)} %get-tuple-element.25), channel_id=1, source_target_pairs={{1,0},{2,1},{3,2},{4,3},{5,4},{6,5},{7,6},{8,7},{9,8},{10,9},{11,1... | collective-permute-start | bytes 1572872 | tf_op jit(solution)/shard_map/ppermute | solution.py:255
  38.9 17.9 %all-to-all-start = ((f32[16,5,8,256]{3,2,1,0:T(8,128)}), f32[16,5,8,256]{3,2,1,0:T(8,128)}, u32[]{:S(2)}, u32[]{:S(2)}) async-start(f32[16,5,8,256]{3,2,1,0:T(8,128)} %add.97), calls=%async_computation | async-start | bytes 1310720 | tf_op jit(solution)/shard_map/all_to_all | solution.py:257
  57.9 8.4 %collective-permute-start.11 = (f32[5,8,256]{2,1,0:T(8,128)S(1)}, f32[5,8,256]{2,1,0:T(8,128)S(1)}, u32[]{:S(2)}, u32[]{:S(2)}) collective-permute-start(f32[5,8,256]{2,1,0:T(8,128)S(1)} %fusion), channel_id=1, source_target_pairs={{0,32},{32,0},{64,96},{96,64},{128,160},{160,128},{192,224},{224,1... | collective-permute-start | bytes 122888 | tf_op jit(solution)/shard_map/ppermute | solution.py:263
  59.2 7.1 %collective-permute-start.10 = (f32[5,8,256]{2,1,0:T(8,128)S(1)}, f32[5,8,256]{2,1,0:T(8,128)S(1)}, u32[]{:S(2)}, u32[]{:S(2)}) collective-permute-start(f32[5,8,256]{2,1,0:T(8,128)S(1)} %fusion), channel_id=1, source_target_pairs={{0,64},{32,96},{64,0},{96,32},{128,192},{160,224},{192,128},{224,1... | collective-permute-start | bytes 122888 | tf_op jit(solution)/shard_map/ppermute | solution.py:263
  62.2 5.1 %collective-permute-start.9 = (f32[5,8,256]{2,1,0:T(8,128)S(1)}, f32[5,8,256]{2,1,0:T(8,128)S(1)}, u32[]{:S(2)}, u32[]{:S(2)}) collective-permute-start(f32[5,8,256]{2,1,0:T(8,128)S(1)} %fusion), channel_id=1, source_target_pairs={{0,96},{32,64},{64,32},{96,0},{128,224},{160,192},{192,160},{224,1... | collective-permute-start | bytes 122888 | tf_op jit(solution)/shard_map/ppermute | solution.py:263
  62.2 11.9 %collective-permute-start.14 = (f32[2,128,256]{2,1,0:T(8,128)S(1)}, f32[2,128,256]{2,1,0:T(8,128)S(1)}, u32[]{:S(2)}, u32[]{:S(2)}) collective-permute-start(f32[2,128,256]{2,1,0:T(8,128)S(1)} %get-tuple-element.32), channel_id=1, source_target_pairs={{0,16},{16,32},{32,48},{48,64},{64,80},{80,96},{96,112},{112,128},... | collective-permute-start | bytes 786440 | tf_op jit(solution)/shard_map/ppermute | solution.py:262
  62.3 11.8 %collective-permute-start.13 = (f32[2,128,256]{2,1,0:T(8,128)S(1)}, f32[2,128,256]{2,1,0:T(8,128)S(1)}, u32[]{:S(2)}, u32[]{:S(2)}) collective-permute-start(f32[2,128,256]{2,1,0:T(8,128)S(1)} %get-tuple-element.33), channel_id=1, source_target_pairs={{16,0},{32,16},{48,32},{64,48},{80,64},{96,80},{112,96},{128,112},... | collective-permute-start | bytes 786440 | tf_op jit(solution)/shard_map/ppermute | solution.py:261
  67.3 6.8 %collective-permute-start.12 = (f32[5,8,256]{2,1,0:T(8,128)S(1)}, f32[5,8,256]{2,1,0:T(8,128)S(1)}, u32[]{:S(2)}, u32[]{:S(2)}) collective-permute-start(f32[5,8,256]{2,1,0:T(8,128)S(1)} %add_add_fusion), channel_id=1, source_target_pairs={{0,128},{32,160},{64,192},{96,224},{128,0},{160,32},{192,64},{224,... | collective-permute-start | bytes 122888 | tf_op jit(solution)/shard_map/ppermute | solution.py:265
  90.5 5.4 %collective-permute-start.15 = (f32[16,4,8,256]{3,2,1,0:T(8,128)S(1)}, f32[16,4,8,256]{3,2,1,0:T(8,128)S(1)}, u32[]{:S(2)}, u32[]{:S(2)}) collective-permute-start(f32[16,4,8,256]{3,2,1,0:T(8,128)S(1)} %all_to_all.10.own), channel_id=1, source_target_pairs={{0,1},{1,0},{2,3},{3,2},{4,5},{5,4},{6,7},{7,6},{8,9},{9,8},{10,11... | collective-permute-start | bytes 1572872 | tf_op jit(solution)/shard_map/ppermute | solution.py:273

commit v16 on v14

--- a/solution.py
+++ b/solution.py
@@ -15,7 +15,7 @@
 HALF = 128
 POS = 4
 MODES = 2
-CH = 32
+CH = 64
 BF = jnp.bfloat16
 F32 = jnp.float32
 

time: 97.2 us -> 97.1 us (level)
  no operation moved by 1% of the time
where the time goes in v16:
time: 97.1 us; the launch traced here: 96.8 us
  starting transfers between devices  41.5 us (43%)
  waiting for transfers between devices  25.1 us (26%)
  blocking collectives  14.8 us (15%)
  Pallas kernels  9.06 us (9%)
  other arithmetic  4.28 us (4%)
  local copies, waits for them, and re-layouts  1.3 us (1%)
    all_to_all x1, blocking collectives, body(): lax.all_to_all(jnp.broadcast_to(local[None], (16,) + local.shape), group,...  14.8 us
    all_to_all x1, waiting for transfers between devices, body(): pieces = lax.all_to_all(part, group, 0, 0, tiled=True)  9.69 us
    pallas_call x1, Pallas kernels, correct(): pl.pallas_call(kernel, out_shape=(part, part, strip, jax.ShapeDtypeStruct...  8.02 us
    all_to_all x1, starting transfers between devices, body(): pieces = lax.all_to_all(part, group, 0, 0, tiled=True)  6.91 us
    ppermute x1, starting transfers between devices, body(): part = part + lax.ppermute(part, 'z', [(i, i ^ 4) for i in range(8)])  6.43 us
    ppermute x1, starting transfers between devices, body(): bot = lax.ppermute(object_field[:, first], GX, DOWN)  5.38 us
    ppermute x3, starting transfers between devices, body(): lax.ppermute(part, 'z', [(i, i ^ step) for i in range(8)])  4.37 us
    ppermute x1, starting transfers between devices, body(): updated_probe = arrange(half, gathered, lax.ppermute(gathered, 'co', SWAP))  3.96 us
  transfers between devices with their start and end apart: 17, of which 9 were waited for; matrix products, arithmetic and copies ran while one was open for 3% of the time, Pallas kernels for 0%

profile of v16, /device:TPU:1, one launch (start us, length us, event | category | flops | bytes accessed | tf_op | source)
XLA Modules:
  0.0 96.8 jit_solution(1149999931562129963)
XLA Ops:
  0.6 0.0 copy-start
  0.7 1.1 %fusion.3 = (f32[2,128,256]{2,1,0:T(8,128)S(1)}, f32[2,128,256]{2,1,0:T(8,128)S(1)}) fusion(f32[2,256,256]{2,1,0:T(8,128)} %tile), kind=kLoop, calls=%fused_computation.30 | loop fusion | bytes 1048576 | tf_op jit(solution)/shard_map/slice | solution.py:245
  1.8 2.1 %collective-permute-start.1 = (f32[2,128,256]{2,1,0:T(8,128)S(1)}, f32[2,128,256]{2,1,0:T(8,128)S(1)}, u32[]{:S(2)}, u32[]{:S(2)}) collective-permute-start(f32[2,128,256]{2,1,0:T(8,128)S(1)} %get-tuple-element.36), channel_id=1, source_target_pairs={{0,16},{16,32},{32,48},{48,64},{64,80},{80,96},{96,112},{112,128},... | collective-permute-start | bytes 786440 | tf_op jit(solution)/shard_map/ppermute | solution.py:245
  3.9 5.4 %collective-permute-start = (f32[2,128,256]{2,1,0:T(8,128)S(1)}, f32[2,128,256]{2,1,0:T(8,128)S(1)}, u32[]{:S(2)}, u32[]{:S(2)}) collective-permute-start(f32[2,128,256]{2,1,0:T(8,128)S(1)} %get-tuple-element.37), channel_id=1, source_target_pairs={{16,0},{32,16},{48,32},{64,48},{80,64},{96,80},{112,96},{128,112},... | collective-permute-start | bytes 786440 | tf_op jit(solution)/shard_map/ppermute | solution.py:246
  9.3 0.0 copy-done
  9.3 1.0 %collective-permute-start.3 = (f32[2,256,128]{2,1,0:T(8,128)S(1)}, f32[2,256,128]{2,1,0:T(8,128)S(1)}, u32[]{:S(2)}, u32[]{:S(2)}) collective-permute-start(f32[2,256,128]{2,1,0:T(8,128)S(1)} %get-tuple-element.34), channel_id=1, source_target_pairs={{1,0},{2,1},{3,2},{4,3},{5,4},{6,5},{7,6},{8,7},{9,8},{10,9},{11,1... | collective-permute-start | bytes 786440 | tf_op jit(solution)/shard_map/ppermute | solution.py:248
  10.4 1.3 %collective-permute-start.2 = (f32[2,256,128]{2,1,0:T(8,128)S(1)}, f32[2,256,128]{2,1,0:T(8,128)S(1)}, u32[]{:S(2)}, u32[]{:S(2)}) collective-permute-start(f32[2,256,128]{2,1,0:T(8,128)S(1)} %get-tuple-element.35), channel_id=1, source_target_pairs={{0,1},{1,2},{2,3},{3,4},{4,5},{5,6},{6,7},{7,8},{8,9},{9,10},{10,1... | collective-permute-start | bytes 786440 | tf_op jit(solution)/shard_map/ppermute | solution.py:247
  11.7 3.6 %collective-permute-done.1.top = f32[2,128,256]{2,1,0:T(8,128)S(1)} collective-permute-done((f32[2,128,256]{2,1,0:T(8,128)S(1)}, f32[2,128,256]{2,1,0:T(8,128)S(1)}, u32[]{:S(2)}, u32[]{:S(2)}) %collective-permute-start.1) | collective-permute-done | bytes 262176 | tf_op jit(solution)/shard_map/ppermute | solution.py:245
  15.3 1.1 %collective-permute-done.bot = f32[2,128,256]{2,1,0:T(8,128)S(1)} collective-permute-done((f32[2,128,256]{2,1,0:T(8,128)S(1)}, f32[2,128,256]{2,1,0:T(8,128)S(1)}, u32[]{:S(2)}, u32[]{:S(2)}) %collective-permute-start) | collective-permute-done | bytes 262176 | tf_op jit(solution)/shard_map/ppermute | solution.py:246
  16.4 3.3 %collective-permute-start.4 = (f32[2,2,128,128]{3,2,1,0:T(8,128)S(1)}, f32[2,2,128,128]{3,2,1,0:T(8,128)S(1)}, u32[]{:S(2)}, u32[]{:S(2)}) collective-permute-start(f32[2,2,128,128]{3,2,1,0:T(8,128)S(1)} %pad_maximum_fusion), channel_id=1, source_target_pairs={{0,1},{1,2},{2,3},{3,4},{4,5},{5,6},{6,7},{7,8},{8,9},{9,10},{10,1... | collective-permute-start | bytes 786440 | tf_op jit(solution)/shard_map/ppermute | solution.py:250
  19.7 0.0 copy-start.5
  19.7 0.1 collective-permute-start.5
  19.8 0.0 collective-permute-done.3.right
  19.8 0.0 collective-permute-done.2.left
  19.9 3.2 %collective-permute-done.4.left_ends = f32[2,2,128,128]{3,2,1,0:T(8,128)S(1)} collective-permute-done((f32[2,2,128,128]{3,2,1,0:T(8,128)S(1)}, f32[2,2,128,128]{3,2,1,0:T(8,128)S(1)}, u32[]{:S(2)}, u32[]{:S(2)}) %collective-permute-start.4) | collective-permute-done | bytes 262176 | tf_op jit(solution)/shard_map/ppermute | solution.py:250
  23.0 2.9 %collective-permute-done.5.right_ends = f32[2,2,128,128]{3,2,1,0:T(8,128)S(1)} collective-permute-done((f32[2,2,128,128]{3,2,1,0:T(8,128)S(1)}, f32[2,2,128,128]{3,2,1,0:T(8,128)S(1)}, u32[]{:S(2)}, u32[]{:S(2)}) %collective-permute-start.5) | collective-permute-done | bytes 262176 | tf_op jit(solution)/shard_map/ppermute | solution.py:251
  25.9 0.0 copy-done.3
  25.9 0.0 copy-done.4
  25.9 0.0 copy-done.1
  25.9 8.0 %shard_map.77 = (f32[16,5,8,256]{3,2,1,0:T(8,128)S(1)}, f32[16,5,8,256]{3,2,1,0:T(8,128)S(1)}, f32[2,512,128]{2,1,0:T(8,128)S(1)}, f32[2,512,256]{2,1,0:T(8,128)S(1)}, f32[2,512,128]{2,1,0:T(8,128)S(1)}) custom-call(s32[2,4]{1,0:T(2,128)S(1)} %bitcast.20, s32[1]{0:T(128)} %bitcast.2.half, f32[2,256,256]{2,1,0:T(8,128)S(1)} %copy-done, ...), custom_call_target="tpu_custom_call" | custom-call | tf_op jit(solution)/shard_map/pallas_call | solution.py:187
  34.0 2.2 %collective-permute-start.6 = (f32[16,5,8,256]{3,2,1,0:T(8,128)S(1)}, f32[16,5,8,256]{3,2,1,0:T(8,128)S(1)}, u32[]{:S(2)}, u32[]{:S(2)}) collective-permute-start(f32[16,5,8,256]{3,2,1,0:T(8,128)S(1)} %get-tuple-element.22), channel_id=1, source_target_pairs={{0,1},{1,0},{2,3},{3,2},{4,5},{5,4},{6,7},{7,6},{8,9},{9,8},{10,11... | collective-permute-start | bytes 1966088 | tf_op jit(solution)/shard_map/ppermute | solution.py:254
  36.1 0.0 collective-permute-start.7
  36.1 0.5 collective-permute-start.8
  36.6 1.2 %collective-permute-done.6 = f32[16,5,8,256]{3,2,1,0:T(8,128)S(1)} collective-permute-done((f32[16,5,8,256]{3,2,1,0:T(8,128)S(1)}, f32[16,5,8,256]{3,2,1,0:T(8,128)S(1)}, u32[]{:S(2)}, u32[]{:S(2)}) %collective-permute-start.6) | collective-permute-done | bytes 655392 | tf_op jit(solution)/shard_map/ppermute | solution.py:254
  37.9 0.9 add.97
  38.8 6.9 %all-to-all-start = ((f32[16,5,8,256]{3,2,1,0:T(8,128)}), f32[16,5,8,256]{3,2,1,0:T(8,128)}, u32[]{:S(2)}, u32[]{:S(2)}) async-start(f32[16,5,8,256]{3,2,1,0:T(8,128)} %add.97), calls=%async_computation | async-start | bytes 1310720 | tf_op jit(solution)/shard_map/all_to_all | solution.py:257
  45.7 0.0 collective-permute-done.7
  45.7 0.0 collective-permute-done.8
  45.7 1.3 %maximum_add_fusion = f32[2,512,256]{2,1,0:T(8,128)S(1)} fusion(f32[2,512,256]{2,1,0:T(8,128)S(1)} %get-tuple-element.23, f32[2,512,128]{2,1,0:T(8,128)} %collective-permute-done.8, f32[2,512,128]{2,1,0:T(8,128)} %collective-permute-done.7), kind=kLoop, calls=%fused_computation | loop fusion | flops 524288 | bytes 3145728 | tf_op jit(solution)/shard_map/add | solution.py:259
  47.0 9.7 %all-to-all-done = f32[16,5,8,256]{3,2,1,0:T(8,128)} async-done(((f32[16,5,8,256]{3,2,1,0:T(8,128)}), f32[16,5,8,256]{3,2,1,0:T(8,128)}, u32[]{:S(2)}, u32[]{:S(2)}) %all-to-all-start) | async-done | bytes 655392 | tf_op jit(solution)/shard_map/all_to_all | solution.py:257
  56.7 1.1 %fusion = f32[5,8,256]{2,1,0:T(8,128)S(1)} fusion(f32[16,5,8,256]{3,2,1,0:T(8,128)} %all-to-all-done), kind=kLoop, calls=%fused_computation.9 | loop fusion | flops 153600 | bytes 696320 | tf_op jit(solution)/shard_map/add | solution.py:258
  57.8 4.0 %collective-permute-start.11 = (f32[5,8,256]{2,1,0:T(8,128)S(1)}, f32[5,8,256]{2,1,0:T(8,128)S(1)}, u32[]{:S(2)}, u32[]{:S(2)}) collective-permute-start(f32[5,8,256]{2,1,0:T(8,128)S(1)} %fusion), channel_id=1, source_target_pairs={{0,96},{32,64},{64,32},{96,0},{128,224},{160,192},{192,160},{224,1... | collective-permute-start | bytes 122888 | tf_op jit(solution)/shard_map/ppermute | solution.py:263
  61.8 0.0 collective-permute-start.10
  61.8 0.4 collective-permute-start.9
  62.2 0.1 collective-permute-start.14
  62.3 3.8 %collective-permute-start.13 = (f32[2,128,256]{2,1,0:T(8,128)S(1)}, f32[2,128,256]{2,1,0:T(8,128)S(1)}, u32[]{:S(2)}, u32[]{:S(2)}) collective-permute-start(f32[2,128,256]{2,1,0:T(8,128)S(1)} %get-tuple-element.33), channel_id=1, source_target_pairs={{16,0},{32,16},{48,32},{64,48},{80,64},{96,80},{112,96},{128,112},... | collective-permute-start | bytes 786440 | tf_op jit(solution)/shard_map/ppermute | solution.py:261
  66.2 0.0 collective-permute-done.11
  66.2 0.0 collective-permute-done.10
  66.2 0.0 collective-permute-done.9
  66.2 6.4 %collective-permute-start.12 = (f32[5,8,256]{2,1,0:T(8,128)S(1)}, f32[5,8,256]{2,1,0:T(8,128)S(1)}, u32[]{:S(2)}, u32[]{:S(2)}) collective-permute-start(f32[5,8,256]{2,1,0:T(8,128)S(1)} %add_add_fusion), channel_id=1, source_target_pairs={{0,128},{32,160},{64,192},{96,224},{128,0},{160,32},{192,64},{224,... | collective-permute-start | bytes 122888 | tf_op jit(solution)/shard_map/ppermute | solution.py:265
  72.6 1.4 %collective-permute-done.12 = f32[5,8,256]{2,1,0:T(8,128)S(1)} collective-permute-done((f32[5,8,256]{2,1,0:T(8,128)S(1)}, f32[5,8,256]{2,1,0:T(8,128)S(1)}, u32[]{:S(2)}, u32[]{:S(2)}) %collective-permute-start.12) | collective-permute-done | bytes 40992 | tf_op jit(solution)/shard_map/ppermute | solution.py:265
  74.0 0.0 collective-permute-done.14
  74.0 1.4 %collective-permute-done.13 = f32[2,128,256]{2,1,0:T(8,128)S(1)} collective-permute-done((f32[2,128,256]{2,1,0:T(8,128)S(1)}, f32[2,128,256]{2,1,0:T(8,128)S(1)}, u32[]{:S(2)}, u32[]{:S(2)}) %collective-permute-start.13) | collective-permute-done | bytes 262176 | tf_op jit(solution)/shard_map/ppermute | solution.py:261
  75.5 14.8 %all_to_all.10.own = f32[16,4,8,256]{3,2,1,0:T(8,128)S(1)} all-to-all(f32[16,4,8,256]{3,2,1,0:T(8,128)S(1)} %broadcast_in_dim.2), channel_id=1, replica_groups=mesh['z'=8,'xl'=2,'xh'=2,'y'=4,'co'=2] {'xh','xl','y'}, dimensions={0} | all-to-all | bytes 1048576 | tf_op jit(solution)/shard_map/all_to_all | solution.py:271
  90.3 4.0 %collective-permute-start.15 = (f32[16,4,8,256]{3,2,1,0:T(8,128)S(1)}, f32[16,4,8,256]{3,2,1,0:T(8,128)S(1)}, u32[]{:S(2)}, u32[]{:S(2)}) collective-permute-start(f32[16,4,8,256]{3,2,1,0:T(8,128)S(1)} %all_to_all.10.own), channel_id=1, source_target_pairs={{0,1},{1,0},{2,3},{3,2},{4,5},{5,4},{6,7},{7,6},{8,9},{9,8},{10,11... | collective-permute-start | bytes 1572872 | tf_op jit(solution)/shard_map/ppermute | solution.py:273
  94.2 0.9 maximum_add_fusion.1
  95.1 0.7 collective-permute-done.15.swapped
  95.8 1.0 %shard_map.78 = f32[2,2,256,256]{3,2,1,0:T(8,128)} custom-call(s32[1]{0:T(128)} %bitcast.2.half, f32[16,4,8,256]{3,2,1,0:T(8,128)S(1)} %all_to_all.10.own, f32[16,4,8,256]{3,2,1,0:T(8,128)S(1)} %collective-permute-done.15.swapped), custom_call_target="tpu_custom_call" | custom-call | tf_op jit(solution)/shard_map/pallas_call | solution.py:228
  (16 shorter events, 0.2 us)
Async XLA Ops:
  0.6 8.6 %copy-start = (f32[2,256,256]{2,1,0:T(8,128)S(1)}, f32[2,256,256]{2,1,0:T(8,128)}, u32[]{:S(2)}) copy-start(f32[2,256,256]{2,1,0:T(8,128)} %tile) | copy-start | bytes 1572868
  1.8 13.5 %collective-permute-start.1 = (f32[2,128,256]{2,1,0:T(8,128)S(1)}, f32[2,128,256]{2,1,0:T(8,128)S(1)}, u32[]{:S(2)}, u32[]{:S(2)}) collective-permute-start(f32[2,128,256]{2,1,0:T(8,128)S(1)} %get-tuple-element.36), channel_id=1, source_target_pairs={{0,16},{16,32},{32,48},{48,64},{64,80},{80,96},{96,112},{112,128},... | collective-permute-start | bytes 786440 | tf_op jit(solution)/shard_map/ppermute | solution.py:245
  3.9 12.4 %collective-permute-start = (f32[2,128,256]{2,1,0:T(8,128)S(1)}, f32[2,128,256]{2,1,0:T(8,128)S(1)}, u32[]{:S(2)}, u32[]{:S(2)}) collective-permute-start(f32[2,128,256]{2,1,0:T(8,128)S(1)} %get-tuple-element.37), channel_id=1, source_target_pairs={{16,0},{32,16},{48,32},{64,48},{80,64},{96,80},{112,96},{128,112},... | collective-permute-start | bytes 786440 | tf_op jit(solution)/shard_map/ppermute | solution.py:246
  9.3 16.6 %copy-start.3 = (bf16[512,512]{1,0:T(8,128)(2,1)S(1)}, bf16[512,512]{1,0:T(8,128)(2,1)}, u32[]{:S(2)}) copy-start(bf16[512,512]{1,0:T(8,128)(2,1)} %constant.32.clone.bwd_hbm) | copy-start | bytes 1572868
  9.3 16.6 %copy-start.4 = (bf16[512,512]{1,0:T(8,128)(2,1)S(1)}, bf16[512,512]{1,0:T(8,128)(2,1)}, u32[]{:S(2)}) copy-start(bf16[512,512]{1,0:T(8,128)(2,1)} %constant.31.clone.fwd_hbm) | copy-start | bytes 1572868
  9.3 10.5 %collective-permute-start.3 = (f32[2,256,128]{2,1,0:T(8,128)S(1)}, f32[2,256,128]{2,1,0:T(8,128)S(1)}, u32[]{:S(2)}, u32[]{:S(2)}) collective-permute-start(f32[2,256,128]{2,1,0:T(8,128)S(1)} %get-tuple-element.34), channel_id=1, source_target_pairs={{1,0},{2,1},{3,2},{4,3},{5,4},{6,5},{7,6},{8,7},{9,8},{10,9},{11,1... | collective-permute-start | bytes 786440 | tf_op jit(solution)/shard_map/ppermute | solution.py:248
  10.4 15.6 %copy-start.1 = (f32[2,2,256,256]{3,2,1,0:T(8,128)S(1)}, f32[2,2,256,256]{3,2,1,0:T(8,128)}, u32[]{:S(2)}) copy-start(f32[2,2,256,256]{3,2,1,0:T(8,128)} %probe.1) | copy-start | bytes 3145732
  10.4 15.6 %copy-start.2 = (f32[4,1,256,256]{3,2,1,0:T(8,128)S(1)}, f32[4,1,256,256]{3,2,1,0:T(8,128)}, u32[]{:S(2)}) copy-start(f32[4,1,256,256]{3,2,1,0:T(8,128)} %amp.1) | copy-start | bytes 3145732
  10.4 9.5 %collective-permute-start.2 = (f32[2,256,128]{2,1,0:T(8,128)S(1)}, f32[2,256,128]{2,1,0:T(8,128)S(1)}, u32[]{:S(2)}, u32[]{:S(2)}) collective-permute-start(f32[2,256,128]{2,1,0:T(8,128)S(1)} %get-tuple-element.35), channel_id=1, source_target_pairs={{0,1},{1,2},{2,3},{3,4},{4,5},{5,6},{6,7},{7,8},{8,9},{9,10},{10,1... | collective-permute-start | bytes 786440 | tf_op jit(solution)/shard_map/ppermute | solution.py:247
  16.4 6.6 %collective-permute-start.4 = (f32[2,2,128,128]{3,2,1,0:T(8,128)S(1)}, f32[2,2,128,128]{3,2,1,0:T(8,128)S(1)}, u32[]{:S(2)}, u32[]{:S(2)}) collective-permute-start(f32[2,2,128,128]{3,2,1,0:T(8,128)S(1)} %pad_maximum_fusion), channel_id=1, source_target_pairs={{0,1},{1,2},{2,3},{3,4},{4,5},{5,6},{6,7},{7,8},{8,9},{9,10},{10,1... | collective-permute-start | bytes 786440 | tf_op jit(solution)/shard_map/ppermute | solution.py:250
  19.7 6.2 %copy-start.5 = (s32[4,1,2]{0,2,1:T(2,128)S(1)}, s32[4,1,2]{0,2,1:T(2,128)}, u32[]{:S(2)}) copy-start(s32[4,1,2]{0,2,1:T(2,128)} %param.9) | copy-start | bytes 100
  19.7 6.2 %collective-permute-start.5 = (f32[2,2,128,128]{3,2,1,0:T(8,128)S(1)}, f32[2,2,128,128]{3,2,1,0:T(8,128)S(1)}, u32[]{:S(2)}, u32[]{:S(2)}) collective-permute-start(f32[2,2,128,128]{3,2,1,0:T(8,128)S(1)} %pad_maximum_fusion.1), channel_id=1, source_target_pairs={{1,0},{2,1},{3,2},{4,3},{5,4},{6,5},{7,6},{8,7},{9,8},{10,9},{11,1... | collective-permute-start | bytes 786440 | tf_op jit(solution)/shard_map/ppermute | solution.py:251
  34.0 3.9 %collective-permute-start.6 = (f32[16,5,8,256]{3,2,1,0:T(8,128)S(1)}, f32[16,5,8,256]{3,2,1,0:T(8,128)S(1)}, u32[]{:S(2)}, u32[]{:S(2)}) collective-permute-start(f32[16,5,8,256]{3,2,1,0:T(8,128)S(1)} %get-tuple-element.22), channel_id=1, source_target_pairs={{0,1},{1,0},{2,3},{3,2},{4,5},{5,4},{6,7},{7,6},{8,9},{9,8},{10,11... | collective-permute-start | bytes 1966088 | tf_op jit(solution)/shard_map/ppermute | solution.py:254
  36.1 9.6 %collective-permute-start.7 = (f32[2,512,128]{2,1,0:T(8,128)S(1)}, f32[2,512,128]{2,1,0:T(8,128)}, u32[]{:S(2)}, u32[]{:S(2)}) collective-permute-start(f32[2,512,128]{2,1,0:T(8,128)S(1)} %get-tuple-element.24), channel_id=1, source_target_pairs={{0,1},{1,2},{2,3},{3,4},{4,5},{5,6},{6,7},{7,8},{8,9},{9,10},{10,1... | collective-permute-start | bytes 1572872 | tf_op jit(solution)/shard_map/ppermute | solution.py:256
  36.1 9.6 %collective-permute-start.8 = (f32[2,512,128]{2,1,0:T(8,128)S(1)}, f32[2,512,128]{2,1,0:T(8,128)}, u32[]{:S(2)}, u32[]{:S(2)}) collective-permute-start(f32[2,512,128]{2,1,0:T(8,128)S(1)} %get-tuple-element.25), channel_id=1, source_target_pairs={{1,0},{2,1},{3,2},{4,3},{5,4},{6,5},{7,6},{8,7},{9,8},{10,9},{11,1... | collective-permute-start | bytes 1572872 | tf_op jit(solution)/shard_map/ppermute | solution.py:255
  38.8 17.9 %all-to-all-start = ((f32[16,5,8,256]{3,2,1,0:T(8,128)}), f32[16,5,8,256]{3,2,1,0:T(8,128)}, u32[]{:S(2)}, u32[]{:S(2)}) async-start(f32[16,5,8,256]{3,2,1,0:T(8,128)} %add.97), calls=%async_computation | async-start | bytes 1310720 | tf_op jit(solution)/shard_map/all_to_all | solution.py:257
  57.8 8.3 %collective-permute-start.11 = (f32[5,8,256]{2,1,0:T(8,128)S(1)}, f32[5,8,256]{2,1,0:T(8,128)S(1)}, u32[]{:S(2)}, u32[]{:S(2)}) collective-permute-start(f32[5,8,256]{2,1,0:T(8,128)S(1)} %fusion), channel_id=1, source_target_pairs={{0,96},{32,64},{64,32},{96,0},{128,224},{160,192},{192,160},{224,1... | collective-permute-start | bytes 122888 | tf_op jit(solution)/shard_map/ppermute | solution.py:263
  61.8 4.4 %collective-permute-start.10 = (f32[5,8,256]{2,1,0:T(8,128)S(1)}, f32[5,8,256]{2,1,0:T(8,128)S(1)}, u32[]{:S(2)}, u32[]{:S(2)}) collective-permute-start(f32[5,8,256]{2,1,0:T(8,128)S(1)} %fusion), channel_id=1, source_target_pairs={{0,64},{32,96},{64,0},{96,32},{128,192},{160,224},{192,128},{224,1... | collective-permute-start | bytes 122888 | tf_op jit(solution)/shard_map/ppermute | solution.py:263
  61.8 4.4 %collective-permute-start.9 = (f32[5,8,256]{2,1,0:T(8,128)S(1)}, f32[5,8,256]{2,1,0:T(8,128)S(1)}, u32[]{:S(2)}, u32[]{:S(2)}) collective-permute-start(f32[5,8,256]{2,1,0:T(8,128)S(1)} %fusion), channel_id=1, source_target_pairs={{0,32},{32,0},{64,96},{96,64},{128,160},{160,128},{192,224},{224,1... | collective-permute-start | bytes 122888 | tf_op jit(solution)/shard_map/ppermute | solution.py:263
  62.2 11.8 %collective-permute-start.14 = (f32[2,128,256]{2,1,0:T(8,128)S(1)}, f32[2,128,256]{2,1,0:T(8,128)S(1)}, u32[]{:S(2)}, u32[]{:S(2)}) collective-permute-start(f32[2,128,256]{2,1,0:T(8,128)S(1)} %get-tuple-element.32), channel_id=1, source_target_pairs={{0,16},{16,32},{32,48},{48,64},{64,80},{80,96},{96,112},{112,128},... | collective-permute-start | bytes 786440 | tf_op jit(solution)/shard_map/ppermute | solution.py:262
  62.3 13.1 %collective-permute-start.13 = (f32[2,128,256]{2,1,0:T(8,128)S(1)}, f32[2,128,256]{2,1,0:T(8,128)S(1)}, u32[]{:S(2)}, u32[]{:S(2)}) collective-permute-start(f32[2,128,256]{2,1,0:T(8,128)S(1)} %get-tuple-element.33), channel_id=1, source_target_pairs={{16,0},{32,16},{48,32},{64,48},{80,64},{96,80},{112,96},{128,112},... | collective-permute-start | bytes 786440 | tf_op jit(solution)/shard_map/ppermute | solution.py:261
  66.2 7.8 %collective-permute-start.12 = (f32[5,8,256]{2,1,0:T(8,128)S(1)}, f32[5,8,256]{2,1,0:T(8,128)S(1)}, u32[]{:S(2)}, u32[]{:S(2)}) collective-permute-start(f32[5,8,256]{2,1,0:T(8,128)S(1)} %add_add_fusion), channel_id=1, source_target_pairs={{0,128},{32,160},{64,192},{96,224},{128,0},{160,32},{192,64},{224,... | collective-permute-start | bytes 122888 | tf_op jit(solution)/shard_map/ppermute | solution.py:265
  90.3 5.5 %collective-permute-start.15 = (f32[16,4,8,256]{3,2,1,0:T(8,128)S(1)}, f32[16,4,8,256]{3,2,1,0:T(8,128)S(1)}, u32[]{:S(2)}, u32[]{:S(2)}) collective-permute-start(f32[16,4,8,256]{3,2,1,0:T(8,128)S(1)} %all_to_all.10.own), channel_id=1, source_target_pairs={{0,1},{1,0},{2,3},{3,2},{4,5},{5,4},{6,7},{7,6},{8,9},{9,8},{10,11... | collective-permute-start | bytes 1572872 | tf_op jit(solution)/shard_map/ppermute | solution.py:273

commit v17 on v15

--- a/solution.py
+++ b/solution.py
@@ -260,9 +260,9 @@
     part, folded = lax.optimization_barrier((part, folded))
     from_below = lax.ppermute(folded[:, :HALF], GX, DOWN)
     from_above = lax.ppermute(folded[:, HALF + W :], GX, UP)
-    peers = [lax.ppermute(part, "z", [(i, i ^ step) for i in range(8)]) for step in (3, 2, 1)]
+    peers = [lax.ppermute(part, "z", [(i, i ^ step) for i in range(8)]) for step in (1, 4, 5)]
     part = (part + peers[0]) + (peers[1] + peers[2])
-    part = part + lax.ppermute(part, "z", [(i, i ^ 4) for i in range(8)])
+    part = part + lax.ppermute(part, "z", [(i, i ^ 2) for i in range(8)])
     part, from_below, from_above = lax.optimization_barrier((part, from_below, from_above))
     planes = probe_field.reshape(2 * MODES, W, W)
     local = lax.dynamic_slice_in_dim(planes, block, 8, 1)

time: 97.3 us -> 100 us (1.028)
  waiting for transfers between devices: 24.8 us -> 31.1 us
  starting transfers between devices: 40.4 us -> 38.5 us
  blocking collectives: 16.2 us -> 14.7 us
    ppermute x1, starting transfers between devices: 5.43 us -> 0.99 us  [body(): part = part + lax.ppermute(part, 'z', [(i, i ^ 2) for i in range(8)])]
    ppermute x3, starting transfers between devices: 4.28 us -> 7.71 us  [body(): lax.ppermute(part, 'z', [(i, i ^ step) for i in range(8)])]
    ppermute x1, waiting for transfers between devices: 0.01 us -> 3.15 us  [body(): from_below = lax.ppermute(folded[:, :HALF], GX, DOWN)]
    ppermute x1, waiting for transfers between devices: 1.42 us -> 3.92 us  [body(): part = part + lax.ppermute(part, 'z', [(i, i ^ 2) for i in range(8)])]
    all_to_all x1, blocking collectives: 16.2 us -> 14.7 us  [body(): lax.all_to_all(jnp.broadcast_to(local[None], (16,) + local.shape), group,...]
  transfers between devices with their start and end apart: 17 -> 17, of which waited for: 9 -> 10; matrix products, arithmetic and copies ran while one was open for 3% -> 3% of each run, Pallas kernels for 0% -> 0%
where the time goes in v17:
time: 100 us; the launch traced here: 99.9 us
  starting transfers between devices  38.5 us (38%)
  waiting for transfers between devices  31.1 us (31%)
  blocking collectives  14.7 us (15%)
  Pallas kernels  9.21 us (9%)
  other arithmetic  4.27 us (4%)
  local copies, waits for them, and re-layouts  1.3 us (1%)
    all_to_all x1, blocking collectives, body(): lax.all_to_all(jnp.broadcast_to(local[None], (16,) + local.shape), group,...  14.7 us
    all_to_all x1, waiting for transfers between devices, body(): pieces = lax.all_to_all(part, group, 0, 0, tiled=True)  9.69 us
    pallas_call x1, Pallas kernels, correct(): pl.pallas_call(kernel, out_shape=(part, part, strip, jax.ShapeDtypeStruct...  8.17 us
    ppermute x3, starting transfers between devices, body(): lax.ppermute(part, 'z', [(i, i ^ step) for i in range(8)])  7.71 us
    all_to_all x1, starting transfers between devices, body(): pieces = lax.all_to_all(part, group, 0, 0, tiled=True)  6.95 us
    ppermute x1, starting transfers between devices, body(): bot = lax.ppermute(object_field[:, first], GX, DOWN)  5.38 us
    ppermute x1, waiting for transfers between devices, body(): part = part + lax.ppermute(part, 'z', [(i, i ^ 2) for i in range(8)])  3.92 us
    ppermute x1, waiting for transfers between devices, body(): top = lax.ppermute(object_field[:, last], GX, UP)  3.61 us
  transfers between devices with their start and end apart: 17, of which 10 were waited for; matrix products, arithmetic and copies ran while one was open for 3% of the time, Pallas kernels for 0%

profile of v17, /device:TPU:1, one launch (start us, length us, event | category | flops | bytes accessed | tf_op | source)
XLA Modules:
  0.0 99.9 jit_solution(8740903929899631808)
XLA Ops:
  0.6 0.0 copy-start
  0.7 1.1 %fusion.3 = (f32[2,128,256]{2,1,0:T(8,128)S(1)}, f32[2,128,256]{2,1,0:T(8,128)S(1)}) fusion(f32[2,256,256]{2,1,0:T(8,128)} %tile), kind=kLoop, calls=%fused_computation.30 | loop fusion | bytes 1048576 | tf_op jit(solution)/shard_map/slice | solution.py:245
  1.8 2.1 %collective-permute-start.1 = (f32[2,128,256]{2,1,0:T(8,128)S(1)}, f32[2,128,256]{2,1,0:T(8,128)S(1)}, u32[]{:S(2)}, u32[]{:S(2)}) collective-permute-start(f32[2,128,256]{2,1,0:T(8,128)S(1)} %get-tuple-element.36), channel_id=1, source_target_pairs={{0,16},{16,32},{32,48},{48,64},{64,80},{80,96},{96,112},{112,128},... | collective-permute-start | bytes 786440 | tf_op jit(solution)/shard_map/ppermute | solution.py:245
  3.9 5.4 %collective-permute-start = (f32[2,128,256]{2,1,0:T(8,128)S(1)}, f32[2,128,256]{2,1,0:T(8,128)S(1)}, u32[]{:S(2)}, u32[]{:S(2)}) collective-permute-start(f32[2,128,256]{2,1,0:T(8,128)S(1)} %get-tuple-element.37), channel_id=1, source_target_pairs={{16,0},{32,16},{48,32},{64,48},{80,64},{96,80},{112,96},{128,112},... | collective-permute-start | bytes 786440 | tf_op jit(solution)/shard_map/ppermute | solution.py:246
  9.3 0.0 copy-done
  9.3 1.0 %collective-permute-start.3 = (f32[2,256,128]{2,1,0:T(8,128)S(1)}, f32[2,256,128]{2,1,0:T(8,128)S(1)}, u32[]{:S(2)}, u32[]{:S(2)}) collective-permute-start(f32[2,256,128]{2,1,0:T(8,128)S(1)} %get-tuple-element.34), channel_id=1, source_target_pairs={{1,0},{2,1},{3,2},{4,3},{5,4},{6,5},{7,6},{8,7},{9,8},{10,9},{11,1... | collective-permute-start | bytes 786440 | tf_op jit(solution)/shard_map/ppermute | solution.py:248
  10.4 1.3 %collective-permute-start.2 = (f32[2,256,128]{2,1,0:T(8,128)S(1)}, f32[2,256,128]{2,1,0:T(8,128)S(1)}, u32[]{:S(2)}, u32[]{:S(2)}) collective-permute-start(f32[2,256,128]{2,1,0:T(8,128)S(1)} %get-tuple-element.35), channel_id=1, source_target_pairs={{0,1},{1,2},{2,3},{3,4},{4,5},{5,6},{6,7},{7,8},{8,9},{9,10},{10,1... | collective-permute-start | bytes 786440 | tf_op jit(solution)/shard_map/ppermute | solution.py:247
  11.7 3.6 %collective-permute-done.1.top = f32[2,128,256]{2,1,0:T(8,128)S(1)} collective-permute-done((f32[2,128,256]{2,1,0:T(8,128)S(1)}, f32[2,128,256]{2,1,0:T(8,128)S(1)}, u32[]{:S(2)}, u32[]{:S(2)}) %collective-permute-start.1) | collective-permute-done | bytes 262176 | tf_op jit(solution)/shard_map/ppermute | solution.py:245
  15.3 1.1 %collective-permute-done.bot = f32[2,128,256]{2,1,0:T(8,128)S(1)} collective-permute-done((f32[2,128,256]{2,1,0:T(8,128)S(1)}, f32[2,128,256]{2,1,0:T(8,128)S(1)}, u32[]{:S(2)}, u32[]{:S(2)}) %collective-permute-start) | collective-permute-done | bytes 262176 | tf_op jit(solution)/shard_map/ppermute | solution.py:246
  16.4 3.3 %collective-permute-start.4 = (f32[2,2,128,128]{3,2,1,0:T(8,128)S(1)}, f32[2,2,128,128]{3,2,1,0:T(8,128)S(1)}, u32[]{:S(2)}, u32[]{:S(2)}) collective-permute-start(f32[2,2,128,128]{3,2,1,0:T(8,128)S(1)} %pad_maximum_fusion), channel_id=1, source_target_pairs={{0,1},{1,2},{2,3},{3,4},{4,5},{5,6},{6,7},{7,8},{8,9},{9,10},{10,1... | collective-permute-start | bytes 786440 | tf_op jit(solution)/shard_map/ppermute | solution.py:250
  19.7 0.0 copy-start.5
  19.7 0.1 collective-permute-start.5
  19.8 0.0 collective-permute-done.3.right
  19.8 0.0 collective-permute-done.2.left
  19.9 3.2 %collective-permute-done.4.left_ends = f32[2,2,128,128]{3,2,1,0:T(8,128)S(1)} collective-permute-done((f32[2,2,128,128]{3,2,1,0:T(8,128)S(1)}, f32[2,2,128,128]{3,2,1,0:T(8,128)S(1)}, u32[]{:S(2)}, u32[]{:S(2)}) %collective-permute-start.4) | collective-permute-done | bytes 262176 | tf_op jit(solution)/shard_map/ppermute | solution.py:250
  23.0 2.9 %collective-permute-done.5.right_ends = f32[2,2,128,128]{3,2,1,0:T(8,128)S(1)} collective-permute-done((f32[2,2,128,128]{3,2,1,0:T(8,128)S(1)}, f32[2,2,128,128]{3,2,1,0:T(8,128)S(1)}, u32[]{:S(2)}, u32[]{:S(2)}) %collective-permute-start.5) | collective-permute-done | bytes 262176 | tf_op jit(solution)/shard_map/ppermute | solution.py:251
  25.9 0.0 copy-done.1
  25.9 0.0 copy-done.2
  25.9 0.0 copy-done.5
  25.9 8.2 %shard_map.77 = (f32[16,5,8,256]{3,2,1,0:T(8,128)S(1)}, f32[16,5,8,256]{3,2,1,0:T(8,128)S(1)}, f32[2,512,128]{2,1,0:T(8,128)S(1)}, f32[2,512,256]{2,1,0:T(8,128)S(1)}, f32[2,512,128]{2,1,0:T(8,128)S(1)}) custom-call(s32[2,4]{1,0:T(2,128)S(1)} %bitcast.20, s32[1]{0:T(128)} %bitcast.2.half, f32[2,256,256]{2,1,0:T(8,128)S(1)} %copy-done, ...), custom_call_target="tpu_custom_call" | custom-call | tf_op jit(solution)/shard_map/pallas_call | solution.py:187
  34.1 2.1 %collective-permute-start.6 = (f32[16,5,8,256]{3,2,1,0:T(8,128)S(1)}, f32[16,5,8,256]{3,2,1,0:T(8,128)S(1)}, u32[]{:S(2)}, u32[]{:S(2)}) collective-permute-start(f32[16,5,8,256]{3,2,1,0:T(8,128)S(1)} %get-tuple-element.22), channel_id=1, source_target_pairs={{0,1},{1,0},{2,3},{3,2},{4,5},{5,4},{6,7},{7,6},{8,9},{9,8},{10,11... | collective-permute-start | bytes 1966088 | tf_op jit(solution)/shard_map/ppermute | solution.py:254
  36.2 0.0 collective-permute-start.7
  36.2 0.5 collective-permute-start.8
  36.7 1.2 %collective-permute-done.6 = f32[16,5,8,256]{3,2,1,0:T(8,128)S(1)} collective-permute-done((f32[16,5,8,256]{3,2,1,0:T(8,128)S(1)}, f32[16,5,8,256]{3,2,1,0:T(8,128)S(1)}, u32[]{:S(2)}, u32[]{:S(2)}) %collective-permute-start.6) | collective-permute-done | bytes 655392 | tf_op jit(solution)/shard_map/ppermute | solution.py:254
  38.0 0.9 add.97
  38.9 7.0 %all-to-all-start = ((f32[16,5,8,256]{3,2,1,0:T(8,128)}), f32[16,5,8,256]{3,2,1,0:T(8,128)}, u32[]{:S(2)}, u32[]{:S(2)}) async-start(f32[16,5,8,256]{3,2,1,0:T(8,128)} %add.97), calls=%async_computation | async-start | bytes 1310720 | tf_op jit(solution)/shard_map/all_to_all | solution.py:257
  45.8 0.0 collective-permute-done.7
  45.8 0.0 collective-permute-done.8
  45.9 1.3 %maximum_add_fusion = f32[2,512,256]{2,1,0:T(8,128)S(1)} fusion(f32[2,512,256]{2,1,0:T(8,128)S(1)} %get-tuple-element.23, f32[2,512,128]{2,1,0:T(8,128)} %collective-permute-done.8, f32[2,512,128]{2,1,0:T(8,128)} %collective-permute-done.7), kind=kLoop, calls=%fused_computation | loop fusion | flops 524288 | bytes 3145728 | tf_op jit(solution)/shard_map/add | solution.py:259
  47.2 9.7 %all-to-all-done = f32[16,5,8,256]{3,2,1,0:T(8,128)} async-done(((f32[16,5,8,256]{3,2,1,0:T(8,128)}), f32[16,5,8,256]{3,2,1,0:T(8,128)}, u32[]{:S(2)}, u32[]{:S(2)}) %all-to-all-start) | async-done | bytes 655392 | tf_op jit(solution)/shard_map/all_to_all | solution.py:257
  56.9 1.1 %fusion = f32[5,8,256]{2,1,0:T(8,128)S(1)} fusion(f32[16,5,8,256]{3,2,1,0:T(8,128)} %all-to-all-done), kind=kLoop, calls=%fused_computation.9 | loop fusion | flops 153600 | bytes 696320 | tf_op jit(solution)/shard_map/add | solution.py:258
  58.0 6.1 %collective-permute-start.11 = (f32[5,8,256]{2,1,0:T(8,128)S(1)}, f32[5,8,256]{2,1,0:T(8,128)S(1)}, u32[]{:S(2)}, u32[]{:S(2)}) collective-permute-start(f32[5,8,256]{2,1,0:T(8,128)S(1)} %fusion), channel_id=1, source_target_pairs={{0,160},{32,128},{64,224},{96,192},{128,32},{160,0},{192,96},{224,... | collective-permute-start | bytes 122888 | tf_op jit(solution)/shard_map/ppermute | solution.py:263
  64.1 1.4 %collective-permute-start.10 = (f32[5,8,256]{2,1,0:T(8,128)S(1)}, f32[5,8,256]{2,1,0:T(8,128)S(1)}, u32[]{:S(2)}, u32[]{:S(2)}) collective-permute-start(f32[5,8,256]{2,1,0:T(8,128)S(1)} %fusion), channel_id=1, source_target_pairs={{0,128},{32,160},{64,192},{96,224},{128,0},{160,32},{192,64},{224,... | collective-permute-start | bytes 122888 | tf_op jit(solution)/shard_map/ppermute | solution.py:263
  65.5 0.2 collective-permute-start.9
  65.7 0.1 collective-permute-start.14
  65.8 3.6 %collective-permute-start.13 = (f32[2,128,256]{2,1,0:T(8,128)S(1)}, f32[2,128,256]{2,1,0:T(8,128)S(1)}, u32[]{:S(2)}, u32[]{:S(2)}) collective-permute-start(f32[2,128,256]{2,1,0:T(8,128)S(1)} %get-tuple-element.33), channel_id=1, source_target_pairs={{16,0},{32,16},{48,32},{64,48},{80,64},{96,80},{112,96},{128,112},... | collective-permute-start | bytes 786440 | tf_op jit(solution)/shard_map/ppermute | solution.py:261
  69.4 0.0 collective-permute-done.11
  69.4 1.7 %collective-permute-done.10 = f32[5,8,256]{2,1,0:T(8,128)S(1)} collective-permute-done((f32[5,8,256]{2,1,0:T(8,128)S(1)}, f32[5,8,256]{2,1,0:T(8,128)S(1)}, u32[]{:S(2)}, u32[]{:S(2)}) %collective-permute-start.10) | collective-permute-done | bytes 40992 | tf_op jit(solution)/shard_map/ppermute | solution.py:263
  71.1 0.0 collective-permute-done.9
  71.1 1.0 collective-permute-start.12
  72.1 3.9 %collective-permute-done.12 = f32[5,8,256]{2,1,0:T(8,128)S(1)} collective-permute-done((f32[5,8,256]{2,1,0:T(8,128)S(1)}, f32[5,8,256]{2,1,0:T(8,128)S(1)}, u32[]{:S(2)}, u32[]{:S(2)}) %collective-permute-start.12) | collective-permute-done | bytes 40992 | tf_op jit(solution)/shard_map/ppermute | solution.py:265
  76.0 0.0 collective-permute-done.14
  76.0 3.2 %collective-permute-done.13 = f32[2,128,256]{2,1,0:T(8,128)S(1)} collective-permute-done((f32[2,128,256]{2,1,0:T(8,128)S(1)}, f32[2,128,256]{2,1,0:T(8,128)S(1)}, u32[]{:S(2)}, u32[]{:S(2)}) %collective-permute-start.13) | collective-permute-done | bytes 262176 | tf_op jit(solution)/shard_map/ppermute | solution.py:261
  79.3 14.7 %all_to_all.10.own = f32[16,4,8,256]{3,2,1,0:T(8,128)S(1)} all-to-all(f32[16,4,8,256]{3,2,1,0:T(8,128)S(1)} %broadcast_in_dim.2), channel_id=1, replica_groups=mesh['z'=8,'xl'=2,'xh'=2,'y'=4,'co'=2] {'xh','xl','y'}, dimensions={0} | all-to-all | bytes 1048576 | tf_op jit(solution)/shard_map/all_to_all | solution.py:271
  94.0 3.4 %collective-permute-start.15 = (f32[16,4,8,256]{3,2,1,0:T(8,128)S(1)}, f32[16,4,8,256]{3,2,1,0:T(8,128)S(1)}, u32[]{:S(2)}, u32[]{:S(2)}) collective-permute-start(f32[16,4,8,256]{3,2,1,0:T(8,128)S(1)} %all_to_all.10.own), channel_id=1, source_target_pairs={{0,1},{1,0},{2,3},{3,2},{4,5},{5,4},{6,7},{7,6},{8,9},{9,8},{10,11... | collective-permute-start | bytes 1572872 | tf_op jit(solution)/shard_map/ppermute | solution.py:273
  97.3 0.9 maximum_add_fusion.1
  98.2 0.7 collective-permute-done.15.swapped
  98.9 1.0 %shard_map.78 = f32[2,2,256,256]{3,2,1,0:T(8,128)} custom-call(s32[1]{0:T(128)} %bitcast.2.half, f32[16,4,8,256]{3,2,1,0:T(8,128)S(1)} %all_to_all.10.own, f32[16,4,8,256]{3,2,1,0:T(8,128)S(1)} %collective-permute-done.15.swapped), custom_call_target="tpu_custom_call" | custom-call | tf_op jit(solution)/shard_map/pallas_call | solution.py:228
  (16 shorter events, 0.2 us)
Async XLA Ops:
  0.6 8.6 %copy-start = (f32[2,256,256]{2,1,0:T(8,128)S(1)}, f32[2,256,256]{2,1,0:T(8,128)}, u32[]{:S(2)}) copy-start(f32[2,256,256]{2,1,0:T(8,128)} %tile) | copy-start | bytes 1572868
  1.8 13.5 %collective-permute-start.1 = (f32[2,128,256]{2,1,0:T(8,128)S(1)}, f32[2,128,256]{2,1,0:T(8,128)S(1)}, u32[]{:S(2)}, u32[]{:S(2)}) collective-permute-start(f32[2,128,256]{2,1,0:T(8,128)S(1)} %get-tuple-element.36), channel_id=1, source_target_pairs={{0,16},{16,32},{32,48},{48,64},{64,80},{80,96},{96,112},{112,128},... | collective-permute-start | bytes 786440 | tf_op jit(solution)/shard_map/ppermute | solution.py:245
  3.9 12.4 %collective-permute-start = (f32[2,128,256]{2,1,0:T(8,128)S(1)}, f32[2,128,256]{2,1,0:T(8,128)S(1)}, u32[]{:S(2)}, u32[]{:S(2)}) collective-permute-start(f32[2,128,256]{2,1,0:T(8,128)S(1)} %get-tuple-element.37), channel_id=1, source_target_pairs={{16,0},{32,16},{48,32},{64,48},{80,64},{96,80},{112,96},{128,112},... | collective-permute-start | bytes 786440 | tf_op jit(solution)/shard_map/ppermute | solution.py:246
  9.3 16.6 %copy-start.3 = (bf16[512,512]{1,0:T(8,128)(2,1)S(1)}, bf16[512,512]{1,0:T(8,128)(2,1)}, u32[]{:S(2)}) copy-start(bf16[512,512]{1,0:T(8,128)(2,1)} %constant.32.clone.bwd_hbm) | copy-start | bytes 1572868
  9.3 16.6 %copy-start.4 = (bf16[512,512]{1,0:T(8,128)(2,1)S(1)}, bf16[512,512]{1,0:T(8,128)(2,1)}, u32[]{:S(2)}) copy-start(bf16[512,512]{1,0:T(8,128)(2,1)} %constant.31.clone.fwd_hbm) | copy-start | bytes 1572868
  9.3 10.5 %collective-permute-start.3 = (f32[2,256,128]{2,1,0:T(8,128)S(1)}, f32[2,256,128]{2,1,0:T(8,128)S(1)}, u32[]{:S(2)}, u32[]{:S(2)}) collective-permute-start(f32[2,256,128]{2,1,0:T(8,128)S(1)} %get-tuple-element.34), channel_id=1, source_target_pairs={{1,0},{2,1},{3,2},{4,3},{5,4},{6,5},{7,6},{8,7},{9,8},{10,9},{11,1... | collective-permute-start | bytes 786440 | tf_op jit(solution)/shard_map/ppermute | solution.py:248
  10.4 15.6 %copy-start.1 = (f32[2,2,256,256]{3,2,1,0:T(8,128)S(1)}, f32[2,2,256,256]{3,2,1,0:T(8,128)}, u32[]{:S(2)}) copy-start(f32[2,2,256,256]{3,2,1,0:T(8,128)} %probe.1) | copy-start | bytes 3145732
  10.4 15.6 %copy-start.2 = (f32[4,1,256,256]{3,2,1,0:T(8,128)S(1)}, f32[4,1,256,256]{3,2,1,0:T(8,128)}, u32[]{:S(2)}) copy-start(f32[4,1,256,256]{3,2,1,0:T(8,128)} %amp.1) | copy-start | bytes 3145732
  10.4 9.5 %collective-permute-start.2 = (f32[2,256,128]{2,1,0:T(8,128)S(1)}, f32[2,256,128]{2,1,0:T(8,128)S(1)}, u32[]{:S(2)}, u32[]{:S(2)}) collective-permute-start(f32[2,256,128]{2,1,0:T(8,128)S(1)} %get-tuple-element.35), channel_id=1, source_target_pairs={{0,1},{1,2},{2,3},{3,4},{4,5},{5,6},{6,7},{7,8},{8,9},{9,10},{10,1... | collective-permute-start | bytes 786440 | tf_op jit(solution)/shard_map/ppermute | solution.py:247
  16.4 6.6 %collective-permute-start.4 = (f32[2,2,128,128]{3,2,1,0:T(8,128)S(1)}, f32[2,2,128,128]{3,2,1,0:T(8,128)S(1)}, u32[]{:S(2)}, u32[]{:S(2)}) collective-permute-start(f32[2,2,128,128]{3,2,1,0:T(8,128)S(1)} %pad_maximum_fusion), channel_id=1, source_target_pairs={{0,1},{1,2},{2,3},{3,4},{4,5},{5,6},{6,7},{7,8},{8,9},{9,10},{10,1... | collective-permute-start | bytes 786440 | tf_op jit(solution)/shard_map/ppermute | solution.py:250
  19.7 6.2 %copy-start.5 = (s32[4,1,2]{0,2,1:T(2,128)S(1)}, s32[4,1,2]{0,2,1:T(2,128)}, u32[]{:S(2)}) copy-start(s32[4,1,2]{0,2,1:T(2,128)} %param.9) | copy-start | bytes 100
  19.7 6.2 %collective-permute-start.5 = (f32[2,2,128,128]{3,2,1,0:T(8,128)S(1)}, f32[2,2,128,128]{3,2,1,0:T(8,128)S(1)}, u32[]{:S(2)}, u32[]{:S(2)}) collective-permute-start(f32[2,2,128,128]{3,2,1,0:T(8,128)S(1)} %pad_maximum_fusion.1), channel_id=1, source_target_pairs={{1,0},{2,1},{3,2},{4,3},{5,4},{6,5},{7,6},{8,7},{9,8},{10,9},{11,1... | collective-permute-start | bytes 786440 | tf_op jit(solution)/shard_map/ppermute | solution.py:251
  34.1 3.8 %collective-permute-start.6 = (f32[16,5,8,256]{3,2,1,0:T(8,128)S(1)}, f32[16,5,8,256]{3,2,1,0:T(8,128)S(1)}, u32[]{:S(2)}, u32[]{:S(2)}) collective-permute-start(f32[16,5,8,256]{3,2,1,0:T(8,128)S(1)} %get-tuple-element.22), channel_id=1, source_target_pairs={{0,1},{1,0},{2,3},{3,2},{4,5},{5,4},{6,7},{7,6},{8,9},{9,8},{10,11... | collective-permute-start | bytes 1966088 | tf_op jit(solution)/shard_map/ppermute | solution.py:254
  36.2 9.6 %collective-permute-start.7 = (f32[2,512,128]{2,1,0:T(8,128)S(1)}, f32[2,512,128]{2,1,0:T(8,128)}, u32[]{:S(2)}, u32[]{:S(2)}) collective-permute-start(f32[2,512,128]{2,1,0:T(8,128)S(1)} %get-tuple-element.24), channel_id=1, source_target_pairs={{0,1},{1,2},{2,3},{3,4},{4,5},{5,6},{6,7},{7,8},{8,9},{9,10},{10,1... | collective-permute-start | bytes 1572872 | tf_op jit(solution)/shard_map/ppermute | solution.py:256
  36.2 9.6 %collective-permute-start.8 = (f32[2,512,128]{2,1,0:T(8,128)S(1)}, f32[2,512,128]{2,1,0:T(8,128)}, u32[]{:S(2)}, u32[]{:S(2)}) collective-permute-start(f32[2,512,128]{2,1,0:T(8,128)S(1)} %get-tuple-element.25), channel_id=1, source_target_pairs={{1,0},{2,1},{3,2},{4,3},{5,4},{6,5},{7,6},{8,7},{9,8},{10,9},{11,1... | collective-permute-start | bytes 1572872 | tf_op jit(solution)/shard_map/ppermute | solution.py:255
  38.9 18.0 %all-to-all-start = ((f32[16,5,8,256]{3,2,1,0:T(8,128)}), f32[16,5,8,256]{3,2,1,0:T(8,128)}, u32[]{:S(2)}, u32[]{:S(2)}) async-start(f32[16,5,8,256]{3,2,1,0:T(8,128)} %add.97), calls=%async_computation | async-start | bytes 1310720 | tf_op jit(solution)/shard_map/all_to_all | solution.py:257
  58.0 11.4 %collective-permute-start.11 = (f32[5,8,256]{2,1,0:T(8,128)S(1)}, f32[5,8,256]{2,1,0:T(8,128)S(1)}, u32[]{:S(2)}, u32[]{:S(2)}) collective-permute-start(f32[5,8,256]{2,1,0:T(8,128)S(1)} %fusion), channel_id=1, source_target_pairs={{0,160},{32,128},{64,224},{96,192},{128,32},{160,0},{192,96},{224,... | collective-permute-start | bytes 122888 | tf_op jit(solution)/shard_map/ppermute | solution.py:263
  64.1 7.0 %collective-permute-start.10 = (f32[5,8,256]{2,1,0:T(8,128)S(1)}, f32[5,8,256]{2,1,0:T(8,128)S(1)}, u32[]{:S(2)}, u32[]{:S(2)}) collective-permute-start(f32[5,8,256]{2,1,0:T(8,128)S(1)} %fusion), channel_id=1, source_target_pairs={{0,128},{32,160},{64,192},{96,224},{128,0},{160,32},{192,64},{224,... | collective-permute-start | bytes 122888 | tf_op jit(solution)/shard_map/ppermute | solution.py:263
  65.5 5.6 %collective-permute-start.9 = (f32[5,8,256]{2,1,0:T(8,128)S(1)}, f32[5,8,256]{2,1,0:T(8,128)S(1)}, u32[]{:S(2)}, u32[]{:S(2)}) collective-permute-start(f32[5,8,256]{2,1,0:T(8,128)S(1)} %fusion), channel_id=1, source_target_pairs={{0,32},{32,0},{64,96},{96,64},{128,160},{160,128},{192,224},{224,1... | collective-permute-start | bytes 122888 | tf_op jit(solution)/shard_map/ppermute | solution.py:263
  65.7 10.3 %collective-permute-start.14 = (f32[2,128,256]{2,1,0:T(8,128)S(1)}, f32[2,128,256]{2,1,0:T(8,128)S(1)}, u32[]{:S(2)}, u32[]{:S(2)}) collective-permute-start(f32[2,128,256]{2,1,0:T(8,128)S(1)} %get-tuple-element.32), channel_id=1, source_target_pairs={{0,16},{16,32},{32,48},{48,64},{64,80},{80,96},{96,112},{112,128},... | collective-permute-start | bytes 786440 | tf_op jit(solution)/shard_map/ppermute | solution.py:262
  65.8 13.4 %collective-permute-start.13 = (f32[2,128,256]{2,1,0:T(8,128)S(1)}, f32[2,128,256]{2,1,0:T(8,128)S(1)}, u32[]{:S(2)}, u32[]{:S(2)}) collective-permute-start(f32[2,128,256]{2,1,0:T(8,128)S(1)} %get-tuple-element.33), channel_id=1, source_target_pairs={{16,0},{32,16},{48,32},{64,48},{80,64},{96,80},{112,96},{128,112},... | collective-permute-start | bytes 786440 | tf_op jit(solution)/shard_map/ppermute | solution.py:261
  71.1 4.9 %collective-permute-start.12 = (f32[5,8,256]{2,1,0:T(8,128)S(1)}, f32[5,8,256]{2,1,0:T(8,128)S(1)}, u32[]{:S(2)}, u32[]{:S(2)}) collective-permute-start(f32[5,8,256]{2,1,0:T(8,128)S(1)} %add_add_fusion), channel_id=1, source_target_pairs={{0,64},{32,96},{64,0},{96,32},{128,192},{160,224},{192,128},{224,1... | collective-permute-start | bytes 122888 | tf_op jit(solution)/shard_map/ppermute | solution.py:265
  94.0 4.9 %collective-permute-start.15 = (f32[16,4,8,256]{3,2,1,0:T(8,128)S(1)}, f32[16,4,8,256]{3,2,1,0:T(8,128)S(1)}, u32[]{:S(2)}, u32[]{:S(2)}) collective-permute-start(f32[16,4,8,256]{3,2,1,0:T(8,128)S(1)} %all_to_all.10.own), channel_id=1, source_target_pairs={{0,1},{1,0},{2,3},{3,2},{4,5},{5,4},{6,7},{7,6},{8,9},{9,8},{10,11... | collective-permute-start | bytes 1572872 | tf_op jit(solution)/shard_map/ppermute | solution.py:273
